TPU v7x, 128 devices: a whole 4x4x4 slice. The times are simulated.
128 devices in a mesh: dp: 2 (over core), context: 2 (over y_lo), expert: 32 (over z, x, y_hi).
Axes of the slice: x: 4, y: 4 (y_hi: 2, y_lo: 2; y = y_hi * 2 + y_lo), z: 4, core: 2. Of those that a mesh axis runs over, the one named last changes fastest.
Arguments:
- tokens: bfloat16 [64, 256, 2048], P(('dp', 'expert'), 'context'), may hold values from -16 to 16
- grad_output: bfloat16 [64, 256, 2048], P(('dp', 'expert'), 'context'), may hold values from -6 to 6
- routes: int32 [64, 256, 8], P(('dp', 'expert'), 'context'), may hold values from 0 to 31, all different within a row; in each aligned block of 128 rows (0 to 127, 128 to 255, ..., all dimensions but the last counted through in order) at most 40 rows name the same one
- positions: int32 [64, 256], P(('dp', 'expert')), may hold values from 0 to 255, as said below
- attn_gain: float32 [2048], replicated, may hold values from 0.5 to 1.5
- q_gain: float32 [2048], replicated, may hold values from 0.1 to 1.9
- k_gain: float32 [2048], replicated, may hold values from 0.1 to 1.9
- ffn_gain: float32 [2048], replicated, may hold values from 0.5 to 1.5
- qkv_weight: bfloat16 [3, 2048, 2048], P(None, ('dp', 'context', 'expert')), may hold values from -0.125 to 0.125
- out_weight: bfloat16 [2048, 2048], P(('dp', 'context', 'expert')), may hold values from -1 to 1
- router_weight: bfloat16 [2048, 32], replicated, may hold values from -0.25 to 0.25
- expert_in: bfloat16 [32, 2, 2048, 1024], P('expert'), may hold values from -0.125 to 0.125
- expert_out: bfloat16 [32, 1024, 2048], P('expert'), may hold values from -0.75 to 0.75
Outputs:
- output: float32 [64, 256, 2048], P(('dp', 'expert'), 'context')
- grad_tokens: float32 [64, 256, 2048], P(('dp', 'expert'), 'context')
- grad_attn_gain: float32 [2048], replicated
- grad_q_gain: float32 [2048], replicated
- grad_k_gain: float32 [2048], replicated
- grad_ffn_gain: float32 [2048], replicated
- grad_router: float32 [2048, 32], replicated
- grad_qkv_weight: float32 [3, 2048, 2048], P(None, ('dp', 'context', 'expert'))
- grad_out_weight: float32 [2048, 2048], P(('dp', 'context', 'expert'))
- grad_expert_in: float32 [32, 2, 2048, 1024], P('expert', None, ('dp', 'context'))
- grad_expert_out: float32 [32, 1024, 2048], P('expert', None, ('dp', 'context'))
Inputs may be any that keep to these rules, and one draw needn't show every extreme that they name: `routes`: each row names 8 different experts; the rows of one device name one expert at most 40 times. Each row is a permutation of the positions of one sequence.
All inputs are finite; a program needn't handle non-finite values.
Results may differ from a plain program's by a relative error of at most 0.019.
Values may be sent and summed in bfloat16 or wider, within the bound.
No kernel may reach another device: no remote copies, remote signals or barrier semaphores. Data moves between devices by JAX's collectives and lax.ppermute only.
A program may use at most 448 MiB of HBM per device.

v0:
```python
import jax
import jax.numpy as jnp
from jax import lax
from jax.sharding import PartitionSpec as P

HDIM = 128


EPS = 1e-05
THETA = 10000.0


def rope_tables(places, head_dim):
    half = head_dim // 2
    freq = THETA ** (-jnp.arange(half, dtype=jnp.float32) * 2.0 / head_dim)
    angle = places.astype(jnp.float32)[:, None] * freq[None, :]
    return (jnp.cos(angle), jnp.sin(angle))


def rotate(values, cosine, sine, sign):
    half = values.shape[-1] // 2
    first = values[..., :half]
    second = values[..., half:]
    cosine = cosine[:, None, :]
    sine = sign * sine[:, None, :]
    return jnp.concatenate(
        [first * cosine - second * sine, second * cosine + first * sine], axis=-1
    )


def rms_forward(values):
    factor = lax.rsqrt(jnp.mean(values * values, axis=-1, keepdims=True) + EPS)
    return (values * factor, factor)


def rms_backward(grad_out, normed, factor, gain):
    scaled = grad_out * gain
    grad_in = factor * (scaled - normed * jnp.mean(scaled * normed, axis=-1, keepdims=True))
    return (grad_in, jnp.sum(grad_out * normed, axis=0))


def slot_index(route_rows, experts, capacity):
    onehot = (route_rows[:, None] == jnp.arange(experts, dtype=jnp.int32)[None, :]).astype(
        jnp.int32
    )
    before = jnp.cumsum(onehot, axis=0) - onehot
    return route_rows * capacity + jnp.sum(before * onehot, axis=1)


def expert_major(received, local_experts, capacity):
    sources, _, width = received.shape
    return (
        received.reshape(sources, local_experts, capacity, width)
        .transpose(1, 0, 2, 3)
        .reshape(local_experts, sources * capacity, width)
    )


def source_major(results, sources, capacity):
    local_experts, _, width = results.shape
    return (
        results.reshape(local_experts, sources, capacity, width)
        .transpose(1, 0, 2, 3)
        .reshape(sources, local_experts * capacity, width)
    )


def body(
    tokens,
    grad_output,
    routes,
    positions,
    attn_gain,
    q_gain,
    k_gain,
    ffn_gain,
    qkv_weight,
    out_weight,
    router_weight,
    expert_in,
    expert_out,
):
    single_precision = jnp.float32
    bf16 = jnp.bfloat16
    seq_tok = tokens.shape[1]
    width = tokens.shape[2]
    top = routes.shape[2]
    heads_width = out_weight.shape[1]
    head_dim = HDIM
    heads = heads_width // head_dim
    local_experts = expert_in.shape[0]
    experts = router_weight.shape[1]
    sources = lax.axis_size("expert")
    capacity = min(seq_tok, seq_tok * top * 5 // (4 * experts))
    scale = head_dim ** (-0.5)
    x = tokens[0].astype(single_precision)
    normed1, factor1 = rms_forward(x)
    attention_input = (normed1 * attn_gain).astype(bf16)
    query_key_value_complete, out_full = (
        lax.all_gather(qkv_weight, ("dp", "context", "expert"), axis=1, tiled=True),
        lax.all_gather(out_weight, ("dp", "context", "expert"), axis=0, tiled=True),
    )
    projected_output = jnp.einsum(
        "hp,lpa->lha",
        attention_input,
        query_key_value_complete,
        preferred_element_type=single_precision,
    )
    q_normed, q_factor = rms_forward(projected_output[0])
    k_normed, k_factor = rms_forward(projected_output[1])
    values = projected_output[2].astype(bf16)
    all_places = positions[0]
    own_places = lax.dynamic_slice_in_dim(all_places, lax.axis_index("context") * seq_tok, seq_tok)
    cosine, sine = rope_tables(own_places, head_dim)
    queries = rotate(
        (q_normed * q_gain).reshape(seq_tok, heads, head_dim), cosine, sine, 1.0
    ).astype(bf16)
    own_keys = rotate(
        (k_normed * k_gain).reshape(seq_tok, heads, head_dim), cosine, sine, 1.0
    ).astype(bf16)
    keys, vals = (
        lax.all_gather(own_keys.reshape(seq_tok, heads_width), "context", axis=0, tiled=True),
        lax.all_gather(values, "context", axis=0, tiled=True),
    )
    seq_len = keys.shape[0]
    keys3 = keys.reshape(seq_len, heads, head_dim)
    vals3 = vals.reshape(seq_len, heads, head_dim)
    allowed = (all_places[None, :] <= own_places[:, None])[None]

    def masked_scores():
        scores = (
            jnp.einsum("qhd,khd->hqk", queries, keys3, preferred_element_type=single_precision)
            * scale
        )
        return jnp.where(allowed, scores, -jnp.inf)

    scores = masked_scores()
    lse = jnp.log(jnp.sum(jnp.exp(scores), axis=-1, keepdims=True))
    probs_b = jnp.exp(scores - lse).astype(bf16)
    attended = (
        jnp.einsum("hqk,khd->qhd", probs_b, vals3, preferred_element_type=single_precision)
        .astype(bf16)
        .reshape(seq_tok, heads_width)
    )
    mid = x + jnp.einsum("tq,dq->td", attended, out_full, preferred_element_type=single_precision)
    normed2, factor2 = rms_forward(mid)
    ffn_in = (normed2 * ffn_gain).astype(bf16)
    router_exp = jnp.exp(jnp.dot(ffn_in, router_weight, preferred_element_type=single_precision))
    router_probs = router_exp / jnp.sum(router_exp, axis=-1, keepdims=True)
    own_routes = routes[0]
    slots = slot_index(own_routes.reshape(-1), experts, capacity)
    send = (
        jnp.zeros((experts * capacity, width), bf16).at[slots].set(jnp.repeat(ffn_in, top, axis=0))
    )
    received = lax.all_to_all(
        send.reshape(sources, local_experts * capacity, width),
        "expert",
        split_axis=0,
        concat_axis=0,
        tiled=True,
    )
    rows = expert_major(received, local_experts, capacity)
    gate_up = jnp.einsum("lrd,lkdh->lkrh", rows, expert_in, preferred_element_type=single_precision)
    gate = gate_up[:, 0]
    up = gate_up[:, 1]
    sig = jax.nn.sigmoid(gate)
    hidden = (gate * sig * up).astype(bf16)
    results = jnp.einsum(
        "lrh,lhd->lrd", hidden, expert_out, preferred_element_type=single_precision
    ).astype(bf16)
    back = lax.all_to_all(
        source_major(results, sources, capacity), "expert", split_axis=0, concat_axis=0, tiled=True
    )
    route_out = back.reshape(experts * capacity, width)[slots].reshape(seq_tok, top, width)
    route_weight = jnp.take_along_axis(router_probs, own_routes, axis=1)
    output = mid + jnp.sum(route_weight[:, :, None] * route_out, axis=1)
    grad = grad_output[0].astype(single_precision)
    route_grad_weight = jnp.sum(grad[:, None, :] * route_out, axis=-1)
    route_grad = (
        (route_weight[:, :, None] * grad[:, None, :]).astype(bf16).reshape(seq_tok * top, width)
    )
    grad_send = jnp.zeros((experts * capacity, width), bf16).at[slots].set(route_grad)
    grad_received = lax.all_to_all(
        grad_send.reshape(sources, local_experts * capacity, width),
        "expert",
        split_axis=0,
        concat_axis=0,
        tiled=True,
    )
    grad_rows = expert_major(grad_received, local_experts, capacity)
    grad_hidden = jnp.einsum(
        "lrd,lhd->lrh", grad_rows, expert_out, preferred_element_type=single_precision
    )
    grad_down = jnp.einsum(
        "lrh,lrd->lhd", hidden, grad_rows, preferred_element_type=single_precision
    )
    grad_gate = (grad_hidden * up * sig * (1.0 + gate * (1.0 - sig))).astype(bf16)
    grad_up = (grad_hidden * gate * sig).astype(bf16)
    grad_gate_up = jnp.stack([grad_gate, grad_up], axis=1)
    grad_gate_up_w = jnp.einsum(
        "lrd,lkrh->lkdh", rows, grad_gate_up, preferred_element_type=single_precision
    )
    grad_rows_in = jnp.einsum(
        "lkrh,lkdh->lrd", grad_gate_up, expert_in, preferred_element_type=single_precision
    ).astype(bf16)
    grad_back = lax.all_to_all(
        source_major(grad_rows_in, sources, capacity),
        "expert",
        split_axis=0,
        concat_axis=0,
        tiled=True,
    )
    grad_route_in = grad_back.reshape(experts * capacity, width)[slots].reshape(seq_tok, top, width)
    grad_ffn_in = jnp.sum(grad_route_in, axis=1, dtype=single_precision)
    chosen = (own_routes[:, :, None] == jnp.arange(experts, dtype=jnp.int32)[None, None, :]).astype(
        single_precision
    )
    grad_probs = jnp.sum(route_grad_weight[:, :, None] * chosen, axis=1)
    grad_logits = (
        router_probs * (grad_probs - jnp.sum(router_probs * grad_probs, axis=-1, keepdims=True))
    ).astype(bf16)
    grad_router = jnp.einsum(
        "td,te->de", ffn_in, grad_logits, preferred_element_type=single_precision
    )
    grad_ffn_in = grad_ffn_in + jnp.einsum(
        "te,de->td", grad_logits, router_weight, preferred_element_type=single_precision
    )
    grad_mid_norm, grad_ffn_gain = rms_backward(grad_ffn_in, normed2, factor2, ffn_gain)
    grad_mid = grad + grad_mid_norm
    grad_mid_b = grad_mid.astype(bf16)
    grad_out_w = jnp.einsum(
        "td,tq->dq", grad_mid_b, attended, preferred_element_type=single_precision
    )
    grad_att = (
        jnp.einsum("td,dq->tq", grad_mid_b, out_full, preferred_element_type=single_precision)
        .astype(bf16)
        .reshape(seq_tok, heads, head_dim)
    )
    delta = jnp.sum(
        grad_att.astype(single_precision)
        * attended.reshape(seq_tok, heads, head_dim).astype(single_precision),
        axis=-1,
    )
    probs = jnp.exp(masked_scores() - lse)
    grad_vals = jnp.einsum(
        "hqk,qhd->khd", probs.astype(bf16), grad_att, preferred_element_type=single_precision
    )
    grad_p = jnp.einsum("qhd,khd->hqk", grad_att, vals3, preferred_element_type=single_precision)
    grad_scores = (probs * (grad_p - delta.T[:, :, None])).astype(bf16)
    grad_queries = (
        jnp.einsum("hqk,khd->qhd", grad_scores, keys3, preferred_element_type=single_precision)
        * scale
    )
    grad_keys_all = (
        jnp.einsum("hqk,qhd->khd", grad_scores, queries, preferred_element_type=single_precision)
        * scale
    )
    grad_keys, grad_values = (
        lax.psum_scatter(
            grad_keys_all.reshape(seq_len, heads_width).astype(jnp.bfloat16),
            "context",
            scatter_dimension=0,
            tiled=True,
        ).astype(jnp.float32),
        lax.psum_scatter(
            grad_vals.reshape(seq_len, heads_width).astype(jnp.bfloat16),
            "context",
            scatter_dimension=0,
            tiled=True,
        ).astype(jnp.float32),
    )
    grad_qn = rotate(grad_queries, cosine, sine, -1.0).reshape(seq_tok, heads_width)
    grad_kn = rotate(grad_keys.reshape(seq_tok, heads, head_dim), cosine, sine, -1.0).reshape(
        seq_tok, heads_width
    )
    grad_q_raw, grad_q_gain = rms_backward(grad_qn, q_normed, q_factor, q_gain)
    grad_k_raw, grad_k_gain = rms_backward(grad_kn, k_normed, k_factor, k_gain)
    projected_gradient = jnp.stack([grad_q_raw, grad_k_raw, grad_values]).astype(bf16)
    query_key_value_gradient = jnp.einsum(
        "gu,sgx->sux", attention_input, projected_gradient, preferred_element_type=single_precision
    )
    attention_input_gradient = jnp.einsum(
        "yaz,ygz->ag",
        projected_gradient,
        query_key_value_complete,
        preferred_element_type=single_precision,
    )
    grad_x_norm, grad_attn_gain = rms_backward(
        attention_input_gradient, normed1, factor1, attn_gain
    )
    grad_tokens = grad_mid + grad_x_norm
    grad_in_shard, grad_down_shard = (
        lax.psum_scatter(
            grad_gate_up_w.astype(jnp.bfloat16), ("dp", "context"), scatter_dimension=2, tiled=True
        ).astype(jnp.float32),
        lax.psum_scatter(
            grad_down.astype(jnp.bfloat16), ("dp", "context"), scatter_dimension=2, tiled=True
        ).astype(jnp.float32),
    )
    grad_qkv_shard, grad_out_shard = (
        lax.psum_scatter(
            query_key_value_gradient, ("dp", "context", "expert"), scatter_dimension=1, tiled=True
        ),
        lax.psum_scatter(grad_out_w, ("dp", "context", "expert"), scatter_dimension=0, tiled=True),
    )
    totals = lax.psum(
        (grad_attn_gain, grad_q_gain, grad_k_gain, grad_ffn_gain, grad_router),
        ("dp", "context", "expert"),
    )
    return (
        output[None],
        grad_tokens[None],
        totals[0],
        totals[1],
        totals[2],
        totals[3],
        totals[4],
        grad_qkv_shard,
        grad_out_shard,
        grad_in_shard,
        grad_down_shard,
    )


def solution(mesh):
    return jax.shard_map(
        body,
        mesh=mesh,
        in_specs=(
            P(("dp", "expert"), "context", None),
            P(("dp", "expert"), "context", None),
            P(("dp", "expert"), "context", None),
            P(("dp", "expert"), None),
            P(),
            P(),
            P(),
            P(),
            P(None, ("dp", "context", "expert"), None),
            P(("dp", "context", "expert"), None),
            P(),
            P("expert", None, None, None),
            P("expert", None, None),
        ),
        out_specs=(
            P(("dp", "expert"), "context", None),
            P(("dp", "expert"), "context", None),
            P(),
            P(),
            P(),
            P(),
            P(),
            P(None, ("dp", "context", "expert"), None),
            P(("dp", "context", "expert"), None),
            P("expert", None, ("dp", "context"), None),
            P("expert", None, ("dp", "context")),
        ),
        check_vma=False,
    )
```

profile of v0, /device:TPU:1, one launch (start us, length us, event | category | flops | bytes accessed | tf_op | source)
XLA Modules:
  0.0 2451.1 jit_solution(18366620147811484429)
XLA Ops:
  10.9 229.2 %all-gather.6.cloned.1.call-done = bf16[3,2048,2048]{2,1,0:T(8,128)(2,1)} async-done(((bf16[3,16,2048]{2,1,0:T(8,128)(2,1)}), bf16[3,2048,2048]{2,1,0:T(8,128)(2,1)}) %all-gather.6.cloned.1.call-update) | async-done | bytes 25165840 | tf_op jit(solution)/shard_map/all_gather | solution.py:100
  240.1 10.2 convolution_bitcast_fusion.1
  259.9 9.0 reduce-window.6
  269.5 6.1 all-gather.12.cloned.1.call-done
  277.0 25.6 %all-gather.8.cloned.1.call-done = bf16[256,2048]{0,1:T(8,128)(2,1)} async-done(((bf16[128,2048]{0,1:T(8,128)(2,1)}), bf16[256,2048]{0,1:T(8,128)(2,1)}) %all-gather.8.cloned.1.call-update) | async-done | bytes 1048592 | tf_op jit(solution)/shard_map/all_gather | solution.py:122
  302.6 3.1 fusion.77
  305.7 3.5 convolution_convert_fusion.3
  309.3 199.0 %all-gather.10.cloned.1.call-done = bf16[2048,2048]{1,0:T(8,128)(2,1)} async-done(((bf16[16,2048]{1,0:T(8,128)(2,1)}), bf16[2048,2048]{1,0:T(8,128)(2,1)}) %all-gather.10.cloned.1.call-update) | async-done | bytes 8388624 | tf_op jit(solution)/shard_map/all_gather | solution.py:101
  508.3 6.4 multiply_reduce_fusion.7
  514.9 9.6 scatter_custom_fusion
  524.6 7.1 all-to-all-start
  533.4 7.0 gather_fusion.2
  540.5 10.0 scatter_custom_fusion.1
  550.5 47.6 %all-to-all-done = bf16[32,40,2048]{2,1,0:T(8,128)(2,1)} async-done(((bf16[32,40,2048]{2,1,0:T(8,128)(2,1)}), bf16[32,40,2048]{2,1,0:T(8,128)(2,1)}, u32[]{:S(2)}, u32[]{:S(2)}) %all-to-all-start) | async-done | bytes 5242912 | tf_op jit(solution)/shard_map/all_to_all | solution.py:155
  598.1 9.5 all-to-all-start.2
  607.6 16.9 fusion.7
  626.2 3.3 copy-done.8
  631.0 7.3 convolution_convert_fusion
  638.3 35.5 %all-to-all-done.2 = bf16[32,40,2048]{2,1,0:T(8,128)(2,1)} async-done(((bf16[32,40,2048]{2,1,0:T(8,128)(2,1)}), bf16[32,40,2048]{2,1,0:T(8,128)(2,1)}, u32[]{:S(2)}, u32[]{:S(2)}) %all-to-all-start.2) | async-done | bytes 5242912 | tf_op jit(solution)/shard_map/all_to_all | solution.py:183
  673.8 8.5 all-to-all-start.1
  682.3 13.1 fusion.33
  697.7 15.1 bitcast_convert_fusion
  712.8 36.3 %all-to-all-done.1 = bf16[32,40,2048]{2,1,0:T(8,128)(2,1)} async-done(((bf16[32,40,2048]{2,1,0:T(8,128)(2,1)}), bf16[32,40,2048]{2,1,0:T(8,128)(2,1)}, u32[]{:S(2)}, u32[]{:S(2)}) %all-to-all-start.1) | async-done | bytes 5242912 | tf_op jit(solution)/shard_map/all_to_all | solution.py:171
  749.0 6.1 all-to-all-start.3
  755.3 4.5 fusion.34
  759.8 12.4 gather_fusion
  772.2 5.9 fusion.2
  778.2 42.9 %all-to-all-done.3 = bf16[32,40,2048]{2,1,0:T(8,128)(2,1)} async-done(((bf16[32,40,2048]{2,1,0:T(8,128)(2,1)}), bf16[32,40,2048]{2,1,0:T(8,128)(2,1)}, u32[]{:S(2)}, u32[]{:S(2)}) %all-to-all-start.3) | async-done | bytes 5242912 | tf_op jit(solution)/shard_map/all_to_all | solution.py:206
  821.1 12.0 gather_fusion.1
  833.1 5.2 convert_reduce_fusion
  841.2 4.7 convolution_convert_fusion.1
  853.2 3.4 convolution_convert_fusion.2
  858.1 10.1 convert_bitcast_fusion.1
  868.2 16.6 convert_bitcast_fusion
  886.5 3.5 reduce-scatter.16.cloned.1.call-done
  908.3 8.5 reduce-scatter.8.cloned.1.call-done
  916.8 21.7 convolution_bitcast_fusion
  938.5 71.2 %copy.148 = f32[3,2048,2048]{2,0,1:T(4,128)} copy(f32[3,2048,2048]{1,2,0:T(8,128)} %convolution_bitcast_fusion) | data formatting | bytes 100663296 | tf_op jit(solution)/shard_map/gu,sgx->sux/transpose | solution.py:279
  1012.0 8.1 fusion.70
  1021.7 14.5 fusion.50
  1036.1 66.7 %all-reduce.1 = (f32[2048]{0:T(1024)}, f32[2048]{0:T(1024)}, f32[2048]{0:T(1024)}, f32[2048]{0:T(1024)}) all-reduce(f32[2048]{0:T(1024)S(1)} %get-tuple-element.78, f32[2048]{0:T(1024)S(1)} %get-tuple-element.73, f32[2048]{0:T(1024)S(1)} %get-tuple-element.66, ...), channel_id=1, replica_groups=mesh['dp'=2,'context'=2,'expert'=32] {'dp','context','expert'}, use_global_device_ids=true, to_apply=%region_24.25 | all-reduce | flops 8192 | bytes 65536 | tf_op jit(solution)/shard_map/psum | solution.py:306
  1102.8 2.6 fusion.49
  1105.4 2.9 convert_element_type.208
  1108.3 43.6 %reduce-scatter.12.cloned.1.call-done = bf16[1,2,512,1024]{2,3,1,0:T(8,128)(2,1)} async-done(((bf16[1,2,2048,1024]{2,3,1,0:T(8,128)(2,1)}), bf16[1,2,512,1024]{2,3,1,0:T(8,128)(2,1)}) %reduce-scatter.12.cloned.1.call-update) | async-done | bytes 2097168 | tf_op jit(solution)/shard_map/reduce_scatter | solution.py:293
  1151.8 4.1 copy.151
  1155.9 453.7 %all-reduce.7.cloned.1.call-done = f32[3,2048,2048]{2,0,1:T(4,128)} async-done(((f32[3,2048,2048]{2,0,1:T(4,128)}), f32[3,2048,2048]{2,0,1:T(4,128)}) %all-reduce.7.cloned.1.call-update) | async-done | bytes 50331664
  1611.8 144.6 %all-reduce.5.cloned.1.call-done = f32[2048,32]{0,1:T(8,128)} async-done(((f32[2048,32]{0,1:T(8,128)}), f32[2048,32]{0,1:T(8,128)}) %all-reduce.5.cloned.1.call-update) | async-done | bytes 262160 | tf_op jit(solution)/shard_map/psum | solution.py:306
  1756.3 686.3 %reduce-scatter.10.cloned.1.call-done = f32[16,2048]{1,0:T(8,128)} async-done(((f32[2048,2048]{1,0:T(8,128)}), f32[16,2048]{1,0:T(8,128)}) %reduce-scatter.10.cloned.1.call-update) | async-done | bytes 131088 | tf_op jit(solution)/shard_map/reduce_scatter | solution.py:304
  (193 shorter events, 61.4 us)
Async XLA Ops:
  7.2 525.9 %copy-start = (bf16[2048,32]{0,1:T(8,128)(2,1)S(1)}, bf16[2048,32]{0,1:T(8,128)(2,1)}, u32[]{:S(2)}) copy-start(bf16[2048,32]{0,1:T(8,128)(2,1)} %param.23) | copy-start | bytes 393220
  7.2 232.9 %all-gather.6.cloned.1.call-start = ((), (), s32[]{:S(2)}) async-start(), calls=%async_computation.9 | async-start | bytes 25362432 | tf_op jit(solution)/shard_map/all_gather | solution.py:100
  7.9 267.6 %all-gather.12.cloned.1.call-start = ((), (), s32[]{:S(2)}) async-start(), calls=%async_computation.17 | async-start | bytes 1572864 | tf_op jit(solution)/shard_map/all_gather | solution.py:123
  9.9 240.5 %copy-start.36 = (f32[128]{0:T(128)}, f32[128]{0:T(128)S(1)}, u32[]{:S(2)}) copy-start(f32[128]{0:T(128)S(1)} %add_rsqrt_fusion.3) | copy-start | bytes 1540
  10.8 245.7 %copy-start.25 = (f32[128,64]{1,0:T(8,128)}, f32[128,64]{1,0:T(8,128)S(1)}, u32[]{:S(2)}) copy-start(f32[128,64]{1,0:T(8,128)S(1)} %get-tuple-element.110) | copy-start | bytes 98308
  250.4 5.5 copy-start.2
  251.3 4.5 copy-start.31
  252.9 3.3 copy-start.33
  252.9 49.7 %all-gather.8.cloned.1.call-start = ((), (), s32[]{:S(2)}) async-start(), calls=%async_computation.10 | async-start | bytes 1572864 | tf_op jit(solution)/shard_map/all_gather | solution.py:122
  253.0 3.6 copy-start.38
  253.0 3.6 copy-start.40
  256.6 2.8 copy-start.35
  256.6 12.8 copy-start.42
  257.4 48.3 %copy-start.13 = (bf16[128,16,64]{2,0,1:T(8,128)(2,1)}, bf16[128,16,64]{2,0,1:T(8,128)(2,1)S(1)}, u32[]{:S(2)}) copy-start(bf16[128,16,64]{2,0,1:T(8,128)(2,1)S(1)} %get-tuple-element.97) | copy-start | bytes 786436
  258.8 249.5 %all-gather.10.cloned.1.call-start = ((), (), s32[]{:S(2)}) async-start(), calls=%async_computation.11 | async-start | bytes 8454144 | tf_op jit(solution)/shard_map/all_gather | solution.py:101
  277.0 32.2 %copy-start.20 = (bf16[32,8,16,128]{3,2,1,0:T(8,128)(2,1)}, bf16[32,8,16,128]{3,2,1,0:T(8,128)(2,1)S(1)}, u32[]{:S(2)}) copy-start(bf16[32,8,16,128]{3,2,1,0:T(8,128)(2,1)S(1)} %copy.164) | copy-start | bytes 3145732
  302.6 205.7 %copy-start.6 = (bf16[1,128,2048]{2,1,0:T(8,128)(2,1)S(1)}, bf16[1,128,2048]{2,1,0:T(8,128)(2,1)}, u32[]{:S(2)}) copy-start(bf16[1,128,2048]{2,1,0:T(8,128)(2,1)} %param.13) | copy-start | bytes 1572868
  309.3 205.5 %copy-start.15 = (bf16[16,128,128]{2,1,0:T(8,128)(2,1)}, bf16[16,128,128]{2,1,0:T(8,128)(2,1)S(1)}, u32[]{:S(2)}) copy-start(bf16[16,128,128]{2,1,0:T(8,128)(2,1)S(1)} %convolution_convert_fusion.3) | copy-start | bytes 1572868
  508.3 6.5 copy-start.30
  514.9 18.2 copy-start.11
  524.6 73.5 %all-to-all-start = ((bf16[32,40,2048]{2,1,0:T(8,128)(2,1)}), bf16[32,40,2048]{2,1,0:T(8,128)(2,1)}, u32[]{:S(2)}, u32[]{:S(2)}) async-start(bf16[32,40,2048]{2,1,0:T(8,128)(2,1)} %bitcast.222), calls=%async_computation | async-start | bytes 10485760 | tf_op jit(solution)/shard_map/all_to_all | solution.py:155
  598.1 75.7 %all-to-all-start.2 = ((bf16[32,40,2048]{2,1,0:T(8,128)(2,1)}), bf16[32,40,2048]{2,1,0:T(8,128)(2,1)}, u32[]{:S(2)}, u32[]{:S(2)}) async-start(bf16[32,40,2048]{2,1,0:T(8,128)(2,1)} %bitcast.223), calls=%async_computation.2 | async-start | bytes 10485760 | tf_op jit(solution)/shard_map/all_to_all | solution.py:183
  624.5 5.0 copy-start.8
  624.5 6.5 copy-start.43
  673.8 75.2 %all-to-all-start.1 = ((bf16[32,40,2048]{2,1,0:T(8,128)(2,1)}), bf16[32,40,2048]{2,1,0:T(8,128)(2,1)}, u32[]{:S(2)}, u32[]{:S(2)}) async-start(bf16[32,40,2048]{2,1,0:T(8,128)(2,1)} %bitcast.225), calls=%async_computation.1 | async-start | bytes 10485760 | tf_op jit(solution)/shard_map/all_to_all | solution.py:171
  749.0 72.1 %all-to-all-start.3 = ((bf16[32,40,2048]{2,1,0:T(8,128)(2,1)}), bf16[32,40,2048]{2,1,0:T(8,128)(2,1)}, u32[]{:S(2)}, u32[]{:S(2)}) async-start(bf16[32,40,2048]{2,1,0:T(8,128)(2,1)} %bitcast.224), calls=%async_computation.3 | async-start | bytes 10485760 | tf_op jit(solution)/shard_map/all_to_all | solution.py:206
  755.1 134.9 %reduce-scatter.16.cloned.1.call-start = ((), (), s32[]{:S(2)}) async-start(), calls=%async_computation.18 | async-start | bytes 1572864
  833.1 5.7 copy-start.18
  833.1 5.7 copy-start.24
  841.2 5.0 copy-start.16
  846.0 3.0 copy-start.14
  853.0 63.9 %reduce-scatter.8.cloned.1.call-start = ((), (), s32[]{:S(2)}) async-start(), calls=%async_computation.12 | async-start | bytes 1572864 | tf_op jit(solution)/shard_map/reduce_scatter | solution.py:265
  858.0 247.4 %reduce-scatter.14.cloned.1.call-start = ((), (), s32[]{:S(2)}) async-start(), calls=%async_computation.16 | async-start | bytes 5242880 | tf_op jit(solution)/shard_map/reduce_scatter | solution.py:296
  868.2 283.6 %reduce-scatter.12.cloned.1.call-start = ((), (), s32[]{:S(2)}) async-start(), calls=%async_computation.15 | async-start | bytes 10485760 | tf_op jit(solution)/shard_map/reduce_scatter | solution.py:293
  884.9 9.2 copy-start.26
  884.9 9.2 copy-start.28
  884.9 724.8 %all-reduce.7.cloned.1.call-start = ((), (), s32[]{:S(2)}) async-start(), calls=%async_computation.19 | async-start | bytes 134217728
  898.3 6.2 copy-start.3
  898.3 6.2 copy-start.32
  898.3 6.2 copy-start.34
  898.3 6.2 copy-start.39
  898.3 6.2 copy-start.41
  904.4 2.4 copy-start.9
  904.5 12.3 copy-start.29
  904.5 12.3 copy-start.37
  1009.7 746.6 %all-reduce.5.cloned.1.call-start = ((), (), s32[]{:S(2)}) async-start(), calls=%async_computation.13 | async-start | bytes 524288 | tf_op jit(solution)/shard_map/psum | solution.py:306
  1011.7 1430.9 %reduce-scatter.10.cloned.1.call-start = ((), (), s32[]{:S(2)}) async-start(), calls=%async_computation.14 | async-start | bytes 16908288 | tf_op jit(solution)/shard_map/reduce_scatter | solution.py:304
  1105.4 1338.9 %copy-start.1 = (bf16[2048,32]{0,1:T(8,128)(2,1)S(1)}, bf16[2048,32]{0,1:T(8,128)(2,1)}, u32[]{:S(2)}) copy-start(bf16[2048,32]{0,1:T(8,128)(2,1)} %param.23) | copy-start | bytes 393220
  (13 other events, 20.6 us)
Sparse Core Ops, SparseCore 0:
  9.8 230.2 all-gather.5
  253.0 22.5 all-gather.11
  277.8 24.7 all-gather.7
  304.2 204.0 all-gather.9
  853.1 36.9 reduce-scatter.15
  893.0 23.8 reduce-scatter.7
  919.8 80.2 reduce-scatter.13
  1002.7 149.0 reduce-scatter.11
  1158.7 450.8 all-reduce.6
  1614.8 141.4 all-reduce.4
  1759.3 683.2 reduce-scatter.9
where the time goes:
time: 2460 us; the launch traced here: 2450 us
  waiting for transfers between devices  1960 us (80%)
  matrix products  161 us (7%)
  local copies, waits for them, and re-layouts  153 us (6%)
  blocking collectives  66.7 us (3%)
  other arithmetic  59.2 us (2%)
  starting transfers between devices  32.7 us (1%)
    reduce_scatter x1, waiting for transfers between devices, body(): lax.psum_scatter(grad_out_w, ('dp', 'context', 'expert'), scatter_dimensi...  686 us
    unnamed x13, waiting for transfers between devices  458 us
    all_gather x1, waiting for transfers between devices, body(): lax.all_gather(qkv_weight, ('dp', 'context', 'expert'), axis=1, tiled=True)  229 us
    all_gather x1, waiting for transfers between devices, body(): lax.all_gather(out_weight, ('dp', 'context', 'expert'), axis=0, tiled=True)  199 us
    psum x1, waiting for transfers between devices, body(): lax.psum((grad_attn_gain, grad_q_gain, grad_k_gain, grad_ffn_gain, grad_r...  145 us
    transpose x1, local copies, waits for them, and re-layouts, body(): jnp.einsum('gu,sgx->sux', attention_input, projected_gradient, preferred_...  71.2 us
    psum x1, blocking collectives, body(): lax.psum((grad_attn_gain, grad_q_gain, grad_k_gain, grad_ffn_gain, grad_r...  66.7 us
  transfers between devices with their start and end apart: 15, of which 14 were waited for; matrix products, arithmetic and copies ran while one was open for 12% of the time, Pallas kernels for 0%

commit v1 on v0

--- a/solution.py
+++ b/solution.py
@@ -96,10 +96,12 @@
     x = tokens[0].astype(single_precision)
     normed1, factor1 = rms_forward(x)
     attention_input = (normed1 * attn_gain).astype(bf16)
-    query_key_value_complete, out_full = (
-        lax.all_gather(qkv_weight, ("dp", "context", "expert"), axis=1, tiled=True),
-        lax.all_gather(out_weight, ("dp", "context", "expert"), axis=0, tiled=True),
-    )
+    all_axes = ("dp", "context", "expert")
+    weights_full = lax.all_gather(
+        jnp.concatenate([qkv_weight, out_weight[None]], axis=0), all_axes, axis=1, tiled=True
+    )
+    query_key_value_complete = weights_full[:3]
+    out_full = weights_full[3]
     projected_output = jnp.einsum(
         "hp,lpa->lha",
         attention_input,
@@ -289,24 +291,34 @@
         attention_input_gradient, normed1, factor1, attn_gain
     )
     grad_tokens = grad_mid + grad_x_norm
-    grad_in_shard, grad_down_shard = (
-        lax.psum_scatter(
-            grad_gate_up_w.astype(jnp.bfloat16), ("dp", "context"), scatter_dimension=2, tiled=True
-        ).astype(jnp.float32),
-        lax.psum_scatter(
-            grad_down.astype(jnp.bfloat16), ("dp", "context"), scatter_dimension=2, tiled=True
-        ).astype(jnp.float32),
-    )
-    grad_qkv_shard, grad_out_shard = (
-        lax.psum_scatter(
-            query_key_value_gradient, ("dp", "context", "expert"), scatter_dimension=1, tiled=True
-        ),
-        lax.psum_scatter(grad_out_w, ("dp", "context", "expert"), scatter_dimension=0, tiled=True),
-    )
-    totals = lax.psum(
-        (grad_attn_gain, grad_q_gain, grad_k_gain, grad_ffn_gain, grad_router),
-        ("dp", "context", "expert"),
-    )
+    def scatter_over_copies(values):
+        values = lax.psum_scatter(values.astype(bf16), "dp", scatter_dimension=1, tiled=True)
+        values = lax.psum_scatter(values, "context", scatter_dimension=1, tiled=True)
+        return values.astype(single_precision)
+
+    grad_in_shard = scatter_over_copies(grad_gate_up_w[0])[None]
+    grad_down_shard = scatter_over_copies(grad_down[0])[None]
+    small = jnp.concatenate(
+        [grad_attn_gain, grad_q_gain, grad_k_gain, grad_ffn_gain, grad_router.reshape(-1)]
+    )
+    small_rows = -(-small.shape[0] // width)
+    pad_rows = 64
+    small = jnp.pad(small, (0, pad_rows * width - small.shape[0])).reshape(pad_rows, width)
+    stacked = jnp.concatenate(
+        [query_key_value_gradient.reshape(3 * width, heads_width), grad_out_w, small], axis=0
+    )
+    summed = lax.psum(stacked, all_axes)
+    shard_rows = width // lax.axis_size(all_axes)
+    start = lax.axis_index(all_axes) * shard_rows
+    weight_sums = summed[: 4 * width].reshape(4, width, heads_width)
+    weight_shard = lax.dynamic_slice_in_dim(weight_sums, start, shard_rows, axis=1)
+    grad_qkv_shard = weight_shard[:3]
+    grad_out_shard = weight_shard[3]
+    small_sum = summed[4 * width : 4 * width + small_rows].reshape(-1)
+    sizes = [width, heads_width, heads_width, width, width * experts]
+    offsets = [sum(sizes[:n]) for n in range(len(sizes))]
+    totals = [small_sum[o : o + n] for o, n in zip(offsets, sizes)]
+    totals[4] = totals[4].reshape(width, experts)
     return (
         output[None],
         grad_tokens[None],

time: 2460 us -> 1450 us (0.59)
  waiting for transfers between devices: 1960 us -> 865 us
  other arithmetic: 59.2 us -> 138 us
  blocking collectives: 66.7 us -> 0 us
  local copies, waits for them, and re-layouts: 153 us -> 208 us
    reduce_scatter x4, waiting for transfers between devices: 738 us -> 16.9 us  [the longest x2 16.9 us: scatter_over_copies(): lax.psum_scatter(values.astype(bf16), 'dp', scatter_dimension=1, tiled=True)]
    unnamed x13 -> x12, waiting for transfers between devices: 458 us -> 3.21 us
    psum x1, waiting for transfers between devices: 145 us -> 448 us  [body(): summed = lax.psum(stacked, all_axes)]
    all_gather x2 -> x1, waiting for transfers between devices: 428 us -> 238 us  [body(): lax.all_gather(jnp.concatenate([qkv_weight, out_weight[None]], axis=0), a...]
    slice x2 -> x7, local copies, waits for them, and re-layouts: 0.22 us -> 71.7 us  [the longest x1 44 us: body(): weight_sums = summed[:4 * width].reshape(4, width, heads_width)]
    transpose x1 -> x0, local copies, waits for them, and re-layouts: 71.2 us -> none  [body(): jnp.einsum('gu,sgx->sux', attention_input, projected_gradient, preferred_...]
    psum x1 -> x0, blocking collectives: 66.7 us -> none  [body(): lax.psum((grad_attn_gain, grad_q_gain, grad_k_gain, grad_ffn_gain, grad_r...]
    concatenate x0 -> x2, other arithmetic: none -> 61.5 us  [the longest x1 60.5 us: body(): jnp.concatenate([query_key_value_gradient.reshape(3 * width, heads_width)...]
  transfers between devices with their start and end apart: 15 -> 14, of which waited for: 14 -> 9; matrix products, arithmetic and copies ran while one was open for 12% -> 25% of each run, Pallas kernels for 0% -> 0%
where the time goes in v1:
time: 1450 us; the launch traced here: 1430 us
  waiting for transfers between devices  865 us (60%)
  local copies, waits for them, and re-layouts  208 us (14%)
  matrix products  172 us (12%)
  other arithmetic  138 us (10%)
  starting transfers between devices  35.6 us (2%)
  between operations  15.3 us (1%)
    psum x1, waiting for transfers between devices, body(): summed = lax.psum(stacked, all_axes)  448 us
    all_gather x1, waiting for transfers between devices, body(): lax.all_gather(jnp.concatenate([qkv_weight, out_weight[None]], axis=0), a...  238 us
    unnamed x106, local copies, waits for them, and re-layouts  73.3 us
    concatenate x1, other arithmetic, body(): jnp.concatenate([query_key_value_gradient.reshape(3 * width, heads_width)...  60.5 us
    all_to_all x1, waiting for transfers between devices, body(): lax.all_to_all(send.reshape(sources, local_experts * capacity, width), 'e...  48.6 us
    slice x1, local copies, waits for them, and re-layouts, body(): weight_sums = summed[:4 * width].reshape(4, width, heads_width)  44 us
    all_to_all x1, waiting for transfers between devices, body(): lax.all_to_all(grad_send.reshape(sources, local_experts * capacity, width...  37.2 us
    all_to_all x1, waiting for transfers between devices, body(): lax.all_to_all(source_major(results, sources, capacity), 'expert', split_...  35.1 us
  transfers between devices with their start and end apart: 14, of which 9 were waited for; matrix products, arithmetic and copies ran while one was open for 25% of the time, Pallas kernels for 0%

profile of v1, /device:TPU:1, one launch (start us, length us, event | category | flops | bytes accessed | tf_op | source)
XLA Modules:
  0.0 1434.6 jit_solution(13009681973752688844)
XLA Ops:
  12.1 238.4 %all-gather.5.cloned.1.call-done = bf16[4,2048,2048]{2,0,1:T(4,128)(2,1)} async-done(((bf16[4,16,2048]{2,0,1:T(4,128)(2,1)}), bf16[4,2048,2048]{2,0,1:T(4,128)(2,1)}) %all-gather.5.cloned.1.call-update) | async-done | bytes 33554448 | tf_op jit(solution)/shard_map/all_gather | solution.py:100
  250.6 48.4 %copy.217 = bf16[3,2048,2048]{1,2,0:T(8,128)(2,1)} copy(bf16[3,2048,2048]{2,0,1:T(4,128)(2,1)} %bitcast.261) | data formatting | bytes 50331648
  299.0 11.9 convolution_bitcast_fusion
  312.6 2.6 copy.169
  326.7 16.1 %reduce-window.6 = s32[32,8,128]{2,1,0:T(8,128)S(1)} reduce-window(s32[32,8,128]{2,1,0:T(8,128)} %fusion.79, s32[]{:T(128)} %constant.31.clone.1), window={size=1x1x128 pad=0_0x0_0x127_0}, to_apply=%region_6.7 | reduce-window | flops 4161536 | bytes 262148 | tf_op jit(solution)/shard_map/reduce-window
  345.9 21.5 %slice.138 = bf16[1,2048,2048]{2,0,1:T(2,128)(2,1)} slice(bf16[4,2048,2048]{2,0,1:T(4,128)(2,1)} %all-gather.5.cloned.1.call-done), slice={[3:4], [0:2048], [0:2048]} | slice | bytes 16777216 | tf_op jit(solution)/shard_map/slice | solution.py:104
  367.5 3.1 fusion.80
  370.6 4.6 all-gather.9.cloned.1.call-done
  375.2 3.7 convolution_convert_fusion.3
  378.9 11.4 multiply_reduce_fusion.5
  390.4 9.7 scatter_custom_fusion
  400.2 9.2 all-to-all-start
  411.1 7.0 gather_fusion.2
  418.1 10.0 scatter_custom_fusion.1
  428.2 48.6 %all-to-all-done = bf16[32,40,2048]{2,1,0:T(8,128)(2,1)} async-done(((bf16[32,40,2048]{2,1,0:T(8,128)(2,1)}), bf16[32,40,2048]{2,1,0:T(8,128)(2,1)}, u32[]{:S(2)}, u32[]{:S(2)}) %all-to-all-start) | async-done | bytes 5242912 | tf_op jit(solution)/shard_map/all_to_all | solution.py:157
  476.8 11.0 all-to-all-start.2
  487.8 16.9 %fusion.7 = f32[1,2,1280,1024]{3,2,1,0:T(8,128)S(1)} fusion(bf16[1280,2048,1]{1,0,2:T(8,128)(2,1)} %bitcast.26, bf16[1,2,2048,1024]{3,2,1,0:T(8,128)(2,1)} %param.24), kind=kOutput, calls=%fused_computation.21 | convolution fusion | flops 10737418240 | bytes 24117248 | tf_op jit(solution)/shard_map/lrd,lkdh->lkrh/dot_general | solution.py:165
  506.3 3.3 copy-done.4
  511.1 7.3 convolution_convert_fusion
  518.5 37.2 %all-to-all-done.2 = bf16[32,40,2048]{2,1,0:T(8,128)(2,1)} async-done(((bf16[32,40,2048]{2,1,0:T(8,128)(2,1)}), bf16[32,40,2048]{2,1,0:T(8,128)(2,1)}, u32[]{:S(2)}, u32[]{:S(2)}) %all-to-all-start.2) | async-done | bytes 5242912 | tf_op jit(solution)/shard_map/all_to_all | solution.py:185
  555.7 6.8 all-to-all-start.1
  562.4 13.1 fusion.35
  577.8 15.1 %bitcast_convert_fusion = bf16[1280,2048]{1,0:T(8,128)(2,1)} fusion(bf16[1,2,2048,1024]{3,2,1,0:T(8,128)(2,1)} %param.24, bf16[1,1,1280,1024]{3,2,1,0:T(8,128)(2,1)S(1)} %get-tuple-element.98, bf16[1,1,1280,1024]{3,2,1,0:T(8,128)(2,1)S(1)} %get-tuple-element.97), kind=kOutput, calls=%fused_computation.9 | convolution fusion | flops 10742661120 | bytes 18874368 | tf_op jit(solution)/shard_map/lkrh,lkdh->lrd/dot_general | solution.py:205
  592.9 35.1 %all-to-all-done.1 = bf16[32,40,2048]{2,1,0:T(8,128)(2,1)} async-done(((bf16[32,40,2048]{2,1,0:T(8,128)(2,1)}), bf16[32,40,2048]{2,1,0:T(8,128)(2,1)}, u32[]{:S(2)}, u32[]{:S(2)}) %all-to-all-start.1) | async-done | bytes 5242912 | tf_op jit(solution)/shard_map/all_to_all | solution.py:173
  628.0 8.0 all-to-all-start.3
  636.1 10.1 convolution_convert_fusion.1
  646.6 4.5 fusion.38
  651.0 12.0 gather_fusion
  663.0 6.2 fusion.2
  669.2 33.6 %all-to-all-done.3 = bf16[32,40,2048]{2,1,0:T(8,128)(2,1)} async-done(((bf16[32,40,2048]{2,1,0:T(8,128)(2,1)}), bf16[32,40,2048]{2,1,0:T(8,128)(2,1)}, u32[]{:S(2)}, u32[]{:S(2)}) %all-to-all-start.3) | async-done | bytes 5242912 | tf_op jit(solution)/shard_map/all_to_all | solution.py:208
  702.9 12.0 gather_fusion.1
  714.9 5.2 convert_reduce_fusion
  722.1 11.3 fusion.37
  740.4 4.4 convolution_convert_fusion.2
  747.1 17.0 %convert_bitcast_fusion = bf16[2,2048,1024]{1,2,0:T(8,128)(2,1)} fusion(bf16[1280,2048,1]{1,0,2:T(8,128)(2,1)} %bitcast.26, bf16[1,1,1280,1024]{3,2,1,0:T(8,128)(2,1)} %copy-done.45, bf16[1,1,1280,1024]{3,2,1,0:T(8,128)(2,1)} %copy-done.44), kind=kOutput, calls=%fused_computation.19 | convolution fusion | flops 10744233984 | bytes 18874368 | tf_op jit(solution)/shard_map/lrd,lkrh->lkdh/dot_general | solution.py:202
  769.7 9.2 fusion.73
  786.4 2.7 copy.187
  789.1 2.9 pad_maximum_fusion.3
  799.0 2.8 fusion.56
  803.5 16.9 %reduce-scatter.11.cloned.1.call-done = bf16[2,1024,1024]{1,2,0:T(8,128)(2,1)} async-done(((bf16[2,2048,1024]{1,2,0:T(8,128)(2,1)}), bf16[2,1024,1024]{1,2,0:T(8,128)(2,1)}) %reduce-scatter.11.cloned.1.call-update) | async-done | bytes 4194320 | tf_op jit(solution)/shard_map/reduce_scatter | solution.py:295
  820.5 10.1 fusion.54
  833.5 19.7 %fusion.61 = f32[3,2048,2048]{1,2,0:T(8,128)} fusion(bf16[1,128,2048]{1,2,0:T(8,128)(2,1)S(1)} %bitcast.267, bf16[1,128,2048]{1,2,0:T(8,128)(2,1)S(1)} %copy-done.14, bf16[1,128,2048]{1,2,0:T(8,128)(2,1)S(1)} %copy-done.13, bf16[1,128,2048]{2,1,0:T(8,128)(2,1)S(1)} %copy-done.10, f32[2048]{0:T(1024)S(1)} %copy-done.34, f32[128]{0:T(128)S(1)} %copy-done.41), kind=kOutput, calls=%fused_computation.124 | convolution fusion | flops 3223846912 | bytes 52437504 | tf_op jit(solution)/shard_map/gu,sgx->sux/dot_general | solution.py:281
  853.1 60.5 %pad_maximum_fusion = f32[8256,2048]{1,0:T(8,128)} fusion(f32[64,2048]{1,0:T(8,128)} %reshape.664, f32[2048,2048]{1,0:T(8,128)} %fusion.73, f32[6144,2048]{1,0:T(8,128)} %bitcast.260), kind=kLoop, calls=%fused_computation.6 | loop fusion | flops 33816576 | bytes 135266304 | tf_op jit(solution)/shard_map/concatenate | solution.py:307
  916.2 2.8 bitcast_convert_fusion.2
  919.1 4.2 bitcast_convert_fusion.1
  923.2 5.3 copy.199
  928.6 447.6 %all-reduce.3.cloned.1.call-done = f32[8256,2048]{1,0:T(8,128)} async-done(((f32[8256,2048]{1,0:T(8,128)}), f32[8256,2048]{1,0:T(8,128)}) %all-reduce.3.cloned.1.call-update) | async-done | bytes 67633168 | tf_op jit(solution)/shard_map/psum | solution.py:310
  1376.2 44.0 %slice.152 = f32[8192,2048]{1,0:T(8,128)} slice(f32[8256,2048]{1,0:T(8,128)} %all-reduce.3.cloned.1.call-done), slice={[0:8192], [0:2048]} | slice | bytes 134217728 | tf_op jit(solution)/shard_map/slice | solution.py:313
  (204 shorter events, 74.3 us)
Async XLA Ops:
  7.2 403.6 %copy-start = (bf16[2048,32]{0,1:T(8,128)(2,1)S(1)}, bf16[2048,32]{0,1:T(8,128)(2,1)}, u32[]{:S(2)}) copy-start(bf16[2048,32]{0,1:T(8,128)(2,1)} %param.23) | copy-start | bytes 393220
  7.2 243.4 %all-gather.5.cloned.1.call-start = ((), (), s32[]{:S(2)}) async-start(), calls=%async_computation.10 | async-start | bytes 33816576 | tf_op jit(solution)/shard_map/all_gather | solution.py:100
  9.2 358.2 %all-gather.7.cloned.1.call-start = ((), (), s32[]{:S(2)}) async-start(), calls=%async_computation.11 | async-start | bytes 1572864 | tf_op jit(solution)/shard_map/all_gather | solution.py:124
  11.2 287.8 %copy-start.40 = (f32[128]{0:T(128)}, f32[128]{0:T(128)S(1)}, u32[]{:S(2)}) copy-start(f32[128]{0:T(128)S(1)} %add_rsqrt_fusion.3) | copy-start | bytes 1540
  12.1 308.5 %copy-start.25 = (f32[128,64]{1,0:T(8,128)}, f32[128,64]{1,0:T(8,128)S(1)}, u32[]{:S(2)}) copy-start(f32[128,64]{1,0:T(8,128)S(1)} %get-tuple-element.121) | copy-start | bytes 98308
  250.6 48.4 %copy-start.33 = (f32[2048]{0:T(1024)S(1)}, f32[2048]{0:T(1024)}, u32[]{:S(2)}) copy-start(f32[2048]{0:T(1024)} %param.17) | copy-start | bytes 24580
  310.9 33.9 %copy-start.2 = (f32[3,128,2048]{1,2,0:T(8,128)}, f32[3,128,2048]{1,2,0:T(8,128)S(1)}, u32[]{:S(2)}) copy-start(f32[3,128,2048]{1,2,0:T(8,128)S(1)} %convolution_bitcast_fusion) | copy-start | bytes 9437188
  310.9 6.8 copy-start.29
  312.6 6.6 copy-start.31
  320.6 4.9 copy-start.35
  322.3 23.5 %copy-start.42 = (s32[1,256]{1,0:T(1,128)S(1)}, s32[1,256]{1,0:T(1,128)}, u32[]{:S(2)}) copy-start(s32[1,256]{1,0:T(1,128)} %param.16) | copy-start | bytes 3076
  325.5 49.7 %all-gather.9.cloned.1.call-start = ((), (), s32[]{:S(2)}) async-start(), calls=%async_computation.17 | async-start | bytes 1572864 | tf_op jit(solution)/shard_map/all_gather | solution.py:125
  345.9 21.6 %copy-start.16 = (bf16[128,16,64]{2,0,1:T(8,128)(2,1)S(1)}, bf16[128,16,64]{2,0,1:T(8,128)(2,1)}, u32[]{:S(2)}) copy-start(bf16[128,16,64]{2,0,1:T(8,128)(2,1)} %get-tuple-element.107) | copy-start | bytes 786436
  345.9 21.6 %copy-start.18 = (bf16[128,16,64]{2,0,1:T(8,128)(2,1)S(1)}, bf16[128,16,64]{2,0,1:T(8,128)(2,1)}, u32[]{:S(2)}) copy-start(bf16[128,16,64]{2,0,1:T(8,128)(2,1)} %get-tuple-element.108) | copy-start | bytes 786436
  367.5 11.4 copy-start.9
  378.9 11.4 copy-start.23
  378.9 11.4 copy-start.28
  390.4 20.3 %copy-start.11 = (bf16[128,2048]{1,0:T(8,128)(2,1)}, bf16[128,2048]{1,0:T(8,128)(2,1)S(1)}, u32[]{:S(2)}) copy-start(bf16[128,2048]{1,0:T(8,128)(2,1)S(1)} %multiply_convert_fusion.5) | copy-start | bytes 1572868
  400.2 76.6 %all-to-all-start = ((bf16[32,40,2048]{2,1,0:T(8,128)(2,1)}), bf16[32,40,2048]{2,1,0:T(8,128)(2,1)}, u32[]{:S(2)}, u32[]{:S(2)}) async-start(bf16[32,40,2048]{2,1,0:T(8,128)(2,1)} %bitcast.262), calls=%async_computation | async-start | bytes 10485760 | tf_op jit(solution)/shard_map/all_to_all | solution.py:157
  476.8 78.9 %all-to-all-start.2 = ((bf16[32,40,2048]{2,1,0:T(8,128)(2,1)}), bf16[32,40,2048]{2,1,0:T(8,128)(2,1)}, u32[]{:S(2)}, u32[]{:S(2)}) async-start(bf16[32,40,2048]{2,1,0:T(8,128)(2,1)} %bitcast.263), calls=%async_computation.2 | async-start | bytes 10485760 | tf_op jit(solution)/shard_map/all_to_all | solution.py:185
  504.6 5.0 copy-start.4
  504.7 6.5 copy-start.43
  555.7 72.3 %all-to-all-start.1 = ((bf16[32,40,2048]{2,1,0:T(8,128)(2,1)}), bf16[32,40,2048]{2,1,0:T(8,128)(2,1)}, u32[]{:S(2)}, u32[]{:S(2)}) async-start(bf16[32,40,2048]{2,1,0:T(8,128)(2,1)} %bitcast.265), calls=%async_computation.1 | async-start | bytes 10485760 | tf_op jit(solution)/shard_map/all_to_all | solution.py:173
  628.0 74.9 %all-to-all-start.3 = ((bf16[32,40,2048]{2,1,0:T(8,128)(2,1)}), bf16[32,40,2048]{2,1,0:T(8,128)(2,1)}, u32[]{:S(2)}, u32[]{:S(2)}) async-start(bf16[32,40,2048]{2,1,0:T(8,128)(2,1)} %bitcast.264), calls=%async_computation.3 | async-start | bytes 10485760 | tf_op jit(solution)/shard_map/all_to_all | solution.py:208
  636.0 128.3 %reduce-scatter.15.cloned.1.call-start = ((), (), s32[]{:S(2)}) async-start(), calls=%async_computation.15 | async-start | bytes 6291456 | tf_op jit(solution)/shard_map/reduce_scatter | solution.py:295
  646.2 132.8 %reduce-scatter.19.cloned.1.call-start = ((), (), s32[]{:S(2)}) async-start(), calls=%async_computation.18 | async-start | bytes 1572864
  714.9 5.7 copy-start.20
  714.9 5.7 copy-start.22
  722.1 47.7 %copy-start.5 = (f32[128,2048]{1,0:T(8,128)}, f32[128,2048]{1,0:T(8,128)S(1)}, u32[]{:S(2)}) copy-start(f32[128,2048]{1,0:T(8,128)S(1)} %get-tuple-element.111) | copy-start | bytes 3145732
  722.1 11.6 copy-start.24
  740.4 56.5 %reduce-scatter.21.cloned.1.call-start = ((), (), s32[]{:S(2)}) async-start(), calls=%async_computation.19 | async-start | bytes 1572864
  747.1 73.3 %reduce-scatter.11.cloned.1.call-start = ((), (), s32[]{:S(2)}) async-start(), calls=%async_computation.13 | async-start | bytes 12582912 | tf_op jit(solution)/shard_map/reduce_scatter | solution.py:295
  764.2 152.0 %reduce-scatter.17.cloned.1.call-start = ((), (), s32[]{:S(2)}) async-start(), calls=%async_computation.16 | async-start | bytes 3145728 | tf_op jit(solution)/shard_map/reduce_scatter | solution.py:296
  765.0 154.1 %reduce-scatter.13.cloned.1.call-start = ((), (), s32[]{:S(2)}) async-start(), calls=%async_computation.14 | async-start | bytes 6291456 | tf_op jit(solution)/shard_map/reduce_scatter | solution.py:296
  779.0 4.0 copy-start.27
  786.4 12.5 copy-start.3
  786.4 12.5 copy-start.30
  786.4 12.5 copy-start.32
  786.4 12.5 copy-start.37
  786.4 12.6 copy-start.39
  801.8 18.6 %copy-start.34 = (f32[2048]{0:T(1024)S(1)}, f32[2048]{0:T(1024)}, u32[]{:S(2)}) copy-start(f32[2048]{0:T(1024)} %param.17) | copy-start | bytes 24580
  801.8 18.6 %copy-start.41 = (f32[128]{0:T(128)S(1)}, f32[128]{0:T(128)}, u32[]{:S(2)}) copy-start(f32[128]{0:T(128)} %copy-done.40) | copy-start | bytes 1540
  803.5 17.0 %copy-start.10 = (bf16[1,128,2048]{2,1,0:T(8,128)(2,1)S(1)}, bf16[1,128,2048]{2,1,0:T(8,128)(2,1)}, u32[]{:S(2)}) copy-start(bf16[1,128,2048]{2,1,0:T(8,128)(2,1)} %param.13) | copy-start | bytes 1572868
  803.5 17.0 %copy-start.13 = (bf16[1,128,2048]{1,2,0:T(8,128)(2,1)S(1)}, bf16[1,128,2048]{1,2,0:T(8,128)(2,1)}, u32[]{:S(2)}) copy-start(bf16[1,128,2048]{1,2,0:T(8,128)(2,1)} %get-tuple-element.99) | copy-start | bytes 1572868
  803.5 17.0 %copy-start.14 = (bf16[1,128,2048]{1,2,0:T(8,128)(2,1)S(1)}, bf16[1,128,2048]{1,2,0:T(8,128)(2,1)}, u32[]{:S(2)}) copy-start(bf16[1,128,2048]{1,2,0:T(8,128)(2,1)} %get-tuple-element.100) | copy-start | bytes 1572868
  803.5 17.0 %copy-start.15 = (bf16[128,2048]{0,1:T(8,128)(2,1)S(1)}, bf16[128,2048]{0,1:T(8,128)(2,1)}, u32[]{:S(2)}) copy-start(bf16[128,2048]{0,1:T(8,128)(2,1)} %copy.216) | copy-start | bytes 1572868
  820.4 555.8 %all-reduce.3.cloned.1.call-start = ((), (), s32[]{:S(2)}) async-start(), calls=%async_computation.12 | async-start | bytes 135266304 | tf_op jit(solution)/shard_map/psum | solution.py:310
  1376.2 51.3 %copy-start.1 = (bf16[2048,32]{0,1:T(8,128)(2,1)S(1)}, bf16[2048,32]{0,1:T(8,128)(2,1)}, u32[]{:S(2)}) copy-start(bf16[2048,32]{0,1:T(8,128)(2,1)} %param.23) | copy-start | bytes 393220
  (12 other events, 28.7 us)
Sparse Core Ops, SparseCore 0:
  10.3 240.2 all-gather.4
  325.6 22.4 all-gather.6
  350.3 24.7 all-gather.8
  646.3 23.4 reduce-scatter.14
  740.5 29.6 reduce-scatter.18
  773.0 23.8 reduce-scatter.20
  799.4 20.9 reduce-scatter.10
  822.7 35.3 reduce-scatter.16
  860.6 57.8 reduce-scatter.12
  924.2 451.9 all-reduce.2

commit v2 on v1

--- a/solution.py
+++ b/solution.py
@@ -43,8 +43,12 @@
     onehot = (route_rows[:, None] == jnp.arange(experts, dtype=jnp.int32)[None, :]).astype(
         jnp.int32
     )
-    before = jnp.cumsum(onehot, axis=0) - onehot
-    return route_rows * capacity + jnp.sum(before * onehot, axis=1)
+    count = route_rows.shape[0]
+    earlier = (
+        jnp.arange(count, dtype=jnp.int32)[None, :] < jnp.arange(count, dtype=jnp.int32)[:, None]
+    ).astype(jnp.bfloat16)
+    before = jnp.dot(earlier, onehot.astype(jnp.bfloat16), preferred_element_type=jnp.float32)
+    return route_rows * capacity + jnp.sum(before.astype(jnp.int32) * onehot, axis=1)
 
 
 def expert_major(received, local_experts, capacity):
@@ -98,16 +102,18 @@
     attention_input = (normed1 * attn_gain).astype(bf16)
     all_axes = ("dp", "context", "expert")
     weights_full = lax.all_gather(
-        jnp.concatenate([qkv_weight, out_weight[None]], axis=0), all_axes, axis=1, tiled=True
-    )
-    query_key_value_complete = weights_full[:3]
-    out_full = weights_full[3]
-    projected_output = jnp.einsum(
-        "hp,lpa->lha",
+        jnp.concatenate([qkv_weight.transpose(1, 0, 2), out_weight[:, None, :]], axis=1),
+        all_axes,
+        axis=0,
+        tiled=True,
+    )
+    out_full = weights_full[:, 3, :]
+    projected_all = jnp.dot(
         attention_input,
-        query_key_value_complete,
+        weights_full.reshape(width, 4 * heads_width),
         preferred_element_type=single_precision,
-    )
+    ).reshape(seq_tok, 4, heads_width)
+    projected_output = projected_all[:, :3].transpose(1, 0, 2)
     q_normed, q_factor = rms_forward(projected_output[0])
     k_normed, k_factor = rms_forward(projected_output[1])
     values = projected_output[2].astype(bf16)
@@ -230,9 +236,6 @@
     grad_mid_norm, grad_ffn_gain = rms_backward(grad_ffn_in, normed2, factor2, ffn_gain)
     grad_mid = grad + grad_mid_norm
     grad_mid_b = grad_mid.astype(bf16)
-    grad_out_w = jnp.einsum(
-        "td,tq->dq", grad_mid_b, attended, preferred_element_type=single_precision
-    )
     grad_att = (
         jnp.einsum("td,dq->tq", grad_mid_b, out_full, preferred_element_type=single_precision)
         .astype(bf16)
@@ -277,14 +280,12 @@
     )
     grad_q_raw, grad_q_gain = rms_backward(grad_qn, q_normed, q_factor, q_gain)
     grad_k_raw, grad_k_gain = rms_backward(grad_kn, k_normed, k_factor, k_gain)
-    projected_gradient = jnp.stack([grad_q_raw, grad_k_raw, grad_values]).astype(bf16)
-    query_key_value_gradient = jnp.einsum(
-        "gu,sgx->sux", attention_input, projected_gradient, preferred_element_type=single_precision
-    )
-    attention_input_gradient = jnp.einsum(
-        "yaz,ygz->ag",
-        projected_gradient,
-        query_key_value_complete,
+    projected_gradient = jnp.stack(
+        [grad_q_raw, grad_k_raw, grad_values, jnp.zeros_like(grad_values)], axis=1
+    ).astype(bf16)
+    attention_input_gradient = jnp.dot(
+        projected_gradient.reshape(seq_tok, 4 * heads_width),
+        weights_full.reshape(width, 4 * heads_width).T,
         preferred_element_type=single_precision,
     )
     grad_x_norm, grad_attn_gain = rms_backward(
@@ -298,23 +299,29 @@
 
     grad_in_shard = scatter_over_copies(grad_gate_up_w[0])[None]
     grad_down_shard = scatter_over_copies(grad_down[0])[None]
+    pad_rows = 16
+    left = jnp.pad(
+        jnp.stack([attention_input] * 3 + [grad_mid_b]), ((0, 0), (0, 0), (0, pad_rows))
+    )
+    right = jnp.concatenate(
+        [projected_gradient[:, :3].transpose(1, 0, 2), attended[None]], axis=0
+    )
+    stacked = jnp.einsum("sta,stb->sab", left, right, preferred_element_type=single_precision)
     small = jnp.concatenate(
         [grad_attn_gain, grad_q_gain, grad_k_gain, grad_ffn_gain, grad_router.reshape(-1)]
     )
-    small_rows = -(-small.shape[0] // width)
-    pad_rows = 64
-    small = jnp.pad(small, (0, pad_rows * width - small.shape[0])).reshape(pad_rows, width)
-    stacked = jnp.concatenate(
-        [query_key_value_gradient.reshape(3 * width, heads_width), grad_out_w, small], axis=0
+    small_rows = -(-small.shape[0] // (4 * heads_width))
+    small = jnp.pad(small, (0, 4 * small_rows * heads_width - small.shape[0]))
+    stacked = lax.dynamic_update_slice(
+        stacked, small.reshape(4, small_rows, heads_width), (0, width, 0)
     )
     summed = lax.psum(stacked, all_axes)
     shard_rows = width // lax.axis_size(all_axes)
     start = lax.axis_index(all_axes) * shard_rows
-    weight_sums = summed[: 4 * width].reshape(4, width, heads_width)
-    weight_shard = lax.dynamic_slice_in_dim(weight_sums, start, shard_rows, axis=1)
+    weight_shard = lax.dynamic_slice_in_dim(summed, start, shard_rows, axis=1)
     grad_qkv_shard = weight_shard[:3]
     grad_out_shard = weight_shard[3]
-    small_sum = summed[4 * width : 4 * width + small_rows].reshape(-1)
+    small_sum = summed[:, width : width + small_rows].reshape(-1)
     sizes = [width, heads_width, heads_width, width, width * experts]
     offsets = [sum(sizes[:n]) for n in range(len(sizes))]
     totals = [small_sum[o : o + n] for o, n in zip(offsets, sizes)]

time: 1450 us -> 1410 us (0.972)
  waiting for transfers between devices: 865 us -> 981 us
  other arithmetic: 138 us -> 55.8 us
  local copies, waits for them, and re-layouts: 208 us -> 138 us
    slice x4 -> x1, local copies, waits for them, and re-layouts: 67.3 us -> 1.08 us  [body(): small_sum = summed[:, width:width + small_rows].reshape(-1)]
    concatenate x2 -> x1, other arithmetic: 61.5 us -> 1.72 us  [body(): jnp.concatenate([qkv_weight.transpose(1, 0, 2), out_weight[:, None, :]],...]
    unnamed x106 -> x132, local copies, waits for them, and re-layouts: 73.3 us -> 28.1 us
    all_gather x0 -> x1, local copies, waits for them, and re-layouts: none -> 42.6 us  [body(): lax.all_gather(jnp.concatenate([qkv_weight.transpose(1, 0, 2), out_weight...]
    reduce_scatter x2, waiting for transfers between devices: 0.01 us -> 36.8 us  [scatter_over_copies(): lax.psum_scatter(values, 'context', scatter_dimension=1, tiled=True)]
    all_gather x1, waiting for transfers between devices: 0.01 us -> 25.6 us  [body(): lax.all_gather(own_keys.reshape(seq_tok, heads_width), 'context', axis=0,...]
    unnamed x12 -> x11, waiting for transfers between devices: 3.21 us -> 23.3 us
    slice x0 -> x1, matrix products: none -> 17.2 us  [body(): projected_output = projected_all[:, :3].transpose(1, 0, 2)]
  transfers between devices with their start and end apart: 14 -> 14, of which waited for: 9 -> 11; matrix products, arithmetic and copies ran while one was open for 25% -> 18% of each run, Pallas kernels for 0% -> 0%
where the time goes in v2:
time: 1410 us; the launch traced here: 1400 us
  waiting for transfers between devices  981 us (70%)
  matrix products  177 us (13%)
  local copies, waits for them, and re-layouts  138 us (10%)
  other arithmetic  55.8 us (4%)
  starting transfers between devices  36.2 us (3%)
  between operations  15.5 us (1%)
    psum x1, waiting for transfers between devices, body(): summed = lax.psum(stacked, all_axes)  448 us
    all_gather x1, waiting for transfers between devices, body(): lax.all_gather(jnp.concatenate([qkv_weight.transpose(1, 0, 2), out_weight...  237 us
    all_to_all x1, waiting for transfers between devices, body(): lax.all_to_all(send.reshape(sources, local_experts * capacity, width), 'e...  49.5 us
    all_to_all x1, waiting for transfers between devices, body(): lax.all_to_all(source_major(results, sources, capacity), 'expert', split_...  47.9 us
    all_to_all x1, waiting for transfers between devices, body(): lax.all_to_all(source_major(grad_rows_in, sources, capacity), 'expert', s...  46.7 us
    all_to_all x1, waiting for transfers between devices, body(): lax.all_to_all(grad_send.reshape(sources, local_experts * capacity, width...  43.7 us
    all_gather x1, local copies, waits for them, and re-layouts, body(): lax.all_gather(jnp.concatenate([qkv_weight.transpose(1, 0, 2), out_weight...  42.6 us
    reduce_scatter x2, waiting for transfers between devices, scatter_over_copies(): lax.psum_scatter(values, 'context', scatter_dimension=1, tiled=True)  36.8 us
  transfers between devices with their start and end apart: 14, of which 11 were waited for; matrix products, arithmetic and copies ran while one was open for 18% of the time, Pallas kernels for 0%

profile of v2, /device:TPU:1, one launch (start us, length us, event | category | flops | bytes accessed | tf_op | source)
XLA Modules:
  0.0 1403.8 jit_solution(14080730176958690389)
XLA Ops:
  13.2 237.4 %all-gather.5.cloned.1.call-done = bf16[2048,4,2048]{2,0,1:T(8,128)(2,1)} async-done(((bf16[16,4,2048]{2,0,1:T(8,128)(2,1)}), bf16[2048,4,2048]{2,0,1:T(8,128)(2,1)}) %all-gather.5.cloned.1.call-update) | async-done | bytes 33554448 | tf_op jit(solution)/shard_map/all_gather | solution.py:104
  250.6 42.6 %copy.130 = bf16[2048,4,2048]{0,2,1:T(8,128)(2,1)} copy(bf16[2048,4,2048]{2,0,1:T(8,128)(2,1)} %all-gather.5.cloned.1.call-done) | data formatting | bytes 67108864 | tf_op jit(solution)/shard_map/all_gather | solution.py:104
  293.2 17.2 %fusion.37 = f32[3,128,2048]{2,1,0:T(8,128)S(1)} fusion(bf16[2048,4,2048]{0,2,1:T(8,128)(2,1)} %copy.130, bf16[1,128,2048]{2,1,0:T(8,128)(2,1)S(1)} %fusion.93), kind=kOutput, calls=%fused_computation.56 | convolution fusion | flops 3221225472 | bytes 37224448 | tf_op jit(solution)/shard_map/slice | solution.py:116
  319.8 17.9 %all-gather.9.cloned.1.call-done = bf16[1,256,2048]{2,1,0:T(8,128)(2,1)} async-done(((bf16[1,128,2048]{2,1,0:T(8,128)(2,1)}), bf16[1,256,2048]{2,1,0:T(8,128)(2,1)}) %all-gather.9.cloned.1.call-update) | async-done | bytes 1048592 | tf_op jit(solution)/shard_map/all_gather | solution.py:131
  339.2 25.6 %all-gather.7.cloned.1.call-done = bf16[256,2048]{0,1:T(8,128)(2,1)} async-done(((bf16[128,2048]{0,1:T(8,128)(2,1)}), bf16[256,2048]{0,1:T(8,128)(2,1)}) %all-gather.7.cloned.1.call-update) | async-done | bytes 1048592 | tf_op jit(solution)/shard_map/all_gather | solution.py:130
  364.7 3.1 fusion.122
  367.8 3.5 convolution_convert_fusion.3
  371.4 6.5 multiply_reduce_fusion.7
  379.1 9.8 scatter_custom_fusion
  389.0 9.4 all-to-all-start
  399.1 7.0 gather_fusion.2
  406.1 10.0 scatter_custom_fusion.1
  416.1 49.5 %all-to-all-done = bf16[32,40,2048]{2,1,0:T(8,128)(2,1)} async-done(((bf16[32,40,2048]{2,1,0:T(8,128)(2,1)}), bf16[32,40,2048]{2,1,0:T(8,128)(2,1)}, u32[]{:S(2)}, u32[]{:S(2)}) %all-to-all-start) | async-done | bytes 5242912 | tf_op jit(solution)/shard_map/all_to_all | solution.py:163
  465.6 10.8 all-to-all-start.2
  476.7 16.8 %fusion.11 = f32[1,2,1280,1024]{3,2,1,0:T(8,128)S(1)} fusion(bf16[1280,2048,1]{1,0,2:T(8,128)(2,1)} %bitcast.25, bf16[1,2,2048,1024]{3,2,1,0:T(8,128)(2,1)} %param.24), kind=kOutput, calls=%fused_computation.24 | convolution fusion | flops 10737418240 | bytes 24117248 | tf_op jit(solution)/shard_map/lrd,lkdh->lkrh/dot_general | solution.py:171
  493.5 4.0 copy-done.5
  497.5 2.7 multiply_convert_fusion
  500.2 43.7 %all-to-all-done.2 = bf16[32,40,2048]{2,1,0:T(8,128)(2,1)} async-done(((bf16[32,40,2048]{2,1,0:T(8,128)(2,1)}), bf16[32,40,2048]{2,1,0:T(8,128)(2,1)}, u32[]{:S(2)}, u32[]{:S(2)}) %all-to-all-start.2) | async-done | bytes 5242912 | tf_op jit(solution)/shard_map/all_to_all | solution.py:191
  543.9 10.1 convolution_convert_fusion.1
  554.3 13.1 fusion.45
  570.0 15.9 %convert_bitcast_fusion = bf16[2,2048,1024]{1,2,0:T(8,128)(2,1)} fusion(bf16[1280,2048,1]{1,0,2:T(8,128)(2,1)} %bitcast.25, bf16[1,1,1280,1024]{3,2,1,0:T(8,128)(2,1)S(1)} %get-tuple-element.85, bf16[1,1,1280,1024]{3,2,1,0:T(8,128)(2,1)S(1)} %get-tuple-element.84), kind=kOutput, calls=%fused_computation.20 | convolution fusion | flops 10744233984 | bytes 18874368 | tf_op jit(solution)/shard_map/lrd,lkrh->lkdh/dot_general | solution.py:208
  586.0 9.8 convolution_convert_fusion
  595.8 6.3 all-to-all-start.1
  602.1 18.0 %bitcast_convert_fusion = bf16[1280,2048]{1,0:T(8,128)(2,1)} fusion(bf16[1,2,2048,1024]{3,2,1,0:T(8,128)(2,1)} %param.24, bf16[1,1,1280,1024]{3,2,1,0:T(8,128)(2,1)} %copy-done.58, bf16[1,1,1280,1024]{3,2,1,0:T(8,128)(2,1)} %copy-done.57), kind=kOutput, calls=%fused_computation.10 | convolution fusion | flops 10742661120 | bytes 18874368 | tf_op jit(solution)/shard_map/lkrh,lkdh->lrd/dot_general | solution.py:211
  620.2 47.9 %all-to-all-done.1 = bf16[32,40,2048]{2,1,0:T(8,128)(2,1)} async-done(((bf16[32,40,2048]{2,1,0:T(8,128)(2,1)}), bf16[32,40,2048]{2,1,0:T(8,128)(2,1)}, u32[]{:S(2)}, u32[]{:S(2)}) %all-to-all-start.1) | async-done | bytes 5242912 | tf_op jit(solution)/shard_map/all_to_all | solution.py:179
  668.1 8.1 all-to-all-start.3
  678.6 12.1 gather_fusion
  690.8 5.0 fusion.4
  695.8 46.7 %all-to-all-done.3 = bf16[32,40,2048]{2,1,0:T(8,128)(2,1)} async-done(((bf16[32,40,2048]{2,1,0:T(8,128)(2,1)}), bf16[32,40,2048]{2,1,0:T(8,128)(2,1)}, u32[]{:S(2)}, u32[]{:S(2)}) %all-to-all-start.3) | async-done | bytes 5242912 | tf_op jit(solution)/shard_map/all_to_all | solution.py:214
  742.5 12.0 gather_fusion.1
  754.7 5.1 convert_reduce_fusion
  763.4 4.7 fusion.47
  768.6 2.5 multiply_convert_fusion.2
  775.4 3.4 convolution_convert_fusion.2
  785.7 21.8 %reduce-scatter.19.cloned.1.call-done = bf16[128,2048]{1,0:T(8,128)(2,1)} async-done(((bf16[256,2048]{1,0:T(8,128)(2,1)}), bf16[128,2048]{1,0:T(8,128)(2,1)}) %reduce-scatter.19.cloned.1.call-update) | async-done | bytes 524304
  811.4 2.9 multiply_subtract_fusion.1
  821.2 2.4 concatenate.34
  823.6 2.4 reshape.796
  826.0 2.9 multiply_reduce_fusion.1
  830.4 4.0 reduce-scatter.9.cloned.1.call-done
  834.4 22.7 %fusion.90 = (f32[2048]{0:T(1024)S(1)}, f32[128]{0:T(128)S(1)}, f32[128,2048]{1,0:T(8,128)}) fusion(bf16[1,128,2048]{2,1,0:T(8,128)(2,1)} %param.13, f32[128]{0:T(128)} %copy-done.55, f32[2048]{0:T(1024)} %param.17, bf16[2048,4,2048]{2,0,1:T(8,128)(2,1)} %all-gather.5.cloned.1.call-done, bf16[128,1,2048]{2,0,1:T(8,128)(2,1)} %bitcast.292, ...), kind=kOutput, calls=%fused_computation.116 | convolution fusion | flops 4299945984 | bytes 36717576 | tf_op jit(solution)/shard_map/dot_general | solution.py:286
  862.5 24.3 %fusion.51 = f32[4,2064,2048]{2,1,0:T(8,128)} fusion(bf16[1,128,2048]{2,1,0:T(8,128)(2,1)S(1)} %copy-done.22, bf16[1,128,2048]{2,1,0:T(8,128)(2,1)S(1)} %copy-done.2, bf16[1,128,2048]{2,1,0:T(8,128)(2,1)S(1)} %copy-done.21, bf16[3,128,2048]{2,1,0:T(8,128)(2,1)S(1)} %maximum_bitcast_fusion.3), kind=kOutput, calls=%fused_computation.70 | convolution fusion | flops 4343308288 | bytes 70778880 | tf_op jit(solution)/shard_map/sta,stb->sab/dot_general | solution.py:309
  886.8 2.8 dynamic_update_slice.3
  892.7 2.9 bitcast_convert_fusion.2
  895.6 36.8 %reduce-scatter.13.cloned.1.call-done = bf16[2,512,1024]{1,2,0:T(8,128)(2,1)} async-done(((bf16[2,1024,1024]{1,2,0:T(8,128)(2,1)}), bf16[2,512,1024]{1,2,0:T(8,128)(2,1)}) %reduce-scatter.13.cloned.1.call-update) | async-done | bytes 2097168 | tf_op jit(solution)/shard_map/reduce_scatter | solution.py:297
  932.5 4.2 bitcast_convert_fusion.1
  936.6 5.3 copy.159
  942.0 448.1 %all-reduce.3.cloned.1.call-done = f32[4,2064,2048]{2,1,0:T(8,128)} async-done(((f32[4,2064,2048]{2,1,0:T(8,128)}), f32[4,2064,2048]{2,1,0:T(8,128)}) %all-reduce.3.cloned.1.call-update) | async-done | bytes 67633168 | tf_op jit(solution)/shard_map/psum | solution.py:318
  (226 shorter events, 66.3 us)
Async XLA Ops:
  7.2 391.5 %copy-start = (bf16[2048,32]{0,1:T(8,128)(2,1)S(1)}, bf16[2048,32]{0,1:T(8,128)(2,1)}, u32[]{:S(2)}) copy-start(bf16[2048,32]{0,1:T(8,128)(2,1)} %param.23) | copy-start | bytes 393220
  7.2 243.4 %all-gather.5.cloned.1.call-start = ((), (), s32[]{:S(2)}) async-start(), calls=%async_computation.10 | async-start | bytes 33816576 | tf_op jit(solution)/shard_map/all_gather | solution.py:104
  9.0 328.7 %all-gather.9.cloned.1.call-start = ((), (), s32[]{:S(2)}) async-start(), calls=%async_computation.18 | async-start | bytes 1572864 | tf_op jit(solution)/shard_map/all_gather | solution.py:131
  11.0 282.2 %copy-start.55 = (f32[128]{0:T(128)}, f32[128]{0:T(128)S(1)}, u32[]{:S(2)}) copy-start(f32[128]{0:T(128)S(1)} %add_rsqrt_fusion.3) | copy-start | bytes 1540
  11.9 304.7 %copy-start.31 = (f32[128,64]{1,0:T(8,128)}, f32[128,64]{1,0:T(8,128)S(1)}, u32[]{:S(2)}) copy-start(f32[128,64]{1,0:T(8,128)S(1)} %get-tuple-element.111) | copy-start | bytes 98308
  13.2 280.0 %copy-start.1 = (bf16[1,128,2048]{2,1,0:T(8,128)(2,1)}, bf16[1,128,2048]{2,1,0:T(8,128)(2,1)S(1)}, u32[]{:S(2)}) copy-start(bf16[1,128,2048]{2,1,0:T(8,128)(2,1)S(1)} %fusion.93) | copy-start | bytes 1572868
  314.8 49.9 %all-gather.7.cloned.1.call-start = ((), (), s32[]{:S(2)}) async-start(), calls=%async_computation.11 | async-start | bytes 1572864 | tf_op jit(solution)/shard_map/all_gather | solution.py:130
  317.4 50.5 %copy-start.12 = (bf16[128,16,64]{2,0,1:T(8,128)(2,1)}, bf16[128,16,64]{2,0,1:T(8,128)(2,1)S(1)}, u32[]{:S(2)}) copy-start(bf16[128,16,64]{2,0,1:T(8,128)(2,1)S(1)} %get-tuple-element.94) | copy-start | bytes 786436
  317.4 50.5 %copy-start.14 = (bf16[128,16,64]{2,0,1:T(8,128)(2,1)}, bf16[128,16,64]{2,0,1:T(8,128)(2,1)S(1)}, u32[]{:S(2)}) copy-start(bf16[128,16,64]{2,0,1:T(8,128)(2,1)S(1)} %get-tuple-element.95) | copy-start | bytes 786436
  339.2 32.2 %copy-start.18 = (bf16[32,8,16,128]{3,2,1,0:T(8,128)(2,1)}, bf16[32,8,16,128]{3,2,1,0:T(8,128)(2,1)S(1)}, u32[]{:S(2)}) copy-start(bf16[32,8,16,128]{3,2,1,0:T(8,128)(2,1)S(1)} %copy.174) | copy-start | bytes 3145732
  364.7 6.7 copy-start.10
  371.4 6.6 copy-start.24
  371.4 7.5 copy-start.34
  378.0 11.0 copy-start.52
  379.1 19.6 %copy-start.8 = (bf16[128,2048]{1,0:T(8,128)(2,1)}, bf16[128,2048]{1,0:T(8,128)(2,1)S(1)}, u32[]{:S(2)}) copy-start(bf16[128,2048]{1,0:T(8,128)(2,1)S(1)} %multiply_convert_fusion.3) | copy-start | bytes 1572868
  389.0 9.6 copy-start.28
  389.0 76.6 %all-to-all-start = ((bf16[32,40,2048]{2,1,0:T(8,128)(2,1)}), bf16[32,40,2048]{2,1,0:T(8,128)(2,1)}, u32[]{:S(2)}, u32[]{:S(2)}) async-start(bf16[32,40,2048]{2,1,0:T(8,128)(2,1)} %bitcast.273), calls=%async_computation | async-start | bytes 10485760 | tf_op jit(solution)/shard_map/all_to_all | solution.py:163
  399.0 7.1 copy-start.32
  399.0 7.1 copy-start.46
  465.6 78.3 %all-to-all-start.2 = ((bf16[32,40,2048]{2,1,0:T(8,128)(2,1)}), bf16[32,40,2048]{2,1,0:T(8,128)(2,1)}, u32[]{:S(2)}, u32[]{:S(2)}) async-start(bf16[32,40,2048]{2,1,0:T(8,128)(2,1)} %bitcast.274), calls=%async_computation.2 | async-start | bytes 10485760 | tf_op jit(solution)/shard_map/all_to_all | solution.py:191
  476.4 303.9 %reduce-scatter.15.cloned.1.call-start = ((), (), s32[]{:S(2)}) async-start(), calls=%async_computation.16 | async-start | bytes 6291456 | tf_op jit(solution)/shard_map/reduce_scatter | solution.py:296
  554.0 227.1 %reduce-scatter.11.cloned.1.call-start = ((), (), s32[]{:S(2)}) async-start(), calls=%async_computation.14 | async-start | bytes 12582912 | tf_op jit(solution)/shard_map/reduce_scatter | solution.py:296
  595.8 72.3 %all-to-all-start.1 = ((bf16[32,40,2048]{2,1,0:T(8,128)(2,1)}), bf16[32,40,2048]{2,1,0:T(8,128)(2,1)}, u32[]{:S(2)}, u32[]{:S(2)}) async-start(bf16[32,40,2048]{2,1,0:T(8,128)(2,1)} %bitcast.276), calls=%async_computation.1 | async-start | bytes 10485760 | tf_op jit(solution)/shard_map/all_to_all | solution.py:179
  668.1 8.3 copy-start.23
  668.1 74.4 %all-to-all-start.3 = ((bf16[32,40,2048]{2,1,0:T(8,128)(2,1)}), bf16[32,40,2048]{2,1,0:T(8,128)(2,1)}, u32[]{:S(2)}, u32[]{:S(2)}) async-start(bf16[32,40,2048]{2,1,0:T(8,128)(2,1)} %bitcast.275), calls=%async_computation.3 | async-start | bytes 10485760 | tf_op jit(solution)/shard_map/all_to_all | solution.py:214
  676.2 131.3 %reduce-scatter.19.cloned.1.call-start = ((), (), s32[]{:S(2)}) async-start(), calls=%async_computation.19 | async-start | bytes 1572864
  742.5 12.0 copy-start.41
  742.5 12.1 copy-start.33
  742.5 12.1 copy-start.47
  754.5 5.3 copy-start.7
  754.6 5.3 copy-start.35
  754.6 5.3 copy-start.53
  754.6 6.3 copy-start.29
  775.2 59.2 %reduce-scatter.9.cloned.1.call-start = ((), (), s32[]{:S(2)}) async-start(), calls=%async_computation.12 | async-start | bytes 1572864 | tf_op jit(solution)/shard_map/reduce_scatter | solution.py:270
  780.2 112.5 %reduce-scatter.17.cloned.1.call-start = ((), (), s32[]{:S(2)}) async-start(), calls=%async_computation.17 | async-start | bytes 3145728 | tf_op jit(solution)/shard_map/reduce_scatter | solution.py:297
  781.0 151.5 %reduce-scatter.13.cloned.1.call-start = ((), (), s32[]{:S(2)}) async-start(), calls=%async_computation.15 | async-start | bytes 6291456 | tf_op jit(solution)/shard_map/reduce_scatter | solution.py:297
  781.7 608.4 %all-reduce.3.cloned.1.call-start = ((), (), s32[]{:S(2)}) async-start(), calls=%async_computation.13 | async-start | bytes 135266304 | tf_op jit(solution)/shard_map/psum | solution.py:318
  817.6 8.4 copy-start.4
  817.6 8.4 copy-start.37
  817.6 8.4 copy-start.39
  834.4 23.4 %copy-start.45 = (f32[2048]{0:T(1024)S(1)}, f32[2048]{0:T(1024)}, u32[]{:S(2)}) copy-start(f32[2048]{0:T(1024)} %get-tuple-element.73) | copy-start | bytes 24580
  834.4 24.0 %copy-start.44 = (f32[2048]{0:T(1024)S(1)}, f32[2048]{0:T(1024)}, u32[]{:S(2)}) copy-start(f32[2048]{0:T(1024)} %get-tuple-element.66) | copy-start | bytes 24580
  834.4 24.6 %copy-start.43 = (f32[2048]{0:T(1024)S(1)}, f32[2048]{0:T(1024)}, u32[]{:S(2)}) copy-start(f32[2048]{0:T(1024)} %get-tuple-element.76) | copy-start | bytes 24580
  834.4 26.9 %copy-start.26 = (bf16[128,1,2048]{2,0,1:T(8,128)(2,1)S(1)}, bf16[128,1,2048]{2,0,1:T(8,128)(2,1)}, u32[]{:S(2)}) copy-start(bf16[128,1,2048]{2,0,1:T(8,128)(2,1)} %get-tuple-element.86) | copy-start | bytes 1572868
  834.4 26.9 %copy-start.27 = (bf16[128,1,2048]{2,0,1:T(8,128)(2,1)S(1)}, bf16[128,1,2048]{2,0,1:T(8,128)(2,1)}, u32[]{:S(2)}) copy-start(bf16[128,1,2048]{2,0,1:T(8,128)(2,1)} %get-tuple-element.87) | copy-start | bytes 1572868
  857.1 5.4 copy-start.2
  857.1 5.4 copy-start.21
  857.1 5.4 copy-start.22
  (25 other events, 57.1 us)
Sparse Core Ops, SparseCore 0:
  10.3 240.1 all-gather.4
  315.0 22.6 all-gather.8
  339.9 24.7 all-gather.6
  554.1 17.0 reduce-scatter.14
  586.1 21.3 reduce-scatter.10
  775.3 32.1 reduce-scatter.18
  810.5 23.8 reduce-scatter.8
  836.7 35.3 reduce-scatter.16
  874.6 57.7 reduce-scatter.12
  938.2 451.8 all-reduce.2

commit v3 on v2

--- a/solution.py
+++ b/solution.py
@@ -67,6 +67,41 @@
         .transpose(1, 0, 2, 3)
         .reshape(sources, local_experts * capacity, width)
     )
+
+
+def swap_context(values):
+    return lax.ppermute(values, "context", [(0, 1), (1, 0)])
+
+
+def gather_context(values):
+    other = swap_context(values)
+    first = lax.axis_index("context") == 0
+    return jnp.concatenate(
+        [jnp.where(first, values, other), jnp.where(first, other, values)], axis=0
+    )
+
+
+def sum_context_halves(values):
+    half = values.shape[0] // 2
+    first = lax.axis_index("context") == 0
+    own = jnp.where(first, values[:half], values[half:])
+    given = jnp.where(first, values[half:], values[:half]).astype(jnp.bfloat16)
+    return own + swap_context(given).astype(own.dtype)
+
+
+def butterfly_sum(values, axes):
+    index = lax.axis_index(axes)
+    count = 1
+    for name in axes:
+        count *= lax.axis_size(name)
+    step = 1
+    while step < count:
+        partner = [(i, i ^ step) for i in range(count)]
+        received = lax.ppermute(values, axes, partner)
+        mine_first = (index & step) == 0
+        values = jnp.where(mine_first, values + received, received + values)
+        step *= 2
+    return values
 
 
 def body(
@@ -126,10 +161,11 @@
     own_keys = rotate(
         (k_normed * k_gain).reshape(seq_tok, heads, head_dim), cosine, sine, 1.0
     ).astype(bf16)
-    keys, vals = (
-        lax.all_gather(own_keys.reshape(seq_tok, heads_width), "context", axis=0, tiled=True),
-        lax.all_gather(values, "context", axis=0, tiled=True),
-    )
+    keys_vals = gather_context(
+        jnp.stack([own_keys.reshape(seq_tok, heads_width), values], axis=1)
+    )
+    keys = keys_vals[:, 0]
+    vals = keys_vals[:, 1]
     seq_len = keys.shape[0]
     keys3 = keys.reshape(seq_len, heads, head_dim)
     vals3 = vals.reshape(seq_len, heads, head_dim)
@@ -260,20 +296,14 @@
         jnp.einsum("hqk,qhd->khd", grad_scores, queries, preferred_element_type=single_precision)
         * scale
     )
-    grad_keys, grad_values = (
-        lax.psum_scatter(
-            grad_keys_all.reshape(seq_len, heads_width).astype(jnp.bfloat16),
-            "context",
-            scatter_dimension=0,
-            tiled=True,
-        ).astype(jnp.float32),
-        lax.psum_scatter(
-            grad_vals.reshape(seq_len, heads_width).astype(jnp.bfloat16),
-            "context",
-            scatter_dimension=0,
-            tiled=True,
-        ).astype(jnp.float32),
-    )
+    grad_keys_values = sum_context_halves(
+        jnp.stack(
+            [grad_keys_all.reshape(seq_len, heads_width), grad_vals.reshape(seq_len, heads_width)],
+            axis=1,
+        )
+    )
+    grad_keys = grad_keys_values[:, 0]
+    grad_values = grad_keys_values[:, 1]
     grad_qn = rotate(grad_queries, cosine, sine, -1.0).reshape(seq_tok, heads_width)
     grad_kn = rotate(grad_keys.reshape(seq_tok, heads, head_dim), cosine, sine, -1.0).reshape(
         seq_tok, heads_width
@@ -299,29 +329,25 @@
 
     grad_in_shard = scatter_over_copies(grad_gate_up_w[0])[None]
     grad_down_shard = scatter_over_copies(grad_down[0])[None]
-    pad_rows = 16
-    left = jnp.pad(
-        jnp.stack([attention_input] * 3 + [grad_mid_b]), ((0, 0), (0, 0), (0, pad_rows))
-    )
+    left = jnp.stack([attention_input] * 3 + [grad_mid_b])
     right = jnp.concatenate(
         [projected_gradient[:, :3].transpose(1, 0, 2), attended[None]], axis=0
     )
     stacked = jnp.einsum("sta,stb->sab", left, right, preferred_element_type=single_precision)
-    small = jnp.concatenate(
-        [grad_attn_gain, grad_q_gain, grad_k_gain, grad_ffn_gain, grad_router.reshape(-1)]
-    )
-    small_rows = -(-small.shape[0] // (4 * heads_width))
-    small = jnp.pad(small, (0, 4 * small_rows * heads_width - small.shape[0]))
-    stacked = lax.dynamic_update_slice(
-        stacked, small.reshape(4, small_rows, heads_width), (0, width, 0)
-    )
-    summed = lax.psum(stacked, all_axes)
+    summed = lax.psum(stacked.astype(bf16), all_axes)
     shard_rows = width // lax.axis_size(all_axes)
     start = lax.axis_index(all_axes) * shard_rows
-    weight_shard = lax.dynamic_slice_in_dim(summed, start, shard_rows, axis=1)
+    weight_shard = lax.dynamic_slice_in_dim(summed, start, shard_rows, axis=1).astype(
+        single_precision
+    )
     grad_qkv_shard = weight_shard[:3]
     grad_out_shard = weight_shard[3]
-    small_sum = summed[:, width : width + small_rows].reshape(-1)
+    small_sum = butterfly_sum(
+        jnp.concatenate(
+            [grad_attn_gain, grad_q_gain, grad_k_gain, grad_ffn_gain, grad_router.reshape(-1)]
+        ),
+        all_axes,
+    )
     sizes = [width, heads_width, heads_width, width, width * experts]
     offsets = [sum(sizes[:n]) for n in range(len(sizes))]
     totals = [small_sum[o : o + n] for o, n in zip(offsets, sizes)]

time: 1410 us -> 1220 us (0.87)
  waiting for transfers between devices: 981 us -> 761 us
  starting transfers between devices: 36.2 us -> 82.7 us
    psum x1, waiting for transfers between devices: 448 us -> 207 us  [body(): summed = lax.psum(stacked.astype(bf16), all_axes)]
    ppermute x0 -> x9, waiting for transfers between devices: none -> 76.8 us  [the longest x7 42 us: butterfly_sum(): received = lax.ppermute(values, axes, partner)]
    ppermute x0 -> x9, starting transfers between devices: none -> 45.8 us  [the longest x7 44.2 us: butterfly_sum(): received = lax.ppermute(values, axes, partner)]
    all_gather x2 -> x0, waiting for transfers between devices: 43.5 us -> none  [the longest x1 25.6 us: body(): lax.all_gather(own_keys.reshape(seq_tok, heads_width), 'context', axis=0,...]
    unnamed x11 -> x6, waiting for transfers between devices: 23.3 us -> 0.31 us
    reduce_scatter x2, waiting for transfers between devices: 36.8 us -> 55.3 us  [scatter_over_copies(): lax.psum_scatter(values, 'context', scatter_dimension=1, tiled=True)]
  transfers between devices with their start and end apart: 14 -> 19, of which waited for: 11 -> 15; matrix products, arithmetic and copies ran while one was open for 18% -> 19% of each run, Pallas kernels for 0% -> 0%
where the time goes in v3:
time: 1220 us; the launch traced here: 1210 us
  waiting for transfers between devices  761 us (62%)
  matrix products  165 us (14%)
  local copies, waits for them, and re-layouts  128 us (10%)
  starting transfers between devices  82.7 us (7%)
  other arithmetic  57.7 us (5%)
  between operations  15.6 us (1%)
    all_gather x1, waiting for transfers between devices, body(): lax.all_gather(jnp.concatenate([qkv_weight.transpose(1, 0, 2), out_weight...  237 us
    psum x1, waiting for transfers between devices, body(): summed = lax.psum(stacked.astype(bf16), all_axes)  207 us
    reduce_scatter x2, waiting for transfers between devices, scatter_over_copies(): lax.psum_scatter(values, 'context', scatter_dimension=1, tiled=True)  55.3 us
    all_to_all x1, waiting for transfers between devices, body(): lax.all_to_all(send.reshape(sources, local_experts * capacity, width), 'e...  49 us
    all_to_all x1, waiting for transfers between devices, body(): lax.all_to_all(source_major(grad_rows_in, sources, capacity), 'expert', s...  46.6 us
    all_to_all x1, waiting for transfers between devices, body(): lax.all_to_all(source_major(results, sources, capacity), 'expert', split_...  46 us
    ppermute x7, starting transfers between devices, butterfly_sum(): received = lax.ppermute(values, axes, partner)  44.2 us
    all_gather x1, local copies, waits for them, and re-layouts, body(): lax.all_gather(jnp.concatenate([qkv_weight.transpose(1, 0, 2), out_weight...  42.7 us
  transfers between devices with their start and end apart: 19, of which 15 were waited for; matrix products, arithmetic and copies ran while one was open for 19% of the time, Pallas kernels for 0%

profile of v3, /device:TPU:1, one launch (start us, length us, event | category | flops | bytes accessed | tf_op | source)
XLA Modules:
  0.0 1210.0 jit_solution(8714754060576962103)
XLA Ops:
  13.1 237.4 %all-gather.2.cloned.1.call-done = bf16[2048,4,2048]{2,0,1:T(8,128)(2,1)} async-done(((bf16[16,4,2048]{2,0,1:T(8,128)(2,1)}), bf16[2048,4,2048]{2,0,1:T(8,128)(2,1)}) %all-gather.2.cloned.1.call-update) | async-done | bytes 33554448 | tf_op jit(solution)/shard_map/all_gather | solution.py:139
  250.6 42.7 %copy.110 = bf16[2048,4,2048]{0,2,1:T(8,128)(2,1)} copy(bf16[2048,4,2048]{2,0,1:T(8,128)(2,1)} %all-gather.2.cloned.1.call-done) | data formatting | bytes 67108864 | tf_op jit(solution)/shard_map/all_gather | solution.py:139
  293.3 17.2 %fusion.33 = f32[3,128,2048]{2,1,0:T(8,128)S(1)} fusion(bf16[2048,4,2048]{0,2,1:T(8,128)(2,1)} %copy.110, bf16[1,128,2048]{2,1,0:T(8,128)(2,1)S(1)} %fusion.83), kind=kOutput, calls=%fused_computation.54 | convolution fusion | flops 3221225472 | bytes 37224448 | tf_op jit(solution)/shard_map/slice | solution.py:151
  318.0 21.8 %collective-permute-done = bf16[128,2,2048]{2,0,1:T(8,128)(2,1)S(1)} collective-permute-done((bf16[128,2,2048]{2,0,1:T(8,128)(2,1)}, bf16[128,2,2048]{2,0,1:T(8,128)(2,1)S(1)}, u32[]{:S(2)}, u32[]{:S(2)}) %collective-permute-start) | collective-permute-done | bytes 1048608 | tf_op jit(solution)/shard_map/ppermute | solution.py:73
  345.3 3.6 convolution_convert_fusion.3
  349.0 6.5 multiply_reduce_fusion.7
  356.7 9.7 scatter_custom_fusion
  366.4 7.4 all-to-all-start
  374.9 7.0 gather_fusion.2
  382.0 10.0 scatter_custom_fusion.1
  392.0 49.0 %all-to-all-done = bf16[32,40,2048]{2,1,0:T(8,128)(2,1)} async-done(((bf16[32,40,2048]{2,1,0:T(8,128)(2,1)}), bf16[32,40,2048]{2,1,0:T(8,128)(2,1)}, u32[]{:S(2)}, u32[]{:S(2)}) %all-to-all-start) | async-done | bytes 5242912 | tf_op jit(solution)/shard_map/all_to_all | solution.py:199
  441.0 6.5 all-to-all-start.2
  447.7 16.8 %fusion.11 = f32[1,2,1280,1024]{3,2,1,0:T(8,128)S(1)} fusion(bf16[1280,2048,1]{1,0,2:T(8,128)(2,1)} %bitcast.24, bf16[1,2,2048,1024]{3,2,1,0:T(8,128)(2,1)} %param.24), kind=kOutput, calls=%fused_computation.25 | convolution fusion | flops 10737418240 | bytes 24117248 | tf_op jit(solution)/shard_map/lrd,lkdh->lkrh/dot_general | solution.py:207
  464.6 3.9 copy-done.5
  471.2 42.6 %all-to-all-done.2 = bf16[32,40,2048]{2,1,0:T(8,128)(2,1)} async-done(((bf16[32,40,2048]{2,1,0:T(8,128)(2,1)}), bf16[32,40,2048]{2,1,0:T(8,128)(2,1)}, u32[]{:S(2)}, u32[]{:S(2)}) %all-to-all-start.2) | async-done | bytes 5242912 | tf_op jit(solution)/shard_map/all_to_all | solution.py:227
  513.8 10.1 convolution_convert_fusion.2
  524.2 13.1 %fusion.41 = (bf16[1,1,1280,1024]{3,2,1,0:T(8,128)(2,1)S(1)}, bf16[1,1,1280,1024]{3,2,1,0:T(8,128)(2,1)S(1)}) fusion(f32[1,2,1280,1024]{3,2,1,0:T(8,128)} %copy-done.5, bf16[1280,2048]{1,0:T(8,128)(2,1)} %bitcast.41, bf16[1,1024,2048]{2,1,0:T(8,128)(2,1)} %param.25), kind=kOutput, calls=%fused_computation.60 | convolution fusion | flops 5385748480 | bytes 25165824 | tf_op jit(solution)/shard_map/lrd,lhd->lrh/dot_general | solution.py:235
  539.6 15.9 %convert_bitcast_fusion = bf16[2,2048,1024]{1,2,0:T(8,128)(2,1)} fusion(bf16[1280,2048,1]{1,0,2:T(8,128)(2,1)} %bitcast.24, bf16[1,1,1280,1024]{3,2,1,0:T(8,128)(2,1)S(1)} %get-tuple-element.74, bf16[1,1,1280,1024]{3,2,1,0:T(8,128)(2,1)S(1)} %get-tuple-element.73), kind=kOutput, calls=%fused_computation.21 | convolution fusion | flops 10744233984 | bytes 18874368 | tf_op jit(solution)/shard_map/lrd,lkrh->lkdh/dot_general | solution.py:244
  555.6 9.8 convolution_convert_fusion.1
  565.4 9.1 all-to-all-start.1
  574.5 18.8 %bitcast_convert_fusion = bf16[1280,2048]{1,0:T(8,128)(2,1)} fusion(bf16[1,2,2048,1024]{3,2,1,0:T(8,128)(2,1)} %param.24, bf16[1,1,1280,1024]{3,2,1,0:T(8,128)(2,1)} %copy-done.64, bf16[1,1,1280,1024]{3,2,1,0:T(8,128)(2,1)} %copy-done.63), kind=kOutput, calls=%fused_computation.11 | convolution fusion | flops 10742661120 | bytes 18874368 | tf_op jit(solution)/shard_map/lkrh,lkdh->lrd/dot_general | solution.py:247
  593.3 46.0 %all-to-all-done.1 = bf16[32,40,2048]{2,1,0:T(8,128)(2,1)} async-done(((bf16[32,40,2048]{2,1,0:T(8,128)(2,1)}), bf16[32,40,2048]{2,1,0:T(8,128)(2,1)}, u32[]{:S(2)}, u32[]{:S(2)}) %all-to-all-start.1) | async-done | bytes 5242912 | tf_op jit(solution)/shard_map/all_to_all | solution.py:215
  639.2 13.1 %all-to-all-start.3 = ((bf16[32,40,2048]{2,1,0:T(8,128)(2,1)}), bf16[32,40,2048]{2,1,0:T(8,128)(2,1)}, u32[]{:S(2)}, u32[]{:S(2)}) async-start(bf16[32,40,2048]{2,1,0:T(8,128)(2,1)} %bitcast.283), calls=%async_computation.3 | async-start | bytes 10485760 | tf_op jit(solution)/shard_map/all_to_all | solution.py:250
  654.7 12.4 %gather_fusion = bf16[1024,2048]{1,0:T(8,128)(2,1)} fusion(bf16[1280,2048]{1,0:T(8,128)(2,1)} %bitcast.34, s32[1024]{0:T(1024)S(1)} %broadcast_clamp_fusion), kind=kCustom, calls=%fused_computation | custom fusion | bytes 8392704 | tf_op jit(solution)/shard_map/gather | solution.py:218
  667.2 5.0 fusion.4
  672.2 46.6 %all-to-all-done.3 = bf16[32,40,2048]{2,1,0:T(8,128)(2,1)} async-done(((bf16[32,40,2048]{2,1,0:T(8,128)(2,1)}), bf16[32,40,2048]{2,1,0:T(8,128)(2,1)}, u32[]{:S(2)}, u32[]{:S(2)}) %all-to-all-start.3) | async-done | bytes 5242912 | tf_op jit(solution)/shard_map/all_to_all | solution.py:250
  718.8 12.0 gather_fusion.1
  731.0 5.1 convert_reduce_fusion
  739.2 4.7 fusion.43
  744.2 4.7 fusion.104
  767.8 13.0 %collective-permute-done.1 = bf16[128,2,2048]{2,0,1:T(8,128)(2,1)} collective-permute-done((bf16[128,2,2048]{2,0,1:T(8,128)(2,1)}, bf16[128,2,2048]{2,0,1:T(8,128)(2,1)}, u32[]{:S(2)}, u32[]{:S(2)}) %collective-permute-start.1) | collective-permute-done | bytes 1048608 | tf_op jit(solution)/shard_map/ppermute | solution.py:73
  800.2 14.3 %convolution_convert_fusion = bf16[4,2048,2048]{2,1,0:T(8,128)(2,1)} fusion(bf16[1,128,2048]{2,1,0:T(8,128)(2,1)S(1)} %copy-done.26, bf16[1,128,2048]{2,1,0:T(8,128)(2,1)S(1)} %copy-done.2, bf16[1,128,2048]{2,1,0:T(8,128)(2,1)S(1)} %copy-done.25, bf16[3,128,2048]{2,1,0:T(8,128)(2,1)S(1)} %maximum_bitcast_fusion.3), kind=kOutput, calls=%fused_computation.8 | convolution fusion | flops 4315938816 | bytes 36700160 | tf_op jit(solution)/shard_map/sta,stb->sab/dot_general | solution.py:336
  816.2 18.4 %fusion.80 = (f32[2048]{0:T(1024)S(1)}, f32[128]{0:T(128)S(1)}, f32[128,2048]{1,0:T(8,128)}) fusion(bf16[1,128,2048]{2,1,0:T(8,128)(2,1)S(1)} %copy-done.15, f32[128]{0:T(128)S(1)} %copy-done.62, f32[2048]{0:T(1024)S(1)} %copy-done.51, bf16[2048,4,2048]{2,0,1:T(8,128)(2,1)} %all-gather.2.cloned.1.call-done, bf16[128,1,2048]{2,0,1:T(8,128)(2,1)} %slice.230, ...), kind=kOutput, calls=%fused_computation.116 | convolution fusion | flops 4299945984 | bytes 36717576 | tf_op jit(solution)/shard_map/dot_general | solution.py:316
  834.8 7.1 collective-permute-done.2
  841.9 4.8 collective-permute-start.3
  846.7 6.0 collective-permute-done.3
  852.7 15.0 %collective-permute-start.4 = (f32[73728]{0:T(1024)S(1)}, f32[73728]{0:T(1024)S(1)}, u32[]{:S(2)}, u32[]{:S(2)}) collective-permute-start(f32[73728]{0:T(1024)S(1)} %add.208), channel_id=1, source_target_pairs={{0,4},{1,5},{2,6},{3,7},{4,0},{5,1},{6,2},{7,3},{8,12},{9,13},{10,... | collective-permute-start | bytes 884744 | tf_op jit(solution)/shard_map/ppermute | solution.py:100
  867.7 7.7 collective-permute-done.4
  877.1 6.9 collective-permute-done.5
  884.0 3.0 collective-permute-start.6
  887.0 7.5 collective-permute-done.6
  894.6 4.7 collective-permute-start.7
  899.3 6.9 collective-permute-done.7
  907.2 14.9 %collective-permute-start.8 = (f32[73728]{0:T(1024)S(1)}, f32[73728]{0:T(1024)S(1)}, u32[]{:S(2)}, u32[]{:S(2)}) collective-permute-start(f32[73728]{0:T(1024)S(1)} %add.212), channel_id=1, source_target_pairs={{0,64},{1,65},{2,66},{3,67},{4,68},{5,69},{6,70},{7,71},{8,72},{9,... | collective-permute-start | bytes 884744 | tf_op jit(solution)/shard_map/ppermute | solution.py:100
  928.4 207.4 %all-reduce.2.cloned.1.call-done = bf16[4,2048,2048]{2,1,0:T(8,128)(2,1)} async-done(((bf16[4,2048,2048]{2,1,0:T(8,128)(2,1)}), bf16[4,2048,2048]{2,1,0:T(8,128)(2,1)}) %all-reduce.2.cloned.1.call-update) | async-done | bytes 33554448 | tf_op jit(solution)/shard_map/psum | solution.py:337
  1138.2 55.3 %reduce-scatter.7.cloned.1.call-done = bf16[2,512,1024]{1,2,0:T(8,128)(2,1)} async-done(((bf16[2,1024,1024]{1,2,0:T(8,128)(2,1)}), bf16[2,512,1024]{1,2,0:T(8,128)(2,1)}) %reduce-scatter.7.cloned.1.call-update) | async-done | bytes 2097168 | tf_op jit(solution)/shard_map/reduce_scatter | solution.py:327
  1193.4 4.2 bitcast_convert_fusion.1
  1197.6 5.3 copy.141
  (255 shorter events, 83.4 us)
Async XLA Ops:
  7.2 366.9 %copy-start = (bf16[2048,32]{0,1:T(8,128)(2,1)S(1)}, bf16[2048,32]{0,1:T(8,128)(2,1)}, u32[]{:S(2)}) copy-start(bf16[2048,32]{0,1:T(8,128)(2,1)} %param.23) | copy-start | bytes 393220
  7.2 243.4 %all-gather.2.cloned.1.call-start = ((), (), s32[]{:S(2)}) async-start(), calls=%async_computation.8 | async-start | bytes 33816576 | tf_op jit(solution)/shard_map/all_gather | solution.py:139
  10.9 282.3 %copy-start.61 = (f32[128]{0:T(128)}, f32[128]{0:T(128)S(1)}, u32[]{:S(2)}) copy-start(f32[128]{0:T(128)S(1)} %add_rsqrt_fusion.3) | copy-start | bytes 1540
  11.9 301.2 %copy-start.38 = (f32[128,64]{1,0:T(8,128)}, f32[128,64]{1,0:T(8,128)S(1)}, u32[]{:S(2)}) copy-start(f32[128,64]{1,0:T(8,128)S(1)} %get-tuple-element.104) | copy-start | bytes 98308
  13.1 280.1 %copy-start.1 = (bf16[1,128,2048]{2,1,0:T(8,128)(2,1)}, bf16[1,128,2048]{2,1,0:T(8,128)(2,1)S(1)}, u32[]{:S(2)}) copy-start(bf16[1,128,2048]{2,1,0:T(8,128)(2,1)S(1)} %fusion.83) | copy-start | bytes 1572868
  313.8 29.7 %copy-start.16 = (bf16[128,16,64]{2,0,1:T(8,128)(2,1)}, bf16[128,16,64]{2,0,1:T(8,128)(2,1)S(1)}, u32[]{:S(2)}) copy-start(bf16[128,16,64]{2,0,1:T(8,128)(2,1)S(1)} %get-tuple-element.87) | copy-start | bytes 786436
  313.8 29.7 %copy-start.18 = (bf16[128,16,64]{2,0,1:T(8,128)(2,1)}, bf16[128,16,64]{2,0,1:T(8,128)(2,1)S(1)}, u32[]{:S(2)}) copy-start(bf16[128,16,64]{2,0,1:T(8,128)(2,1)S(1)} %get-tuple-element.88) | copy-start | bytes 786436
  315.8 24.0 %collective-permute-start = (bf16[128,2,2048]{2,0,1:T(8,128)(2,1)}, bf16[128,2,2048]{2,0,1:T(8,128)(2,1)S(1)}, u32[]{:S(2)}, u32[]{:S(2)}) collective-permute-start(bf16[128,2,2048]{2,0,1:T(8,128)(2,1)} %pad_maximum_fusion.2), channel_id=1, source_target_pairs={{0,32},{32,0},{1,33},{33,1},{2,34},{34,2},{3,35},{35,3},{4,36},{36... | collective-permute-start | bytes 3145736 | tf_op jit(solution)/shard_map/ppermute | solution.py:73
  343.5 5.5 copy-start.22
  348.9 6.6 copy-start.28
  349.0 7.5 copy-start.43
  355.6 10.8 copy-start.58
  356.7 17.4 %copy-start.12 = (bf16[128,2048]{1,0:T(8,128)(2,1)}, bf16[128,2048]{1,0:T(8,128)(2,1)S(1)}, u32[]{:S(2)}) copy-start(bf16[128,2048]{1,0:T(8,128)(2,1)S(1)} %multiply_convert_fusion.2) | copy-start | bytes 1572868
  366.4 7.6 copy-start.35
  366.4 74.6 %all-to-all-start = ((bf16[32,40,2048]{2,1,0:T(8,128)(2,1)}), bf16[32,40,2048]{2,1,0:T(8,128)(2,1)}, u32[]{:S(2)}, u32[]{:S(2)}) async-start(bf16[32,40,2048]{2,1,0:T(8,128)(2,1)} %bitcast.277), calls=%async_computation | async-start | bytes 10485760 | tf_op jit(solution)/shard_map/all_to_all | solution.py:199
  374.4 7.5 copy-start.41
  441.0 72.8 %all-to-all-start.2 = ((bf16[32,40,2048]{2,1,0:T(8,128)(2,1)}), bf16[32,40,2048]{2,1,0:T(8,128)(2,1)}, u32[]{:S(2)}, u32[]{:S(2)}) async-start(bf16[32,40,2048]{2,1,0:T(8,128)(2,1)} %bitcast.278), calls=%async_computation.2 | async-start | bytes 10485760 | tf_op jit(solution)/shard_map/all_to_all | solution.py:227
  447.5 320.2 %reduce-scatter.9.cloned.1.call-start = ((), (), s32[]{:S(2)}) async-start(), calls=%async_computation.12 | async-start | bytes 6291456 | tf_op jit(solution)/shard_map/reduce_scatter | solution.py:326
  523.9 290.9 %reduce-scatter.5.cloned.1.call-start = ((), (), s32[]{:S(2)}) async-start(), calls=%async_computation.10 | async-start | bytes 12582912 | tf_op jit(solution)/shard_map/reduce_scatter | solution.py:326
  565.4 73.8 %all-to-all-start.1 = ((bf16[32,40,2048]{2,1,0:T(8,128)(2,1)}), bf16[32,40,2048]{2,1,0:T(8,128)(2,1)}, u32[]{:S(2)}, u32[]{:S(2)}) async-start(bf16[32,40,2048]{2,1,0:T(8,128)(2,1)} %bitcast.284), calls=%async_computation.1 | async-start | bytes 10485760 | tf_op jit(solution)/shard_map/all_to_all | solution.py:215
  639.2 13.3 %copy-start.27 = (f32[16,128,256]{2,1,0:T(8,128)S(1)}, f32[16,128,256]{2,1,0:T(8,128)}, u32[]{:S(2)}) copy-start(f32[16,128,256]{2,1,0:T(8,128)} %fusion.116) | copy-start | bytes 6291460
  639.2 79.6 %all-to-all-start.3 = ((bf16[32,40,2048]{2,1,0:T(8,128)(2,1)}), bf16[32,40,2048]{2,1,0:T(8,128)(2,1)}, u32[]{:S(2)}, u32[]{:S(2)}) async-start(bf16[32,40,2048]{2,1,0:T(8,128)(2,1)} %bitcast.283), calls=%async_computation.3 | async-start | bytes 10485760 | tf_op jit(solution)/shard_map/all_to_all | solution.py:250
  652.3 273.2 %reduce-scatter.11.cloned.1.call-start = ((), (), s32[]{:S(2)}) async-start(), calls=%async_computation.13 | async-start | bytes 3145728 | tf_op jit(solution)/shard_map/reduce_scatter | solution.py:327
  718.8 12.0 copy-start.50
  718.8 12.1 copy-start.42
  718.8 12.1 copy-start.53
  730.9 5.3 copy-start.44
  730.9 5.3 copy-start.59
  731.0 5.7 copy-start.36
  744.2 6.8 copy-start.29
  759.7 5.3 copy-start.7
  762.6 18.1 %collective-permute-start.1 = (bf16[128,2,2048]{2,0,1:T(8,128)(2,1)}, bf16[128,2,2048]{2,0,1:T(8,128)(2,1)}, u32[]{:S(2)}, u32[]{:S(2)}) collective-permute-start(bf16[128,2,2048]{2,0,1:T(8,128)(2,1)} %select_convert_fusion), channel_id=1, source_target_pairs={{0,32},{32,0},{1,33},{33,1},{2,34},{34,2},{3,35},{35,3},{4,36},{36... | collective-permute-start | bytes 3145736 | tf_op jit(solution)/shard_map/ppermute | solution.py:73
  767.7 368.0 %all-reduce.2.cloned.1.call-start = ((), (), s32[]{:S(2)}) async-start(), calls=%async_computation.9 | async-start | bytes 67108864 | tf_op jit(solution)/shard_map/psum | solution.py:337
  789.8 6.4 copy-start.4
  789.8 6.4 copy-start.46
  789.8 6.4 copy-start.48
  789.8 6.4 copy-start.55
  789.8 6.4 copy-start.57
  814.5 378.9 %reduce-scatter.7.cloned.1.call-start = ((), (), s32[]{:S(2)}) async-start(), calls=%async_computation.11 | async-start | bytes 6291456 | tf_op jit(solution)/shard_map/reduce_scatter | solution.py:327
  834.6 87.5 %copy-start.24 = (f32[128,2048]{1,0:T(8,128)S(1)}, f32[128,2048]{1,0:T(8,128)}, u32[]{:S(2)}) copy-start(f32[128,2048]{1,0:T(8,128)} %copy-done.23) | copy-start | bytes 3145732
  834.6 87.5 %copy-start.37 = (f32[128,2048]{1,0:T(8,128)S(1)}, f32[128,2048]{1,0:T(8,128)}, u32[]{:S(2)}) copy-start(f32[128,2048]{1,0:T(8,128)} %get-tuple-element.110) | copy-start | bytes 3145732
  834.7 7.2 collective-permute-start.2
  841.9 10.7 collective-permute-start.3
  852.7 22.7 %collective-permute-start.4 = (f32[73728]{0:T(1024)S(1)}, f32[73728]{0:T(1024)S(1)}, u32[]{:S(2)}, u32[]{:S(2)}) collective-permute-start(f32[73728]{0:T(1024)S(1)} %add.208), channel_id=1, source_target_pairs={{0,4},{1,5},{2,6},{3,7},{4,0},{5,1},{6,2},{7,3},{8,12},{9,13},{10,... | collective-permute-start | bytes 884744 | tf_op jit(solution)/shard_map/ppermute | solution.py:100
  875.4 8.6 collective-permute-start.5
  884.0 10.6 collective-permute-start.6
  894.6 11.7 collective-permute-start.7
  907.2 16.3 %collective-permute-start.8 = (f32[73728]{0:T(1024)S(1)}, f32[73728]{0:T(1024)S(1)}, u32[]{:S(2)}, u32[]{:S(2)}) collective-permute-start(f32[73728]{0:T(1024)S(1)} %add.212), channel_id=1, source_target_pairs={{0,64},{1,65},{2,66},{3,67},{4,68},{5,69},{6,70},{7,71},{8,72},{9,... | collective-permute-start | bytes 884744 | tf_op jit(solution)/shard_map/ppermute | solution.py:100
  (36 other events, 68.5 us)
Sparse Core Ops, SparseCore 0:
  10.3 240.1 all-gather.1
  524.0 22.0 reduce-scatter.8
  555.7 26.7 reduce-scatter.4
  767.8 43.8 reduce-scatter.10
  818.0 317.6 all-reduce.1
  1138.1 55.2 reduce-scatter.6

commit v4 on v3

--- a/solution.py
+++ b/solution.py
@@ -1,6 +1,10 @@
+import functools
+
 import jax
 import jax.numpy as jnp
 from jax import lax
+from jax.experimental import pallas as pl
+from jax.experimental.pallas import tpu as pltpu
 from jax.sharding import PartitionSpec as P
 
 HDIM = 128
@@ -67,6 +71,40 @@
         .transpose(1, 0, 2, 3)
         .reshape(sources, local_experts * capacity, width)
     )
+
+
+def _project_kernel(inputs_ref, weights_ref, out_ref):
+    out_ref[0] = jnp.dot(inputs_ref[...], weights_ref[0], preferred_element_type=jnp.float32)
+
+
+def project(inputs, weights, blocks, tile=512):
+    tokens, depth = inputs.shape
+    columns = weights.shape[2]
+    return pl.pallas_call(
+        _project_kernel,
+        out_shape=jax.ShapeDtypeStruct((blocks, tokens, columns), jnp.float32),
+        grid=(blocks, columns // tile),
+        in_specs=[
+            pl.BlockSpec((tokens, depth), lambda s, j: (0, 0)),
+            pl.BlockSpec((1, depth, tile), lambda s, j: (s, 0, j)),
+        ],
+        out_specs=pl.BlockSpec((1, tokens, tile), lambda s, j: (s, 0, j)),
+        cost_estimate=pl.CostEstimate(
+            flops=2 * tokens * depth * columns * blocks,
+            transcendentals=0,
+            bytes_accessed=2 * depth * columns * blocks + 2 * tokens * depth
+            + 4 * tokens * columns * blocks,
+        ),
+    )(inputs, weights)
+
+
+def sum_halves(values, axis, dim):
+    half = values.shape[dim] // 2
+    index = lax.axis_index(axis)
+    own = lax.dynamic_slice_in_dim(values, index * half, half, axis=dim)
+    given = lax.dynamic_slice_in_dim(values, (1 - index) * half, half, axis=dim)
+    received = lax.ppermute(given.astype(jnp.bfloat16), axis, [(0, 1), (1, 0)])
+    return own + received.astype(own.dtype)
 
 
 def swap_context(values):
@@ -143,12 +181,7 @@
         tiled=True,
     )
     out_full = weights_full[:, 3, :]
-    projected_all = jnp.dot(
-        attention_input,
-        weights_full.reshape(width, 4 * heads_width),
-        preferred_element_type=single_precision,
-    ).reshape(seq_tok, 4, heads_width)
-    projected_output = projected_all[:, :3].transpose(1, 0, 2)
+    projected_output = project(attention_input, weights_full.transpose(1, 0, 2), 3)
     q_normed, q_factor = rms_forward(projected_output[0])
     k_normed, k_factor = rms_forward(projected_output[1])
     values = projected_output[2].astype(bf16)
@@ -323,9 +356,7 @@
     )
     grad_tokens = grad_mid + grad_x_norm
     def scatter_over_copies(values):
-        values = lax.psum_scatter(values.astype(bf16), "dp", scatter_dimension=1, tiled=True)
-        values = lax.psum_scatter(values, "context", scatter_dimension=1, tiled=True)
-        return values.astype(single_precision)
+        return sum_halves(sum_halves(values, "dp", 1), "context", 1)
 
     grad_in_shard = scatter_over_copies(grad_gate_up_w[0])[None]
     grad_down_shard = scatter_over_copies(grad_down[0])[None]

time: 1220 us -> 1090 us (0.89)
  waiting for transfers between devices: 761 us -> 671 us
  matrix products: 165 us -> 137 us
  local copies, waits for them, and re-layouts: 128 us -> 101 us
  other arithmetic: 57.7 us -> 83.7 us
  starting transfers between devices: 82.7 us -> 61.1 us
  Pallas kernels: 0 us -> 15 us
    reduce_scatter x4 -> x0, waiting for transfers between devices: 55.3 us -> none  [the longest x2 55.3 us: scatter_over_copies(): lax.psum_scatter(values, 'context', scatter_dimension=1, tiled=True)]
    all_gather x1 -> x0, local copies, waits for them, and re-layouts: 42.7 us -> none  [body(): lax.all_gather(jnp.concatenate([qkv_weight.transpose(1, 0, 2), out_weight...]
    psum x1, waiting for transfers between devices: 207 us -> 166 us  [body(): summed = lax.psum(stacked.astype(bf16), all_axes)]
    ppermute x7, starting transfers between devices: 44.2 us -> 12.1 us  [butterfly_sum(): received = lax.ppermute(values, axes, partner)]
    ppermute x7, waiting for transfers between devices: 42 us -> 65.9 us  [butterfly_sum(): received = lax.ppermute(values, axes, partner)]
    slice x1 -> x0, matrix products: 17.2 us -> none  [body(): projected_output = projected_all[:, :3].transpose(1, 0, 2)]
    add x0 -> x2, other arithmetic: none -> 15.2 us  [sum_halves(): return own + received.astype(own.dtype)]
    pallas_call x0 -> x1, Pallas kernels: none -> 15 us  [project(): pl.pallas_call(_project_kernel, out_shape=jax.ShapeDtypeStruct((blocks, t...]
  transfers between devices with their start and end apart: 19 -> 19, of which waited for: 15 -> 15; matrix products, arithmetic and copies ran while one was open for 19% -> 17% of each run, Pallas kernels for 0% -> 0%
where the time goes in v4:
time: 1090 us; the launch traced here: 1080 us
  waiting for transfers between devices  671 us (62%)
  matrix products  137 us (13%)
  local copies, waits for them, and re-layouts  101 us (9%)
  other arithmetic  83.7 us (8%)
  starting transfers between devices  61.1 us (6%)
  between operations  15.3 us (1%)
  Pallas kernels  15 us (1%)
    all_gather x1, waiting for transfers between devices, body(): lax.all_gather(jnp.concatenate([qkv_weight.transpose(1, 0, 2), out_weight...  237 us
    psum x1, waiting for transfers between devices, body(): summed = lax.psum(stacked.astype(bf16), all_axes)  166 us
    ppermute x7, waiting for transfers between devices, butterfly_sum(): received = lax.ppermute(values, axes, partner)  65.9 us
    all_to_all x1, waiting for transfers between devices, body(): lax.all_to_all(send.reshape(sources, local_experts * capacity, width), 'e...  48.5 us
    all_to_all x1, waiting for transfers between devices, body(): lax.all_to_all(source_major(grad_rows_in, sources, capacity), 'expert', s...  43.8 us
    all_to_all x1, waiting for transfers between devices, body(): lax.all_to_all(grad_send.reshape(sources, local_experts * capacity, width...  35.6 us
    all_to_all x1, waiting for transfers between devices, body(): lax.all_to_all(source_major(results, sources, capacity), 'expert', split_...  35.5 us
    ppermute x2, waiting for transfers between devices, swap_context(): return lax.ppermute(values, 'context', [(0, 1), (1, 0)])  35.4 us
  transfers between devices with their start and end apart: 19, of which 15 were waited for; matrix products, arithmetic and copies ran while one was open for 17% of the time, Pallas kernels for 0%

profile of v4, /device:TPU:1, one launch (start us, length us, event | category | flops | bytes accessed | tf_op | source)
XLA Modules:
  0.0 1083.7 jit_solution(12681830691330583733)
XLA Ops:
  13.9 236.6 %all-gather.2.cloned.1.call-done = bf16[2048,4,2048]{2,0,1:T(8,128)(2,1)} async-done(((bf16[16,4,2048]{2,0,1:T(8,128)(2,1)}), bf16[2048,4,2048]{2,0,1:T(8,128)(2,1)}) %all-gather.2.cloned.1.call-update) | async-done | bytes 33554448 | tf_op jit(solution)/shard_map/all_gather | solution.py:177
  250.6 15.0 %shard_map.215 = f32[3,128,2048]{2,1,0:T(8,128)} custom-call(bf16[128,2048]{1,0:T(8,128)(2,1)} %fusion.74.inputs_ref, bf16[4,2048,2048]{2,1,0:T(8,128)(2,1)} %bitcast.271), custom_call_target="tpu_custom_call" | custom-call | flops 3221225472 | bytes 28835840 | tf_op jit(solution)/shard_map/pallas_call | solution.py:83
  273.9 21.7 %collective-permute-done = bf16[128,2,2048]{2,0,1:T(8,128)(2,1)} collective-permute-done((bf16[128,2,2048]{2,0,1:T(8,128)(2,1)S(1)}, bf16[128,2,2048]{2,0,1:T(8,128)(2,1)}, u32[]{:S(2)}, u32[]{:S(2)}) %collective-permute-start) | collective-permute-done | bytes 1048608 | tf_op jit(solution)/shard_map/ppermute | solution.py:111
  304.6 4.7 convolution_convert_fusion.2
  309.3 6.5 multiply_reduce_fusion.7
  316.0 9.7 scatter_custom_fusion
  325.6 6.9 all-to-all-start
  334.3 7.0 gather_fusion.2
  341.3 10.0 scatter_custom_fusion.1
  351.3 48.5 %all-to-all-done = bf16[32,40,2048]{2,1,0:T(8,128)(2,1)} async-done(((bf16[32,40,2048]{2,1,0:T(8,128)(2,1)}), bf16[32,40,2048]{2,1,0:T(8,128)(2,1)}, u32[]{:S(2)}, u32[]{:S(2)}) %all-to-all-start) | async-done | bytes 5242912 | tf_op jit(solution)/shard_map/all_to_all | solution.py:232
  399.8 6.9 all-to-all-start.2
  406.7 16.8 %fusion.9 = f32[1,2,1280,1024]{3,2,1,0:T(8,128)S(1)} fusion(bf16[1280,2048,1]{1,0,2:T(8,128)(2,1)} %bitcast.19, bf16[1,2,2048,1024]{3,2,1,0:T(8,128)(2,1)} %param.24), kind=kOutput, calls=%fused_computation.24 | convolution fusion | flops 10737418240 | bytes 24117248 | tf_op jit(solution)/shard_map/lrd,lkdh->lkrh/dot_general | solution.py:240
  430.1 7.3 convolution_convert_fusion.1
  437.4 35.6 %all-to-all-done.2 = bf16[32,40,2048]{2,1,0:T(8,128)(2,1)} async-done(((bf16[32,40,2048]{2,1,0:T(8,128)(2,1)}), bf16[32,40,2048]{2,1,0:T(8,128)(2,1)}, u32[]{:S(2)}, u32[]{:S(2)}) %all-to-all-start.2) | async-done | bytes 5242912 | tf_op jit(solution)/shard_map/all_to_all | solution.py:260
  473.0 8.7 all-to-all-start.1
  481.7 13.1 %fusion.39 = (bf16[1,1,1280,1024]{3,2,1,0:T(8,128)(2,1)S(1)}, bf16[1,1,1280,1024]{3,2,1,0:T(8,128)(2,1)S(1)}) fusion(f32[1,2,1280,1024]{3,2,1,0:T(8,128)} %copy-done.5, bf16[1280,2048]{1,0:T(8,128)(2,1)} %bitcast.36, bf16[1,1024,2048]{2,1,0:T(8,128)(2,1)} %param.25), kind=kOutput, calls=%fused_computation.64 | convolution fusion | flops 5385748480 | bytes 25165824 | tf_op jit(solution)/shard_map/lrd,lhd->lrh/dot_general | solution.py:268
  497.1 15.1 %bitcast_convert_fusion = bf16[1280,2048]{1,0:T(8,128)(2,1)} fusion(bf16[1,2,2048,1024]{3,2,1,0:T(8,128)(2,1)} %param.24, bf16[1,1,1280,1024]{3,2,1,0:T(8,128)(2,1)S(1)} %get-tuple-element.74, bf16[1,1,1280,1024]{3,2,1,0:T(8,128)(2,1)S(1)} %get-tuple-element.73), kind=kOutput, calls=%fused_computation.9 | convolution fusion | flops 10742661120 | bytes 18874368 | tf_op jit(solution)/shard_map/lkrh,lkdh->lrd/dot_general | solution.py:280
  512.2 35.5 %all-to-all-done.1 = bf16[32,40,2048]{2,1,0:T(8,128)(2,1)} async-done(((bf16[32,40,2048]{2,1,0:T(8,128)(2,1)}), bf16[32,40,2048]{2,1,0:T(8,128)(2,1)}, u32[]{:S(2)}, u32[]{:S(2)}) %all-to-all-start.1) | async-done | bytes 5242912 | tf_op jit(solution)/shard_map/all_to_all | solution.py:248
  547.7 11.1 %all-to-all-start.3 = ((bf16[32,40,2048]{2,1,0:T(8,128)(2,1)}), bf16[32,40,2048]{2,1,0:T(8,128)(2,1)}, u32[]{:S(2)}, u32[]{:S(2)}) async-start(bf16[32,40,2048]{2,1,0:T(8,128)(2,1)} %bitcast.278), calls=%async_computation.3 | async-start | bytes 10485760 | tf_op jit(solution)/shard_map/all_to_all | solution.py:283
  558.9 4.4 fusion.43
  563.3 12.2 %gather_fusion = bf16[1024,2048]{1,0:T(8,128)(2,1)} fusion(bf16[1280,2048]{1,0:T(8,128)(2,1)} %bitcast.29, s32[1024]{0:T(1024)S(1)} %broadcast_clamp_fusion), kind=kCustom, calls=%fused_computation | custom fusion | bytes 8392704 | tf_op jit(solution)/shard_map/gather | solution.py:251
  575.5 5.9 fusion.2
  581.6 43.8 %all-to-all-done.3 = bf16[32,40,2048]{2,1,0:T(8,128)(2,1)} async-done(((bf16[32,40,2048]{2,1,0:T(8,128)(2,1)}), bf16[32,40,2048]{2,1,0:T(8,128)(2,1)}, u32[]{:S(2)}, u32[]{:S(2)}) %all-to-all-start.3) | async-done | bytes 5242912 | tf_op jit(solution)/shard_map/all_to_all | solution.py:283
  625.3 12.0 %gather_fusion.1 = bf16[1024,2048]{1,0:T(8,128)(2,1)} fusion(bf16[1280,2048]{1,0:T(8,128)(2,1)} %bitcast.44, s32[1024]{0:T(1024)S(1)} %broadcast_clamp_fusion), kind=kCustom, calls=%fused_computation.1 | custom fusion | bytes 8392704 | tf_op jit(solution)/shard_map/gather | solution.py:290
  637.3 5.2 convert_reduce_fusion
  645.6 4.7 fusion.41
  650.8 4.7 fusion.103
  677.2 13.7 %collective-permute-done.1 = bf16[128,2,2048]{2,0,1:T(8,128)(2,1)} collective-permute-done((bf16[128,2,2048]{2,0,1:T(8,128)(2,1)}, bf16[128,2,2048]{2,0,1:T(8,128)(2,1)}, u32[]{:S(2)}, u32[]{:S(2)}) %collective-permute-start.1) | collective-permute-done | bytes 1048608 | tf_op jit(solution)/shard_map/ppermute | solution.py:111
  712.3 14.4 %convolution_convert_fusion = bf16[4,2048,2048]{2,1,0:T(8,128)(2,1)} fusion(bf16[1,128,2048]{2,1,0:T(8,128)(2,1)S(1)} %copy-done.27, bf16[1,128,2048]{2,1,0:T(8,128)(2,1)S(1)} %copy-done.25, bf16[1,128,2048]{2,1,0:T(8,128)(2,1)S(1)} %copy-done.26, bf16[3,128,2048]{2,1,0:T(8,128)(2,1)S(1)} %maximum_bitcast_fusion.3), kind=kOutput, calls=%fused_computation.6 | convolution fusion | flops 4315938816 | bytes 36700160 | tf_op jit(solution)/shard_map/sta,stb->sab/dot_general | solution.py:367
  728.4 14.3 %fusion.32 = f32[2,1024,2048]{2,1,0:T(8,128)S(1)} fusion(bf16[1280,2048,1]{1,0,2:T(8,128)(2,1)} %bitcast.19, bf16[1,1,1280,1024]{3,2,1,0:T(8,128)(2,1)} %copy-done.58, bf16[1,1,1280,1024]{3,2,1,0:T(8,128)(2,1)S(1)} %copy-done.57), kind=kOutput, calls=%fused_computation.57 | convolution fusion | flops 10740039680 | bytes 27262976 | tf_op jit(solution)/shard_map/lrd,lkrh->lkdh/dot_general | solution.py:277
  745.5 5.9 collective-permute-start.9
  751.4 7.8 fusion.33
  765.7 3.9 collective-permute-done.11
  769.6 3.6 convert_add_fusion
  777.9 11.5 %bitcast_add_fusion = f32[2,1024,1024]{1,2,0:T(8,128)} fusion(bf16[2,1024,1024]{1,2,0:T(8,128)(2,1)} %collective-permute-done.9, f32[2,1024,2048]{2,1,0:T(8,128)} %copy-done.6, s32[]{:T(128)S(6)} %select_n.124), kind=kLoop, calls=%fused_computation.13 | loop fusion | flops 4194304 | bytes 20971524 | tf_op jit(solution)/shard_map/add | solution.py:107
  790.1 17.3 %fusion.80 = (f32[2048]{0:T(1024)S(1)}, f32[128]{0:T(128)S(1)}, f32[128,2048]{1,0:T(8,128)}) fusion(bf16[1,128,2048]{2,1,0:T(8,128)(2,1)S(1)} %copy-done.14, f32[128]{0:T(128)S(1)} %copy-done.53, f32[2048]{0:T(1024)S(1)} %copy-done.45, bf16[2048,4,2048]{2,0,1:T(8,128)(2,1)} %all-gather.2.cloned.1.call-done, bf16[128,1,2048]{2,0,1:T(8,128)(2,1)S(1)} %copy-done.34, ...), kind=kOutput, calls=%fused_computation.123 | convolution fusion | flops 4299945984 | bytes 36717576 | tf_op jit(solution)/shard_map/dot_general | solution.py:349
  808.0 3.9 dynamic-slice_convert_fusion.2
  812.3 10.0 collective-permute-done.2
  822.4 9.4 collective-permute-done.3
  831.9 7.3 collective-permute-start.4
  839.2 9.5 collective-permute-done.4
  848.8 8.0 collective-permute-done.5
  859.3 3.7 add_bitcast_fusion.1
  863.0 3.7 collective-permute-done.6
  868.6 25.3 %collective-permute-done.7 = f32[73728]{0:T(1024)S(1)} collective-permute-done((f32[73728]{0:T(1024)S(1)}, f32[73728]{0:T(1024)S(1)}, u32[]{:S(2)}, u32[]{:S(2)}) %collective-permute-start.7) | collective-permute-done | bytes 294944 | tf_op jit(solution)/shard_map/ppermute | solution.py:138
  894.9 5.5 add_bitcast_fusion
  900.5 5.5 copy.138
  907.9 166.3 %all-reduce.2.cloned.1.call-done = bf16[4,2048,2048]{2,1,0:T(8,128)(2,1)} async-done(((bf16[4,2048,2048]{2,1,0:T(8,128)(2,1)}), bf16[4,2048,2048]{2,1,0:T(8,128)(2,1)}) %all-reduce.2.cloned.1.call-update) | async-done | bytes 33554448 | tf_op jit(solution)/shard_map/psum | solution.py:368
  (245 shorter events, 108.4 us)
Async XLA Ops:
  7.2 326.8 %copy-start = (bf16[2048,32]{0,1:T(8,128)(2,1)S(1)}, bf16[2048,32]{0,1:T(8,128)(2,1)}, u32[]{:S(2)}) copy-start(bf16[2048,32]{0,1:T(8,128)(2,1)} %param.23) | copy-start | bytes 393220
  7.2 243.4 %all-gather.2.cloned.1.call-start = ((), (), s32[]{:S(2)}) async-start(), calls=%async_computation.4 | async-start | bytes 33816576 | tf_op jit(solution)/shard_map/all_gather | solution.py:177
  11.9 258.1 %copy-start.37 = (f32[128,64]{1,0:T(8,128)}, f32[128,64]{1,0:T(8,128)S(1)}, u32[]{:S(2)}) copy-start(f32[128,64]{1,0:T(8,128)S(1)} %get-tuple-element.104) | copy-start | bytes 98308
  270.7 32.1 %copy-start.16 = (bf16[128,16,64]{2,0,1:T(8,128)(2,1)}, bf16[128,16,64]{2,0,1:T(8,128)(2,1)S(1)}, u32[]{:S(2)}) copy-start(bf16[128,16,64]{2,0,1:T(8,128)(2,1)S(1)} %get-tuple-element.88) | copy-start | bytes 786436
  271.7 23.9 %collective-permute-start = (bf16[128,2,2048]{2,0,1:T(8,128)(2,1)S(1)}, bf16[128,2,2048]{2,0,1:T(8,128)(2,1)}, u32[]{:S(2)}, u32[]{:S(2)}) collective-permute-start(bf16[128,2,2048]{2,0,1:T(8,128)(2,1)S(1)} %pad_maximum_fusion.2), channel_id=1, source_target_pairs={{0,32},{32,0},{1,33},{33,1},{2,34},{34,2},{3,35},{35,3},{4,36},{36... | collective-permute-start | bytes 3145736 | tf_op jit(solution)/shard_map/ppermute | solution.py:111
  299.9 9.3 copy-start.7
  302.8 6.5 copy-start.12
  309.3 6.6 copy-start.40
  316.0 18.0 %copy-start.10 = (bf16[128,2048]{1,0:T(8,128)(2,1)}, bf16[128,2048]{1,0:T(8,128)(2,1)S(1)}, u32[]{:S(2)}) copy-start(bf16[128,2048]{1,0:T(8,128)(2,1)S(1)} %multiply_convert_fusion.2) | copy-start | bytes 1572868
  325.6 74.1 %all-to-all-start = ((bf16[32,40,2048]{2,1,0:T(8,128)(2,1)}), bf16[32,40,2048]{2,1,0:T(8,128)(2,1)}, u32[]{:S(2)}, u32[]{:S(2)}) async-start(bf16[32,40,2048]{2,1,0:T(8,128)(2,1)} %bitcast.272), calls=%async_computation | async-start | bytes 10485760 | tf_op jit(solution)/shard_map/all_to_all | solution.py:232
  399.8 73.2 %all-to-all-start.2 = ((bf16[32,40,2048]{2,1,0:T(8,128)(2,1)}), bf16[32,40,2048]{2,1,0:T(8,128)(2,1)}, u32[]{:S(2)}, u32[]{:S(2)}) async-start(bf16[32,40,2048]{2,1,0:T(8,128)(2,1)} %bitcast.273), calls=%async_computation.2 | async-start | bytes 10485760 | tf_op jit(solution)/shard_map/all_to_all | solution.py:260
  423.6 6.5 copy-start.55
  473.0 74.6 %all-to-all-start.1 = ((bf16[32,40,2048]{2,1,0:T(8,128)(2,1)}), bf16[32,40,2048]{2,1,0:T(8,128)(2,1)}, u32[]{:S(2)}, u32[]{:S(2)}) async-start(bf16[32,40,2048]{2,1,0:T(8,128)(2,1)} %bitcast.279), calls=%async_computation.1 | async-start | bytes 10485760 | tf_op jit(solution)/shard_map/all_to_all | solution.py:248
  547.7 77.7 %all-to-all-start.3 = ((bf16[32,40,2048]{2,1,0:T(8,128)(2,1)}), bf16[32,40,2048]{2,1,0:T(8,128)(2,1)}, u32[]{:S(2)}, u32[]{:S(2)}) async-start(bf16[32,40,2048]{2,1,0:T(8,128)(2,1)} %bitcast.278), calls=%async_computation.3 | async-start | bytes 10485760 | tf_op jit(solution)/shard_map/all_to_all | solution.py:283
  558.7 515.5 %all-reduce.2.cloned.1.call-start = ((), (), s32[]{:S(2)}) async-start(), calls=%async_computation.5 | async-start | bytes 67108864 | tf_op jit(solution)/shard_map/psum | solution.py:368
  663.4 8.9 copy-start.45
  663.4 8.9 copy-start.52
  666.3 6.0 copy-start.13
  666.3 9.0 copy-start.8
  669.2 21.7 %collective-permute-start.1 = (bf16[128,2,2048]{2,0,1:T(8,128)(2,1)}, bf16[128,2,2048]{2,0,1:T(8,128)(2,1)}, u32[]{:S(2)}, u32[]{:S(2)}) collective-permute-start(bf16[128,2,2048]{2,0,1:T(8,128)(2,1)} %select_convert_fusion), channel_id=1, source_target_pairs={{0,32},{32,0},{1,33},{33,1},{2,34},{34,2},{3,35},{35,3},{4,36},{36... | collective-permute-start | bytes 3145736 | tf_op jit(solution)/shard_map/ppermute | solution.py:111
  675.4 15.5 %copy-start.3 = (f32[256,1,2048]{2,0,1:T(8,128)S(1)}, f32[256,1,2048]{2,0,1:T(8,128)}, u32[]{:S(2)}) copy-start(f32[256,1,2048]{2,0,1:T(8,128)} %copy.146) | copy-start | bytes 6291460
  700.0 8.4 copy-start.2
  700.0 8.4 copy-start.42
  700.0 8.4 copy-start.44
  700.0 8.4 copy-start.48
  700.0 8.4 copy-start.50
  742.7 16.4 %copy-start.6 = (f32[2,1024,2048]{2,1,0:T(8,128)}, f32[2,1024,2048]{2,1,0:T(8,128)S(1)}, u32[]{:S(2)}) copy-start(f32[2,1024,2048]{2,1,0:T(8,128)S(1)} %fusion.32) | copy-start | bytes 50331652
  742.7 8.6 copy-start.24
  745.5 32.4 %collective-permute-start.9 = (bf16[2,1024,1024]{1,2,0:T(8,128)(2,1)}, bf16[2,1024,1024]{1,2,0:T(8,128)(2,1)}, u32[]{:S(2)}, u32[]{:S(2)}) collective-permute-start(bf16[2,1024,1024]{1,2,0:T(8,128)(2,1)} %fusion.21), channel_id=1, source_target_pairs={{0,64},{64,0},{1,65},{65,1},{2,66},{66,2},{3,67},{67,3},{4,68},{68... | collective-permute-start | bytes 12582920 | tf_op jit(solution)/shard_map/ppermute | solution.py:106
  762.5 7.1 collective-permute-start.11
  776.3 13.1 %copy-start.11 = (bf16[128,2048]{1,0:T(8,128)(2,1)S(1)}, bf16[128,2048]{1,0:T(8,128)(2,1)}, u32[]{:S(2)}) copy-start(bf16[128,2048]{1,0:T(8,128)(2,1)} %copy-done.10) | copy-start | bytes 1572868
  776.3 13.8 %copy-start.14 = (bf16[1,128,2048]{2,1,0:T(8,128)(2,1)S(1)}, bf16[1,128,2048]{2,1,0:T(8,128)(2,1)}, u32[]{:S(2)}) copy-start(bf16[1,128,2048]{2,1,0:T(8,128)(2,1)} %param.13) | copy-start | bytes 1572868
  776.3 13.8 %copy-start.30 = (bf16[128,1,2048]{2,0,1:T(8,128)(2,1)S(1)}, bf16[128,1,2048]{2,0,1:T(8,128)(2,1)}, u32[]{:S(2)}) copy-start(bf16[128,1,2048]{2,0,1:T(8,128)(2,1)} %copy-done.29) | copy-start | bytes 1572868
  776.3 13.8 %copy-start.32 = (bf16[128,1,2048]{2,0,1:T(8,128)(2,1)S(1)}, bf16[128,1,2048]{2,0,1:T(8,128)(2,1)}, u32[]{:S(2)}) copy-start(bf16[128,1,2048]{2,0,1:T(8,128)(2,1)} %copy-done.31) | copy-start | bytes 1572868
  776.3 13.8 %copy-start.34 = (bf16[128,1,2048]{2,0,1:T(8,128)(2,1)S(1)}, bf16[128,1,2048]{2,0,1:T(8,128)(2,1)}, u32[]{:S(2)}) copy-start(bf16[128,1,2048]{2,0,1:T(8,128)(2,1)} %slice.226) | copy-start | bytes 1572868
  776.3 13.8 %copy-start.53 = (f32[128]{0:T(128)S(1)}, f32[128]{0:T(128)}, u32[]{:S(2)}) copy-start(f32[128]{0:T(128)} %copy-done.51) | copy-start | bytes 1540
  776.3 83.0 %collective-permute-start.12 = (bf16[1024,512]{1,0:T(8,128)(2,1)}, bf16[1024,512]{1,0:T(8,128)(2,1)}, u32[]{:S(2)}, u32[]{:S(2)}) collective-permute-start(bf16[1024,512]{1,0:T(8,128)(2,1)} %dynamic-slice_convert_fusion.3), channel_id=1, source_target_pairs={{0,32},{32,0},{1,33},{33,1},{2,34},{34,2},{3,35},{35,3},{4,36},{36... | collective-permute-start | bytes 3145736 | tf_op jit(solution)/shard_map/ppermute | solution.py:106
  807.4 14.9 %collective-permute-start.2 = (f32[73728]{0:T(1024)S(1)}, f32[73728]{0:T(1024)S(1)}, u32[]{:S(2)}, u32[]{:S(2)}) collective-permute-start(f32[73728]{0:T(1024)S(1)} %constant_dynamic-update-slice_fusion), channel_id=1, source_target_pairs={{0,1},{1,0},{2,3},{3,2},{4,5},{5,4},{6,7},{7,6},{8,9},{9,8},{10,11... | collective-permute-start | bytes 884744 | tf_op jit(solution)/shard_map/ppermute | solution.py:138
  811.9 83.0 %collective-permute-start.10 = (bf16[2,512,1024]{1,2,0:T(8,128)(2,1)}, bf16[2,512,1024]{1,2,0:T(8,128)(2,1)}, u32[]{:S(2)}, u32[]{:S(2)}) collective-permute-start(bf16[2,512,1024]{1,2,0:T(8,128)(2,1)} %dynamic-slice_convert_fusion.2), channel_id=1, source_target_pairs={{0,32},{32,0},{1,33},{33,1},{2,34},{34,2},{3,35},{35,3},{4,36},{36... | collective-permute-start | bytes 6291464 | tf_op jit(solution)/shard_map/ppermute | solution.py:106
  822.3 44.9 %copy-start.22 = (f32[128,2048]{1,0:T(8,128)S(1)}, f32[128,2048]{1,0:T(8,128)}, u32[]{:S(2)}) copy-start(f32[128,2048]{1,0:T(8,128)} %copy-done.21) | copy-start | bytes 3145732
  822.3 44.9 %copy-start.36 = (f32[128,2048]{1,0:T(8,128)S(1)}, f32[128,2048]{1,0:T(8,128)}, u32[]{:S(2)}) copy-start(f32[128,2048]{1,0:T(8,128)} %get-tuple-element.110) | copy-start | bytes 3145732
  822.4 9.5 collective-permute-start.3
  831.9 16.8 %collective-permute-start.4 = (f32[73728]{0:T(1024)S(1)}, f32[73728]{0:T(1024)S(1)}, u32[]{:S(2)}, u32[]{:S(2)}) collective-permute-start(f32[73728]{0:T(1024)S(1)} %add.228), channel_id=1, source_target_pairs={{0,4},{1,5},{2,6},{3,7},{4,0},{5,1},{6,2},{7,3},{8,12},{9,13},{10,... | collective-permute-start | bytes 884744 | tf_op jit(solution)/shard_map/ppermute | solution.py:138
  848.7 8.1 collective-permute-start.5
  856.9 9.8 collective-permute-start.6
  866.7 27.1 %collective-permute-start.7 = (f32[73728]{0:T(1024)S(1)}, f32[73728]{0:T(1024)S(1)}, u32[]{:S(2)}, u32[]{:S(2)}) collective-permute-start(f32[73728]{0:T(1024)S(1)} %add.231), channel_id=1, source_target_pairs={{0,32},{1,33},{2,34},{3,35},{4,36},{5,37},{6,38},{7,39},{8,40},{9,... | collective-permute-start | bytes 884744 | tf_op jit(solution)/shard_map/ppermute | solution.py:138
  893.9 12.0 %collective-permute-start.8 = (f32[73728]{0:T(1024)S(1)}, f32[73728]{0:T(1024)S(1)}, u32[]{:S(2)}, u32[]{:S(2)}) collective-permute-start(f32[73728]{0:T(1024)S(1)} %add.232), channel_id=1, source_target_pairs={{0,64},{1,65},{2,66},{3,67},{4,68},{5,69},{6,70},{7,71},{8,72},{9,... | collective-permute-start | bytes 884744 | tf_op jit(solution)/shard_map/ppermute | solution.py:138
  900.5 176.2 %copy-start.1 = (bf16[2048,32]{0,1:T(8,128)(2,1)S(1)}, bf16[2048,32]{0,1:T(8,128)(2,1)}, u32[]{:S(2)}) copy-start(bf16[2048,32]{0,1:T(8,128)(2,1)} %param.23) | copy-start | bytes 393220
  (30 other events, 66.6 us)
Sparse Core Ops, SparseCore 0:
  10.3 240.1 all-gather.1
  726.8 347.3 all-reduce.1

commit v5 on v4

--- a/solution.py
+++ b/solution.py
@@ -268,15 +268,9 @@
     grad_hidden = jnp.einsum(
         "lrd,lhd->lrh", grad_rows, expert_out, preferred_element_type=single_precision
     )
-    grad_down = jnp.einsum(
-        "lrh,lrd->lhd", hidden, grad_rows, preferred_element_type=single_precision
-    )
     grad_gate = (grad_hidden * up * sig * (1.0 + gate * (1.0 - sig))).astype(bf16)
     grad_up = (grad_hidden * gate * sig).astype(bf16)
     grad_gate_up = jnp.stack([grad_gate, grad_up], axis=1)
-    grad_gate_up_w = jnp.einsum(
-        "lrd,lkrh->lkdh", rows, grad_gate_up, preferred_element_type=single_precision
-    )
     grad_rows_in = jnp.einsum(
         "lkrh,lkdh->lrd", grad_gate_up, expert_in, preferred_element_type=single_precision
     ).astype(bf16)
@@ -305,6 +299,15 @@
     grad_mid_norm, grad_ffn_gain = rms_backward(grad_ffn_in, normed2, factor2, ffn_gain)
     grad_mid = grad + grad_mid_norm
     grad_mid_b = grad_mid.astype(bf16)
+    all_axes_size = lax.axis_size(all_axes)
+    shard_rows = width // all_axes_size
+    start = lax.axis_index(all_axes) * shard_rows
+    out_weight_sum = lax.psum(
+        jnp.einsum("td,tq->dq", grad_mid_b, attended, preferred_element_type=single_precision).astype(
+            bf16
+        ),
+        all_axes,
+    )
     grad_att = (
         jnp.einsum("td,dq->tq", grad_mid_b, out_full, preferred_element_type=single_precision)
         .astype(bf16)
@@ -355,24 +358,34 @@
         attention_input_gradient, normed1, factor1, attn_gain
     )
     grad_tokens = grad_mid + grad_x_norm
+    stacked = jnp.einsum(
+        "ta,stb->sab",
+        attention_input,
+        projected_gradient[:, :3].transpose(1, 0, 2),
+        preferred_element_type=single_precision,
+    ).astype(bf16)
+    stacked, out_weight_sum, rows, grad_gate_up, hidden, grad_rows = lax.optimization_barrier(
+        (stacked, out_weight_sum, rows, grad_gate_up, hidden, grad_rows)
+    )
+    summed = lax.psum(stacked, all_axes)
+    grad_out_shard = lax.dynamic_slice_in_dim(out_weight_sum, start, shard_rows, axis=0).astype(
+        single_precision
+    )
+    grad_qkv_shard = lax.dynamic_slice_in_dim(summed, start, shard_rows, axis=1).astype(
+        single_precision
+    )
+    grad_gate_up_w = jnp.einsum(
+        "lrd,lkrh->lkdh", rows, grad_gate_up, preferred_element_type=single_precision
+    )
+    grad_down = jnp.einsum(
+        "lrh,lrd->lhd", hidden, grad_rows, preferred_element_type=single_precision
+    )
+
     def scatter_over_copies(values):
         return sum_halves(sum_halves(values, "dp", 1), "context", 1)
 
     grad_in_shard = scatter_over_copies(grad_gate_up_w[0])[None]
     grad_down_shard = scatter_over_copies(grad_down[0])[None]
-    left = jnp.stack([attention_input] * 3 + [grad_mid_b])
-    right = jnp.concatenate(
-        [projected_gradient[:, :3].transpose(1, 0, 2), attended[None]], axis=0
-    )
-    stacked = jnp.einsum("sta,stb->sab", left, right, preferred_element_type=single_precision)
-    summed = lax.psum(stacked.astype(bf16), all_axes)
-    shard_rows = width // lax.axis_size(all_axes)
-    start = lax.axis_index(all_axes) * shard_rows
-    weight_shard = lax.dynamic_slice_in_dim(summed, start, shard_rows, axis=1).astype(
-        single_precision
-    )
-    grad_qkv_shard = weight_shard[:3]
-    grad_out_shard = weight_shard[3]
     small_sum = butterfly_sum(
         jnp.concatenate(
             [grad_attn_gain, grad_q_gain, grad_k_gain, grad_ffn_gain, grad_router.reshape(-1)]

time: 1090 us -> 1120 us (1.028)
  starting transfers between devices: 61.1 us -> 75.9 us
    ppermute x7, starting transfers between devices: 12.1 us -> 31.9 us  [butterfly_sum(): received = lax.ppermute(values, axes, partner)]
    ppermute x7, waiting for transfers between devices: 65.9 us -> 80.6 us  [butterfly_sum(): received = lax.ppermute(values, axes, partner)]
    unnamed x130 -> x123, local copies, waits for them, and re-layouts: 27 us -> 34.1 us
    psum x1 -> x2, waiting for transfers between devices: 166 us -> 169 us  [the longest x1 121 us: body(): lax.psum(jnp.einsum('td,tq->dq', grad_mid_b, attended, preferred_element_...]
  transfers between devices with their start and end apart: 19 -> 20, of which waited for: 15 -> 15; matrix products, arithmetic and copies ran while one was open for 17% -> 21% of each run, Pallas kernels for 0% -> 0%
where the time goes in v5:
time: 1120 us
  waiting for transfers between devices  676 us (60%)
  matrix products  145 us (13%)
  local copies, waits for them, and re-layouts  101 us (9%)
  other arithmetic  89.4 us (8%)
  starting transfers between devices  75.9 us (7%)
  Pallas kernels  15.1 us (1%)
  between operations  15 us (1%)
    all_gather x1, waiting for transfers between devices, body(): lax.all_gather(jnp.concatenate([qkv_weight.transpose(1, 0, 2), out_weight...  237 us
    psum x1, waiting for transfers between devices, body(): lax.psum(jnp.einsum('td,tq->dq', grad_mid_b, attended, preferred_element_...  121 us
    ppermute x7, waiting for transfers between devices, butterfly_sum(): received = lax.ppermute(values, axes, partner)  80.6 us
    all_to_all x1, waiting for transfers between devices, body(): lax.all_to_all(send.reshape(sources, local_experts * capacity, width), 'e...  49.5 us
    psum x1, waiting for transfers between devices, body(): summed = lax.psum(stacked, all_axes)  47.9 us
    all_to_all x1, waiting for transfers between devices, body(): lax.all_to_all(grad_send.reshape(sources, local_experts * capacity, width...  38.2 us
    all_to_all x1, waiting for transfers between devices, body(): lax.all_to_all(source_major(grad_rows_in, sources, capacity), 'expert', s...  37.5 us
    all_to_all x1, waiting for transfers between devices, body(): lax.all_to_all(source_major(results, sources, capacity), 'expert', split_...  35.3 us
  transfers between devices with their start and end apart: 20, of which 15 were waited for; matrix products, arithmetic and copies ran while one was open for 21% of the time, Pallas kernels for 0%

profile of v5, /device:TPU:1, one launch (start us, length us, event | category | flops | bytes accessed | tf_op | source)
XLA Modules:
  0.0 1116.1 jit_solution(2450981368675510970)
XLA Ops:
  13.9 236.6 %all-gather.2.cloned.1.call-done = bf16[2048,4,2048]{2,0,1:T(8,128)(2,1)} async-done(((bf16[16,4,2048]{2,0,1:T(8,128)(2,1)}), bf16[2048,4,2048]{2,0,1:T(8,128)(2,1)}) %all-gather.2.cloned.1.call-update) | async-done | bytes 33554448 | tf_op jit(solution)/shard_map/all_gather | solution.py:177
  250.6 15.1 %shard_map.215 = f32[3,128,2048]{2,1,0:T(8,128)} custom-call(bf16[128,2048]{1,0:T(8,128)(2,1)} %fusion.74.inputs_ref, bf16[4,2048,2048]{2,1,0:T(8,128)(2,1)} %bitcast.274), custom_call_target="tpu_custom_call" | custom-call | flops 3221225472 | bytes 28835840 | tf_op jit(solution)/shard_map/pallas_call | solution.py:83
  275.2 21.9 %collective-permute-done = bf16[128,2,2048]{2,0,1:T(8,128)(2,1)} collective-permute-done((bf16[128,2,2048]{2,0,1:T(8,128)(2,1)}, bf16[128,2,2048]{2,0,1:T(8,128)(2,1)}, u32[]{:S(2)}, u32[]{:S(2)}) %collective-permute-start) | collective-permute-done | bytes 1048608 | tf_op jit(solution)/shard_map/ppermute | solution.py:111
  306.0 3.9 convolution_convert_fusion.2
  309.9 6.6 multiply_reduce_fusion.7
  316.8 9.7 scatter_custom_fusion
  326.4 7.0 all-to-all-start
  334.1 7.0 gather_fusion.2
  341.2 10.0 scatter_custom_fusion.1
  351.2 49.5 %all-to-all-done = bf16[32,40,2048]{2,1,0:T(8,128)(2,1)} async-done(((bf16[32,40,2048]{2,1,0:T(8,128)(2,1)}), bf16[32,40,2048]{2,1,0:T(8,128)(2,1)}, u32[]{:S(2)}, u32[]{:S(2)}) %all-to-all-start) | async-done | bytes 5242912 | tf_op jit(solution)/shard_map/all_to_all | solution.py:232
  400.7 6.8 all-to-all-start.2
  407.5 17.0 %fusion.9 = f32[1,2,1280,1024]{3,2,1,0:T(8,128)S(1)} fusion(bf16[1280,2048,1]{1,0,2:T(8,128)(2,1)} %bitcast.20, bf16[1,2,2048,1024]{3,2,1,0:T(8,128)(2,1)} %param.24), kind=kOutput, calls=%fused_computation.25 | convolution fusion | flops 10737418240 | bytes 24117248 | tf_op jit(solution)/shard_map/lrd,lkdh->lkrh/dot_general | solution.py:240
  424.4 4.0 copy-done.8
  428.4 7.4 convolution_convert_fusion
  435.8 38.2 %all-to-all-done.2 = bf16[32,40,2048]{2,1,0:T(8,128)(2,1)} async-done(((bf16[32,40,2048]{2,1,0:T(8,128)(2,1)}), bf16[32,40,2048]{2,1,0:T(8,128)(2,1)}, u32[]{:S(2)}, u32[]{:S(2)}) %all-to-all-start.2) | async-done | bytes 5242912 | tf_op jit(solution)/shard_map/all_to_all | solution.py:260
  474.0 8.2 all-to-all-start.1
  482.2 13.1 %fusion.47 = (bf16[1,1,1280,1024]{3,2,1,0:T(8,128)(2,1)S(1)}, bf16[1,1,1280,1024]{3,2,1,0:T(8,128)(2,1)S(1)}) fusion(f32[1,2,1280,1024]{3,2,1,0:T(8,128)} %copy-done.8, bf16[1280,2048]{1,0:T(8,128)(2,1)} %bitcast.37, bf16[1,1024,2048]{2,1,0:T(8,128)(2,1)} %param.25), kind=kOutput, calls=%fused_computation.76 | convolution fusion | flops 5385748480 | bytes 25165824 | tf_op jit(solution)/shard_map/lrd,lhd->lrh/dot_general | solution.py:268
  497.6 15.1 %bitcast_convert_fusion = bf16[1280,2048]{1,0:T(8,128)(2,1)} fusion(bf16[1,2,2048,1024]{3,2,1,0:T(8,128)(2,1)} %param.24, bf16[1,1,1280,1024]{3,2,1,0:T(8,128)(2,1)S(1)} %get-tuple-element.84, bf16[1,1,1280,1024]{3,2,1,0:T(8,128)(2,1)S(1)} %get-tuple-element.83), kind=kOutput, calls=%fused_computation.9 | convolution fusion | flops 10742661120 | bytes 18874368 | tf_op jit(solution)/shard_map/lkrh,lkdh->lrd/dot_general | solution.py:274
  512.7 35.3 %all-to-all-done.1 = bf16[32,40,2048]{2,1,0:T(8,128)(2,1)} async-done(((bf16[32,40,2048]{2,1,0:T(8,128)(2,1)}), bf16[32,40,2048]{2,1,0:T(8,128)(2,1)}, u32[]{:S(2)}, u32[]{:S(2)}) %all-to-all-start.1) | async-done | bytes 5242912 | tf_op jit(solution)/shard_map/all_to_all | solution.py:248
  548.0 10.1 all-to-all-start.3
  558.7 4.4 fusion.51
  563.1 5.9 fusion.17
  569.0 12.0 %gather_fusion = bf16[1024,2048]{1,0:T(8,128)(2,1)} fusion(bf16[1280,2048]{1,0:T(8,128)(2,1)} %bitcast.30, s32[1024]{0:T(1024)S(1)} %broadcast_clamp_fusion), kind=kCustom, calls=%fused_computation | custom fusion | bytes 8392704 | tf_op jit(solution)/shard_map/gather | solution.py:251
  581.0 5.9 fusion.2
  587.0 37.5 %all-to-all-done.3 = bf16[32,40,2048]{2,1,0:T(8,128)(2,1)} async-done(((bf16[32,40,2048]{2,1,0:T(8,128)(2,1)}), bf16[32,40,2048]{2,1,0:T(8,128)(2,1)}, u32[]{:S(2)}, u32[]{:S(2)}) %all-to-all-start.3) | async-done | bytes 5242912 | tf_op jit(solution)/shard_map/all_to_all | solution.py:277
  624.5 12.1 %gather_fusion.1 = bf16[1024,2048]{1,0:T(8,128)(2,1)} fusion(bf16[1280,2048]{1,0:T(8,128)(2,1)} %bitcast.45, s32[1024]{0:T(1024)S(1)} %broadcast_clamp_fusion), kind=kCustom, calls=%fused_computation.1 | custom fusion | bytes 8392704 | tf_op jit(solution)/shard_map/gather | solution.py:284
  636.7 5.2 convert_reduce_fusion
  643.8 5.0 fusion.49
  649.3 4.7 fusion.102
  667.6 5.7 collective-permute-start.1
  676.1 5.6 convolution_convert_fusion.1
  684.7 5.7 collective-permute-done.1
  712.0 14.1 %convert_bitcast_fusion = bf16[3,2048,2048]{1,2,0:T(8,128)(2,1)} fusion(bf16[128,1,2048]{2,0,1:T(8,128)(2,1)} %slice.223, bf16[128,1,2048]{2,0,1:T(8,128)(2,1)} %get-tuple-element.86, bf16[128,1,2048]{2,0,1:T(8,128)(2,1)} %get-tuple-element.85, bf16[128,2048]{1,0:T(8,128)(2,1)} %fusion.74.inputs_ref), kind=kOutput, calls=%fused_computation.6 | convolution fusion | flops 3235381248 | bytes 27262976 | tf_op jit(solution)/shard_map/ta,stb->sab/dot_general | solution.py:361
  726.1 121.4 %all-reduce.3.cloned.1.call-done = bf16[2048,2048]{1,0:T(8,128)(2,1)} async-done(((bf16[2048,2048]{1,0:T(8,128)(2,1)}), bf16[2048,2048]{1,0:T(8,128)(2,1)}) %all-reduce.3.cloned.1.call-update) | async-done | bytes 8388624 | tf_op jit(solution)/shard_map/psum | solution.py:305
  849.1 15.2 %fusion.14 = f32[2,1024,2048]{2,1,0:T(8,128)S(1)} fusion(bf16[1,1280,2048]{2,1,0:T(8,128)(2,1)} %bitcast.64, bf16[1,2,1280,1024]{3,2,1,0:T(8,128)(2,1)} %pad_maximum_fusion), kind=kOutput, calls=%fused_computation.29 | convolution fusion | flops 10737418240 | bytes 27262976 | tf_op jit(solution)/shard_map/lrd,lkrh->lkdh/dot_general | solution.py:377
  864.3 6.2 copy-done.9
  874.2 19.3 %fusion.80 = (f32[2048]{0:T(1024)S(1)}, f32[128]{0:T(128)S(1)}, f32[128,2048]{1,0:T(8,128)}) fusion(bf16[1,128,2048]{2,1,0:T(8,128)(2,1)S(1)} %copy-done.18, f32[128]{0:T(128)S(1)} %copy-done.53, f32[2048]{0:T(1024)S(1)} %copy-done.46, bf16[2048,4,2048]{2,0,1:T(8,128)(2,1)} %all-gather.2.cloned.1.call-done, bf16[128,1,2048]{2,0,1:T(8,128)(2,1)} %slice.223, ...), kind=kOutput, calls=%fused_computation.128 | convolution fusion | flops 4299945984 | bytes 36717576 | tf_op jit(solution)/shard_map/dot_general | solution.py:352
  893.6 7.7 fusion.12
  907.7 10.5 collective-permute-done.2
  918.9 10.6 collective-permute-done.3
  931.2 9.0 collective-permute-done.4
  940.4 6.6 collective-permute-done.5
  948.7 6.3 bitcast_add_fusion
  967.3 44.0 %collective-permute-done.7 = f32[73728]{0:T(1024)S(1)} collective-permute-done((f32[73728]{0:T(1024)S(1)}, f32[73728]{0:T(1024)S(1)}, u32[]{:S(2)}, u32[]{:S(2)}) %collective-permute-start.7) | collective-permute-done | bytes 294944 | tf_op jit(solution)/shard_map/ppermute | solution.py:138
  1011.3 25.1 %collective-permute-start.8 = (f32[73728]{0:T(1024)S(1)}, f32[73728]{0:T(1024)S(1)}, u32[]{:S(2)}, u32[]{:S(2)}) collective-permute-start(f32[73728]{0:T(1024)S(1)} %add.241), channel_id=1, source_target_pairs={{0,64},{1,65},{2,66},{3,67},{4,68},{5,69},{6,70},{7,71},{8,72},{9,... | collective-permute-start | bytes 884744 | tf_op jit(solution)/shard_map/ppermute | solution.py:138
  1045.7 6.5 add_bitcast_fusion
  1052.2 5.5 copy.138
  1057.7 47.9 %all-reduce.5.cloned.1.call-done = bf16[3,2048,2048]{1,2,0:T(8,128)(2,1)} async-done(((bf16[3,2048,2048]{1,2,0:T(8,128)(2,1)}), bf16[3,2048,2048]{1,2,0:T(8,128)(2,1)}) %all-reduce.5.cloned.1.call-update) | async-done | bytes 25165840 | tf_op jit(solution)/shard_map/psum | solution.py:370
  (239 shorter events, 113.3 us)
Async XLA Ops:
  7.2 326.6 %copy-start = (bf16[2048,32]{0,1:T(8,128)(2,1)S(1)}, bf16[2048,32]{0,1:T(8,128)(2,1)}, u32[]{:S(2)}) copy-start(bf16[2048,32]{0,1:T(8,128)(2,1)} %param.23) | copy-start | bytes 393220
  7.2 243.4 %all-gather.2.cloned.1.call-start = ((), (), s32[]{:S(2)}) async-start(), calls=%async_computation.4 | async-start | bytes 33816576 | tf_op jit(solution)/shard_map/all_gather | solution.py:177
  11.9 258.1 %copy-start.37 = (f32[128,64]{1,0:T(8,128)}, f32[128,64]{1,0:T(8,128)S(1)}, u32[]{:S(2)}) copy-start(f32[128,64]{1,0:T(8,128)S(1)} %get-tuple-element.115) | copy-start | bytes 98308
  270.7 33.5 %copy-start.19 = (bf16[128,16,64]{2,0,1:T(8,128)(2,1)}, bf16[128,16,64]{2,0,1:T(8,128)(2,1)S(1)}, u32[]{:S(2)}) copy-start(bf16[128,16,64]{2,0,1:T(8,128)(2,1)S(1)} %get-tuple-element.97) | copy-start | bytes 786436
  270.7 33.5 %copy-start.21 = (bf16[128,16,64]{2,0,1:T(8,128)(2,1)}, bf16[128,16,64]{2,0,1:T(8,128)(2,1)S(1)}, u32[]{:S(2)}) copy-start(bf16[128,16,64]{2,0,1:T(8,128)(2,1)S(1)} %get-tuple-element.98) | copy-start | bytes 786436
  272.7 24.4 %collective-permute-start = (bf16[128,2,2048]{2,0,1:T(8,128)(2,1)}, bf16[128,2,2048]{2,0,1:T(8,128)(2,1)}, u32[]{:S(2)}, u32[]{:S(2)}) collective-permute-start(bf16[128,2,2048]{2,0,1:T(8,128)(2,1)} %pad_maximum_fusion.3), channel_id=1, source_target_pairs={{0,32},{32,0},{1,33},{33,1},{2,34},{34,2},{3,35},{35,3},{4,36},{36... | collective-permute-start | bytes 3145736 | tf_op jit(solution)/shard_map/ppermute | solution.py:111
  301.4 8.5 copy-start.10
  309.9 6.6 copy-start.33
  309.9 6.6 copy-start.40
  316.7 17.1 %copy-start.13 = (bf16[128,2048]{1,0:T(8,128)(2,1)}, bf16[128,2048]{1,0:T(8,128)(2,1)S(1)}, u32[]{:S(2)}) copy-start(bf16[128,2048]{1,0:T(8,128)(2,1)S(1)} %multiply_convert_fusion.3) | copy-start | bytes 1572868
  326.4 7.2 copy-start.31
  326.4 74.2 %all-to-all-start = ((bf16[32,40,2048]{2,1,0:T(8,128)(2,1)}), bf16[32,40,2048]{2,1,0:T(8,128)(2,1)}, u32[]{:S(2)}, u32[]{:S(2)}) async-start(bf16[32,40,2048]{2,1,0:T(8,128)(2,1)} %bitcast.275), calls=%async_computation | async-start | bytes 10485760 | tf_op jit(solution)/shard_map/all_to_all | solution.py:232
  400.7 73.3 %all-to-all-start.2 = ((bf16[32,40,2048]{2,1,0:T(8,128)(2,1)}), bf16[32,40,2048]{2,1,0:T(8,128)(2,1)}, u32[]{:S(2)}, u32[]{:S(2)}) async-start(bf16[32,40,2048]{2,1,0:T(8,128)(2,1)} %bitcast.276), calls=%async_computation.2 | async-start | bytes 10485760 | tf_op jit(solution)/shard_map/all_to_all | solution.py:260
  407.4 21.0 %copy-start.54 = (bf16[1,1024,2048]{2,1,0:T(8,128)(2,1)S(1)}, bf16[1,1024,2048]{2,1,0:T(8,128)(2,1)}, u32[]{:S(2)}) copy-start(bf16[1,1024,2048]{2,1,0:T(8,128)(2,1)} %param.25) | copy-start | bytes 12582916
  474.0 74.0 %all-to-all-start.1 = ((bf16[32,40,2048]{2,1,0:T(8,128)(2,1)}), bf16[32,40,2048]{2,1,0:T(8,128)(2,1)}, u32[]{:S(2)}, u32[]{:S(2)}) async-start(bf16[32,40,2048]{2,1,0:T(8,128)(2,1)} %bitcast.282), calls=%async_computation.1 | async-start | bytes 10485760 | tf_op jit(solution)/shard_map/all_to_all | solution.py:248
  548.0 76.6 %all-to-all-start.3 = ((bf16[32,40,2048]{2,1,0:T(8,128)(2,1)}), bf16[32,40,2048]{2,1,0:T(8,128)(2,1)}, u32[]{:S(2)}, u32[]{:S(2)}) async-start(bf16[32,40,2048]{2,1,0:T(8,128)(2,1)} %bitcast.281), calls=%async_computation.3 | async-start | bytes 10485760 | tf_op jit(solution)/shard_map/all_to_all | solution.py:277
  558.0 289.4 %all-reduce.3.cloned.1.call-start = ((), (), s32[]{:S(2)}) async-start(), calls=%async_computation.5 | async-start | bytes 16777216 | tf_op jit(solution)/shard_map/psum | solution.py:305
  636.7 5.8 copy-start.23
  636.7 5.7 copy-start.32
  643.8 32.2 %copy-start.5 = (f32[128,2048]{1,0:T(8,128)}, f32[128,2048]{1,0:T(8,128)S(1)}, u32[]{:S(2)}) copy-start(f32[128,2048]{1,0:T(8,128)S(1)} %get-tuple-element.103) | copy-start | bytes 3145732
  664.6 8.7 copy-start.27
  664.6 8.7 copy-start.29
  667.5 8.5 copy-start.35
  667.6 22.9 %collective-permute-start.1 = (bf16[128,2,2048]{2,0,1:T(8,128)(2,1)}, bf16[128,2,2048]{2,0,1:T(8,128)(2,1)}, u32[]{:S(2)}, u32[]{:S(2)}) collective-permute-start(bf16[128,2,2048]{2,0,1:T(8,128)(2,1)} %select_convert_fusion), channel_id=1, source_target_pairs={{0,32},{32,0},{1,33},{33,1},{2,34},{34,2},{3,35},{35,3},{4,36},{36... | collective-permute-start | bytes 3145736 | tf_op jit(solution)/shard_map/ppermute | solution.py:111
  681.7 424.0 %all-reduce.5.cloned.1.call-start = ((), (), s32[]{:S(2)}) async-start(), calls=%async_computation.6 | async-start | bytes 50331648 | tf_op jit(solution)/shard_map/psum | solution.py:370
  682.9 7.6 copy-start.4
  699.5 8.5 copy-start.2
  699.5 8.5 copy-start.42
  699.5 8.5 copy-start.44
  699.5 8.5 copy-start.48
  699.6 8.5 copy-start.50
  864.3 6.2 copy-start.9
  873.2 20.4 %copy-start.30 = (bf16[1,1280,1024]{2,1,0:T(8,128)(2,1)S(1)}, bf16[1,1280,1024]{2,1,0:T(8,128)(2,1)}, u32[]{:S(2)}) copy-start(bf16[1,1280,1024]{2,1,0:T(8,128)(2,1)} %fusion.17) | copy-start | bytes 7864324
  873.2 75.5 %collective-permute-start.9 = (bf16[2,1024,1024]{1,2,0:T(8,128)(2,1)}, bf16[2,1024,1024]{1,2,0:T(8,128)(2,1)}, u32[]{:S(2)}, u32[]{:S(2)}) collective-permute-start(bf16[2,1024,1024]{1,2,0:T(8,128)(2,1)} %fusion.31), channel_id=1, source_target_pairs={{0,64},{64,0},{1,65},{65,1},{2,66},{66,2},{3,67},{67,3},{4,68},{68... | collective-permute-start | bytes 12582920 | tf_op jit(solution)/shard_map/ppermute | solution.py:106
  904.8 57.9 %collective-permute-start.11 = (bf16[1024,1024]{1,0:T(8,128)(2,1)S(1)}, bf16[1024,1024]{1,0:T(8,128)(2,1)}, u32[]{:S(2)}, u32[]{:S(2)}) collective-permute-start(bf16[1024,1024]{1,0:T(8,128)(2,1)S(1)} %dynamic-slice_convert_fusion.1), channel_id=1, source_target_pairs={{0,64},{64,0},{1,65},{65,1},{2,66},{66,2},{3,67},{67,3},{4,68},{68... | collective-permute-start | bytes 6291464 | tf_op jit(solution)/shard_map/ppermute | solution.py:106
  905.0 13.2 %collective-permute-start.2 = (f32[73728]{0:T(1024)S(1)}, f32[73728]{0:T(1024)S(1)}, u32[]{:S(2)}, u32[]{:S(2)}) collective-permute-start(f32[73728]{0:T(1024)S(1)} %constant_dynamic-update-slice_fusion), channel_id=1, source_target_pairs={{0,1},{1,0},{2,3},{3,2},{4,5},{5,4},{6,7},{7,6},{8,9},{9,8},{10,11... | collective-permute-start | bytes 884744 | tf_op jit(solution)/shard_map/ppermute | solution.py:138
  918.2 11.2 %collective-permute-start.3 = (f32[73728]{0:T(1024)S(1)}, f32[73728]{0:T(1024)S(1)}, u32[]{:S(2)}, u32[]{:S(2)}) collective-permute-start(f32[73728]{0:T(1024)S(1)} %add.236), channel_id=1, source_target_pairs={{0,2},{1,3},{2,0},{3,1},{4,6},{5,7},{6,4},{7,5},{8,10},{9,11},{10,... | collective-permute-start | bytes 884744 | tf_op jit(solution)/shard_map/ppermute | solution.py:138
  929.5 10.7 collective-permute-start.4
  940.3 6.7 collective-permute-start.5
  947.9 13.9 %collective-permute-start.6 = (f32[73728]{0:T(1024)S(1)}, f32[73728]{0:T(1024)S(1)}, u32[]{:S(2)}, u32[]{:S(2)}) collective-permute-start(f32[73728]{0:T(1024)S(1)} %add.239), channel_id=1, source_target_pairs={{0,16},{1,17},{2,18},{3,19},{4,20},{5,21},{6,22},{7,23},{8,24},{9,... | collective-permute-start | bytes 884744 | tf_op jit(solution)/shard_map/ppermute | solution.py:138
  959.9 85.8 %collective-permute-start.10 = (bf16[2,512,1024]{1,2,0:T(8,128)(2,1)}, bf16[2,512,1024]{1,2,0:T(8,128)(2,1)}, u32[]{:S(2)}, u32[]{:S(2)}) collective-permute-start(bf16[2,512,1024]{1,2,0:T(8,128)(2,1)} %dynamic-slice_convert_fusion.2), channel_id=1, source_target_pairs={{0,32},{32,0},{1,33},{33,1},{2,34},{34,2},{3,35},{35,3},{4,36},{36... | collective-permute-start | bytes 6291464 | tf_op jit(solution)/shard_map/ppermute | solution.py:106
  961.9 74.6 %copy-start.6 = (f32[128,2048]{1,0:T(8,128)S(1)}, f32[128,2048]{1,0:T(8,128)}, u32[]{:S(2)}) copy-start(f32[128,2048]{1,0:T(8,128)} %copy-done.5) | copy-start | bytes 3145732
  961.9 74.5 %copy-start.36 = (f32[128,2048]{1,0:T(8,128)S(1)}, f32[128,2048]{1,0:T(8,128)}, u32[]{:S(2)}) copy-start(f32[128,2048]{1,0:T(8,128)} %get-tuple-element.121) | copy-start | bytes 3145732
  961.9 49.4 %collective-permute-start.7 = (f32[73728]{0:T(1024)S(1)}, f32[73728]{0:T(1024)S(1)}, u32[]{:S(2)}, u32[]{:S(2)}) collective-permute-start(f32[73728]{0:T(1024)S(1)} %add.240), channel_id=1, source_target_pairs={{0,32},{1,33},{2,34},{3,35},{4,36},{5,37},{6,38},{7,39},{8,40},{9,... | collective-permute-start | bytes 884744 | tf_op jit(solution)/shard_map/ppermute | solution.py:138
  966.2 71.6 %copy-start.7 = (f32[1024,1024]{1,0:T(8,128)}, f32[1024,1024]{1,0:T(8,128)S(1)}, u32[]{:S(2)}) copy-start(f32[1024,1024]{1,0:T(8,128)S(1)} %convert_add_fusion) | copy-start | bytes 12582916
  966.4 75.7 %collective-permute-start.12 = (bf16[1024,512]{1,0:T(8,128)(2,1)S(1)}, bf16[1024,512]{1,0:T(8,128)(2,1)}, u32[]{:S(2)}, u32[]{:S(2)}) collective-permute-start(bf16[1024,512]{1,0:T(8,128)(2,1)S(1)} %dynamic-slice_convert_fusion.3), channel_id=1, source_target_pairs={{0,32},{32,0},{1,33},{33,1},{2,34},{34,2},{3,35},{35,3},{4,36},{36... | collective-permute-start | bytes 3145736 | tf_op jit(solution)/shard_map/ppermute | solution.py:106
  1011.3 26.5 %collective-permute-start.8 = (f32[73728]{0:T(1024)S(1)}, f32[73728]{0:T(1024)S(1)}, u32[]{:S(2)}, u32[]{:S(2)}) collective-permute-start(f32[73728]{0:T(1024)S(1)} %add.241), channel_id=1, source_target_pairs={{0,64},{1,65},{2,66},{3,67},{4,68},{5,69},{6,70},{7,71},{8,72},{9,... | collective-permute-start | bytes 884744 | tf_op jit(solution)/shard_map/ppermute | solution.py:138
  1052.2 57.2 %copy-start.1 = (bf16[2048,32]{0,1:T(8,128)(2,1)S(1)}, bf16[2048,32]{0,1:T(8,128)(2,1)}, u32[]{:S(2)}) copy-start(bf16[2048,32]{0,1:T(8,128)(2,1)} %param.23) | copy-start | bytes 393220
  (27 other events, 71.9 us)
Sparse Core Ops, SparseCore 0:
  10.3 240.1 all-gather.1
  681.8 165.6 all-reduce.2
  853.7 251.9 all-reduce.4

commit v6 on v4

--- a/solution.py
+++ b/solution.py
@@ -226,17 +226,22 @@
     router_probs = router_exp / jnp.sum(router_exp, axis=-1, keepdims=True)
     own_routes = routes[0]
     slots = slot_index(own_routes.reshape(-1), experts, capacity)
-    send = (
-        jnp.zeros((experts * capacity, width), bf16).at[slots].set(jnp.repeat(ffn_in, top, axis=0))
-    )
+    route_weight = jnp.take_along_axis(router_probs, own_routes, axis=1)
+    grad = grad_output[0].astype(single_precision)
+    route_grad = (
+        (route_weight[:, :, None] * grad[:, None, :]).astype(bf16).reshape(seq_tok * top, width)
+    )
+    send = jnp.stack(
+        [
+            jnp.zeros((experts * capacity, width), bf16).at[slots].set(jnp.repeat(ffn_in, top, axis=0)),
+            jnp.zeros((experts * capacity, width), bf16).at[slots].set(route_grad),
+        ]
+    ).reshape(2, sources, local_experts * capacity, width)
     received = lax.all_to_all(
-        send.reshape(sources, local_experts * capacity, width),
-        "expert",
-        split_axis=0,
-        concat_axis=0,
-        tiled=True,
-    )
-    rows = expert_major(received, local_experts, capacity)
+        send.transpose(1, 0, 2, 3), "expert", split_axis=0, concat_axis=0, tiled=True
+    )
+    rows = expert_major(received[:, 0], local_experts, capacity)
+    grad_rows = expert_major(received[:, 1], local_experts, capacity)
     gate_up = jnp.einsum("lrd,lkdh->lkrh", rows, expert_in, preferred_element_type=single_precision)
     gate = gate_up[:, 0]
     up = gate_up[:, 1]
@@ -245,48 +250,36 @@
     results = jnp.einsum(
         "lrh,lhd->lrd", hidden, expert_out, preferred_element_type=single_precision
     ).astype(bf16)
-    back = lax.all_to_all(
-        source_major(results, sources, capacity), "expert", split_axis=0, concat_axis=0, tiled=True
-    )
-    route_out = back.reshape(experts * capacity, width)[slots].reshape(seq_tok, top, width)
-    route_weight = jnp.take_along_axis(router_probs, own_routes, axis=1)
-    output = mid + jnp.sum(route_weight[:, :, None] * route_out, axis=1)
-    grad = grad_output[0].astype(single_precision)
-    route_grad_weight = jnp.sum(grad[:, None, :] * route_out, axis=-1)
-    route_grad = (
-        (route_weight[:, :, None] * grad[:, None, :]).astype(bf16).reshape(seq_tok * top, width)
-    )
-    grad_send = jnp.zeros((experts * capacity, width), bf16).at[slots].set(route_grad)
-    grad_received = lax.all_to_all(
-        grad_send.reshape(sources, local_experts * capacity, width),
+    grad_hidden = jnp.einsum(
+        "lrd,lhd->lrh", grad_rows, expert_out, preferred_element_type=single_precision
+    )
+    grad_gate = (grad_hidden * up * sig * (1.0 + gate * (1.0 - sig))).astype(bf16)
+    grad_up = (grad_hidden * gate * sig).astype(bf16)
+    grad_gate_up = jnp.stack([grad_gate, grad_up], axis=1)
+    grad_rows_in = jnp.einsum(
+        "lkrh,lkdh->lrd", grad_gate_up, expert_in, preferred_element_type=single_precision
+    ).astype(bf16)
+    grad_down = jnp.einsum(
+        "lrh,lrd->lhd", hidden, grad_rows, preferred_element_type=single_precision
+    )
+    grad_gate_up_w = jnp.einsum(
+        "lrd,lkrh->lkdh", rows, grad_gate_up, preferred_element_type=single_precision
+    )
+    back_both = lax.all_to_all(
+        jnp.stack(
+            [source_major(results, sources, capacity), source_major(grad_rows_in, sources, capacity)],
+            axis=1,
+        ),
         "expert",
         split_axis=0,
         concat_axis=0,
         tiled=True,
     )
-    grad_rows = expert_major(grad_received, local_experts, capacity)
-    grad_hidden = jnp.einsum(
-        "lrd,lhd->lrh", grad_rows, expert_out, preferred_element_type=single_precision
-    )
-    grad_down = jnp.einsum(
-        "lrh,lrd->lhd", hidden, grad_rows, preferred_element_type=single_precision
-    )
-    grad_gate = (grad_hidden * up * sig * (1.0 + gate * (1.0 - sig))).astype(bf16)
-    grad_up = (grad_hidden * gate * sig).astype(bf16)
-    grad_gate_up = jnp.stack([grad_gate, grad_up], axis=1)
-    grad_gate_up_w = jnp.einsum(
-        "lrd,lkrh->lkdh", rows, grad_gate_up, preferred_element_type=single_precision
-    )
-    grad_rows_in = jnp.einsum(
-        "lkrh,lkdh->lrd", grad_gate_up, expert_in, preferred_element_type=single_precision
-    ).astype(bf16)
-    grad_back = lax.all_to_all(
-        source_major(grad_rows_in, sources, capacity),
-        "expert",
-        split_axis=0,
-        concat_axis=0,
-        tiled=True,
-    )
+    back = back_both[:, 0]
+    grad_back = back_both[:, 1]
+    route_out = back.reshape(experts * capacity, width)[slots].reshape(seq_tok, top, width)
+    output = mid + jnp.sum(route_weight[:, :, None] * route_out, axis=1)
+    route_grad_weight = jnp.sum(grad[:, None, :] * route_out, axis=-1)
     grad_route_in = grad_back.reshape(experts * capacity, width)[slots].reshape(seq_tok, top, width)
     grad_ffn_in = jnp.sum(grad_route_in, axis=1, dtype=single_precision)
     chosen = (own_routes[:, :, None] == jnp.arange(experts, dtype=jnp.int32)[None, None, :]).astype(

time: 1090 us -> 1220 us (1.12)
  blocking collectives: 0 us -> 125 us
  waiting for transfers between devices: 671 us -> 635 us
  other arithmetic: 83.7 us -> 101 us
  local copies, waits for them, and re-layouts: 101 us -> 116 us
    all_to_all x0 -> x1, blocking collectives: none -> 125 us  [body(): lax.all_to_all(send.transpose(1, 0, 2, 3), 'expert', split_axis=0, concat...]
    ppermute x7, starting transfers between devices: 12.1 us -> 49.6 us  [butterfly_sum(): received = lax.ppermute(values, axes, partner)]
    all_to_all x4 -> x1, waiting for transfers between devices: 163 us -> 129 us  [body(): lax.all_to_all(jnp.stack([source_major(results, sources, capacity), sourc...]
    all_to_all x4 -> x1, starting transfers between devices: 33.7 us -> 5.15 us  [body(): lax.all_to_all(jnp.stack([source_major(results, sources, capacity), sourc...]
    slice x0 -> x2, local copies, waits for them, and re-layouts: none -> 20.3 us  [the longest x1 10.1 us: body(): rows = expert_major(received[:, 0], local_experts, capacity)]
    ppermute x7, waiting for transfers between devices: 65.9 us -> 80.6 us  [butterfly_sum(): received = lax.ppermute(values, axes, partner)]
    psum x1, waiting for transfers between devices: 166 us -> 152 us  [body(): summed = lax.psum(stacked.astype(bf16), all_axes)]
    unnamed x130 -> x158, local copies, waits for them, and re-layouts: 27 us -> 22.8 us
  transfers between devices with their start and end apart: 19 -> 16, of which waited for: 15 -> 11; matrix products, arithmetic and copies ran while one was open for 17% -> 8% of each run, Pallas kernels for 0% -> 0%
where the time goes in v6:
time: 1220 us; the launch traced here: 1210 us
  waiting for transfers between devices  635 us (52%)
  matrix products  139 us (11%)
  blocking collectives  125 us (10%)
  local copies, waits for them, and re-layouts  116 us (10%)
  other arithmetic  101 us (8%)
  starting transfers between devices  66.3 us (5%)
  between operations  15.4 us (1%)
  Pallas kernels  15.1 us (1%)
    all_gather x1, waiting for transfers between devices, body(): lax.all_gather(jnp.concatenate([qkv_weight.transpose(1, 0, 2), out_weight...  234 us
    psum x1, waiting for transfers between devices, body(): summed = lax.psum(stacked.astype(bf16), all_axes)  152 us
    all_to_all x1, waiting for transfers between devices, body(): lax.all_to_all(jnp.stack([source_major(results, sources, capacity), sourc...  129 us
    all_to_all x1, blocking collectives, body(): lax.all_to_all(send.transpose(1, 0, 2, 3), 'expert', split_axis=0, concat...  125 us
    ppermute x7, waiting for transfers between devices, butterfly_sum(): received = lax.ppermute(values, axes, partner)  80.6 us
    ppermute x7, starting transfers between devices, butterfly_sum(): received = lax.ppermute(values, axes, partner)  49.6 us
    ppermute x2, waiting for transfers between devices, swap_context(): return lax.ppermute(values, 'context', [(0, 1), (1, 0)])  35.8 us
  transfers between devices with their start and end apart: 16, of which 11 were waited for; matrix products, arithmetic and copies ran while one was open for 8% of the time, Pallas kernels for 0%

profile of v6, /device:TPU:1, one launch (start us, length us, event | category | flops | bytes accessed | tf_op | source)
XLA Modules:
  0.0 1212.9 jit_solution(13751600033608038819)
XLA Ops:
  16.6 234.0 %all-gather.2.cloned.1.call-done = bf16[2048,4,2048]{2,0,1:T(8,128)(2,1)} async-done(((bf16[16,4,2048]{2,0,1:T(8,128)(2,1)}), bf16[2048,4,2048]{2,0,1:T(8,128)(2,1)}) %all-gather.2.cloned.1.call-update) | async-done | bytes 33554448 | tf_op jit(solution)/shard_map/all_gather | solution.py:177
  250.6 15.1 %shard_map.215 = f32[3,128,2048]{2,1,0:T(8,128)} custom-call(bf16[128,2048]{1,0:T(8,128)(2,1)} %fusion.74.inputs_ref, bf16[4,2048,2048]{2,1,0:T(8,128)(2,1)} %bitcast.279), custom_call_target="tpu_custom_call" | custom-call | flops 3221225472 | bytes 28835840 | tf_op jit(solution)/shard_map/pallas_call | solution.py:83
  274.4 21.9 %collective-permute-done = bf16[128,2,2048]{2,0,1:T(8,128)(2,1)S(1)} collective-permute-done((bf16[128,2,2048]{2,0,1:T(8,128)(2,1)S(1)}, bf16[128,2,2048]{2,0,1:T(8,128)(2,1)S(1)}, u32[]{:S(2)}, u32[]{:S(2)}) %collective-permute-start) | collective-permute-done | bytes 1048608 | tf_op jit(solution)/shard_map/ppermute | solution.py:111
  305.2 3.9 convolution_convert_fusion.2
  309.1 6.6 multiply_reduce_fusion.7
  317.4 7.0 gather_fusion.2
  324.4 9.9 scatter_custom_fusion
  334.3 10.0 scatter_custom_fusion.1
  344.3 9.0 maximum_bitcast_fusion
  353.3 125.1 %all_to_all.10 = bf16[32,2,40,2048]{3,2,1,0:T(8,128)(2,1)} all-to-all(bf16[32,2,40,2048]{3,2,1,0:T(8,128)(2,1)} %maximum_bitcast_fusion), channel_id=1, replica_groups=mesh['dp'=2,'context'=2,'expert'=32] {'expert'}, dimensions={0} | all-to-all | bytes 20971520 | tf_op jit(solution)/shard_map/all_to_all | solution.py:240
  478.3 10.1 fusion.142
  488.5 16.8 %fusion.9 = f32[1,2,1280,1024]{3,2,1,0:T(8,128)S(1)} fusion(bf16[1280,2048,1]{1,0,2:T(8,128)(2,1)} %bitcast.290, bf16[1,2,2048,1024]{3,2,1,0:T(8,128)(2,1)} %param.24), kind=kOutput, calls=%fused_computation.26 | convolution fusion | flops 10737418240 | bytes 24117248 | tf_op jit(solution)/shard_map/lrd,lkdh->lkrh/dot_general | solution.py:245
  507.8 11.1 fusion.39
  518.9 9.9 convolution_convert_fusion.1
  528.8 15.1 %bitcast_convert_fusion = bf16[1280,2048]{1,0:T(8,128)(2,1)} fusion(bf16[1,2,2048,1024]{3,2,1,0:T(8,128)(2,1)} %param.24, bf16[1,1,1280,1024]{3,2,1,0:T(8,128)(2,1)S(1)} %copy-done.70, bf16[1,1,1280,1024]{3,2,1,0:T(8,128)(2,1)S(1)} %copy-done.69), kind=kOutput, calls=%fused_computation.11 | convolution fusion | flops 10742661120 | bytes 18874368 | tf_op jit(solution)/shard_map/lkrh,lkdh->lrd/dot_general | solution.py:259
  543.9 8.9 pad_maximum_fusion
  552.8 5.1 all-to-all-start.1
  558.2 4.4 fusion.43
  562.6 129.2 %all-to-all-done.1 = bf16[32,2,40,2048]{3,2,1,0:T(8,128)(2,1)} async-done(((bf16[32,2,40,2048]{3,2,1,0:T(8,128)(2,1)}), bf16[32,2,40,2048]{3,2,1,0:T(8,128)(2,1)}, u32[]{:S(2)}, u32[]{:S(2)}) %all-to-all-start.1) | async-done | bytes 10485792 | tf_op jit(solution)/shard_map/all_to_all | solution.py:268
  691.8 10.1 fusion.141
  701.9 12.2 %gather_fusion.1 = bf16[1024,2048]{1,0:T(8,128)(2,1)} fusion(bf16[1280,2048]{1,0:T(8,128)(2,1)} %bitcast.278, s32[1024]{0:T(1024)S(1)} %broadcast_clamp_fusion), kind=kCustom, calls=%fused_computation.1 | custom fusion | bytes 8392704 | tf_op jit(solution)/shard_map/gather | solution.py:283
  714.1 5.1 convert_reduce_fusion
  719.2 12.0 gather_fusion
  731.2 6.0 fusion.2
  742.0 4.7 fusion.41
  747.2 4.7 fusion.103
  771.4 13.9 %collective-permute-done.1 = bf16[128,2,2048]{2,0,1:T(8,128)(2,1)} collective-permute-done((bf16[128,2,2048]{2,0,1:T(8,128)(2,1)}, bf16[128,2,2048]{2,0,1:T(8,128)(2,1)}, u32[]{:S(2)}, u32[]{:S(2)}) %collective-permute-start.1) | collective-permute-done | bytes 1048608 | tf_op jit(solution)/shard_map/ppermute | solution.py:111
  807.2 14.5 %convolution_convert_fusion = bf16[4,2048,2048]{2,1,0:T(8,128)(2,1)} fusion(bf16[1,128,2048]{2,1,0:T(8,128)(2,1)S(1)} %copy-done.28, bf16[1,128,2048]{2,1,0:T(8,128)(2,1)S(1)} %copy-done.26, bf16[1,128,2048]{2,1,0:T(8,128)(2,1)S(1)} %copy-done.27, bf16[3,128,2048]{2,1,0:T(8,128)(2,1)S(1)} %maximum_bitcast_fusion.4), kind=kOutput, calls=%fused_computation.6 | convolution fusion | flops 4315938816 | bytes 36700160 | tf_op jit(solution)/shard_map/sta,stb->sab/dot_general | solution.py:360
  821.7 15.1 %fusion.32 = f32[2,1024,2048]{2,1,0:T(8,128)S(1)} fusion(bf16[1280,2048,1]{1,0,2:T(8,128)(2,1)} %bitcast.291, bf16[1,1,1280,1024]{3,2,1,0:T(8,128)(2,1)} %get-tuple-element.85, bf16[1,1,1280,1024]{3,2,1,0:T(8,128)(2,1)} %get-tuple-element.84), kind=kOutput, calls=%fused_computation.59 | convolution fusion | flops 10740039680 | bytes 27262976 | tf_op jit(solution)/shard_map/lrd,lkrh->lkdh/dot_general | solution.py:265
  839.9 6.5 collective-permute-start.9
  846.4 7.5 fusion.33
  863.2 6.3 convert_add_fusion
  869.5 6.4 bitcast_add_fusion
  882.0 17.8 %fusion.80 = (f32[2048]{0:T(1024)S(1)}, f32[128]{0:T(128)}, f32[128,2048]{1,0:T(8,128)}) fusion(bf16[1,128,2048]{2,1,0:T(8,128)(2,1)S(1)} %copy-done.14, f32[128]{0:T(128)} %copy-done.62, f32[2048]{0:T(1024)S(1)} %copy-done.52, bf16[2048,4,2048]{2,0,1:T(8,128)(2,1)} %all-gather.2.cloned.1.call-done, bf16[128,1,2048]{2,0,1:T(8,128)(2,1)S(1)} %copy-done.36, ...), kind=kOutput, calls=%fused_computation.125 | convolution fusion | flops 4299945984 | bytes 36717576 | tf_op jit(solution)/shard_map/dot_general | solution.py:342
  899.9 10.9 collective-permute-start.2
  913.4 56.8 %collective-permute-done.2 = f32[73728]{0:T(1024)S(1)} collective-permute-done((f32[73728]{0:T(1024)S(1)}, f32[73728]{0:T(1024)S(1)}, u32[]{:S(2)}, u32[]{:S(2)}) %collective-permute-start.2) | collective-permute-done | bytes 294944 | tf_op jit(solution)/shard_map/ppermute | solution.py:138
  970.2 3.9 collective-permute-start.3
  974.0 7.8 collective-permute-done.3
  981.9 16.0 %collective-permute-start.4 = (f32[73728]{0:T(1024)S(1)}, f32[73728]{0:T(1024)S(1)}, u32[]{:S(2)}, u32[]{:S(2)}) collective-permute-start(f32[73728]{0:T(1024)S(1)} %add.228), channel_id=1, source_target_pairs={{0,4},{1,5},{2,6},{3,7},{4,0},{5,1},{6,2},{7,3},{8,12},{9,13},{10,... | collective-permute-start | bytes 884744 | tf_op jit(solution)/shard_map/ppermute | solution.py:138
  997.9 7.3 collective-permute-done.4
  1007.0 4.2 collective-permute-done.5
  1012.3 6.8 collective-permute-start.6
  1022.4 4.5 collective-permute-done.6
  1026.9 3.9 collective-permute-start.7
  1030.8 5.7 add_bitcast_fusion
  1036.5 5.6 copy.173
  1042.1 6.2 collective-permute-start.8
  1051.7 151.7 %all-reduce.2.cloned.1.call-done = bf16[4,2048,2048]{2,1,0:T(8,128)(2,1)} async-done(((bf16[4,2048,2048]{2,1,0:T(8,128)(2,1)}), bf16[4,2048,2048]{2,1,0:T(8,128)(2,1)}) %all-reduce.2.cloned.1.call-update) | async-done | bytes 33554448 | tf_op jit(solution)/shard_map/psum | solution.py:361
  (273 shorter events, 110.5 us)
Async XLA Ops:
  7.2 309.3 %copy-start = (bf16[2048,32]{0,1:T(8,128)(2,1)S(1)}, bf16[2048,32]{0,1:T(8,128)(2,1)}, u32[]{:S(2)}) copy-start(bf16[2048,32]{0,1:T(8,128)(2,1)} %param.23) | copy-start | bytes 393220
  7.2 243.4 %all-gather.2.cloned.1.call-start = ((), (), s32[]{:S(2)}) async-start(), calls=%async_computation.2 | async-start | bytes 33816576 | tf_op jit(solution)/shard_map/all_gather | solution.py:177
  9.8 240.8 %copy-start.41 = (s32[1,128,8]{2,1,0:T(8,128)}, s32[1,128,8]{2,1,0:T(8,128)S(1)}, u32[]{:S(2)}) copy-start(s32[1,128,8]{2,1,0:T(8,128)S(1)} %copy.146) | copy-start | bytes 12292
  13.6 252.1 %copy-start.62 = (f32[128]{0:T(128)}, f32[128]{0:T(128)S(1)}, u32[]{:S(2)}) copy-start(f32[128]{0:T(128)S(1)} %add_rsqrt_fusion.3) | copy-start | bytes 1540
  14.6 255.4 %copy-start.39 = (f32[128,64]{1,0:T(8,128)}, f32[128,64]{1,0:T(8,128)S(1)}, u32[]{:S(2)}) copy-start(f32[128,64]{1,0:T(8,128)S(1)} %get-tuple-element.119) | copy-start | bytes 98308
  271.5 30.7 %copy-start.17 = (bf16[128,16,64]{2,0,1:T(8,128)(2,1)}, bf16[128,16,64]{2,0,1:T(8,128)(2,1)S(1)}, u32[]{:S(2)}) copy-start(bf16[128,16,64]{2,0,1:T(8,128)(2,1)S(1)} %get-tuple-element.102) | copy-start | bytes 786436
  272.5 23.8 %collective-permute-start = (bf16[128,2,2048]{2,0,1:T(8,128)(2,1)S(1)}, bf16[128,2,2048]{2,0,1:T(8,128)(2,1)S(1)}, u32[]{:S(2)}, u32[]{:S(2)}) collective-permute-start(bf16[128,2,2048]{2,0,1:T(8,128)(2,1)S(1)} %pad_maximum_fusion.3), channel_id=1, source_target_pairs={{0,32},{32,0},{1,33},{33,1},{2,34},{34,2},{3,35},{35,3},{4,36},{36... | collective-permute-start | bytes 3145736 | tf_op jit(solution)/shard_map/ppermute | solution.py:111
  299.4 9.6 copy-start.5
  302.2 6.8 copy-start.12
  309.0 6.6 copy-start.29
  309.1 7.2 copy-start.46
  316.4 8.0 copy-start.10
  507.0 11.9 copy-start.25
  518.9 9.9 copy-start.69
  518.9 9.9 copy-start.70
  552.8 139.0 %all-to-all-start.1 = ((bf16[32,2,40,2048]{3,2,1,0:T(8,128)(2,1)}), bf16[32,2,40,2048]{3,2,1,0:T(8,128)(2,1)}, u32[]{:S(2)}, u32[]{:S(2)}) async-start(bf16[32,2,40,2048]{3,2,1,0:T(8,128)(2,1)} %pad_maximum_fusion), calls=%async_computation.1 | async-start | bytes 20971520 | tf_op jit(solution)/shard_map/all_to_all | solution.py:268
  558.0 645.4 %all-reduce.2.cloned.1.call-start = ((), (), s32[]{:S(2)}) async-start(), calls=%async_computation.3 | async-start | bytes 67108864 | tf_op jit(solution)/shard_map/psum | solution.py:361
  731.1 6.2 copy-start.8
  731.2 6.2 copy-start.47
  759.9 6.6 copy-start.52
  759.9 6.6 copy-start.63
  762.8 6.8 copy-start.6
  765.7 19.5 %collective-permute-start.1 = (bf16[128,2,2048]{2,0,1:T(8,128)(2,1)}, bf16[128,2,2048]{2,0,1:T(8,128)(2,1)}, u32[]{:S(2)}, u32[]{:S(2)}) collective-permute-start(bf16[128,2,2048]{2,0,1:T(8,128)(2,1)} %select_convert_fusion), channel_id=1, source_target_pairs={{0,32},{32,0},{1,33},{33,1},{2,34},{34,2},{3,35},{35,3},{4,36},{36... | collective-permute-start | bytes 3145736 | tf_op jit(solution)/shard_map/ppermute | solution.py:111
  769.6 15.7 %copy-start.3 = (f32[256,1,2048]{2,0,1:T(8,128)S(1)}, f32[256,1,2048]{2,0,1:T(8,128)}, u32[]{:S(2)}) copy-start(f32[256,1,2048]{2,0,1:T(8,128)} %copy.181) | copy-start | bytes 6291460
  794.4 8.3 copy-start.1
  794.4 8.3 copy-start.49
  794.4 8.3 copy-start.51
  794.4 8.3 copy-start.59
  794.4 8.4 copy-start.61
  821.7 24.8 %slice-start = ((s8[5242880]{0:T(1024)(128)(4,1)}), s8[1048576]{0:T(1024)(128)(4,1)S(1)}, s32[]{:S(2)}) async-start(s8[5242880]{0:T(1024)(128)(4,1)} %bitcast.287), calls=%async_computation.4 | async-start | bytes 2097152
  821.7 24.7 %slice-start.1 = ((s8[5242880]{0:T(1024)(128)(4,1)}), s8[4194304]{0:T(1024)(128)(4,1)S(1)}, s32[]{:S(2)}) async-start(s8[5242880]{0:T(1024)(128)(4,1)} %bitcast.287), calls=%async_computation.5 | async-start | bytes 8388608
  836.8 17.2 %copy-start.4 = (f32[2,1024,2048]{2,1,0:T(8,128)}, f32[2,1024,2048]{2,1,0:T(8,128)S(1)}, u32[]{:S(2)}) copy-start(f32[2,1024,2048]{2,1,0:T(8,128)S(1)} %fusion.32) | copy-start | bytes 50331652
  839.9 29.6 %collective-permute-start.9 = (bf16[2,1024,1024]{1,2,0:T(8,128)(2,1)}, bf16[2,1024,1024]{1,2,0:T(8,128)(2,1)}, u32[]{:S(2)}, u32[]{:S(2)}) collective-permute-start(bf16[2,1024,1024]{1,2,0:T(8,128)(2,1)} %fusion.21), channel_id=1, source_target_pairs={{0,64},{64,0},{1,65},{65,1},{2,66},{66,2},{3,67},{67,3},{4,68},{68... | collective-permute-start | bytes 12582920 | tf_op jit(solution)/shard_map/ppermute | solution.py:106
  857.3 5.9 collective-permute-start.11
  880.9 149.9 %collective-permute-start.10 = (bf16[2,512,1024]{1,2,0:T(8,128)(2,1)}, bf16[2,512,1024]{1,2,0:T(8,128)(2,1)}, u32[]{:S(2)}, u32[]{:S(2)}) collective-permute-start(bf16[2,512,1024]{1,2,0:T(8,128)(2,1)} %dynamic-slice_convert_fusion.2), channel_id=1, source_target_pairs={{0,32},{32,0},{1,33},{33,1},{2,34},{34,2},{3,35},{35,3},{4,36},{36... | collective-permute-start | bytes 6291464 | tf_op jit(solution)/shard_map/ppermute | solution.py:106
  882.0 17.8 %copy-start.55 = (f32[2048]{0:T(1024)S(1)}, f32[2048]{0:T(1024)}, u32[]{:S(2)}) copy-start(f32[2048]{0:T(1024)} %get-tuple-element.73) | copy-start | bytes 24580
  882.0 17.8 %copy-start.54 = (f32[2048]{0:T(1024)S(1)}, f32[2048]{0:T(1024)}, u32[]{:S(2)}) copy-start(f32[2048]{0:T(1024)} %get-tuple-element.66) | copy-start | bytes 24580
  899.9 70.3 %collective-permute-start.2 = (f32[73728]{0:T(1024)S(1)}, f32[73728]{0:T(1024)S(1)}, u32[]{:S(2)}, u32[]{:S(2)}) collective-permute-start(f32[73728]{0:T(1024)S(1)} %constant_dynamic-update-slice_fusion), channel_id=1, source_target_pairs={{0,1},{1,0},{2,3},{3,2},{4,5},{5,4},{6,7},{7,6},{8,9},{9,8},{10,11... | collective-permute-start | bytes 884744 | tf_op jit(solution)/shard_map/ppermute | solution.py:138
  912.8 106.3 %collective-permute-start.12 = (bf16[1024,512]{1,0:T(8,128)(2,1)S(1)}, bf16[1024,512]{1,0:T(8,128)(2,1)S(1)}, u32[]{:S(2)}, u32[]{:S(2)}) collective-permute-start(bf16[1024,512]{1,0:T(8,128)(2,1)S(1)} %dynamic-slice_convert_fusion.3), channel_id=1, source_target_pairs={{0,32},{32,0},{1,33},{33,1},{2,34},{34,2},{3,35},{35,3},{4,36},{36... | collective-permute-start | bytes 3145736 | tf_op jit(solution)/shard_map/ppermute | solution.py:106
  970.2 11.7 collective-permute-start.3
  981.9 23.3 %collective-permute-start.4 = (f32[73728]{0:T(1024)S(1)}, f32[73728]{0:T(1024)S(1)}, u32[]{:S(2)}, u32[]{:S(2)}) collective-permute-start(f32[73728]{0:T(1024)S(1)} %add.228), channel_id=1, source_target_pairs={{0,4},{1,5},{2,6},{3,7},{4,0},{5,1},{6,2},{7,3},{8,12},{9,13},{10,... | collective-permute-start | bytes 884744 | tf_op jit(solution)/shard_map/ppermute | solution.py:138
  1005.2 6.0 collective-permute-start.5
  1012.3 14.6 %collective-permute-start.6 = (f32[73728]{0:T(1024)S(1)}, f32[73728]{0:T(1024)S(1)}, u32[]{:S(2)}, u32[]{:S(2)}) collective-permute-start(f32[73728]{0:T(1024)S(1)} %add.230), channel_id=1, source_target_pairs={{0,16},{1,17},{2,18},{3,19},{4,20},{5,21},{6,22},{7,23},{8,24},{9,... | collective-permute-start | bytes 884744 | tf_op jit(solution)/shard_map/ppermute | solution.py:138
  1026.9 15.2 %collective-permute-start.7 = (f32[73728]{0:T(1024)S(1)}, f32[73728]{0:T(1024)S(1)}, u32[]{:S(2)}, u32[]{:S(2)}) collective-permute-start(f32[73728]{0:T(1024)S(1)} %add.231), channel_id=1, source_target_pairs={{0,32},{1,33},{2,34},{3,35},{4,36},{5,37},{6,38},{7,39},{8,40},{9,... | collective-permute-start | bytes 884744 | tf_op jit(solution)/shard_map/ppermute | solution.py:138
  1036.5 11.9 copy-start.24
  1036.5 11.9 copy-start.38
  1036.5 11.9 copy-start.64
  1042.1 7.6 collective-permute-start.8
  (41 other events, 110.5 us)
Sparse Core Ops, SparseCore 0:
  10.3 240.1 all-gather.1
  821.8 381.4 all-reduce.1

commit v7 on v4

--- a/solution.py
+++ b/solution.py
@@ -96,6 +96,83 @@
             + 4 * tokens * columns * blocks,
         ),
     )(inputs, weights)
+
+
+def _dispatch_kernel(token_ref, weight_ref, rows_ref, grad_ref, send_ref, grad_send_ref):
+    tile = token_ref.shape[0]
+    tokens = rows_ref.shape[0]
+    pick = (
+        token_ref[...] == lax.broadcasted_iota(jnp.int32, (tile, tokens), 1)
+    ).astype(jnp.bfloat16)
+    send_ref[...] = jnp.dot(pick, rows_ref[...], preferred_element_type=jnp.float32).astype(
+        send_ref.dtype
+    )
+    picked_grad = jnp.dot(pick, grad_ref[...], preferred_element_type=jnp.float32)
+    grad_send_ref[...] = (weight_ref[...] * picked_grad).astype(grad_send_ref.dtype)
+
+
+def dispatch(slot_token, slot_weight, rows, grad, tile=256):
+    slots = slot_token.shape[0]
+    tokens, width = rows.shape
+    out = jax.ShapeDtypeStruct((slots, width), jnp.bfloat16)
+    return pl.pallas_call(
+        _dispatch_kernel,
+        out_shape=(out, out),
+        grid=(slots // tile,),
+        in_specs=[
+            pl.BlockSpec((tile, 1), lambda i: (i, 0)),
+            pl.BlockSpec((tile, 1), lambda i: (i, 0)),
+            pl.BlockSpec((tokens, width), lambda i: (0, 0)),
+            pl.BlockSpec((tokens, width), lambda i: (0, 0)),
+        ],
+        out_specs=(
+            pl.BlockSpec((tile, width), lambda i: (i, 0)),
+            pl.BlockSpec((tile, width), lambda i: (i, 0)),
+        ),
+        cost_estimate=pl.CostEstimate(
+            flops=4 * slots * tokens * width,
+            transcendentals=0,
+            bytes_accessed=4 * slots * width + 4 * tokens * width + 8 * slots,
+        ),
+    )(slot_token, slot_weight, rows, grad)
+
+
+def _combine_kernel(with_dots, slot_ref, weight_ref, table_ref, base_ref, other_ref, out_ref, dots_ref):
+    tokens, top = slot_ref.shape
+    count = table_ref.shape[0]
+    total = base_ref[...]
+    for k in range(top):
+        pick = (
+            slot_ref[:, k : k + 1] == lax.broadcasted_iota(jnp.int32, (tokens, count), 1)
+        ).astype(jnp.bfloat16)
+        row = jnp.dot(pick, table_ref[...], preferred_element_type=jnp.float32)
+        total = total + weight_ref[:, k : k + 1] * row
+        if with_dots:
+            dots_ref[:, k : k + 1] = jnp.sum(
+                other_ref[...].astype(jnp.float32) * row, axis=1, keepdims=True
+            )
+    out_ref[...] = total
+    if not with_dots:
+        dots_ref[...] = jnp.zeros_like(dots_ref)
+
+
+def combine(slots, weights, table, base, other, with_dots):
+    tokens, top = slots.shape
+    count, width = table.shape
+    return pl.pallas_call(
+        functools.partial(_combine_kernel, with_dots),
+        out_shape=(
+            jax.ShapeDtypeStruct((tokens, width), jnp.float32),
+            jax.ShapeDtypeStruct((tokens, top), jnp.float32),
+        ),
+        in_specs=[pl.BlockSpec(memory_space=pltpu.VMEM)] * 5,
+        out_specs=(pl.BlockSpec(memory_space=pltpu.VMEM), pl.BlockSpec(memory_space=pltpu.VMEM)),
+        cost_estimate=pl.CostEstimate(
+            flops=2 * tokens * count * width * top,
+            transcendentals=0,
+            bytes_accessed=2 * count * width + 10 * tokens * width,
+        ),
+    )(slots, weights, table, base, other)
 
 
 def sum_halves(values, axis, dim):
@@ -226,9 +303,13 @@
     router_probs = router_exp / jnp.sum(router_exp, axis=-1, keepdims=True)
     own_routes = routes[0]
     slots = slot_index(own_routes.reshape(-1), experts, capacity)
-    send = (
-        jnp.zeros((experts * capacity, width), bf16).at[slots].set(jnp.repeat(ffn_in, top, axis=0))
-    )
+    route_weight = jnp.take_along_axis(router_probs, own_routes, axis=1)
+    route_index = jnp.arange(seq_tok * top, dtype=jnp.int32)
+    slot_token = jnp.full((experts * capacity,), -1, jnp.int32).at[slots].set(route_index // top)
+    slot_weight = jnp.zeros((experts * capacity,), single_precision).at[slots].set(
+        route_weight.reshape(-1)
+    )
+    send, grad_send = dispatch(slot_token[:, None], slot_weight[:, None], ffn_in, grad_output[0])
     received = lax.all_to_all(
         send.reshape(sources, local_experts * capacity, width),
         "expert",
@@ -248,15 +329,16 @@
     back = lax.all_to_all(
         source_major(results, sources, capacity), "expert", split_axis=0, concat_axis=0, tiled=True
     )
-    route_out = back.reshape(experts * capacity, width)[slots].reshape(seq_tok, top, width)
-    route_weight = jnp.take_along_axis(router_probs, own_routes, axis=1)
-    output = mid + jnp.sum(route_weight[:, :, None] * route_out, axis=1)
+    route_slots = slots.reshape(seq_tok, top)
+    output, route_grad_weight = combine(
+        route_slots,
+        route_weight,
+        back.reshape(experts * capacity, width),
+        mid,
+        grad_output[0],
+        True,
+    )
     grad = grad_output[0].astype(single_precision)
-    route_grad_weight = jnp.sum(grad[:, None, :] * route_out, axis=-1)
-    route_grad = (
-        (route_weight[:, :, None] * grad[:, None, :]).astype(bf16).reshape(seq_tok * top, width)
-    )
-    grad_send = jnp.zeros((experts * capacity, width), bf16).at[slots].set(route_grad)
     grad_received = lax.all_to_all(
         grad_send.reshape(sources, local_experts * capacity, width),
         "expert",
@@ -287,8 +369,6 @@
         concat_axis=0,
         tiled=True,
     )
-    grad_route_in = grad_back.reshape(experts * capacity, width)[slots].reshape(seq_tok, top, width)
-    grad_ffn_in = jnp.sum(grad_route_in, axis=1, dtype=single_precision)
     chosen = (own_routes[:, :, None] == jnp.arange(experts, dtype=jnp.int32)[None, None, :]).astype(
         single_precision
     )
@@ -299,8 +379,13 @@
     grad_router = jnp.einsum(
         "td,te->de", ffn_in, grad_logits, preferred_element_type=single_precision
     )
-    grad_ffn_in = grad_ffn_in + jnp.einsum(
-        "te,de->td", grad_logits, router_weight, preferred_element_type=single_precision
+    grad_ffn_in, _ = combine(
+        route_slots,
+        jnp.ones((seq_tok, top), single_precision),
+        grad_back.reshape(experts * capacity, width),
+        jnp.einsum("te,de->td", grad_logits, router_weight, preferred_element_type=single_precision),
+        grad_output[0],
+        False,
     )
     grad_mid_norm, grad_ffn_gain = rms_backward(grad_ffn_in, normed2, factor2, ffn_gain)
     grad_mid = grad + grad_mid_norm

time: 1090 us -> 1090 us (level)
  blocking collectives: 0 us -> 68.5 us
  waiting for transfers between devices: 671 us -> 621 us
  Pallas kernels: 15 us -> 42.6 us
  other arithmetic: 83.7 us -> 60.3 us
  local copies, waits for them, and re-layouts: 101 us -> 80.1 us
    all_to_all x0 -> x1, blocking collectives: none -> 68.5 us  [body(): lax.all_to_all(send.reshape(sources, local_experts * capacity, width), 'e...]
    all_to_all x1 -> x0, waiting for transfers between devices: 48.5 us -> none  [body(): lax.all_to_all(send.reshape(sources, local_experts * capacity, width), 'e...]
    pallas_call x0 -> x3, Pallas kernels: none -> 27.6 us  [the longest x2 20.3 us: combine(): pl.pallas_call(functools.partial(_combine_kernel, with_dots), out_shape=(...]
    gather x2 -> x0, local copies, waits for them, and re-layouts: 24.2 us -> none  [the longest x1 12.2 us: body(): back.reshape(experts * capacity, width)[slots].reshape(seq_tok, top, width)]
    reduce_sum x2 -> x0, other arithmetic: 11.1 us -> none  [the longest x1 5.91 us: body(): route_grad_weight = jnp.sum(grad[:, None, :] * route_out, axis=-1)]
  transfers between devices with their start and end apart: 19 -> 18, of which waited for: 15 -> 14; matrix products, arithmetic and copies ran while one was open for 17% -> 15% of each run, Pallas kernels for 0% -> 1%
where the time goes in v7:
time: 1090 us; the launch traced here: 1080 us
  waiting for transfers between devices  621 us (57%)
  matrix products  137 us (13%)
  local copies, waits for them, and re-layouts  80.1 us (7%)
  blocking collectives  68.5 us (6%)
  other arithmetic  60.3 us (6%)
  starting transfers between devices  54 us (5%)
  Pallas kernels  42.6 us (4%)
  between operations  15.3 us (1%)
    all_gather x1, waiting for transfers between devices, body(): lax.all_gather(jnp.concatenate([qkv_weight.transpose(1, 0, 2), out_weight...  236 us
    psum x1, waiting for transfers between devices, body(): summed = lax.psum(stacked.astype(bf16), all_axes)  164 us
    all_to_all x1, blocking collectives, body(): lax.all_to_all(send.reshape(sources, local_experts * capacity, width), 'e...  68.5 us
    ppermute x7, waiting for transfers between devices, butterfly_sum(): received = lax.ppermute(values, axes, partner)  66.1 us
    all_to_all x1, waiting for transfers between devices, body(): lax.all_to_all(source_major(grad_rows_in, sources, capacity), 'expert', s...  48.8 us
    all_to_all x1, waiting for transfers between devices, body(): lax.all_to_all(grad_send.reshape(sources, local_experts * capacity, width...  36.9 us
    all_to_all x1, waiting for transfers between devices, body(): lax.all_to_all(source_major(results, sources, capacity), 'expert', split_...  35.3 us
    ppermute x2, waiting for transfers between devices, swap_context(): return lax.ppermute(values, 'context', [(0, 1), (1, 0)])  29.5 us
  transfers between devices with their start and end apart: 18, of which 14 were waited for; matrix products, arithmetic and copies ran while one was open for 15% of the time, Pallas kernels for 1%

profile of v7, /device:TPU:1, one launch (start us, length us, event | category | flops | bytes accessed | tf_op | source)
XLA Modules:
  0.0 1078.7 jit_solution(7554327610314662194)
XLA Ops:
  14.7 235.9 %all-gather.2.cloned.1.call-done = bf16[2048,4,2048]{2,0,1:T(8,128)(2,1)} async-done(((bf16[16,4,2048]{2,0,1:T(8,128)(2,1)}), bf16[2048,4,2048]{2,0,1:T(8,128)(2,1)}) %all-gather.2.cloned.1.call-update) | async-done | bytes 33554448 | tf_op jit(solution)/shard_map/all_gather | solution.py:254
  250.6 15.0 %shard_map.215 = f32[3,128,2048]{2,1,0:T(8,128)} custom-call(bf16[128,2048]{1,0:T(8,128)(2,1)} %fusion.62.inputs_ref, bf16[4,2048,2048]{2,1,0:T(8,128)(2,1)} %bitcast.255), custom_call_target="tpu_custom_call" | custom-call | flops 3221225472 | bytes 28835840 | tf_op jit(solution)/shard_map/pallas_call | solution.py:83
  275.6 4.5 scatter_custom_fusion
  281.3 16.2 %collective-permute-done = bf16[128,2,2048]{2,0,1:T(8,128)(2,1)S(1)} collective-permute-done((bf16[128,2,2048]{2,0,1:T(8,128)(2,1)}, bf16[128,2,2048]{2,0,1:T(8,128)(2,1)S(1)}, u32[]{:S(2)}, u32[]{:S(2)}) %collective-permute-start) | collective-permute-done | bytes 1048608 | tf_op jit(solution)/shard_map/ppermute | solution.py:188
  304.8 4.7 convolution_convert_fusion.2
  309.6 6.5 multiply_reduce_fusion.7
  316.6 7.0 gather_fusion
  323.7 4.3 scatter_custom_fusion.1
  329.1 7.3 shard_map.216
  336.3 68.5 %all_to_all.20 = bf16[32,40,2048]{2,1,0:T(8,128)(2,1)} all-to-all(bf16[32,40,2048]{2,1,0:T(8,128)(2,1)} %bitcast.265), channel_id=1, replica_groups=mesh['dp'=2,'context'=2,'expert'=32] {'expert'}, dimensions={0} | all-to-all | bytes 10485760 | tf_op jit(solution)/shard_map/all_to_all | solution.py:313
  404.8 5.1 all-to-all-start.2
  409.9 16.9 %fusion.6 = f32[1,2,1280,1024]{3,2,1,0:T(8,128)S(1)} fusion(bf16[1280,2048,1]{1,0,2:T(8,128)(2,1)} %bitcast.260, bf16[1,2,2048,1024]{3,2,1,0:T(8,128)(2,1)} %param.24), kind=kOutput, calls=%fused_computation.15 | convolution fusion | flops 10737418240 | bytes 24117248 | tf_op jit(solution)/shard_map/lrd,lkdh->lkrh/dot_general | solution.py:321
  428.5 3.3 copy-done.5
  433.3 7.3 convolution_convert_fusion.1
  440.7 36.9 %all-to-all-done.2 = bf16[32,40,2048]{2,1,0:T(8,128)(2,1)} async-done(((bf16[32,40,2048]{2,1,0:T(8,128)(2,1)}), bf16[32,40,2048]{2,1,0:T(8,128)(2,1)}, u32[]{:S(2)}, u32[]{:S(2)}) %all-to-all-start.2) | async-done | bytes 5242912 | tf_op jit(solution)/shard_map/all_to_all | solution.py:342
  477.5 6.9 all-to-all-start.1
  484.4 13.1 %fusion.28 = (bf16[1,1,1280,1024]{3,2,1,0:T(8,128)(2,1)S(1)}, bf16[1,1,1280,1024]{3,2,1,0:T(8,128)(2,1)S(1)}) fusion(f32[1,2,1280,1024]{3,2,1,0:T(8,128)} %copy-done.5, bf16[1280,2048]{1,0:T(8,128)(2,1)} %bitcast.32, bf16[1,1024,2048]{2,1,0:T(8,128)(2,1)} %param.25), kind=kOutput, calls=%fused_computation.48 | convolution fusion | flops 5385748480 | bytes 25165824 | tf_op jit(solution)/shard_map/lrd,lhd->lrh/dot_general | solution.py:350
  499.8 15.1 %bitcast_convert_fusion = bf16[1280,2048]{1,0:T(8,128)(2,1)} fusion(bf16[1,2,2048,1024]{3,2,1,0:T(8,128)(2,1)} %param.24, bf16[1,1,1280,1024]{3,2,1,0:T(8,128)(2,1)S(1)} %get-tuple-element.71, bf16[1,1,1280,1024]{3,2,1,0:T(8,128)(2,1)S(1)} %get-tuple-element.70), kind=kOutput, calls=%fused_computation.5 | convolution fusion | flops 10742661120 | bytes 18874368 | tf_op jit(solution)/shard_map/lkrh,lkdh->lrd/dot_general | solution.py:362
  514.9 35.3 %all-to-all-done.1 = bf16[32,40,2048]{2,1,0:T(8,128)(2,1)} async-done(((bf16[32,40,2048]{2,1,0:T(8,128)(2,1)}), bf16[32,40,2048]{2,1,0:T(8,128)(2,1)}, u32[]{:S(2)}, u32[]{:S(2)}) %all-to-all-start.1) | async-done | bytes 5242912 | tf_op jit(solution)/shard_map/all_to_all | solution.py:329
  550.1 10.4 all-to-all-start.3
  564.4 10.2 shard_map.217
  576.9 48.8 %all-to-all-done.3 = bf16[32,40,2048]{2,1,0:T(8,128)(2,1)} async-done(((bf16[32,40,2048]{2,1,0:T(8,128)(2,1)}), bf16[32,40,2048]{2,1,0:T(8,128)(2,1)}, u32[]{:S(2)}, u32[]{:S(2)}) %all-to-all-start.3) | async-done | bytes 5242912 | tf_op jit(solution)/shard_map/all_to_all | solution.py:365
  626.3 10.1 shard_map.218
  641.2 4.7 fusion.30
  646.4 4.7 fusion.91
  664.6 6.0 collective-permute-start.1
  675.4 13.4 %collective-permute-done.1 = bf16[128,2,2048]{2,0,1:T(8,128)(2,1)} collective-permute-done((bf16[128,2,2048]{2,0,1:T(8,128)(2,1)}, bf16[128,2,2048]{2,0,1:T(8,128)(2,1)}, u32[]{:S(2)}, u32[]{:S(2)}) %collective-permute-start.1) | collective-permute-done | bytes 1048608 | tf_op jit(solution)/shard_map/ppermute | solution.py:188
  708.3 14.4 %convolution_convert_fusion = bf16[4,2048,2048]{2,1,0:T(8,128)(2,1)} fusion(bf16[1,128,2048]{2,1,0:T(8,128)(2,1)S(1)} %copy-done.28, bf16[1,128,2048]{2,1,0:T(8,128)(2,1)S(1)} %copy-done.29, bf16[1,128,2048]{2,1,0:T(8,128)(2,1)S(1)} %copy-done.30, bf16[3,128,2048]{2,1,0:T(8,128)(2,1)S(1)} %maximum_bitcast_fusion.3), kind=kOutput, calls=%fused_computation.4 | convolution fusion | flops 4315938816 | bytes 36700160 | tf_op jit(solution)/shard_map/sta,stb->sab/dot_general | solution.py:452
  724.5 14.3 %fusion.23 = f32[2,1024,2048]{2,1,0:T(8,128)S(1)} fusion(bf16[1280,2048,1]{1,0,2:T(8,128)(2,1)} %bitcast.261, bf16[1,1,1280,1024]{3,2,1,0:T(8,128)(2,1)} %copy-done.58, bf16[1,1,1280,1024]{3,2,1,0:T(8,128)(2,1)S(1)} %copy-done.57), kind=kOutput, calls=%fused_computation.43 | convolution fusion | flops 10740039680 | bytes 27262976 | tf_op jit(solution)/shard_map/lrd,lkrh->lkdh/dot_general | solution.py:359
  741.6 6.2 collective-permute-start.9
  747.7 7.8 fusion.24
  755.8 3.0 copy-done.16
  758.8 3.2 collective-permute-start.11
  762.1 4.1 collective-permute-done.11
  766.2 3.8 convert_add_fusion
  774.2 11.4 %bitcast_add_fusion = f32[2,1024,1024]{1,2,0:T(8,128)} fusion(bf16[2,1024,1024]{1,2,0:T(8,128)(2,1)} %collective-permute-done.9, f32[2,1024,2048]{2,1,0:T(8,128)} %copy-done.8, s32[]{:T(128)S(6)} %select_n.120), kind=kLoop, calls=%fused_computation.7 | loop fusion | flops 4194304 | bytes 20971524 | tf_op jit(solution)/shard_map/add | solution.py:184
  787.1 17.1 %fusion.68 = (f32[2048]{0:T(1024)S(1)}, f32[128]{0:T(128)S(1)}, f32[128,2048]{1,0:T(8,128)}) fusion(bf16[1,128,2048]{2,1,0:T(8,128)(2,1)S(1)} %copy-done.12, f32[128]{0:T(128)S(1)} %copy-done.53, f32[2048]{0:T(1024)S(1)} %copy-done.46, bf16[2048,4,2048]{2,0,1:T(8,128)(2,1)} %all-gather.2.cloned.1.call-done, bf16[128,1,2048]{2,0,1:T(8,128)(2,1)S(1)} %copy-done.38, ...), kind=kOutput, calls=%fused_computation.105 | convolution fusion | flops 4299945984 | bytes 36717576 | tf_op jit(solution)/shard_map/dot_general | solution.py:434
  808.3 11.0 %collective-permute-done.2 = f32[73728]{0:T(1024)S(1)} collective-permute-done((f32[73728]{0:T(1024)S(1)}, f32[73728]{0:T(1024)S(1)}, u32[]{:S(2)}, u32[]{:S(2)}) %collective-permute-start.2) | collective-permute-done | bytes 294944 | tf_op jit(solution)/shard_map/ppermute | solution.py:215
  819.4 9.9 collective-permute-done.3
  829.3 8.6 collective-permute-start.4
  837.9 7.2 collective-permute-done.4
  845.3 7.1 collective-permute-done.5
  852.6 3.7 add_bitcast_fusion.1
  856.3 4.6 collective-permute-done.6
  864.5 26.2 %collective-permute-done.7 = f32[73728]{0:T(1024)S(1)} collective-permute-done((f32[73728]{0:T(1024)S(1)}, f32[73728]{0:T(1024)S(1)}, u32[]{:S(2)}, u32[]{:S(2)}) %collective-permute-start.7) | collective-permute-done | bytes 294944 | tf_op jit(solution)/shard_map/ppermute | solution.py:215
  892.2 5.6 add_bitcast_fusion
  897.8 5.4 copy.111
  905.2 164.1 %all-reduce.2.cloned.1.call-done = bf16[4,2048,2048]{2,1,0:T(8,128)(2,1)} async-done(((bf16[4,2048,2048]{2,1,0:T(8,128)(2,1)}), bf16[4,2048,2048]{2,1,0:T(8,128)(2,1)}) %all-reduce.2.cloned.1.call-update) | async-done | bytes 33554448 | tf_op jit(solution)/shard_map/psum | solution.py:453
  (248 shorter events, 107.1 us)
Async XLA Ops:
  7.2 309.1 %copy-start = (bf16[2048,32]{0,1:T(8,128)(2,1)S(1)}, bf16[2048,32]{0,1:T(8,128)(2,1)}, u32[]{:S(2)}) copy-start(bf16[2048,32]{0,1:T(8,128)(2,1)} %param.23) | copy-start | bytes 393220
  7.2 243.4 %all-gather.2.cloned.1.call-start = ((), (), s32[]{:S(2)}) async-start(), calls=%async_computation.4 | async-start | bytes 33816576 | tf_op jit(solution)/shard_map/all_gather | solution.py:254
  11.7 253.9 %copy-start.52 = (f32[128]{0:T(128)}, f32[128]{0:T(128)S(1)}, u32[]{:S(2)}) copy-start(f32[128]{0:T(128)S(1)} %add_rsqrt_fusion.3) | copy-start | bytes 1540
  271.7 31.3 %copy-start.17 = (bf16[128,16,64]{2,0,1:T(8,128)(2,1)}, bf16[128,16,64]{2,0,1:T(8,128)(2,1)S(1)}, u32[]{:S(2)}) copy-start(bf16[128,16,64]{2,0,1:T(8,128)(2,1)S(1)} %get-tuple-element.84) | copy-start | bytes 786436
  272.4 8.8 copy-start.54
  273.7 23.8 %collective-permute-start = (bf16[128,2,2048]{2,0,1:T(8,128)(2,1)}, bf16[128,2,2048]{2,0,1:T(8,128)(2,1)S(1)}, u32[]{:S(2)}, u32[]{:S(2)}) collective-permute-start(bf16[128,2,2048]{2,0,1:T(8,128)(2,1)} %pad_maximum_fusion.2), channel_id=1, source_target_pairs={{0,32},{32,0},{1,33},{33,1},{2,34},{34,2},{3,35},{35,3},{4,36},{36... | collective-permute-start | bytes 3145736 | tf_op jit(solution)/shard_map/ppermute | solution.py:188
  299.0 4.0 copy-start.19
  304.8 4.7 copy-start.10
  309.6 6.6 copy-start.41
  316.1 7.6 copy-start.6
  316.3 7.4 copy-start.13
  404.8 72.7 %all-to-all-start.2 = ((bf16[32,40,2048]{2,1,0:T(8,128)(2,1)}), bf16[32,40,2048]{2,1,0:T(8,128)(2,1)}, u32[]{:S(2)}, u32[]{:S(2)}) async-start(bf16[32,40,2048]{2,1,0:T(8,128)(2,1)} %bitcast.264), calls=%async_computation.2 | async-start | bytes 10485760 | tf_op jit(solution)/shard_map/all_to_all | solution.py:342
  426.8 5.0 copy-start.5
  426.8 6.5 copy-start.55
  477.5 72.6 %all-to-all-start.1 = ((bf16[32,40,2048]{2,1,0:T(8,128)(2,1)}), bf16[32,40,2048]{2,1,0:T(8,128)(2,1)}, u32[]{:S(2)}, u32[]{:S(2)}) async-start(bf16[32,40,2048]{2,1,0:T(8,128)(2,1)} %bitcast.263), calls=%async_computation.1 | async-start | bytes 10485760 | tf_op jit(solution)/shard_map/all_to_all | solution.py:329
  550.1 12.1 %copy-start.31 = (f32[16,128,256]{2,1,0:T(8,128)S(1)}, f32[16,128,256]{2,1,0:T(8,128)}, u32[]{:S(2)}) copy-start(f32[16,128,256]{2,1,0:T(8,128)} %fusion.103) | copy-start | bytes 6291460
  550.1 75.5 %all-to-all-start.3 = ((bf16[32,40,2048]{2,1,0:T(8,128)(2,1)}), bf16[32,40,2048]{2,1,0:T(8,128)(2,1)}, u32[]{:S(2)}, u32[]{:S(2)}) async-start(bf16[32,40,2048]{2,1,0:T(8,128)(2,1)} %bitcast.262), calls=%async_computation.3 | async-start | bytes 10485760 | tf_op jit(solution)/shard_map/all_to_all | solution.py:365
  560.5 508.8 %all-reduce.2.cloned.1.call-start = ((), (), s32[]{:S(2)}) async-start(), calls=%async_computation.5 | async-start | bytes 67108864 | tf_op jit(solution)/shard_map/psum | solution.py:453
  626.3 10.1 copy-start.7
  641.2 5.0 copy-start.32
  646.3 4.8 copy-start.15
  661.8 8.8 copy-start.11
  661.8 8.8 copy-start.46
  661.8 8.8 copy-start.53
  664.6 24.2 %collective-permute-start.1 = (bf16[128,2,2048]{2,0,1:T(8,128)(2,1)}, bf16[128,2,2048]{2,0,1:T(8,128)(2,1)}, u32[]{:S(2)}, u32[]{:S(2)}) collective-permute-start(bf16[128,2,2048]{2,0,1:T(8,128)(2,1)} %select_convert_fusion), channel_id=1, source_target_pairs={{0,32},{32,0},{1,33},{33,1},{2,34},{34,2},{3,35},{35,3},{4,36},{36... | collective-permute-start | bytes 3145736 | tf_op jit(solution)/shard_map/ppermute | solution.py:188
  673.6 15.2 %copy-start.3 = (f32[256,1,2048]{2,0,1:T(8,128)S(1)}, f32[256,1,2048]{2,0,1:T(8,128)}, u32[]{:S(2)}) copy-start(f32[256,1,2048]{2,0,1:T(8,128)} %copy.119) | copy-start | bytes 6291460
  698.7 4.9 copy-start.2
  698.7 4.9 copy-start.43
  698.7 4.9 copy-start.45
  698.7 5.0 copy-start.49
  698.7 5.0 copy-start.51
  738.8 16.7 %copy-start.8 = (f32[2,1024,2048]{2,1,0:T(8,128)}, f32[2,1024,2048]{2,1,0:T(8,128)S(1)}, u32[]{:S(2)}) copy-start(f32[2,1024,2048]{2,1,0:T(8,128)S(1)} %fusion.23) | copy-start | bytes 50331652
  738.8 8.9 copy-start.27
  741.6 32.7 %collective-permute-start.9 = (bf16[2,1024,1024]{1,2,0:T(8,128)(2,1)}, bf16[2,1024,1024]{1,2,0:T(8,128)(2,1)}, u32[]{:S(2)}, u32[]{:S(2)}) collective-permute-start(bf16[2,1024,1024]{1,2,0:T(8,128)(2,1)} %fusion.18), channel_id=1, source_target_pairs={{0,64},{64,0},{1,65},{65,1},{2,66},{66,2},{3,67},{67,3},{4,68},{68... | collective-permute-start | bytes 12582920 | tf_op jit(solution)/shard_map/ppermute | solution.py:183
  758.8 7.4 collective-permute-start.11
  773.1 12.5 %copy-start.14 = (bf16[128,2048]{1,0:T(8,128)(2,1)S(1)}, bf16[128,2048]{1,0:T(8,128)(2,1)}, u32[]{:S(2)}) copy-start(bf16[128,2048]{1,0:T(8,128)(2,1)} %copy-done.13) | copy-start | bytes 1572868
  773.1 79.5 %collective-permute-start.12 = (bf16[1024,512]{1,0:T(8,128)(2,1)}, bf16[1024,512]{1,0:T(8,128)(2,1)}, u32[]{:S(2)}, u32[]{:S(2)}) collective-permute-start(bf16[1024,512]{1,0:T(8,128)(2,1)} %dynamic-slice_convert_fusion.3), channel_id=1, source_target_pairs={{0,32},{32,0},{1,33},{33,1},{2,34},{34,2},{3,35},{35,3},{4,36},{36... | collective-permute-start | bytes 3145736 | tf_op jit(solution)/shard_map/ppermute | solution.py:183
  804.3 15.0 %collective-permute-start.2 = (f32[73728]{0:T(1024)S(1)}, f32[73728]{0:T(1024)S(1)}, u32[]{:S(2)}, u32[]{:S(2)}) collective-permute-start(f32[73728]{0:T(1024)S(1)} %constant_dynamic-update-slice_fusion), channel_id=1, source_target_pairs={{0,1},{1,0},{2,3},{3,2},{4,5},{5,4},{6,7},{7,6},{8,9},{9,8},{10,11... | collective-permute-start | bytes 884744 | tf_op jit(solution)/shard_map/ppermute | solution.py:215
  808.2 84.0 %collective-permute-start.10 = (bf16[2,512,1024]{1,2,0:T(8,128)(2,1)S(1)}, bf16[2,512,1024]{1,2,0:T(8,128)(2,1)}, u32[]{:S(2)}, u32[]{:S(2)}) collective-permute-start(bf16[2,512,1024]{1,2,0:T(8,128)(2,1)S(1)} %dynamic-slice_convert_fusion.2), channel_id=1, source_target_pairs={{0,32},{32,0},{1,33},{33,1},{2,34},{34,2},{3,35},{35,3},{4,36},{36... | collective-permute-start | bytes 6291464 | tf_op jit(solution)/shard_map/ppermute | solution.py:183
  819.3 10.0 collective-permute-start.3
  829.3 15.8 %collective-permute-start.4 = (f32[73728]{0:T(1024)S(1)}, f32[73728]{0:T(1024)S(1)}, u32[]{:S(2)}, u32[]{:S(2)}) collective-permute-start(f32[73728]{0:T(1024)S(1)} %add.220), channel_id=1, source_target_pairs={{0,4},{1,5},{2,6},{3,7},{4,0},{5,1},{6,2},{7,3},{8,12},{9,13},{10,... | collective-permute-start | bytes 884744 | tf_op jit(solution)/shard_map/ppermute | solution.py:215
  845.2 7.2 collective-permute-start.5
  852.4 10.7 copy-start.25
  852.4 10.6 copy-start.39
  852.5 8.4 collective-permute-start.6
  860.9 29.8 %collective-permute-start.7 = (f32[73728]{0:T(1024)S(1)}, f32[73728]{0:T(1024)S(1)}, u32[]{:S(2)}, u32[]{:S(2)}) collective-permute-start(f32[73728]{0:T(1024)S(1)} %add.223), channel_id=1, source_target_pairs={{0,32},{1,33},{2,34},{3,35},{4,36},{5,37},{6,38},{7,39},{8,40},{9,... | collective-permute-start | bytes 884744 | tf_op jit(solution)/shard_map/ppermute | solution.py:215
  890.7 12.5 %collective-permute-start.8 = (f32[73728]{0:T(1024)S(1)}, f32[73728]{0:T(1024)S(1)}, u32[]{:S(2)}, u32[]{:S(2)}) collective-permute-start(f32[73728]{0:T(1024)S(1)} %add.224), channel_id=1, source_target_pairs={{0,64},{1,65},{2,66},{3,67},{4,68},{5,69},{6,70},{7,71},{8,72},{9,... | collective-permute-start | bytes 884744 | tf_op jit(solution)/shard_map/ppermute | solution.py:215
  903.2 168.4 %copy-start.1 = (bf16[2048,32]{0,1:T(8,128)(2,1)S(1)}, bf16[2048,32]{0,1:T(8,128)(2,1)}, u32[]{:S(2)}) copy-start(bf16[2048,32]{0,1:T(8,128)(2,1)} %param.23) | copy-start | bytes 393220
  (29 other events, 48.5 us)
Sparse Core Ops, SparseCore 0:
  10.3 240.1 all-gather.1
  722.9 346.2 all-reduce.1

commit v8 on v7

--- a/solution.py
+++ b/solution.py
@@ -98,30 +98,36 @@
     )(inputs, weights)
 
 
-def _dispatch_kernel(token_ref, weight_ref, rows_ref, grad_ref, send_ref, grad_send_ref):
-    tile = token_ref.shape[0]
-    tokens = rows_ref.shape[0]
-    pick = (
-        token_ref[...] == lax.broadcasted_iota(jnp.int32, (tile, tokens), 1)
-    ).astype(jnp.bfloat16)
+def _dispatch_kernel(slot_ref, weight_ref, rows_ref, grad_ref, send_ref, grad_send_ref):
+    tile = send_ref.shape[0]
+    top, tokens = slot_ref.shape
+    slot = pl.program_id(0) * tile + lax.broadcasted_iota(jnp.int32, (tile, tokens), 0)
+    hit = slot == slot_ref[0:1, :]
+    weight = jnp.where(hit, weight_ref[0:1, :], 0.0)
+    for k in range(1, top):
+        match = slot == slot_ref[k : k + 1, :]
+        hit = hit | match
+        weight = weight + jnp.where(match, weight_ref[k : k + 1, :], 0.0)
+    pick = hit.astype(jnp.bfloat16)
     send_ref[...] = jnp.dot(pick, rows_ref[...], preferred_element_type=jnp.float32).astype(
         send_ref.dtype
     )
     picked_grad = jnp.dot(pick, grad_ref[...], preferred_element_type=jnp.float32)
-    grad_send_ref[...] = (weight_ref[...] * picked_grad).astype(grad_send_ref.dtype)
-
-
-def dispatch(slot_token, slot_weight, rows, grad, tile=256):
-    slots = slot_token.shape[0]
-    tokens, width = rows.shape
+    slot_weight = jnp.sum(weight, axis=1, keepdims=True)
+    grad_send_ref[...] = (slot_weight * picked_grad).astype(grad_send_ref.dtype)
+
+
+def dispatch(route_slots, route_weights, rows, grad, slots, tile=256):
+    top, tokens = route_slots.shape
+    width = rows.shape[1]
     out = jax.ShapeDtypeStruct((slots, width), jnp.bfloat16)
     return pl.pallas_call(
         _dispatch_kernel,
         out_shape=(out, out),
         grid=(slots // tile,),
         in_specs=[
-            pl.BlockSpec((tile, 1), lambda i: (i, 0)),
-            pl.BlockSpec((tile, 1), lambda i: (i, 0)),
+            pl.BlockSpec((top, tokens), lambda i: (0, 0)),
+            pl.BlockSpec((top, tokens), lambda i: (0, 0)),
             pl.BlockSpec((tokens, width), lambda i: (0, 0)),
             pl.BlockSpec((tokens, width), lambda i: (0, 0)),
         ],
@@ -132,9 +138,9 @@
         cost_estimate=pl.CostEstimate(
             flops=4 * slots * tokens * width,
             transcendentals=0,
-            bytes_accessed=4 * slots * width + 4 * tokens * width + 8 * slots,
-        ),
-    )(slot_token, slot_weight, rows, grad)
+            bytes_accessed=4 * slots * width + 4 * tokens * width + 8 * top * tokens,
+        ),
+    )(route_slots, route_weights, rows, grad)
 
 
 def _combine_kernel(with_dots, slot_ref, weight_ref, table_ref, base_ref, other_ref, out_ref, dots_ref):
@@ -303,13 +309,14 @@
     router_probs = router_exp / jnp.sum(router_exp, axis=-1, keepdims=True)
     own_routes = routes[0]
     slots = slot_index(own_routes.reshape(-1), experts, capacity)
-    route_weight = jnp.take_along_axis(router_probs, own_routes, axis=1)
-    route_index = jnp.arange(seq_tok * top, dtype=jnp.int32)
-    slot_token = jnp.full((experts * capacity,), -1, jnp.int32).at[slots].set(route_index // top)
-    slot_weight = jnp.zeros((experts * capacity,), single_precision).at[slots].set(
-        route_weight.reshape(-1)
-    )
-    send, grad_send = dispatch(slot_token[:, None], slot_weight[:, None], ffn_in, grad_output[0])
+    expert_ids = jnp.arange(experts, dtype=jnp.int32)
+    route_weight = jnp.sum(
+        jnp.where(own_routes[:, :, None] == expert_ids, router_probs[:, None, :], 0.0), axis=2
+    )
+    route_slots = slots.reshape(seq_tok, top)
+    send, grad_send = dispatch(
+        route_slots.T, route_weight.T, ffn_in, grad_output[0], experts * capacity
+    )
     received = lax.all_to_all(
         send.reshape(sources, local_experts * capacity, width),
         "expert",
@@ -329,7 +336,6 @@
     back = lax.all_to_all(
         source_major(results, sources, capacity), "expert", split_axis=0, concat_axis=0, tiled=True
     )
-    route_slots = slots.reshape(seq_tok, top)
     output, route_grad_weight = combine(
         route_slots,
         route_weight,

time: 1090 us -> 1070 us (0.982)
  local copies, waits for them, and re-layouts: 80.1 us -> 60.8 us
    unnamed x130 -> x136, local copies, waits for them, and re-layouts: 29.5 us -> 27.5 us
  transfers between devices with their start and end apart: 18 -> 18, of which waited for: 14 -> 14; matrix products, arithmetic and copies ran while one was open for 15% -> 14% of each run, Pallas kernels for 1% -> 1%
where the time goes in v8:
time: 1070 us; the launch traced here: 1060 us
  waiting for transfers between devices  631 us (59%)
  matrix products  137 us (13%)
  blocking collectives  68.5 us (6%)
  local copies, waits for them, and re-layouts  60.8 us (6%)
  other arithmetic  59.8 us (6%)
  starting transfers between devices  43.9 us (4%)
  Pallas kernels  42 us (4%)
  between operations  15.2 us (1%)
    all_gather x1, waiting for transfers between devices, body(): lax.all_gather(jnp.concatenate([qkv_weight.transpose(1, 0, 2), out_weight...  237 us
    psum x1, waiting for transfers between devices, body(): summed = lax.psum(stacked.astype(bf16), all_axes)  159 us
    ppermute x7, waiting for transfers between devices, butterfly_sum(): received = lax.ppermute(values, axes, partner)  75.5 us
    all_to_all x1, blocking collectives, body(): lax.all_to_all(send.reshape(sources, local_experts * capacity, width), 'e...  68.5 us
    all_to_all x1, waiting for transfers between devices, body(): lax.all_to_all(source_major(grad_rows_in, sources, capacity), 'expert', s...  49.7 us
    all_to_all x1, waiting for transfers between devices, body(): lax.all_to_all(grad_send.reshape(sources, local_experts * capacity, width...  36.9 us
    all_to_all x1, waiting for transfers between devices, body(): lax.all_to_all(source_major(results, sources, capacity), 'expert', split_...  35.2 us
    ppermute x2, waiting for transfers between devices, swap_context(): return lax.ppermute(values, 'context', [(0, 1), (1, 0)])  34.1 us
  transfers between devices with their start and end apart: 18, of which 14 were waited for; matrix products, arithmetic and copies ran while one was open for 14% of the time, Pallas kernels for 1%

profile of v8, /device:TPU:1, one launch (start us, length us, event | category | flops | bytes accessed | tf_op | source)
XLA Modules:
  0.0 1058.6 jit_solution(12252229424526086497)
XLA Ops:
  14.0 236.6 %all-gather.2.cloned.1.call-done = bf16[2048,4,2048]{2,0,1:T(8,128)(2,1)} async-done(((bf16[16,4,2048]{2,0,1:T(8,128)(2,1)}), bf16[2048,4,2048]{2,0,1:T(8,128)(2,1)}) %all-gather.2.cloned.1.call-update) | async-done | bytes 33554448 | tf_op jit(solution)/shard_map/all_gather | solution.py:260
  250.6 15.0 %shard_map.215 = f32[3,128,2048]{2,1,0:T(8,128)} custom-call(bf16[128,2048]{1,0:T(8,128)(2,1)} %fusion.62.inputs_ref, bf16[4,2048,2048]{2,1,0:T(8,128)(2,1)} %bitcast.246), custom_call_target="tpu_custom_call" | custom-call | flops 3221225472 | bytes 28835840 | tf_op jit(solution)/shard_map/pallas_call | solution.py:83
  277.5 19.1 %collective-permute-done = bf16[128,2,2048]{2,0,1:T(8,128)(2,1)S(1)} collective-permute-done((bf16[128,2,2048]{2,0,1:T(8,128)(2,1)}, bf16[128,2,2048]{2,0,1:T(8,128)(2,1)S(1)}, u32[]{:S(2)}, u32[]{:S(2)}) %collective-permute-start) | collective-permute-done | bytes 1048608 | tf_op jit(solution)/shard_map/ppermute | solution.py:194
  301.8 3.6 convolution_convert_fusion.2
  305.4 6.5 multiply_reduce_fusion.7
  313.1 6.6 shard_map.216
  319.8 68.5 %all_to_all.20 = bf16[32,40,2048]{2,1,0:T(8,128)(2,1)} all-to-all(bf16[32,40,2048]{2,1,0:T(8,128)(2,1)} %bitcast.256), channel_id=1, replica_groups=mesh['dp'=2,'context'=2,'expert'=32] {'expert'}, dimensions={0} | all-to-all | bytes 10485760 | tf_op jit(solution)/shard_map/all_to_all | solution.py:320
  388.3 5.1 all-to-all-start.2
  393.4 16.8 %fusion.6 = f32[1,2,1280,1024]{3,2,1,0:T(8,128)S(1)} fusion(bf16[1280,2048,1]{1,0,2:T(8,128)(2,1)} %bitcast.251, bf16[1,2,2048,1024]{3,2,1,0:T(8,128)(2,1)} %param.24), kind=kOutput, calls=%fused_computation.12 | convolution fusion | flops 10737418240 | bytes 24117248 | tf_op jit(solution)/shard_map/lrd,lkdh->lkrh/dot_general | solution.py:328
  411.9 3.3 copy-done.5
  416.7 7.3 convolution_convert_fusion.1
  424.1 36.9 %all-to-all-done.2 = bf16[32,40,2048]{2,1,0:T(8,128)(2,1)} async-done(((bf16[32,40,2048]{2,1,0:T(8,128)(2,1)}), bf16[32,40,2048]{2,1,0:T(8,128)(2,1)}, u32[]{:S(2)}, u32[]{:S(2)}) %all-to-all-start.2) | async-done | bytes 5242912 | tf_op jit(solution)/shard_map/all_to_all | solution.py:348
  460.9 6.8 all-to-all-start.1
  467.8 13.1 %fusion.28 = (bf16[1,1,1280,1024]{3,2,1,0:T(8,128)(2,1)S(1)}, bf16[1,1,1280,1024]{3,2,1,0:T(8,128)(2,1)S(1)}) fusion(f32[1,2,1280,1024]{3,2,1,0:T(8,128)} %copy-done.5, bf16[1280,2048]{1,0:T(8,128)(2,1)} %bitcast.32, bf16[1,1024,2048]{2,1,0:T(8,128)(2,1)} %param.25), kind=kOutput, calls=%fused_computation.45 | convolution fusion | flops 5385748480 | bytes 25165824 | tf_op jit(solution)/shard_map/lrd,lhd->lrh/dot_general | solution.py:356
  483.2 15.1 %bitcast_convert_fusion = bf16[1280,2048]{1,0:T(8,128)(2,1)} fusion(bf16[1,2,2048,1024]{3,2,1,0:T(8,128)(2,1)} %param.24, bf16[1,1,1280,1024]{3,2,1,0:T(8,128)(2,1)S(1)} %get-tuple-element.71, bf16[1,1,1280,1024]{3,2,1,0:T(8,128)(2,1)S(1)} %get-tuple-element.70), kind=kOutput, calls=%fused_computation.2 | convolution fusion | flops 10742661120 | bytes 18874368 | tf_op jit(solution)/shard_map/lkrh,lkdh->lrd/dot_general | solution.py:368
  498.2 35.2 %all-to-all-done.1 = bf16[32,40,2048]{2,1,0:T(8,128)(2,1)} async-done(((bf16[32,40,2048]{2,1,0:T(8,128)(2,1)}), bf16[32,40,2048]{2,1,0:T(8,128)(2,1)}, u32[]{:S(2)}, u32[]{:S(2)}) %all-to-all-start.1) | async-done | bytes 5242912 | tf_op jit(solution)/shard_map/all_to_all | solution.py:336
  533.5 10.7 %all-to-all-start.3 = ((bf16[32,40,2048]{2,1,0:T(8,128)(2,1)}), bf16[32,40,2048]{2,1,0:T(8,128)(2,1)}, u32[]{:S(2)}, u32[]{:S(2)}) async-start(bf16[32,40,2048]{2,1,0:T(8,128)(2,1)} %bitcast.253), calls=%async_computation.3 | async-start | bytes 10485760 | tf_op jit(solution)/shard_map/all_to_all | solution.py:371
  547.3 10.2 shard_map.217
  559.8 49.7 %all-to-all-done.3 = bf16[32,40,2048]{2,1,0:T(8,128)(2,1)} async-done(((bf16[32,40,2048]{2,1,0:T(8,128)(2,1)}), bf16[32,40,2048]{2,1,0:T(8,128)(2,1)}, u32[]{:S(2)}, u32[]{:S(2)}) %all-to-all-start.3) | async-done | bytes 5242912 | tf_op jit(solution)/shard_map/all_to_all | solution.py:371
  610.1 10.1 shard_map.218
  625.0 4.7 fusion.30
  630.2 4.7 fusion.91
  636.9 2.7 multiply_convert_fusion.1
  642.7 2.9 copy.119
  645.6 2.8 select_convert_fusion
  648.4 6.5 collective-permute-start.1
  659.8 15.0 %collective-permute-done.1 = bf16[128,2,2048]{2,0,1:T(8,128)(2,1)} collective-permute-done((bf16[128,2,2048]{2,0,1:T(8,128)(2,1)}, bf16[128,2,2048]{2,0,1:T(8,128)(2,1)}, u32[]{:S(2)}, u32[]{:S(2)}) %collective-permute-start.1) | collective-permute-done | bytes 1048608 | tf_op jit(solution)/shard_map/ppermute | solution.py:194
  693.7 14.5 %convolution_convert_fusion = bf16[4,2048,2048]{2,1,0:T(8,128)(2,1)} fusion(bf16[1,128,2048]{2,1,0:T(8,128)(2,1)S(1)} %copy-done.29, bf16[1,128,2048]{2,1,0:T(8,128)(2,1)S(1)} %copy-done.30, bf16[1,128,2048]{2,1,0:T(8,128)(2,1)S(1)} %copy-done.31, bf16[3,128,2048]{2,1,0:T(8,128)(2,1)S(1)} %maximum_bitcast_fusion.3), kind=kOutput, calls=%fused_computation.1 | convolution fusion | flops 4315938816 | bytes 36700160 | tf_op jit(solution)/shard_map/sta,stb->sab/dot_general | solution.py:458
  709.9 14.3 %fusion.23 = f32[2,1024,2048]{2,1,0:T(8,128)S(1)} fusion(bf16[1280,2048,1]{1,0,2:T(8,128)(2,1)} %bitcast.252, bf16[1,1,1280,1024]{3,2,1,0:T(8,128)(2,1)} %copy-done.61, bf16[1,1,1280,1024]{3,2,1,0:T(8,128)(2,1)S(1)} %copy-done.60), kind=kOutput, calls=%fused_computation.40 | convolution fusion | flops 10740039680 | bytes 27262976 | tf_op jit(solution)/shard_map/lrd,lkrh->lkdh/dot_general | solution.py:365
  724.3 2.7 fusion.18
  727.0 4.5 collective-permute-start.9
  731.5 8.8 fusion.24
  740.7 2.9 copy-done.16
  745.8 3.8 collective-permute-done.11
  749.7 3.7 convert_add_fusion
  758.1 11.1 %bitcast_add_fusion = f32[2,1024,1024]{1,2,0:T(8,128)} fusion(bf16[2,1024,1024]{1,2,0:T(8,128)(2,1)} %collective-permute-done.9, f32[2,1024,2048]{2,1,0:T(8,128)} %copy-done.8, s32[]{:T(128)S(6)} %select_n.78), kind=kLoop, calls=%fused_computation.4 | loop fusion | flops 4194304 | bytes 20971524 | tf_op jit(solution)/shard_map/add | solution.py:190
  770.8 17.1 %fusion.68 = (f32[2048]{0:T(1024)S(1)}, f32[128]{0:T(128)S(1)}, f32[128,2048]{1,0:T(8,128)}) fusion(bf16[1,128,2048]{2,1,0:T(8,128)(2,1)S(1)} %copy-done.12, f32[128]{0:T(128)S(1)} %copy-done.57, f32[2048]{0:T(1024)S(1)} %copy-done.46, bf16[2048,4,2048]{2,0,1:T(8,128)(2,1)} %all-gather.2.cloned.1.call-done, bf16[128,1,2048]{2,0,1:T(8,128)(2,1)S(1)} %copy-done.40, ...), kind=kOutput, calls=%fused_computation.102 | convolution fusion | flops 4299945984 | bytes 36717576 | tf_op jit(solution)/shard_map/dot_general | solution.py:440
  791.1 11.2 %collective-permute-done.2 = f32[73728]{0:T(1024)S(1)} collective-permute-done((f32[73728]{0:T(1024)S(1)}, f32[73728]{0:T(1024)S(1)}, u32[]{:S(2)}, u32[]{:S(2)}) %collective-permute-start.2) | collective-permute-done | bytes 294944 | tf_op jit(solution)/shard_map/ppermute | solution.py:221
  802.5 10.1 collective-permute-done.3
  812.6 3.2 collective-permute-start.4
  815.8 9.7 collective-permute-done.4
  825.6 9.1 collective-permute-done.5
  834.9 3.8 add_bitcast_fusion.1
  838.7 4.3 collective-permute-done.6
  844.6 31.1 %collective-permute-done.7 = f32[73728]{0:T(1024)S(1)} collective-permute-done((f32[73728]{0:T(1024)S(1)}, f32[73728]{0:T(1024)S(1)}, u32[]{:S(2)}, u32[]{:S(2)}) %collective-permute-start.7) | collective-permute-done | bytes 294944 | tf_op jit(solution)/shard_map/ppermute | solution.py:221
  876.9 5.7 add_bitcast_fusion
  882.6 5.4 copy.111
  890.0 159.1 %all-reduce.2.cloned.1.call-done = bf16[4,2048,2048]{2,1,0:T(8,128)(2,1)} async-done(((bf16[4,2048,2048]{2,1,0:T(8,128)(2,1)}), bf16[4,2048,2048]{2,1,0:T(8,128)(2,1)}) %all-reduce.2.cloned.1.call-update) | async-done | bytes 33554448 | tf_op jit(solution)/shard_map/psum | solution.py:459
  (241 shorter events, 91.4 us)
Async XLA Ops:
  7.2 305.0 %copy-start = (bf16[2048,32]{0,1:T(8,128)(2,1)S(1)}, bf16[2048,32]{0,1:T(8,128)(2,1)}, u32[]{:S(2)}) copy-start(bf16[2048,32]{0,1:T(8,128)(2,1)} %param.23) | copy-start | bytes 393220
  7.2 243.4 %all-gather.2.cloned.1.call-start = ((), (), s32[]{:S(2)}) async-start(), calls=%async_computation.4 | async-start | bytes 33816576 | tf_op jit(solution)/shard_map/all_gather | solution.py:260
  270.9 29.0 %copy-start.17 = (bf16[128,16,64]{2,0,1:T(8,128)(2,1)}, bf16[128,16,64]{2,0,1:T(8,128)(2,1)S(1)}, u32[]{:S(2)}) copy-start(bf16[128,16,64]{2,0,1:T(8,128)(2,1)S(1)} %get-tuple-element.84) | copy-start | bytes 786436
  270.9 29.0 %copy-start.19 = (bf16[128,16,64]{2,0,1:T(8,128)(2,1)}, bf16[128,16,64]{2,0,1:T(8,128)(2,1)S(1)}, u32[]{:S(2)}) copy-start(bf16[128,16,64]{2,0,1:T(8,128)(2,1)S(1)} %get-tuple-element.85) | copy-start | bytes 786436
  272.9 23.8 %collective-permute-start = (bf16[128,2,2048]{2,0,1:T(8,128)(2,1)}, bf16[128,2,2048]{2,0,1:T(8,128)(2,1)S(1)}, u32[]{:S(2)}, u32[]{:S(2)}) collective-permute-start(bf16[128,2,2048]{2,0,1:T(8,128)(2,1)} %pad_maximum_fusion.2), channel_id=1, source_target_pairs={{0,32},{32,0},{1,33},{33,1},{2,34},{34,2},{3,35},{35,3},{4,36},{36... | collective-permute-start | bytes 3145736 | tf_op jit(solution)/shard_map/ppermute | solution.py:194
  276.1 21.8 %copy-start.42 = (s32[128,8]{1,0:T(8,128)}, s32[128,8]{1,0:T(8,128)S(1)}, u32[]{:S(2)}) copy-start(s32[128,8]{1,0:T(8,128)S(1)} %fusion.104.slot_ref) | copy-start | bytes 12292
  277.5 24.2 %copy-start.49 = (pred[128,256]{1,0:T(8,128)(4,1)}, pred[128,256]{1,0:T(8,128)(4,1)S(1)}, u32[]{:S(2)}) copy-start(pred[128,256]{1,0:T(8,128)(4,1)S(1)} %broadcast_compare_fusion) | copy-start | bytes 98308
  299.9 5.5 copy-start.26
  305.4 6.6 copy-start.33
  305.4 6.6 copy-start.43
  305.4 7.1 copy-start.48
  312.0 7.8 copy-start.6
  388.3 72.7 %all-to-all-start.2 = ((bf16[32,40,2048]{2,1,0:T(8,128)(2,1)}), bf16[32,40,2048]{2,1,0:T(8,128)(2,1)}, u32[]{:S(2)}, u32[]{:S(2)}) async-start(bf16[32,40,2048]{2,1,0:T(8,128)(2,1)} %bitcast.255), calls=%async_computation.2 | async-start | bytes 10485760 | tf_op jit(solution)/shard_map/all_to_all | solution.py:348
  410.2 5.0 copy-start.5
  410.2 6.5 copy-start.58
  460.9 72.5 %all-to-all-start.1 = ((bf16[32,40,2048]{2,1,0:T(8,128)(2,1)}), bf16[32,40,2048]{2,1,0:T(8,128)(2,1)}, u32[]{:S(2)}, u32[]{:S(2)}) async-start(bf16[32,40,2048]{2,1,0:T(8,128)(2,1)} %bitcast.254), calls=%async_computation.1 | async-start | bytes 10485760 | tf_op jit(solution)/shard_map/all_to_all | solution.py:336
  533.5 10.9 %copy-start.51 = (f32[128,8]{0,1:T(8,128)S(1)}, f32[128,8]{0,1:T(8,128)}, u32[]{:S(2)}) copy-start(f32[128,8]{0,1:T(8,128)} %select_reduce_fusion.1) | copy-start | bytes 12292
  533.5 11.7 %copy-start.32 = (f32[16,128,256]{2,1,0:T(8,128)S(1)}, f32[16,128,256]{2,1,0:T(8,128)}, u32[]{:S(2)}) copy-start(f32[16,128,256]{2,1,0:T(8,128)} %fusion.103) | copy-start | bytes 6291460
  533.5 11.7 %copy-start.50 = (pred[128,256]{1,0:T(8,128)(4,1)S(1)}, pred[128,256]{1,0:T(8,128)(4,1)}, u32[]{:S(2)}) copy-start(pred[128,256]{1,0:T(8,128)(4,1)} %copy-done.49) | copy-start | bytes 98308
  533.5 76.0 %all-to-all-start.3 = ((bf16[32,40,2048]{2,1,0:T(8,128)(2,1)}), bf16[32,40,2048]{2,1,0:T(8,128)(2,1)}, u32[]{:S(2)}, u32[]{:S(2)}) async-start(bf16[32,40,2048]{2,1,0:T(8,128)(2,1)} %bitcast.253), calls=%async_computation.3 | async-start | bytes 10485760 | tf_op jit(solution)/shard_map/all_to_all | solution.py:371
  544.2 505.0 %all-reduce.2.cloned.1.call-start = ((), (), s32[]{:S(2)}) async-start(), calls=%async_computation.5 | async-start | bytes 67108864 | tf_op jit(solution)/shard_map/psum | solution.py:459
  610.1 10.1 copy-start.7
  625.0 5.0 copy-start.34
  645.6 9.3 copy-start.11
  645.6 9.3 copy-start.46
  645.6 9.3 copy-start.57
  648.4 26.3 %collective-permute-start.1 = (bf16[128,2,2048]{2,0,1:T(8,128)(2,1)}, bf16[128,2,2048]{2,0,1:T(8,128)(2,1)}, u32[]{:S(2)}, u32[]{:S(2)}) collective-permute-start(bf16[128,2,2048]{2,0,1:T(8,128)(2,1)} %select_convert_fusion), channel_id=1, source_target_pairs={{0,32},{32,0},{1,33},{33,1},{2,34},{34,2},{3,35},{35,3},{4,36},{36... | collective-permute-start | bytes 3145736 | tf_op jit(solution)/shard_map/ppermute | solution.py:194
  658.0 16.8 %copy-start.3 = (f32[256,1,2048]{2,0,1:T(8,128)S(1)}, f32[256,1,2048]{2,0,1:T(8,128)}, u32[]{:S(2)}) copy-start(f32[256,1,2048]{2,0,1:T(8,128)} %copy.119) | copy-start | bytes 6291460
  684.2 4.9 copy-start.2
  684.2 4.9 copy-start.53
  684.2 4.9 copy-start.55
  724.2 16.1 %copy-start.8 = (f32[2,1024,2048]{2,1,0:T(8,128)}, f32[2,1024,2048]{2,1,0:T(8,128)S(1)}, u32[]{:S(2)}) copy-start(f32[2,1024,2048]{2,1,0:T(8,128)S(1)} %fusion.23) | copy-start | bytes 50331652
  724.3 7.3 copy-start.28
  727.0 31.1 %collective-permute-start.9 = (bf16[2,1024,1024]{1,2,0:T(8,128)(2,1)}, bf16[2,1024,1024]{1,2,0:T(8,128)(2,1)}, u32[]{:S(2)}, u32[]{:S(2)}) collective-permute-start(bf16[2,1024,1024]{1,2,0:T(8,128)(2,1)} %fusion.18), channel_id=1, source_target_pairs={{0,64},{64,0},{1,65},{65,1},{2,66},{66,2},{3,67},{67,3},{4,68},{68... | collective-permute-start | bytes 12582920 | tf_op jit(solution)/shard_map/ppermute | solution.py:189
  743.6 6.1 collective-permute-start.11
  756.5 12.7 %copy-start.14 = (bf16[128,2048]{1,0:T(8,128)(2,1)S(1)}, bf16[128,2048]{1,0:T(8,128)(2,1)}, u32[]{:S(2)}) copy-start(bf16[128,2048]{1,0:T(8,128)(2,1)} %copy-done.13) | copy-start | bytes 1572868
  756.5 78.4 %collective-permute-start.12 = (bf16[1024,512]{1,0:T(8,128)(2,1)}, bf16[1024,512]{1,0:T(8,128)(2,1)}, u32[]{:S(2)}, u32[]{:S(2)}) collective-permute-start(bf16[1024,512]{1,0:T(8,128)(2,1)} %dynamic-slice_convert_fusion.3), channel_id=1, source_target_pairs={{0,32},{32,0},{1,33},{33,1},{2,34},{34,2},{3,35},{35,3},{4,36},{36... | collective-permute-start | bytes 3145736 | tf_op jit(solution)/shard_map/ppermute | solution.py:189
  787.9 14.5 %collective-permute-start.2 = (f32[73728]{0:T(1024)S(1)}, f32[73728]{0:T(1024)S(1)}, u32[]{:S(2)}, u32[]{:S(2)}) collective-permute-start(f32[73728]{0:T(1024)S(1)} %constant_dynamic-update-slice_fusion), channel_id=1, source_target_pairs={{0,1},{1,0},{2,3},{3,2},{4,5},{5,4},{6,7},{7,6},{8,9},{9,8},{10,11... | collective-permute-start | bytes 884744 | tf_op jit(solution)/shard_map/ppermute | solution.py:221
  791.0 85.9 %collective-permute-start.10 = (bf16[2,512,1024]{1,2,0:T(8,128)(2,1)S(1)}, bf16[2,512,1024]{1,2,0:T(8,128)(2,1)}, u32[]{:S(2)}, u32[]{:S(2)}) collective-permute-start(bf16[2,512,1024]{1,2,0:T(8,128)(2,1)S(1)} %dynamic-slice_convert_fusion.2), channel_id=1, source_target_pairs={{0,32},{32,0},{1,33},{33,1},{2,34},{34,2},{3,35},{35,3},{4,36},{36... | collective-permute-start | bytes 6291464 | tf_op jit(solution)/shard_map/ppermute | solution.py:189
  802.4 10.2 collective-permute-start.3
  812.6 12.8 %collective-permute-start.4 = (f32[73728]{0:T(1024)S(1)}, f32[73728]{0:T(1024)S(1)}, u32[]{:S(2)}, u32[]{:S(2)}) collective-permute-start(f32[73728]{0:T(1024)S(1)} %add.165), channel_id=1, source_target_pairs={{0,4},{1,5},{2,6},{3,7},{4,0},{5,1},{6,2},{7,3},{8,12},{9,13},{10,... | collective-permute-start | bytes 884744 | tf_op jit(solution)/shard_map/ppermute | solution.py:221
  825.5 9.2 collective-permute-start.5
  834.8 8.5 copy-start.25
  834.8 8.5 copy-start.41
  834.8 8.3 collective-permute-start.6
  843.1 32.7 %collective-permute-start.7 = (f32[73728]{0:T(1024)S(1)}, f32[73728]{0:T(1024)S(1)}, u32[]{:S(2)}, u32[]{:S(2)}) collective-permute-start(f32[73728]{0:T(1024)S(1)} %add.168), channel_id=1, source_target_pairs={{0,32},{1,33},{2,34},{3,35},{4,36},{5,37},{6,38},{7,39},{8,40},{9,... | collective-permute-start | bytes 884744 | tf_op jit(solution)/shard_map/ppermute | solution.py:221
  875.8 12.2 %collective-permute-start.8 = (f32[73728]{0:T(1024)S(1)}, f32[73728]{0:T(1024)S(1)}, u32[]{:S(2)}, u32[]{:S(2)}) collective-permute-start(f32[73728]{0:T(1024)S(1)} %add.169), channel_id=1, source_target_pairs={{0,64},{1,65},{2,66},{3,67},{4,68},{5,69},{6,70},{7,71},{8,72},{9,... | collective-permute-start | bytes 884744 | tf_op jit(solution)/shard_map/ppermute | solution.py:221
  888.0 163.5 %copy-start.1 = (bf16[2048,32]{0,1:T(8,128)(2,1)S(1)}, bf16[2048,32]{0,1:T(8,128)(2,1)}, u32[]{:S(2)}) copy-start(bf16[2048,32]{0,1:T(8,128)(2,1)} %param.23) | copy-start | bytes 393220
  (32 other events, 59.2 us)
Sparse Core Ops, SparseCore 0:
  10.3 240.1 all-gather.1
  708.4 340.7 all-reduce.1

commit v9 on v8

--- a/solution.py
+++ b/solution.py
@@ -98,7 +98,7 @@
     )(inputs, weights)
 
 
-def _dispatch_kernel(slot_ref, weight_ref, rows_ref, grad_ref, send_ref, grad_send_ref):
+def _dispatch_kernel(scaled, slot_ref, weight_ref, rows_ref, send_ref):
     tile = send_ref.shape[0]
     top, tokens = slot_ref.shape
     slot = pl.program_id(0) * tile + lax.broadcasted_iota(jnp.int32, (tile, tokens), 0)
@@ -108,39 +108,31 @@
         match = slot == slot_ref[k : k + 1, :]
         hit = hit | match
         weight = weight + jnp.where(match, weight_ref[k : k + 1, :], 0.0)
-    pick = hit.astype(jnp.bfloat16)
-    send_ref[...] = jnp.dot(pick, rows_ref[...], preferred_element_type=jnp.float32).astype(
-        send_ref.dtype
-    )
-    picked_grad = jnp.dot(pick, grad_ref[...], preferred_element_type=jnp.float32)
-    slot_weight = jnp.sum(weight, axis=1, keepdims=True)
-    grad_send_ref[...] = (slot_weight * picked_grad).astype(grad_send_ref.dtype)
-
-
-def dispatch(route_slots, route_weights, rows, grad, slots, tile=256):
+    picked = jnp.dot(hit.astype(jnp.bfloat16), rows_ref[...], preferred_element_type=jnp.float32)
+    if scaled:
+        picked = jnp.sum(weight, axis=1, keepdims=True) * picked
+    send_ref[...] = picked.astype(send_ref.dtype)
+
+
+def dispatch(route_slots, route_weights, rows, slots, scaled, tile=256):
     top, tokens = route_slots.shape
     width = rows.shape[1]
-    out = jax.ShapeDtypeStruct((slots, width), jnp.bfloat16)
     return pl.pallas_call(
-        _dispatch_kernel,
-        out_shape=(out, out),
+        functools.partial(_dispatch_kernel, scaled),
+        out_shape=jax.ShapeDtypeStruct((slots, width), jnp.bfloat16),
         grid=(slots // tile,),
         in_specs=[
             pl.BlockSpec((top, tokens), lambda i: (0, 0)),
             pl.BlockSpec((top, tokens), lambda i: (0, 0)),
             pl.BlockSpec((tokens, width), lambda i: (0, 0)),
-            pl.BlockSpec((tokens, width), lambda i: (0, 0)),
         ],
-        out_specs=(
-            pl.BlockSpec((tile, width), lambda i: (i, 0)),
-            pl.BlockSpec((tile, width), lambda i: (i, 0)),
-        ),
+        out_specs=pl.BlockSpec((tile, width), lambda i: (i, 0)),
         cost_estimate=pl.CostEstimate(
-            flops=4 * slots * tokens * width,
+            flops=2 * slots * tokens * width,
             transcendentals=0,
-            bytes_accessed=4 * slots * width + 4 * tokens * width + 8 * top * tokens,
-        ),
-    )(route_slots, route_weights, rows, grad)
+            bytes_accessed=2 * slots * width + 2 * tokens * width + 8 * top * tokens,
+        ),
+    )(route_slots, route_weights, rows)
 
 
 def _combine_kernel(with_dots, slot_ref, weight_ref, table_ref, base_ref, other_ref, out_ref, dots_ref):
@@ -314,9 +306,8 @@
         jnp.where(own_routes[:, :, None] == expert_ids, router_probs[:, None, :], 0.0), axis=2
     )
     route_slots = slots.reshape(seq_tok, top)
-    send, grad_send = dispatch(
-        route_slots.T, route_weight.T, ffn_in, grad_output[0], experts * capacity
-    )
+    send = dispatch(route_slots.T, route_weight.T, ffn_in, experts * capacity, False)
+    grad_send = dispatch(route_slots.T, route_weight.T, grad_output[0], experts * capacity, True)
     received = lax.all_to_all(
         send.reshape(sources, local_experts * capacity, width),
         "expert",

time: 1070 us -> 1080 us (level)
  blocking collectives: 68.5 us -> 0 us
  waiting for transfers between devices: 631 us -> 690 us
  starting transfers between devices: 43.9 us -> 62.7 us
    all_to_all x1 -> x0, blocking collectives: 68.5 us -> none  [body(): lax.all_to_all(send.reshape(sources, local_experts * capacity, width), 'e...]
    all_to_all x0 -> x1, waiting for transfers between devices: none -> 61.9 us  [body(): lax.all_to_all(send.reshape(sources, local_experts * capacity, width), 'e...]
  transfers between devices with their start and end apart: 18 -> 19, of which waited for: 14 -> 15; matrix products, arithmetic and copies ran while one was open for 14% -> 14% of each run, Pallas kernels for 1% -> 1%
where the time goes in v9:
time: 1080 us; the launch traced here: 1070 us
  waiting for transfers between devices  690 us (64%)
  matrix products  137 us (13%)
  starting transfers between devices  62.7 us (6%)
  local copies, waits for them, and re-layouts  60.9 us (6%)
  other arithmetic  59.4 us (6%)
  Pallas kernels  46.4 us (4%)
  between operations  15.3 us (1%)
    all_gather x1, waiting for transfers between devices, body(): lax.all_gather(jnp.concatenate([qkv_weight.transpose(1, 0, 2), out_weight...  237 us
    psum x1, waiting for transfers between devices, body(): summed = lax.psum(stacked.astype(bf16), all_axes)  167 us
    ppermute x7, waiting for transfers between devices, butterfly_sum(): received = lax.ppermute(values, axes, partner)  65.7 us
    all_to_all x1, waiting for transfers between devices, body(): lax.all_to_all(send.reshape(sources, local_experts * capacity, width), 'e...  61.9 us
    all_to_all x1, waiting for transfers between devices, body(): lax.all_to_all(source_major(grad_rows_in, sources, capacity), 'expert', s...  51 us
    all_to_all x1, waiting for transfers between devices, body(): lax.all_to_all(source_major(results, sources, capacity), 'expert', split_...  35.6 us
    all_to_all x1, waiting for transfers between devices, body(): lax.all_to_all(grad_send.reshape(sources, local_experts * capacity, width...  35.4 us
    ppermute x2, waiting for transfers between devices, swap_context(): return lax.ppermute(values, 'context', [(0, 1), (1, 0)])  32.1 us
  transfers between devices with their start and end apart: 19, of which 15 were waited for; matrix products, arithmetic and copies ran while one was open for 14% of the time, Pallas kernels for 1%

profile of v9, /device:TPU:1, one launch (start us, length us, event | category | flops | bytes accessed | tf_op | source)
XLA Modules:
  0.0 1070.9 jit_solution(7588069113888174476)
XLA Ops:
  14.0 236.6 %all-gather.2.cloned.1.call-done = bf16[2048,4,2048]{2,0,1:T(8,128)(2,1)} async-done(((bf16[16,4,2048]{2,0,1:T(8,128)(2,1)}), bf16[2048,4,2048]{2,0,1:T(8,128)(2,1)}) %all-gather.2.cloned.1.call-update) | async-done | bytes 33554448 | tf_op jit(solution)/shard_map/all_gather | solution.py:252
  250.6 15.0 %shard_map.215 = f32[3,128,2048]{2,1,0:T(8,128)} custom-call(bf16[128,2048]{1,0:T(8,128)(2,1)} %fusion.62.inputs_ref, bf16[4,2048,2048]{2,1,0:T(8,128)(2,1)} %bitcast.246), custom_call_target="tpu_custom_call" | custom-call | flops 3221225472 | bytes 28835840 | tf_op jit(solution)/shard_map/pallas_call | solution.py:83
  277.5 19.1 %collective-permute-done = bf16[128,2,2048]{2,0,1:T(8,128)(2,1)S(1)} collective-permute-done((bf16[128,2,2048]{2,0,1:T(8,128)(2,1)}, bf16[128,2,2048]{2,0,1:T(8,128)(2,1)S(1)}, u32[]{:S(2)}, u32[]{:S(2)}) %collective-permute-start) | collective-permute-done | bytes 1048608 | tf_op jit(solution)/shard_map/ppermute | solution.py:186
  301.8 3.6 convolution_convert_fusion.2
  305.4 6.5 multiply_reduce_fusion.7
  313.1 5.4 shard_map.216
  318.6 6.7 all-to-all-start
  325.3 5.6 shard_map.218
  330.9 61.9 %all-to-all-done = bf16[32,40,2048]{2,1,0:T(8,128)(2,1)} async-done(((bf16[32,40,2048]{2,1,0:T(8,128)(2,1)}), bf16[32,40,2048]{2,1,0:T(8,128)(2,1)}, u32[]{:S(2)}, u32[]{:S(2)}) %all-to-all-start) | async-done | bytes 5242912 | tf_op jit(solution)/shard_map/all_to_all | solution.py:311
  392.7 6.1 all-to-all-start.2
  398.8 16.8 %fusion.6 = f32[1,2,1280,1024]{3,2,1,0:T(8,128)S(1)} fusion(bf16[1280,2048,1]{1,0,2:T(8,128)(2,1)} %bitcast.18, bf16[1,2,2048,1024]{3,2,1,0:T(8,128)(2,1)} %param.24), kind=kOutput, calls=%fused_computation.12 | convolution fusion | flops 10737418240 | bytes 24117248 | tf_op jit(solution)/shard_map/lrd,lkdh->lkrh/dot_general | solution.py:319
  417.4 3.3 copy-done.5
  422.3 7.3 convolution_convert_fusion.1
  429.5 35.4 %all-to-all-done.2 = bf16[32,40,2048]{2,1,0:T(8,128)(2,1)} async-done(((bf16[32,40,2048]{2,1,0:T(8,128)(2,1)}), bf16[32,40,2048]{2,1,0:T(8,128)(2,1)}, u32[]{:S(2)}, u32[]{:S(2)}) %all-to-all-start.2) | async-done | bytes 5242912 | tf_op jit(solution)/shard_map/all_to_all | solution.py:339
  465.0 9.0 all-to-all-start.1
  474.0 13.1 %fusion.28 = (bf16[1,1,1280,1024]{3,2,1,0:T(8,128)(2,1)S(1)}, bf16[1,1,1280,1024]{3,2,1,0:T(8,128)(2,1)S(1)}) fusion(f32[1,2,1280,1024]{3,2,1,0:T(8,128)} %copy-done.5, bf16[1280,2048]{1,0:T(8,128)(2,1)} %bitcast.32, bf16[1,1024,2048]{2,1,0:T(8,128)(2,1)} %param.25), kind=kOutput, calls=%fused_computation.45 | convolution fusion | flops 5385748480 | bytes 25165824 | tf_op jit(solution)/shard_map/lrd,lhd->lrh/dot_general | solution.py:347
  489.4 15.1 %bitcast_convert_fusion = bf16[1280,2048]{1,0:T(8,128)(2,1)} fusion(bf16[1,2,2048,1024]{3,2,1,0:T(8,128)(2,1)} %param.24, bf16[1,1,1280,1024]{3,2,1,0:T(8,128)(2,1)S(1)} %get-tuple-element.67, bf16[1,1,1280,1024]{3,2,1,0:T(8,128)(2,1)S(1)} %get-tuple-element.66), kind=kOutput, calls=%fused_computation.2 | convolution fusion | flops 10742661120 | bytes 18874368 | tf_op jit(solution)/shard_map/lkrh,lkdh->lrd/dot_general | solution.py:359
  504.5 35.6 %all-to-all-done.1 = bf16[32,40,2048]{2,1,0:T(8,128)(2,1)} async-done(((bf16[32,40,2048]{2,1,0:T(8,128)(2,1)}), bf16[32,40,2048]{2,1,0:T(8,128)(2,1)}, u32[]{:S(2)}, u32[]{:S(2)}) %all-to-all-start.1) | async-done | bytes 5242912 | tf_op jit(solution)/shard_map/all_to_all | solution.py:327
  540.1 12.3 %all-to-all-start.3 = ((bf16[32,40,2048]{2,1,0:T(8,128)(2,1)}), bf16[32,40,2048]{2,1,0:T(8,128)(2,1)}, u32[]{:S(2)}, u32[]{:S(2)}) async-start(bf16[32,40,2048]{2,1,0:T(8,128)(2,1)} %bitcast.253), calls=%async_computation.3 | async-start | bytes 10485760 | tf_op jit(solution)/shard_map/all_to_all | solution.py:362
  555.6 10.2 shard_map.217
  568.0 51.0 %all-to-all-done.3 = bf16[32,40,2048]{2,1,0:T(8,128)(2,1)} async-done(((bf16[32,40,2048]{2,1,0:T(8,128)(2,1)}), bf16[32,40,2048]{2,1,0:T(8,128)(2,1)}, u32[]{:S(2)}, u32[]{:S(2)}) %all-to-all-start.3) | async-done | bytes 5242912 | tf_op jit(solution)/shard_map/all_to_all | solution.py:362
  619.7 10.1 shard_map.219
  634.6 4.7 fusion.30
  639.9 4.7 fusion.91
  652.3 2.9 copy.122
  655.2 2.8 select_convert_fusion
  663.2 13.0 %collective-permute-done.1 = bf16[128,2,2048]{2,0,1:T(8,128)(2,1)} collective-permute-done((bf16[128,2,2048]{2,0,1:T(8,128)(2,1)}, bf16[128,2,2048]{2,0,1:T(8,128)(2,1)}, u32[]{:S(2)}, u32[]{:S(2)}) %collective-permute-start.1) | collective-permute-done | bytes 1048608 | tf_op jit(solution)/shard_map/ppermute | solution.py:186
  695.3 14.5 %convolution_convert_fusion = bf16[4,2048,2048]{2,1,0:T(8,128)(2,1)} fusion(bf16[1,128,2048]{2,1,0:T(8,128)(2,1)S(1)} %copy-done.29, bf16[1,128,2048]{2,1,0:T(8,128)(2,1)S(1)} %copy-done.30, bf16[1,128,2048]{2,1,0:T(8,128)(2,1)S(1)} %copy-done.31, bf16[3,128,2048]{2,1,0:T(8,128)(2,1)S(1)} %maximum_bitcast_fusion.3), kind=kOutput, calls=%fused_computation.1 | convolution fusion | flops 4315938816 | bytes 36700160 | tf_op jit(solution)/shard_map/sta,stb->sab/dot_general | solution.py:449
  711.5 14.3 %fusion.23 = f32[2,1024,2048]{2,1,0:T(8,128)S(1)} fusion(bf16[1280,2048,1]{1,0,2:T(8,128)(2,1)} %bitcast.18, bf16[1,1,1280,1024]{3,2,1,0:T(8,128)(2,1)} %copy-done.61, bf16[1,1,1280,1024]{3,2,1,0:T(8,128)(2,1)S(1)} %copy-done.60), kind=kOutput, calls=%fused_computation.40 | convolution fusion | flops 10740039680 | bytes 27262976 | tf_op jit(solution)/shard_map/lrd,lkrh->lkdh/dot_general | solution.py:356
  728.5 7.7 collective-permute-start.9
  736.2 7.9 fusion.24
  744.4 2.9 copy-done.16
  747.4 3.0 collective-permute-start.11
  750.4 3.8 collective-permute-done.11
  754.3 3.7 convert_add_fusion
  761.5 11.0 %bitcast_add_fusion = f32[2,1024,1024]{1,2,0:T(8,128)} fusion(bf16[2,1024,1024]{1,2,0:T(8,128)(2,1)} %collective-permute-done.9, f32[2,1024,2048]{2,1,0:T(8,128)} %copy-done.8, s32[]{:T(128)S(6)} %select_n.78), kind=kLoop, calls=%fused_computation.4 | loop fusion | flops 4194304 | bytes 20971524 | tf_op jit(solution)/shard_map/add | solution.py:182
  774.1 17.2 %fusion.68 = (f32[2048]{0:T(1024)S(1)}, f32[128]{0:T(128)S(1)}, f32[128,2048]{1,0:T(8,128)}) fusion(bf16[1,128,2048]{2,1,0:T(8,128)(2,1)S(1)} %copy-done.12, f32[128]{0:T(128)S(1)} %copy-done.57, f32[2048]{0:T(1024)S(1)} %copy-done.46, bf16[2048,4,2048]{2,0,1:T(8,128)(2,1)} %all-gather.2.cloned.1.call-done, bf16[128,1,2048]{2,0,1:T(8,128)(2,1)S(1)} %copy-done.40, ...), kind=kOutput, calls=%fused_computation.102 | convolution fusion | flops 4299945984 | bytes 36717576 | tf_op jit(solution)/shard_map/dot_general | solution.py:431
  795.7 11.4 %collective-permute-done.2 = f32[73728]{0:T(1024)S(1)} collective-permute-done((f32[73728]{0:T(1024)S(1)}, f32[73728]{0:T(1024)S(1)}, u32[]{:S(2)}, u32[]{:S(2)}) %collective-permute-start.2) | collective-permute-done | bytes 294944 | tf_op jit(solution)/shard_map/ppermute | solution.py:213
  808.3 8.4 collective-permute-done.3
  816.7 9.0 collective-permute-start.4
  825.7 9.7 collective-permute-done.4
  835.6 8.6 collective-permute-done.5
  846.0 3.6 add_bitcast_fusion.1
  849.6 4.1 collective-permute-done.6
  856.5 23.5 %collective-permute-done.7 = f32[73728]{0:T(1024)S(1)} collective-permute-done((f32[73728]{0:T(1024)S(1)}, f32[73728]{0:T(1024)S(1)}, u32[]{:S(2)}, u32[]{:S(2)}) %collective-permute-start.7) | collective-permute-done | bytes 294944 | tf_op jit(solution)/shard_map/ppermute | solution.py:213
  880.9 5.7 add_bitcast_fusion
  886.6 5.5 copy.114
  894.0 167.3 %all-reduce.2.cloned.1.call-done = bf16[4,2048,2048]{2,1,0:T(8,128)(2,1)} async-done(((bf16[4,2048,2048]{2,1,0:T(8,128)(2,1)}), bf16[4,2048,2048]{2,1,0:T(8,128)(2,1)}) %all-reduce.2.cloned.1.call-update) | async-done | bytes 33554448 | tf_op jit(solution)/shard_map/psum | solution.py:450
  (243 shorter events, 98.6 us)
Async XLA Ops:
  7.2 305.0 %copy-start = (bf16[2048,32]{0,1:T(8,128)(2,1)S(1)}, bf16[2048,32]{0,1:T(8,128)(2,1)}, u32[]{:S(2)}) copy-start(bf16[2048,32]{0,1:T(8,128)(2,1)} %param.23) | copy-start | bytes 393220
  7.2 243.4 %all-gather.2.cloned.1.call-start = ((), (), s32[]{:S(2)}) async-start(), calls=%async_computation.4 | async-start | bytes 33816576 | tf_op jit(solution)/shard_map/all_gather | solution.py:252
  270.9 29.0 %copy-start.17 = (bf16[128,16,64]{2,0,1:T(8,128)(2,1)}, bf16[128,16,64]{2,0,1:T(8,128)(2,1)S(1)}, u32[]{:S(2)}) copy-start(bf16[128,16,64]{2,0,1:T(8,128)(2,1)S(1)} %get-tuple-element.80) | copy-start | bytes 786436
  270.9 29.0 %copy-start.19 = (bf16[128,16,64]{2,0,1:T(8,128)(2,1)}, bf16[128,16,64]{2,0,1:T(8,128)(2,1)S(1)}, u32[]{:S(2)}) copy-start(bf16[128,16,64]{2,0,1:T(8,128)(2,1)S(1)} %get-tuple-element.81) | copy-start | bytes 786436
  272.9 23.8 %collective-permute-start = (bf16[128,2,2048]{2,0,1:T(8,128)(2,1)}, bf16[128,2,2048]{2,0,1:T(8,128)(2,1)S(1)}, u32[]{:S(2)}, u32[]{:S(2)}) collective-permute-start(bf16[128,2,2048]{2,0,1:T(8,128)(2,1)} %pad_maximum_fusion.2), channel_id=1, source_target_pairs={{0,32},{32,0},{1,33},{33,1},{2,34},{34,2},{3,35},{35,3},{4,36},{36... | collective-permute-start | bytes 3145736 | tf_op jit(solution)/shard_map/ppermute | solution.py:186
  276.1 21.8 %copy-start.42 = (s32[128,8]{1,0:T(8,128)}, s32[128,8]{1,0:T(8,128)S(1)}, u32[]{:S(2)}) copy-start(s32[128,8]{1,0:T(8,128)S(1)} %fusion.104.slot_ref) | copy-start | bytes 12292
  277.5 24.2 %copy-start.50 = (pred[128,256]{1,0:T(8,128)(4,1)}, pred[128,256]{1,0:T(8,128)(4,1)S(1)}, u32[]{:S(2)}) copy-start(pred[128,256]{1,0:T(8,128)(4,1)S(1)} %broadcast_compare_fusion) | copy-start | bytes 98308
  299.9 5.5 copy-start.26
  305.4 6.6 copy-start.33
  305.4 6.6 copy-start.43
  305.4 7.1 copy-start.49
  312.0 6.6 copy-start.6
  318.6 74.2 %all-to-all-start = ((bf16[32,40,2048]{2,1,0:T(8,128)(2,1)}), bf16[32,40,2048]{2,1,0:T(8,128)(2,1)}, u32[]{:S(2)}, u32[]{:S(2)}) async-start(bf16[32,40,2048]{2,1,0:T(8,128)(2,1)} %bitcast.248), calls=%async_computation | async-start | bytes 10485760 | tf_op jit(solution)/shard_map/all_to_all | solution.py:311
  392.7 72.3 %all-to-all-start.2 = ((bf16[32,40,2048]{2,1,0:T(8,128)(2,1)}), bf16[32,40,2048]{2,1,0:T(8,128)(2,1)}, u32[]{:S(2)}, u32[]{:S(2)}) async-start(bf16[32,40,2048]{2,1,0:T(8,128)(2,1)} %bitcast.247), calls=%async_computation.2 | async-start | bytes 10485760 | tf_op jit(solution)/shard_map/all_to_all | solution.py:339
  415.7 5.0 copy-start.5
  415.7 6.5 copy-start.58
  465.0 75.1 %all-to-all-start.1 = ((bf16[32,40,2048]{2,1,0:T(8,128)(2,1)}), bf16[32,40,2048]{2,1,0:T(8,128)(2,1)}, u32[]{:S(2)}, u32[]{:S(2)}) async-start(bf16[32,40,2048]{2,1,0:T(8,128)(2,1)} %bitcast.254), calls=%async_computation.1 | async-start | bytes 10485760 | tf_op jit(solution)/shard_map/all_to_all | solution.py:327
  540.1 12.5 %copy-start.47 = (f32[128,8]{0,1:T(8,128)S(1)}, f32[128,8]{0,1:T(8,128)}, u32[]{:S(2)}) copy-start(f32[128,8]{0,1:T(8,128)} %select_reduce_fusion.1) | copy-start | bytes 12292
  540.1 13.3 %copy-start.32 = (f32[16,128,256]{2,1,0:T(8,128)S(1)}, f32[16,128,256]{2,1,0:T(8,128)}, u32[]{:S(2)}) copy-start(f32[16,128,256]{2,1,0:T(8,128)} %fusion.103) | copy-start | bytes 6291460
  540.1 13.3 %copy-start.51 = (pred[128,256]{1,0:T(8,128)(4,1)S(1)}, pred[128,256]{1,0:T(8,128)(4,1)}, u32[]{:S(2)}) copy-start(pred[128,256]{1,0:T(8,128)(4,1)} %copy-done.50) | copy-start | bytes 98308
  540.1 79.0 %all-to-all-start.3 = ((bf16[32,40,2048]{2,1,0:T(8,128)(2,1)}), bf16[32,40,2048]{2,1,0:T(8,128)(2,1)}, u32[]{:S(2)}, u32[]{:S(2)}) async-start(bf16[32,40,2048]{2,1,0:T(8,128)(2,1)} %bitcast.253), calls=%async_computation.3 | async-start | bytes 10485760 | tf_op jit(solution)/shard_map/all_to_all | solution.py:362
  552.4 509.0 %all-reduce.2.cloned.1.call-start = ((), (), s32[]{:S(2)}) async-start(), calls=%async_computation.5 | async-start | bytes 67108864 | tf_op jit(solution)/shard_map/psum | solution.py:450
  619.7 10.1 copy-start.7
  634.6 5.0 copy-start.34
  639.7 4.9 copy-start.15
  646.5 3.8 copy-start.18
  658.0 18.2 %collective-permute-start.1 = (bf16[128,2,2048]{2,0,1:T(8,128)(2,1)}, bf16[128,2,2048]{2,0,1:T(8,128)(2,1)}, u32[]{:S(2)}, u32[]{:S(2)}) collective-permute-start(bf16[128,2,2048]{2,0,1:T(8,128)(2,1)} %select_convert_fusion), channel_id=1, source_target_pairs={{0,32},{32,0},{1,33},{33,1},{2,34},{34,2},{3,35},{35,3},{4,36},{36... | collective-permute-start | bytes 3145736 | tf_op jit(solution)/shard_map/ppermute | solution.py:186
  661.4 14.8 %copy-start.3 = (f32[256,1,2048]{2,0,1:T(8,128)S(1)}, f32[256,1,2048]{2,0,1:T(8,128)}, u32[]{:S(2)}) copy-start(f32[256,1,2048]{2,0,1:T(8,128)} %copy.122) | copy-start | bytes 6291460
  685.7 4.9 copy-start.2
  685.7 4.9 copy-start.53
  685.7 4.9 copy-start.55
  725.8 18.3 %copy-start.8 = (f32[2,1024,2048]{2,1,0:T(8,128)}, f32[2,1024,2048]{2,1,0:T(8,128)S(1)}, u32[]{:S(2)}) copy-start(f32[2,1024,2048]{2,1,0:T(8,128)S(1)} %fusion.23) | copy-start | bytes 50331652
  725.8 10.4 copy-start.28
  728.5 33.1 %collective-permute-start.9 = (bf16[2,1024,1024]{1,2,0:T(8,128)(2,1)}, bf16[2,1024,1024]{1,2,0:T(8,128)(2,1)}, u32[]{:S(2)}, u32[]{:S(2)}) collective-permute-start(bf16[2,1024,1024]{1,2,0:T(8,128)(2,1)} %fusion.18), channel_id=1, source_target_pairs={{0,64},{64,0},{1,65},{65,1},{2,66},{66,2},{3,67},{67,3},{4,68},{68... | collective-permute-start | bytes 12582920 | tf_op jit(solution)/shard_map/ppermute | solution.py:181
  747.4 6.9 collective-permute-start.11
  761.1 11.4 %copy-start.14 = (bf16[128,2048]{1,0:T(8,128)(2,1)S(1)}, bf16[128,2048]{1,0:T(8,128)(2,1)}, u32[]{:S(2)}) copy-start(bf16[128,2048]{1,0:T(8,128)(2,1)} %copy-done.13) | copy-start | bytes 1572868
  761.2 84.9 %collective-permute-start.12 = (bf16[1024,512]{1,0:T(8,128)(2,1)}, bf16[1024,512]{1,0:T(8,128)(2,1)}, u32[]{:S(2)}, u32[]{:S(2)}) collective-permute-start(bf16[1024,512]{1,0:T(8,128)(2,1)} %dynamic-slice_convert_fusion.3), channel_id=1, source_target_pairs={{0,32},{32,0},{1,33},{33,1},{2,34},{34,2},{3,35},{35,3},{4,36},{36... | collective-permute-start | bytes 3145736 | tf_op jit(solution)/shard_map/ppermute | solution.py:181
  791.4 15.8 %collective-permute-start.2 = (f32[73728]{0:T(1024)S(1)}, f32[73728]{0:T(1024)S(1)}, u32[]{:S(2)}, u32[]{:S(2)}) collective-permute-start(f32[73728]{0:T(1024)S(1)} %constant_dynamic-update-slice_fusion), channel_id=1, source_target_pairs={{0,1},{1,0},{2,3},{3,2},{4,5},{5,4},{6,7},{7,6},{8,9},{9,8},{10,11... | collective-permute-start | bytes 884744 | tf_op jit(solution)/shard_map/ppermute | solution.py:213
  795.6 85.3 %collective-permute-start.10 = (bf16[2,512,1024]{1,2,0:T(8,128)(2,1)S(1)}, bf16[2,512,1024]{1,2,0:T(8,128)(2,1)}, u32[]{:S(2)}, u32[]{:S(2)}) collective-permute-start(bf16[2,512,1024]{1,2,0:T(8,128)(2,1)S(1)} %dynamic-slice_convert_fusion.2), channel_id=1, source_target_pairs={{0,32},{32,0},{1,33},{33,1},{2,34},{34,2},{3,35},{35,3},{4,36},{36... | collective-permute-start | bytes 6291464 | tf_op jit(solution)/shard_map/ppermute | solution.py:181
  807.2 9.5 collective-permute-start.3
  816.7 18.7 %collective-permute-start.4 = (f32[73728]{0:T(1024)S(1)}, f32[73728]{0:T(1024)S(1)}, u32[]{:S(2)}, u32[]{:S(2)}) collective-permute-start(f32[73728]{0:T(1024)S(1)} %add.165), channel_id=1, source_target_pairs={{0,4},{1,5},{2,6},{3,7},{4,0},{5,1},{6,2},{7,3},{8,12},{9,13},{10,... | collective-permute-start | bytes 884744 | tf_op jit(solution)/shard_map/ppermute | solution.py:213
  835.5 8.7 collective-permute-start.5
  844.2 10.9 %copy-start.25 = (f32[128,2048]{1,0:T(8,128)S(1)}, f32[128,2048]{1,0:T(8,128)}, u32[]{:S(2)}) copy-start(f32[128,2048]{1,0:T(8,128)} %copy-done.24) | copy-start | bytes 3145732
  844.2 10.9 %copy-start.41 = (f32[128,2048]{1,0:T(8,128)S(1)}, f32[128,2048]{1,0:T(8,128)}, u32[]{:S(2)}) copy-start(f32[128,2048]{1,0:T(8,128)} %get-tuple-element.101) | copy-start | bytes 3145732
  844.2 9.4 collective-permute-start.6
  853.7 26.3 %collective-permute-start.7 = (f32[73728]{0:T(1024)S(1)}, f32[73728]{0:T(1024)S(1)}, u32[]{:S(2)}, u32[]{:S(2)}) collective-permute-start(f32[73728]{0:T(1024)S(1)} %add.168), channel_id=1, source_target_pairs={{0,32},{1,33},{2,34},{3,35},{4,36},{5,37},{6,38},{7,39},{8,40},{9,... | collective-permute-start | bytes 884744 | tf_op jit(solution)/shard_map/ppermute | solution.py:213
  880.0 12.0 %collective-permute-start.8 = (f32[73728]{0:T(1024)S(1)}, f32[73728]{0:T(1024)S(1)}, u32[]{:S(2)}, u32[]{:S(2)}) collective-permute-start(f32[73728]{0:T(1024)S(1)} %add.169), channel_id=1, source_target_pairs={{0,64},{1,65},{2,66},{3,67},{4,68},{5,69},{6,70},{7,71},{8,72},{9,... | collective-permute-start | bytes 884744 | tf_op jit(solution)/shard_map/ppermute | solution.py:213
  892.0 171.7 %copy-start.1 = (bf16[2048,32]{0,1:T(8,128)(2,1)S(1)}, bf16[2048,32]{0,1:T(8,128)(2,1)}, u32[]{:S(2)}) copy-start(bf16[2048,32]{0,1:T(8,128)(2,1)} %param.23) | copy-start | bytes 393220
  (33 other events, 60.0 us)
Sparse Core Ops, SparseCore 0:
  10.3 240.1 all-gather.1
  709.9 351.4 all-reduce.1

commit v10 on v8

--- a/solution.py
+++ b/solution.py
@@ -264,25 +264,25 @@
         tiled=True,
     )
     out_full = weights_full[:, 3, :]
-    projected_output = project(attention_input, weights_full.transpose(1, 0, 2), 3)
+    both_inputs = gather_context(attention_input)
+    projected_both = project(both_inputs, weights_full.transpose(1, 0, 2), 3)
+    own_start = lax.axis_index("context") * seq_tok
+    projected_output = lax.dynamic_slice_in_dim(projected_both, own_start, seq_tok, axis=1)
     q_normed, q_factor = rms_forward(projected_output[0])
     k_normed, k_factor = rms_forward(projected_output[1])
-    values = projected_output[2].astype(bf16)
     all_places = positions[0]
-    own_places = lax.dynamic_slice_in_dim(all_places, lax.axis_index("context") * seq_tok, seq_tok)
+    own_places = lax.dynamic_slice_in_dim(all_places, own_start, seq_tok)
     cosine, sine = rope_tables(own_places, head_dim)
+    all_cosine, all_sine = rope_tables(all_places, head_dim)
     queries = rotate(
         (q_normed * q_gain).reshape(seq_tok, heads, head_dim), cosine, sine, 1.0
     ).astype(bf16)
-    own_keys = rotate(
-        (k_normed * k_gain).reshape(seq_tok, heads, head_dim), cosine, sine, 1.0
+    seq_len = both_inputs.shape[0]
+    keys_normed, _ = rms_forward(projected_both[1])
+    keys = rotate(
+        (keys_normed * k_gain).reshape(seq_len, heads, head_dim), all_cosine, all_sine, 1.0
     ).astype(bf16)
-    keys_vals = gather_context(
-        jnp.stack([own_keys.reshape(seq_tok, heads_width), values], axis=1)
-    )
-    keys = keys_vals[:, 0]
-    vals = keys_vals[:, 1]
-    seq_len = keys.shape[0]
+    vals = projected_both[2].astype(bf16)
     keys3 = keys.reshape(seq_len, heads, head_dim)
     vals3 = vals.reshape(seq_len, heads, head_dim)
     allowed = (all_places[None, :] <= own_places[:, None])[None]

time: 1070 us -> 1050 us (0.981)
  waiting for transfers between devices: 631 us -> 608 us
    unnamed x136 -> x113, local copies, waits for them, and re-layouts: 27.5 us -> 25.1 us
  transfers between devices with their start and end apart: 18 -> 18, of which waited for: 14 -> 14; matrix products, arithmetic and copies ran while one was open for 14% -> 15% of each run, Pallas kernels for 1% -> 1%
where the time goes in v10:
time: 1050 us; the launch traced here: 1030 us
  waiting for transfers between devices  608 us (58%)
  matrix products  139 us (13%)
  blocking collectives  69.6 us (7%)
  other arithmetic  61.5 us (6%)
  local copies, waits for them, and re-layouts  50.7 us (5%)
  starting transfers between devices  46 us (4%)
  Pallas kernels  44.7 us (4%)
  between operations  15.2 us (1%)
    all_gather x1, waiting for transfers between devices, body(): lax.all_gather(jnp.concatenate([qkv_weight.transpose(1, 0, 2), out_weight...  226 us
    psum x1, waiting for transfers between devices, body(): summed = lax.psum(stacked.astype(bf16), all_axes)  160 us
    ppermute x7, waiting for transfers between devices, butterfly_sum(): received = lax.ppermute(values, axes, partner)  70.6 us
    all_to_all x1, blocking collectives, body(): lax.all_to_all(send.reshape(sources, local_experts * capacity, width), 'e...  69.6 us
    all_to_all x1, waiting for transfers between devices, body(): lax.all_to_all(source_major(grad_rows_in, sources, capacity), 'expert', s...  49.5 us
    all_to_all x1, waiting for transfers between devices, body(): lax.all_to_all(grad_send.reshape(sources, local_experts * capacity, width...  37 us
    all_to_all x1, waiting for transfers between devices, body(): lax.all_to_all(source_major(results, sources, capacity), 'expert', split_...  36.6 us
    unnamed x113, local copies, waits for them, and re-layouts  25.1 us
  transfers between devices with their start and end apart: 18, of which 14 were waited for; matrix products, arithmetic and copies ran while one was open for 15% of the time, Pallas kernels for 1%

profile of v10, /device:TPU:1, one launch (start us, length us, event | category | flops | bytes accessed | tf_op | source)
XLA Modules:
  0.0 1034.8 jit_solution(6280063889416815862)
XLA Ops:
  16.2 8.7 collective-permute-done
  26.4 226.3 %all-gather.2.cloned.1.call-done = bf16[2048,4,2048]{2,0,1:T(8,128)(2,1)} async-done(((bf16[16,4,2048]{2,0,1:T(8,128)(2,1)}), bf16[2048,4,2048]{2,0,1:T(8,128)(2,1)}) %all-gather.2.cloned.1.call-update) | async-done | bytes 33554448 | tf_op jit(solution)/shard_map/all_gather | solution.py:260
  252.7 17.7 %shard_map.215 = f32[3,256,2048]{2,1,0:T(8,128)} custom-call(bf16[256,2048]{1,0:T(8,128)(2,1)} %pad_maximum_fusion.1.inputs_ref, bf16[4,2048,2048]{2,1,0:T(8,128)(2,1)} %bitcast.242), custom_call_target="tpu_custom_call" | custom-call | flops 6442450944 | bytes 32505856 | tf_op jit(solution)/shard_map/pallas_call | solution.py:83
  282.2 3.5 convolution_convert_fusion.2
  285.8 6.5 multiply_reduce_fusion.9
  293.5 6.7 shard_map.216
  300.2 69.6 %all_to_all.20 = bf16[32,40,2048]{2,1,0:T(8,128)(2,1)} all-to-all(bf16[32,40,2048]{2,1,0:T(8,128)(2,1)} %bitcast.251), channel_id=1, replica_groups=mesh['dp'=2,'context'=2,'expert'=32] {'expert'}, dimensions={0} | all-to-all | bytes 10485760 | tf_op jit(solution)/shard_map/all_to_all | solution.py:320
  369.8 5.1 all-to-all-start.2
  374.9 16.9 %fusion.6 = f32[1,2,1280,1024]{3,2,1,0:T(8,128)S(1)} fusion(bf16[1280,2048,1]{1,0,2:T(8,128)(2,1)} %bitcast.246, bf16[1,2,2048,1024]{3,2,1,0:T(8,128)(2,1)} %param.24), kind=kOutput, calls=%fused_computation.12 | convolution fusion | flops 10737418240 | bytes 24117248 | tf_op jit(solution)/shard_map/lrd,lkdh->lkrh/dot_general | solution.py:328
  393.4 3.3 copy-done.5
  398.3 7.3 convolution_convert_fusion.1
  405.6 37.0 %all-to-all-done.2 = bf16[32,40,2048]{2,1,0:T(8,128)(2,1)} async-done(((bf16[32,40,2048]{2,1,0:T(8,128)(2,1)}), bf16[32,40,2048]{2,1,0:T(8,128)(2,1)}, u32[]{:S(2)}, u32[]{:S(2)}) %all-to-all-start.2) | async-done | bytes 5242912 | tf_op jit(solution)/shard_map/all_to_all | solution.py:348
  442.5 6.7 all-to-all-start.1
  449.3 13.1 %fusion.28 = (bf16[1,1,1280,1024]{3,2,1,0:T(8,128)(2,1)S(1)}, bf16[1,1,1280,1024]{3,2,1,0:T(8,128)(2,1)S(1)}) fusion(f32[1,2,1280,1024]{3,2,1,0:T(8,128)} %copy-done.5, bf16[1280,2048]{1,0:T(8,128)(2,1)} %bitcast.31, bf16[1,1024,2048]{2,1,0:T(8,128)(2,1)} %param.25), kind=kOutput, calls=%fused_computation.45 | convolution fusion | flops 5385748480 | bytes 25165824 | tf_op jit(solution)/shard_map/lrd,lhd->lrh/dot_general | solution.py:356
  464.7 15.1 %bitcast_convert_fusion = bf16[1280,2048]{1,0:T(8,128)(2,1)} fusion(bf16[1,2,2048,1024]{3,2,1,0:T(8,128)(2,1)} %param.24, bf16[1,1,1280,1024]{3,2,1,0:T(8,128)(2,1)S(1)} %get-tuple-element.71, bf16[1,1,1280,1024]{3,2,1,0:T(8,128)(2,1)S(1)} %get-tuple-element.70), kind=kOutput, calls=%fused_computation.2 | convolution fusion | flops 10742661120 | bytes 18874368 | tf_op jit(solution)/shard_map/lkrh,lkdh->lrd/dot_general | solution.py:368
  479.8 36.6 %all-to-all-done.1 = bf16[32,40,2048]{2,1,0:T(8,128)(2,1)} async-done(((bf16[32,40,2048]{2,1,0:T(8,128)(2,1)}), bf16[32,40,2048]{2,1,0:T(8,128)(2,1)}, u32[]{:S(2)}, u32[]{:S(2)}) %all-to-all-start.1) | async-done | bytes 5242912 | tf_op jit(solution)/shard_map/all_to_all | solution.py:336
  516.4 7.3 all-to-all-start.3
  526.9 10.2 shard_map.217
  539.5 49.5 %all-to-all-done.3 = bf16[32,40,2048]{2,1,0:T(8,128)(2,1)} async-done(((bf16[32,40,2048]{2,1,0:T(8,128)(2,1)}), bf16[32,40,2048]{2,1,0:T(8,128)(2,1)}, u32[]{:S(2)}, u32[]{:S(2)}) %all-to-all-start.3) | async-done | bytes 5242912 | tf_op jit(solution)/shard_map/all_to_all | solution.py:371
  589.6 10.1 shard_map.218
  603.5 4.7 fusion.30
  608.7 4.7 fusion.89
  620.0 2.9 copy.114
  622.9 2.8 select_convert_fusion
  625.7 5.3 collective-permute-start.1
  633.3 2.8 fusion.53
  636.1 14.9 %collective-permute-done.1 = bf16[128,2,2048]{2,0,1:T(8,128)(2,1)} collective-permute-done((bf16[128,2,2048]{2,0,1:T(8,128)(2,1)}, bf16[128,2,2048]{2,0,1:T(8,128)(2,1)}, u32[]{:S(2)}, u32[]{:S(2)}) %collective-permute-start.1) | collective-permute-done | bytes 1048608 | tf_op jit(solution)/shard_map/ppermute | solution.py:194
  663.7 2.9 multiply_reduce_fusion.2
  670.2 14.4 %convolution_convert_fusion = bf16[4,2048,2048]{2,1,0:T(8,128)(2,1)} fusion(bf16[1,128,2048]{2,1,0:T(8,128)(2,1)S(1)} %copy-done.26, bf16[1,128,2048]{2,1,0:T(8,128)(2,1)S(1)} %fusion.72, bf16[1,128,2048]{2,1,0:T(8,128)(2,1)S(1)} %copy-done.27, bf16[3,128,2048]{2,1,0:T(8,128)(2,1)S(1)} %maximum_bitcast_fusion.3), kind=kOutput, calls=%fused_computation.1 | convolution fusion | flops 4315938816 | bytes 36700160 | tf_op jit(solution)/shard_map/sta,stb->sab/dot_general | solution.py:458
  684.7 15.0 %fusion.23 = f32[2,1024,2048]{2,1,0:T(8,128)S(1)} fusion(bf16[1280,2048,1]{1,0,2:T(8,128)(2,1)} %bitcast.247, bf16[1,1,1280,1024]{3,2,1,0:T(8,128)(2,1)} %copy-done.49, bf16[1,1,1280,1024]{3,2,1,0:T(8,128)(2,1)} %copy-done.48), kind=kOutput, calls=%fused_computation.40 | convolution fusion | flops 10740039680 | bytes 27262976 | tf_op jit(solution)/shard_map/lrd,lkrh->lkdh/dot_general | solution.py:365
  702.4 4.4 collective-permute-start.9
  706.8 8.9 fusion.24
  716.0 3.0 copy-done.14
  721.1 4.2 collective-permute-done.11
  725.4 3.7 convert_add_fusion
  734.2 10.8 %bitcast_add_fusion = f32[2,1024,1024]{1,2,0:T(8,128)} fusion(bf16[2,1024,1024]{1,2,0:T(8,128)(2,1)} %collective-permute-done.9, f32[2,1024,2048]{2,1,0:T(8,128)} %copy-done.10, s32[]{:T(128)S(6)} %select_n.82), kind=kLoop, calls=%fused_computation.4 | loop fusion | flops 4194304 | bytes 20971524 | tf_op jit(solution)/shard_map/add | solution.py:190
  746.4 17.1 %fusion.69 = (f32[2048]{0:T(1024)S(1)}, f32[128]{0:T(128)S(1)}, f32[128,2048]{1,0:T(8,128)}) fusion(bf16[1,128,2048]{2,1,0:T(8,128)(2,1)S(1)} %copy-done.3, f32[128]{0:T(128)S(1)} %add_rsqrt_fusion.4, f32[2048]{0:T(1024)S(1)} %copy-done.40, bf16[2048,4,2048]{2,0,1:T(8,128)(2,1)} %all-gather.2.cloned.1.call-done, bf16[128,1,2048]{2,0,1:T(8,128)(2,1)S(1)} %copy-done.32, ...), kind=kOutput, calls=%fused_computation.107 | convolution fusion | flops 4299945984 | bytes 36717576 | tf_op jit(solution)/shard_map/dot_general | solution.py:440
  766.6 10.9 %collective-permute-done.2 = f32[73728]{0:T(1024)S(1)} collective-permute-done((f32[73728]{0:T(1024)S(1)}, f32[73728]{0:T(1024)S(1)}, u32[]{:S(2)}, u32[]{:S(2)}) %collective-permute-start.2) | collective-permute-done | bytes 294944 | tf_op jit(solution)/shard_map/ppermute | solution.py:221
  777.9 8.6 collective-permute-done.3
  786.5 5.3 collective-permute-start.4
  791.8 9.8 collective-permute-done.4
  801.7 7.6 collective-permute-done.5
  812.0 3.6 add_bitcast_fusion.1
  815.6 4.4 collective-permute-done.6
  822.1 29.2 %collective-permute-done.7 = f32[73728]{0:T(1024)S(1)} collective-permute-done((f32[73728]{0:T(1024)S(1)}, f32[73728]{0:T(1024)S(1)}, u32[]{:S(2)}, u32[]{:S(2)}) %collective-permute-start.7) | collective-permute-done | bytes 294944 | tf_op jit(solution)/shard_map/ppermute | solution.py:221
  852.4 5.7 add_bitcast_fusion
  858.1 5.4 copy.105
  865.5 159.8 %all-reduce.2.cloned.1.call-done = bf16[4,2048,2048]{2,1,0:T(8,128)(2,1)} async-done(((bf16[4,2048,2048]{2,1,0:T(8,128)(2,1)}), bf16[4,2048,2048]{2,1,0:T(8,128)(2,1)}) %all-reduce.2.cloned.1.call-update) | async-done | bytes 33554448 | tf_op jit(solution)/shard_map/psum | solution.py:459
  (217 shorter events, 89.5 us)
Async XLA Ops:
  7.2 285.3 %copy-start = (bf16[2048,32]{0,1:T(8,128)(2,1)S(1)}, bf16[2048,32]{0,1:T(8,128)(2,1)}, u32[]{:S(2)}) copy-start(bf16[2048,32]{0,1:T(8,128)(2,1)} %param.23) | copy-start | bytes 393220
  7.2 6.5 copy-start.46
  7.2 6.5 copy-start.44
  7.2 245.5 %all-gather.2.cloned.1.call-start = ((), (), s32[]{:S(2)}) async-start(), calls=%async_computation.4 | async-start | bytes 33816576 | tf_op jit(solution)/shard_map/all_gather | solution.py:260
  9.0 16.0 %copy-start.3 = (bf16[1,128,2048]{2,1,0:T(8,128)(2,1)S(1)}, bf16[1,128,2048]{2,1,0:T(8,128)(2,1)}, u32[]{:S(2)}) copy-start(bf16[1,128,2048]{2,1,0:T(8,128)(2,1)} %param.13) | copy-start | bytes 1572868
  9.0 16.0 %copy-start.40 = (f32[2048]{0:T(1024)S(1)}, f32[2048]{0:T(1024)}, u32[]{:S(2)}) copy-start(f32[2048]{0:T(1024)} %param.17) | copy-start | bytes 24580
  11.5 13.4 %collective-permute-start = (bf16[128,2048]{1,0:T(8,128)(2,1)S(1)}, bf16[128,2048]{1,0:T(8,128)(2,1)S(1)}, u32[]{:S(2)}, u32[]{:S(2)}) collective-permute-start(bf16[128,2048]{1,0:T(8,128)(2,1)S(1)} %fusion.63), channel_id=1, source_target_pairs={{0,32},{32,0},{1,33},{33,1},{2,34},{34,2},{3,35},{35,3},{4,36},{36... | collective-permute-start | bytes 1572872 | tf_op jit(solution)/shard_map/ppermute | solution.py:194
  14.6 11.8 %copy-start.39 = (s32[128,8]{1,0:T(8,128)}, s32[128,8]{1,0:T(8,128)S(1)}, u32[]{:S(2)}) copy-start(s32[128,8]{1,0:T(8,128)S(1)} %fusion.102.slot_ref) | copy-start | bytes 12292
  274.2 8.0 copy-start.22
  279.9 2.3 copy-start.6
  279.9 2.3 copy-start.7
  285.7 6.6 copy-start.29
  285.8 6.6 copy-start.41
  292.3 7.8 copy-start.8
  369.8 72.7 %all-to-all-start.2 = ((bf16[32,40,2048]{2,1,0:T(8,128)(2,1)}), bf16[32,40,2048]{2,1,0:T(8,128)(2,1)}, u32[]{:S(2)}, u32[]{:S(2)}) async-start(bf16[32,40,2048]{2,1,0:T(8,128)(2,1)} %bitcast.250), calls=%async_computation.2 | async-start | bytes 10485760 | tf_op jit(solution)/shard_map/all_to_all | solution.py:348
  391.7 5.0 copy-start.5
  391.7 6.5 copy-start.47
  442.5 73.9 %all-to-all-start.1 = ((bf16[32,40,2048]{2,1,0:T(8,128)(2,1)}), bf16[32,40,2048]{2,1,0:T(8,128)(2,1)}, u32[]{:S(2)}, u32[]{:S(2)}) async-start(bf16[32,40,2048]{2,1,0:T(8,128)(2,1)} %bitcast.249), calls=%async_computation.1 | async-start | bytes 10485760 | tf_op jit(solution)/shard_map/all_to_all | solution.py:336
  462.4 2.3 copy-start.49
  516.4 7.6 copy-start.45
  516.4 8.3 copy-start.28
  516.4 72.6 %all-to-all-start.3 = ((bf16[32,40,2048]{2,1,0:T(8,128)(2,1)}), bf16[32,40,2048]{2,1,0:T(8,128)(2,1)}, u32[]{:S(2)}, u32[]{:S(2)}) async-start(bf16[32,40,2048]{2,1,0:T(8,128)(2,1)} %bitcast.248), calls=%async_computation.3 | async-start | bytes 10485760 | tf_op jit(solution)/shard_map/all_to_all | solution.py:371
  523.8 501.5 %all-reduce.2.cloned.1.call-start = ((), (), s32[]{:S(2)}) async-start(), calls=%async_computation.5 | async-start | bytes 67108864 | tf_op jit(solution)/shard_map/psum | solution.py:459
  589.6 10.1 copy-start.9
  603.5 5.0 copy-start.30
  615.3 2.6 copy-start.16
  615.4 2.6 copy-start.18
  625.7 25.3 %collective-permute-start.1 = (bf16[128,2,2048]{2,0,1:T(8,128)(2,1)}, bf16[128,2,2048]{2,0,1:T(8,128)(2,1)}, u32[]{:S(2)}, u32[]{:S(2)}) collective-permute-start(bf16[128,2,2048]{2,0,1:T(8,128)(2,1)} %select_convert_fusion), channel_id=1, source_target_pairs={{0,32},{32,0},{1,33},{33,1},{2,34},{34,2},{3,35},{35,3},{4,36},{36... | collective-permute-start | bytes 3145736 | tf_op jit(solution)/shard_map/ppermute | solution.py:194
  633.3 17.7 %copy-start.2 = (f32[256,1,2048]{2,0,1:T(8,128)S(1)}, f32[256,1,2048]{2,0,1:T(8,128)}, u32[]{:S(2)}) copy-start(f32[256,1,2048]{2,0,1:T(8,128)} %copy.114) | copy-start | bytes 6291460
  663.6 2.9 copy-start.23
  699.6 16.1 %copy-start.10 = (f32[2,1024,2048]{2,1,0:T(8,128)}, f32[2,1024,2048]{2,1,0:T(8,128)S(1)}, u32[]{:S(2)}) copy-start(f32[2,1024,2048]{2,1,0:T(8,128)S(1)} %fusion.23) | copy-start | bytes 50331652
  699.6 7.2 copy-start.25
  702.4 31.8 %collective-permute-start.9 = (bf16[2,1024,1024]{1,2,0:T(8,128)(2,1)}, bf16[2,1024,1024]{1,2,0:T(8,128)(2,1)}, u32[]{:S(2)}, u32[]{:S(2)}) collective-permute-start(bf16[2,1024,1024]{1,2,0:T(8,128)(2,1)} %fusion.18), channel_id=1, source_target_pairs={{0,64},{64,0},{1,65},{65,1},{2,66},{66,2},{3,67},{67,3},{4,68},{68... | collective-permute-start | bytes 12582920 | tf_op jit(solution)/shard_map/ppermute | solution.py:189
  715.7 3.3 copy-start.14
  719.0 6.4 collective-permute-start.11
  732.2 12.8 %copy-start.13 = (bf16[128,2048]{1,0:T(8,128)(2,1)S(1)}, bf16[128,2048]{1,0:T(8,128)(2,1)}, u32[]{:S(2)}) copy-start(bf16[128,2048]{1,0:T(8,128)(2,1)} %copy-done.12) | copy-start | bytes 1572868
  732.2 79.8 %collective-permute-start.12 = (bf16[1024,512]{1,0:T(8,128)(2,1)}, bf16[1024,512]{1,0:T(8,128)(2,1)}, u32[]{:S(2)}, u32[]{:S(2)}) collective-permute-start(bf16[1024,512]{1,0:T(8,128)(2,1)} %dynamic-slice_convert_fusion.3), channel_id=1, source_target_pairs={{0,32},{32,0},{1,33},{33,1},{2,34},{34,2},{3,35},{35,3},{4,36},{36... | collective-permute-start | bytes 3145736 | tf_op jit(solution)/shard_map/ppermute | solution.py:189
  763.5 14.0 %collective-permute-start.2 = (f32[73728]{0:T(1024)S(1)}, f32[73728]{0:T(1024)S(1)}, u32[]{:S(2)}, u32[]{:S(2)}) collective-permute-start(f32[73728]{0:T(1024)S(1)} %constant_dynamic-update-slice_fusion), channel_id=1, source_target_pairs={{0,1},{1,0},{2,3},{3,2},{4,5},{5,4},{6,7},{7,6},{8,9},{9,8},{10,11... | collective-permute-start | bytes 884744 | tf_op jit(solution)/shard_map/ppermute | solution.py:221
  766.2 86.3 %collective-permute-start.10 = (bf16[2,512,1024]{1,2,0:T(8,128)(2,1)S(1)}, bf16[2,512,1024]{1,2,0:T(8,128)(2,1)}, u32[]{:S(2)}, u32[]{:S(2)}) collective-permute-start(bf16[2,512,1024]{1,2,0:T(8,128)(2,1)S(1)} %dynamic-slice_convert_fusion.2), channel_id=1, source_target_pairs={{0,32},{32,0},{1,33},{33,1},{2,34},{34,2},{3,35},{35,3},{4,36},{36... | collective-permute-start | bytes 6291464 | tf_op jit(solution)/shard_map/ppermute | solution.py:189
  777.5 9.0 collective-permute-start.3
  786.5 15.1 %collective-permute-start.4 = (f32[73728]{0:T(1024)S(1)}, f32[73728]{0:T(1024)S(1)}, u32[]{:S(2)}, u32[]{:S(2)}) collective-permute-start(f32[73728]{0:T(1024)S(1)} %add.179), channel_id=1, source_target_pairs={{0,4},{1,5},{2,6},{3,7},{4,0},{5,1},{6,2},{7,3},{8,12},{9,13},{10,... | collective-permute-start | bytes 884744 | tf_op jit(solution)/shard_map/ppermute | solution.py:221
  801.6 7.7 collective-permute-start.5
  809.4 11.3 %copy-start.21 = (f32[128,2048]{1,0:T(8,128)S(1)}, f32[128,2048]{1,0:T(8,128)}, u32[]{:S(2)}) copy-start(f32[128,2048]{1,0:T(8,128)} %copy-done.20) | copy-start | bytes 3145732
  809.4 11.3 %copy-start.37 = (f32[128,2048]{1,0:T(8,128)S(1)}, f32[128,2048]{1,0:T(8,128)}, u32[]{:S(2)}) copy-start(f32[128,2048]{1,0:T(8,128)} %get-tuple-element.104) | copy-start | bytes 3145732
  809.4 10.6 %collective-permute-start.6 = (f32[73728]{0:T(1024)S(1)}, f32[73728]{0:T(1024)S(1)}, u32[]{:S(2)}, u32[]{:S(2)}) collective-permute-start(f32[73728]{0:T(1024)S(1)} %add.181), channel_id=1, source_target_pairs={{0,16},{1,17},{2,18},{3,19},{4,20},{5,21},{6,22},{7,23},{8,24},{9,... | collective-permute-start | bytes 884744 | tf_op jit(solution)/shard_map/ppermute | solution.py:221
  820.1 31.2 %collective-permute-start.7 = (f32[73728]{0:T(1024)S(1)}, f32[73728]{0:T(1024)S(1)}, u32[]{:S(2)}, u32[]{:S(2)}) collective-permute-start(f32[73728]{0:T(1024)S(1)} %add.182), channel_id=1, source_target_pairs={{0,32},{1,33},{2,34},{3,35},{4,36},{5,37},{6,38},{7,39},{8,40},{9,... | collective-permute-start | bytes 884744 | tf_op jit(solution)/shard_map/ppermute | solution.py:221
  851.3 12.2 %collective-permute-start.8 = (f32[73728]{0:T(1024)S(1)}, f32[73728]{0:T(1024)S(1)}, u32[]{:S(2)}, u32[]{:S(2)}) collective-permute-start(f32[73728]{0:T(1024)S(1)} %add.183), channel_id=1, source_target_pairs={{0,64},{1,65},{2,66},{3,67},{4,68},{5,69},{6,70},{7,71},{8,72},{9,... | collective-permute-start | bytes 884744 | tf_op jit(solution)/shard_map/ppermute | solution.py:221
  863.5 164.2 %copy-start.1 = (bf16[2048,32]{0,1:T(8,128)(2,1)S(1)}, bf16[2048,32]{0,1:T(8,128)(2,1)}, u32[]{:S(2)}) copy-start(bf16[2048,32]{0,1:T(8,128)(2,1)} %param.23) | copy-start | bytes 393220
  (20 other events, 27.7 us)
Sparse Core Ops, SparseCore 0:
  10.4 242.2 all-gather.1
  684.8 340.4 all-reduce.1

commit v11 on v10

--- a/solution.py
+++ b/solution.py
@@ -420,14 +420,8 @@
         jnp.einsum("hqk,qhd->khd", grad_scores, queries, preferred_element_type=single_precision)
         * scale
     )
-    grad_keys_values = sum_context_halves(
-        jnp.stack(
-            [grad_keys_all.reshape(seq_len, heads_width), grad_vals.reshape(seq_len, heads_width)],
-            axis=1,
-        )
-    )
-    grad_keys = grad_keys_values[:, 0]
-    grad_values = grad_keys_values[:, 1]
+    grad_values = sum_context_halves(grad_vals.reshape(seq_len, heads_width))
+    grad_keys = sum_context_halves(grad_keys_all.reshape(seq_len, heads_width))
     grad_qn = rotate(grad_queries, cosine, sine, -1.0).reshape(seq_tok, heads_width)
     grad_kn = rotate(grad_keys.reshape(seq_tok, heads, head_dim), cosine, sine, -1.0).reshape(
         seq_tok, heads_width

time: 1050 us -> 1040 us (level)
  waiting for transfers between devices: 608 us -> 591 us
    ppermute x2 -> x3, waiting for transfers between devices: 23.6 us -> 10.4 us  [swap_context(): return lax.ppermute(values, 'context', [(0, 1), (1, 0)])]
    unnamed x113 -> x131, local copies, waits for them, and re-layouts: 25.1 us -> 28.2 us
  transfers between devices with their start and end apart: 18 -> 19, of which waited for: 14 -> 14; matrix products, arithmetic and copies ran while one was open for 15% -> 17% of each run, Pallas kernels for 1% -> 1%
where the time goes in v11:
time: 1040 us; the launch traced here: 1030 us
  waiting for transfers between devices  591 us (57%)
  matrix products  138 us (13%)
  blocking collectives  69.4 us (7%)
  other arithmetic  66.8 us (6%)
  local copies, waits for them, and re-layouts  52.3 us (5%)
  starting transfers between devices  51.5 us (5%)
  Pallas kernels  44.7 us (4%)
  between operations  15.3 us (1%)
    all_gather x1, waiting for transfers between devices, body(): lax.all_gather(jnp.concatenate([qkv_weight.transpose(1, 0, 2), out_weight...  226 us
    psum x1, waiting for transfers between devices, body(): summed = lax.psum(stacked.astype(bf16), all_axes)  159 us
    ppermute x7, waiting for transfers between devices, butterfly_sum(): received = lax.ppermute(values, axes, partner)  72 us
    all_to_all x1, blocking collectives, body(): lax.all_to_all(send.reshape(sources, local_experts * capacity, width), 'e...  69.4 us
    all_to_all x1, waiting for transfers between devices, body(): lax.all_to_all(source_major(grad_rows_in, sources, capacity), 'expert', s...  46.4 us
    all_to_all x1, waiting for transfers between devices, body(): lax.all_to_all(grad_send.reshape(sources, local_experts * capacity, width...  37 us
    all_to_all x1, waiting for transfers between devices, body(): lax.all_to_all(source_major(results, sources, capacity), 'expert', split_...  36.6 us
    unnamed x131, local copies, waits for them, and re-layouts  28.2 us
  transfers between devices with their start and end apart: 19, of which 14 were waited for; matrix products, arithmetic and copies ran while one was open for 17% of the time, Pallas kernels for 1%

profile of v11, /device:TPU:1, one launch (start us, length us, event | category | flops | bytes accessed | tf_op | source)
XLA Modules:
  0.0 1029.2 jit_solution(9574171739128403400)
XLA Ops:
  19.5 5.5 collective-permute-done
  26.5 226.2 %all-gather.2.cloned.1.call-done = bf16[2048,4,2048]{2,0,1:T(8,128)(2,1)} async-done(((bf16[16,4,2048]{2,0,1:T(8,128)(2,1)}), bf16[2048,4,2048]{2,0,1:T(8,128)(2,1)}) %all-gather.2.cloned.1.call-update) | async-done | bytes 33554448 | tf_op jit(solution)/shard_map/all_gather | solution.py:260
  252.7 17.7 %shard_map.215 = f32[3,256,2048]{2,1,0:T(8,128)} custom-call(bf16[256,2048]{1,0:T(8,128)(2,1)} %pad_maximum_fusion.inputs_ref, bf16[4,2048,2048]{2,1,0:T(8,128)(2,1)} %bitcast.243), custom_call_target="tpu_custom_call" | custom-call | flops 6442450944 | bytes 32505856 | tf_op jit(solution)/shard_map/pallas_call | solution.py:83
  282.8 3.5 convolution_convert_fusion.2
  286.4 6.5 multiply_reduce_fusion.9
  294.1 6.7 shard_map.216
  300.8 69.4 %all_to_all.20 = bf16[32,40,2048]{2,1,0:T(8,128)(2,1)} all-to-all(bf16[32,40,2048]{2,1,0:T(8,128)(2,1)} %bitcast.250), channel_id=1, replica_groups=mesh['dp'=2,'context'=2,'expert'=32] {'expert'}, dimensions={0} | all-to-all | bytes 10485760 | tf_op jit(solution)/shard_map/all_to_all | solution.py:320
  370.1 5.1 all-to-all-start.2
  375.2 16.8 %fusion.6 = f32[1,2,1280,1024]{3,2,1,0:T(8,128)S(1)} fusion(bf16[1280,2048,1]{1,0,2:T(8,128)(2,1)} %bitcast.245, bf16[1,2,2048,1024]{3,2,1,0:T(8,128)(2,1)} %param.24), kind=kOutput, calls=%fused_computation.12 | convolution fusion | flops 10737418240 | bytes 24117248 | tf_op jit(solution)/shard_map/lrd,lkdh->lkrh/dot_general | solution.py:328
  393.8 3.3 copy-done.4
  398.6 7.3 convolution_convert_fusion.1
  405.9 37.0 %all-to-all-done.2 = bf16[32,40,2048]{2,1,0:T(8,128)(2,1)} async-done(((bf16[32,40,2048]{2,1,0:T(8,128)(2,1)}), bf16[32,40,2048]{2,1,0:T(8,128)(2,1)}, u32[]{:S(2)}, u32[]{:S(2)}) %all-to-all-start.2) | async-done | bytes 5242912 | tf_op jit(solution)/shard_map/all_to_all | solution.py:348
  442.9 6.7 all-to-all-start.1
  449.6 13.1 %fusion.28 = (bf16[1,1,1280,1024]{3,2,1,0:T(8,128)(2,1)S(1)}, bf16[1,1,1280,1024]{3,2,1,0:T(8,128)(2,1)S(1)}) fusion(f32[1,2,1280,1024]{3,2,1,0:T(8,128)} %copy-done.4, bf16[1280,2048]{1,0:T(8,128)(2,1)} %bitcast.31, bf16[1,1024,2048]{2,1,0:T(8,128)(2,1)} %param.25), kind=kOutput, calls=%fused_computation.43 | convolution fusion | flops 5385748480 | bytes 25165824 | tf_op jit(solution)/shard_map/lrd,lhd->lrh/dot_general | solution.py:356
  465.1 15.1 %bitcast_convert_fusion = bf16[1280,2048]{1,0:T(8,128)(2,1)} fusion(bf16[1,2,2048,1024]{3,2,1,0:T(8,128)(2,1)} %param.24, bf16[1,1,1280,1024]{3,2,1,0:T(8,128)(2,1)S(1)} %get-tuple-element.71, bf16[1,1,1280,1024]{3,2,1,0:T(8,128)(2,1)S(1)} %get-tuple-element.70), kind=kOutput, calls=%fused_computation.2 | convolution fusion | flops 10742661120 | bytes 18874368 | tf_op jit(solution)/shard_map/lkrh,lkdh->lrd/dot_general | solution.py:368
  480.2 36.6 %all-to-all-done.1 = bf16[32,40,2048]{2,1,0:T(8,128)(2,1)} async-done(((bf16[32,40,2048]{2,1,0:T(8,128)(2,1)}), bf16[32,40,2048]{2,1,0:T(8,128)(2,1)}, u32[]{:S(2)}, u32[]{:S(2)}) %all-to-all-start.1) | async-done | bytes 5242912 | tf_op jit(solution)/shard_map/all_to_all | solution.py:336
  516.8 7.4 all-to-all-start.3
  530.4 10.2 shard_map.217
  543.0 46.4 %all-to-all-done.3 = bf16[32,40,2048]{2,1,0:T(8,128)(2,1)} async-done(((bf16[32,40,2048]{2,1,0:T(8,128)(2,1)}), bf16[32,40,2048]{2,1,0:T(8,128)(2,1)}, u32[]{:S(2)}, u32[]{:S(2)}) %all-to-all-start.3) | async-done | bytes 5242912 | tf_op jit(solution)/shard_map/all_to_all | solution.py:371
  590.0 10.1 shard_map.218
  605.0 4.7 fusion.30
  610.2 4.8 convolution_bitcast_fusion.1
  624.9 5.9 collective-permute-start.1
  630.9 3.6 fusion.52
  634.6 4.9 collective-permute-done.1
  643.3 3.3 multiply_subtract_fusion.1
  653.6 2.9 multiply_reduce_fusion.2
  660.5 14.4 %convolution_convert_fusion = bf16[4,2048,2048]{2,1,0:T(8,128)(2,1)} fusion(bf16[1,128,2048]{2,1,0:T(8,128)(2,1)S(1)} %copy-done.27, bf16[1,128,2048]{2,1,0:T(8,128)(2,1)S(1)} %copy-done.28, bf16[1,128,2048]{2,1,0:T(8,128)(2,1)S(1)} %copy-done.29, bf16[3,128,2048]{2,1,0:T(8,128)(2,1)S(1)} %maximum_bitcast_fusion.3), kind=kOutput, calls=%fused_computation.1 | convolution fusion | flops 4315938816 | bytes 36700160 | tf_op jit(solution)/shard_map/sta,stb->sab/dot_general | solution.py:452
  674.9 15.0 %fusion.23 = f32[2,1024,2048]{2,1,0:T(8,128)S(1)} fusion(bf16[1280,2048,1]{1,0,2:T(8,128)(2,1)} %bitcast.246, bf16[1,1,1280,1024]{3,2,1,0:T(8,128)(2,1)} %copy-done.58, bf16[1,1,1280,1024]{3,2,1,0:T(8,128)(2,1)} %copy-done.57), kind=kOutput, calls=%fused_computation.38 | convolution fusion | flops 10740039680 | bytes 27262976 | tf_op jit(solution)/shard_map/lrd,lkrh->lkdh/dot_general | solution.py:365
  692.7 8.3 collective-permute-start.10
  701.0 7.9 fusion.24
  709.2 3.0 copy-done.14
  712.2 3.1 collective-permute-start.12
  715.4 4.0 collective-permute-done.12
  719.4 3.7 convert_add_fusion
  728.4 10.8 %bitcast_add_fusion = f32[2,1024,1024]{1,2,0:T(8,128)} fusion(bf16[2,1024,1024]{1,2,0:T(8,128)(2,1)} %collective-permute-done.10, f32[2,1024,2048]{2,1,0:T(8,128)} %copy-done.9, s32[]{:T(128)S(6)} %select_n.102), kind=kLoop, calls=%fused_computation.4 | loop fusion | flops 4194304 | bytes 20971524 | tf_op jit(solution)/shard_map/add | solution.py:190
  740.5 17.2 %fusion.68 = (f32[2048]{0:T(1024)S(1)}, f32[128]{0:T(128)S(1)}, f32[128,2048]{1,0:T(8,128)}) fusion(bf16[1,128,2048]{2,1,0:T(8,128)(2,1)S(1)} %copy-done.2, f32[128]{0:T(128)S(1)} %copy-done.51, f32[2048]{0:T(1024)S(1)} %copy-done.41, bf16[2048,4,2048]{2,0,1:T(8,128)(2,1)} %all-gather.2.cloned.1.call-done, bf16[128,1,2048]{2,0,1:T(8,128)(2,1)S(1)} %fusion.88, ...), kind=kOutput, calls=%fused_computation.102 | convolution fusion | flops 4299945984 | bytes 36717576 | tf_op jit(solution)/shard_map/dot_general | solution.py:434
  760.6 11.3 %collective-permute-done.3 = f32[73728]{0:T(1024)S(1)} collective-permute-done((f32[73728]{0:T(1024)S(1)}, f32[73728]{0:T(1024)S(1)}, u32[]{:S(2)}, u32[]{:S(2)}) %collective-permute-start.3) | collective-permute-done | bytes 294944 | tf_op jit(solution)/shard_map/ppermute | solution.py:221
  773.3 8.2 collective-permute-done.4
  781.5 6.3 collective-permute-start.5
  787.8 9.7 collective-permute-done.5
  797.6 9.2 collective-permute-done.6
  807.6 3.6 add_bitcast_fusion.1
  811.3 5.6 collective-permute-done.7
  818.3 28.1 %collective-permute-done.8 = f32[73728]{0:T(1024)S(1)} collective-permute-done((f32[73728]{0:T(1024)S(1)}, f32[73728]{0:T(1024)S(1)}, u32[]{:S(2)}, u32[]{:S(2)}) %collective-permute-start.8) | collective-permute-done | bytes 294944 | tf_op jit(solution)/shard_map/ppermute | solution.py:221
  847.8 5.7 add_bitcast_fusion
  853.4 5.4 copy.103
  860.8 158.9 %all-reduce.2.cloned.1.call-done = bf16[4,2048,2048]{2,1,0:T(8,128)(2,1)} async-done(((bf16[4,2048,2048]{2,1,0:T(8,128)(2,1)}), bf16[4,2048,2048]{2,1,0:T(8,128)(2,1)}) %all-reduce.2.cloned.1.call-update) | async-done | bytes 33554448 | tf_op jit(solution)/shard_map/psum | solution.py:453
  (240 shorter events, 94.1 us)
Async XLA Ops:
  7.2 286.0 %copy-start = (bf16[2048,32]{0,1:T(8,128)(2,1)S(1)}, bf16[2048,32]{0,1:T(8,128)(2,1)}, u32[]{:S(2)}) copy-start(bf16[2048,32]{0,1:T(8,128)(2,1)} %param.23) | copy-start | bytes 393220
  7.2 17.8 %copy-start.2 = (bf16[1,128,2048]{2,1,0:T(8,128)(2,1)S(1)}, bf16[1,128,2048]{2,1,0:T(8,128)(2,1)}, u32[]{:S(2)}) copy-start(bf16[1,128,2048]{2,1,0:T(8,128)(2,1)} %param.13) | copy-start | bytes 1572868
  7.2 17.8 %copy-start.41 = (f32[2048]{0:T(1024)S(1)}, f32[2048]{0:T(1024)}, u32[]{:S(2)}) copy-start(f32[2048]{0:T(1024)} %param.17) | copy-start | bytes 24580
  7.2 9.4 copy-start.52
  7.2 245.4 %all-gather.2.cloned.1.call-start = ((), (), s32[]{:S(2)}) async-start(), calls=%async_computation.4 | async-start | bytes 33816576 | tf_op jit(solution)/shard_map/all_gather | solution.py:260
  10.3 15.1 %copy-start.49 = (f32[128]{0:T(128)}, f32[128]{0:T(128)S(1)}, u32[]{:S(2)}) copy-start(f32[128]{0:T(128)S(1)} %add_rsqrt_fusion.4) | copy-start | bytes 1540
  11.5 13.4 %collective-permute-start = (bf16[128,2048]{1,0:T(8,128)(2,1)S(1)}, bf16[128,2048]{1,0:T(8,128)(2,1)S(1)}, u32[]{:S(2)}, u32[]{:S(2)}) collective-permute-start(bf16[128,2048]{1,0:T(8,128)(2,1)S(1)} %fusion.62), channel_id=1, source_target_pairs={{0,32},{32,0},{1,33},{33,1},{2,34},{34,2},{3,35},{35,3},{4,36},{36... | collective-permute-start | bytes 1572872 | tf_op jit(solution)/shard_map/ppermute | solution.py:194
  16.0 254.4 %copy-start.40 = (s32[128,8]{1,0:T(8,128)}, s32[128,8]{1,0:T(8,128)S(1)}, u32[]{:S(2)}) copy-start(s32[128,8]{1,0:T(8,128)S(1)} %fusion.101.slot_ref) | copy-start | bytes 12292
  274.2 8.6 copy-start.22
  286.4 6.6 copy-start.31
  286.4 6.6 copy-start.42
  286.4 7.1 copy-start.46
  292.9 7.8 copy-start.7
  370.1 72.7 %all-to-all-start.2 = ((bf16[32,40,2048]{2,1,0:T(8,128)(2,1)}), bf16[32,40,2048]{2,1,0:T(8,128)(2,1)}, u32[]{:S(2)}, u32[]{:S(2)}) async-start(bf16[32,40,2048]{2,1,0:T(8,128)(2,1)} %bitcast.249), calls=%async_computation.2 | async-start | bytes 10485760 | tf_op jit(solution)/shard_map/all_to_all | solution.py:348
  392.1 5.0 copy-start.4
  392.1 6.5 copy-start.56
  442.9 73.9 %all-to-all-start.1 = ((bf16[32,40,2048]{2,1,0:T(8,128)(2,1)}), bf16[32,40,2048]{2,1,0:T(8,128)(2,1)}, u32[]{:S(2)}, u32[]{:S(2)}) async-start(bf16[32,40,2048]{2,1,0:T(8,128)(2,1)} %bitcast.248), calls=%async_computation.1 | async-start | bytes 10485760 | tf_op jit(solution)/shard_map/all_to_all | solution.py:336
  516.8 7.6 copy-start.50
  516.8 8.6 copy-start.48
  516.8 11.4 %copy-start.55 = (f32[128]{0:T(128)S(1)}, f32[128]{0:T(128)}, u32[]{:S(2)}) copy-start(f32[128]{0:T(128)} %get-tuple-element.60) | copy-start | bytes 1540
  516.8 11.4 %copy-start.30 = (f32[16,128,256]{2,1,0:T(8,128)S(1)}, f32[16,128,256]{2,1,0:T(8,128)}, u32[]{:S(2)}) copy-start(f32[16,128,256]{2,1,0:T(8,128)} %fusion.100) | copy-start | bytes 6291460
  516.8 72.6 %all-to-all-start.3 = ((bf16[32,40,2048]{2,1,0:T(8,128)(2,1)}), bf16[32,40,2048]{2,1,0:T(8,128)(2,1)}, u32[]{:S(2)}, u32[]{:S(2)}) async-start(bf16[32,40,2048]{2,1,0:T(8,128)(2,1)} %bitcast.247), calls=%async_computation.3 | async-start | bytes 10485760 | tf_op jit(solution)/shard_map/all_to_all | solution.py:371
  524.2 495.5 %all-reduce.2.cloned.1.call-start = ((), (), s32[]{:S(2)}) async-start(), calls=%async_computation.5 | async-start | bytes 67108864 | tf_op jit(solution)/shard_map/psum | solution.py:453
  590.0 10.1 copy-start.8
  605.0 5.0 copy-start.32
  610.0 4.9 copy-start.23
  617.2 3.1 copy-start.11
  624.9 14.6 %collective-permute-start.1 = (bf16[128,2048]{0,1:T(8,128)(2,1)}, bf16[128,2048]{0,1:T(8,128)(2,1)S(1)}, u32[]{:S(2)}, u32[]{:S(2)}) collective-permute-start(bf16[128,2048]{0,1:T(8,128)(2,1)} %bitcast.264), channel_id=1, source_target_pairs={{0,32},{32,0},{1,33},{33,1},{2,34},{34,2},{3,35},{35,3},{4,36},{36... | collective-permute-start | bytes 1572872 | tf_op jit(solution)/shard_map/ppermute | solution.py:194
  630.8 27.8 %collective-permute-start.2 = (bf16[128,2048]{1,0:T(8,128)(2,1)}, bf16[128,2048]{1,0:T(8,128)(2,1)}, u32[]{:S(2)}, u32[]{:S(2)}) collective-permute-start(bf16[128,2048]{1,0:T(8,128)(2,1)} %copy.113), channel_id=1, source_target_pairs={{0,32},{32,0},{1,33},{33,1},{2,34},{34,2},{3,35},{35,3},{4,36},{36... | collective-permute-start | bytes 1572872 | tf_op jit(solution)/shard_map/ppermute | solution.py:194
  639.6 3.6 copy-start.10
  689.9 19.0 %copy-start.9 = (f32[2,1024,2048]{2,1,0:T(8,128)}, f32[2,1024,2048]{2,1,0:T(8,128)S(1)}, u32[]{:S(2)}) copy-start(f32[2,1024,2048]{2,1,0:T(8,128)S(1)} %fusion.23) | copy-start | bytes 50331652
  689.9 11.1 %copy-start.26 = (bf16[1,1,1280,1024]{3,2,1,0:T(8,128)(2,1)S(1)}, bf16[1,1,1280,1024]{3,2,1,0:T(8,128)(2,1)}, u32[]{:S(2)}) copy-start(bf16[1,1,1280,1024]{3,2,1,0:T(8,128)(2,1)} %copy-done.25) | copy-start | bytes 7864324
  692.7 35.7 %collective-permute-start.10 = (bf16[2,1024,1024]{1,2,0:T(8,128)(2,1)}, bf16[2,1024,1024]{1,2,0:T(8,128)(2,1)}, u32[]{:S(2)}, u32[]{:S(2)}) collective-permute-start(bf16[2,1024,1024]{1,2,0:T(8,128)(2,1)} %fusion.18), channel_id=1, source_target_pairs={{0,64},{64,0},{1,65},{65,1},{2,66},{66,2},{3,67},{67,3},{4,68},{68... | collective-permute-start | bytes 12582920 | tf_op jit(solution)/shard_map/ppermute | solution.py:189
  708.9 3.3 copy-start.14
  712.2 7.2 collective-permute-start.12
  726.1 13.1 %copy-start.13 = (bf16[128,2048]{1,0:T(8,128)(2,1)S(1)}, bf16[128,2048]{1,0:T(8,128)(2,1)}, u32[]{:S(2)}) copy-start(bf16[128,2048]{1,0:T(8,128)(2,1)} %copy-done.12) | copy-start | bytes 1572868
  726.1 81.5 %collective-permute-start.13 = (bf16[1024,512]{1,0:T(8,128)(2,1)}, bf16[1024,512]{1,0:T(8,128)(2,1)}, u32[]{:S(2)}, u32[]{:S(2)}) collective-permute-start(bf16[1024,512]{1,0:T(8,128)(2,1)} %dynamic-slice_convert_fusion.3), channel_id=1, source_target_pairs={{0,32},{32,0},{1,33},{33,1},{2,34},{34,2},{3,35},{35,3},{4,36},{36... | collective-permute-start | bytes 3145736 | tf_op jit(solution)/shard_map/ppermute | solution.py:189
  757.7 14.2 %collective-permute-start.3 = (f32[73728]{0:T(1024)S(1)}, f32[73728]{0:T(1024)S(1)}, u32[]{:S(2)}, u32[]{:S(2)}) collective-permute-start(f32[73728]{0:T(1024)S(1)} %constant_dynamic-update-slice_fusion), channel_id=1, source_target_pairs={{0,1},{1,0},{2,3},{3,2},{4,5},{5,4},{6,7},{7,6},{8,9},{9,8},{10,11... | collective-permute-start | bytes 884744 | tf_op jit(solution)/shard_map/ppermute | solution.py:221
  760.4 87.4 %collective-permute-start.11 = (bf16[2,512,1024]{1,2,0:T(8,128)(2,1)S(1)}, bf16[2,512,1024]{1,2,0:T(8,128)(2,1)}, u32[]{:S(2)}, u32[]{:S(2)}) collective-permute-start(bf16[2,512,1024]{1,2,0:T(8,128)(2,1)S(1)} %dynamic-slice_convert_fusion.2), channel_id=1, source_target_pairs={{0,32},{32,0},{1,33},{33,1},{2,34},{34,2},{3,35},{35,3},{4,36},{36... | collective-permute-start | bytes 6291464 | tf_op jit(solution)/shard_map/ppermute | solution.py:189
  771.9 9.5 collective-permute-start.4
  781.5 16.0 %collective-permute-start.5 = (f32[73728]{0:T(1024)S(1)}, f32[73728]{0:T(1024)S(1)}, u32[]{:S(2)}, u32[]{:S(2)}) collective-permute-start(f32[73728]{0:T(1024)S(1)} %add.183), channel_id=1, source_target_pairs={{0,4},{1,5},{2,6},{3,7},{4,0},{5,1},{6,2},{7,3},{8,12},{9,13},{10,... | collective-permute-start | bytes 884744 | tf_op jit(solution)/shard_map/ppermute | solution.py:221
  797.5 9.3 collective-permute-start.6
  806.9 10.1 copy-start.20
  806.9 10.1 copy-start.37
  806.9 9.9 collective-permute-start.7
  816.8 29.6 %collective-permute-start.8 = (f32[73728]{0:T(1024)S(1)}, f32[73728]{0:T(1024)S(1)}, u32[]{:S(2)}, u32[]{:S(2)}) collective-permute-start(f32[73728]{0:T(1024)S(1)} %add.186), channel_id=1, source_target_pairs={{0,32},{1,33},{2,34},{3,35},{4,36},{5,37},{6,38},{7,39},{8,40},{9,... | collective-permute-start | bytes 884744 | tf_op jit(solution)/shard_map/ppermute | solution.py:221
  846.5 12.4 %collective-permute-start.9 = (f32[73728]{0:T(1024)S(1)}, f32[73728]{0:T(1024)S(1)}, u32[]{:S(2)}, u32[]{:S(2)}) collective-permute-start(f32[73728]{0:T(1024)S(1)} %add.187), channel_id=1, source_target_pairs={{0,64},{1,65},{2,66},{3,67},{4,68},{5,69},{6,70},{7,71},{8,72},{9,... | collective-permute-start | bytes 884744 | tf_op jit(solution)/shard_map/ppermute | solution.py:221
  858.8 163.3 %copy-start.1 = (bf16[2048,32]{0,1:T(8,128)(2,1)S(1)}, bf16[2048,32]{0,1:T(8,128)(2,1)}, u32[]{:S(2)}) copy-start(bf16[2048,32]{0,1:T(8,128)(2,1)} %param.23) | copy-start | bytes 393220
  (30 other events, 48.8 us)
Sparse Core Ops, SparseCore 0:
  10.4 242.2 all-gather.1
  675.1 344.5 all-reduce.1

commit v12 on v11

--- a/solution.py
+++ b/solution.py
@@ -77,7 +77,7 @@
     out_ref[0] = jnp.dot(inputs_ref[...], weights_ref[0], preferred_element_type=jnp.float32)
 
 
-def project(inputs, weights, blocks, tile=512):
+def project(inputs, weights, blocks, tile=1024):
     tokens, depth = inputs.shape
     columns = weights.shape[2]
     return pl.pallas_call(

time: 1040 us -> 1040 us (level)
  no operation moved by 1% of the time
where the time goes in v12:
time: 1040 us; the launch traced here: 1030 us
  waiting for transfers between devices  591 us (57%)
  matrix products  138 us (13%)
  blocking collectives  69.6 us (7%)
  other arithmetic  66.8 us (6%)
  local copies, waits for them, and re-layouts  52.4 us (5%)
  starting transfers between devices  51.2 us (5%)
  Pallas kernels  41.5 us (4%)
  between operations  15.3 us (1%)
    all_gather x1, waiting for transfers between devices, body(): lax.all_gather(jnp.concatenate([qkv_weight.transpose(1, 0, 2), out_weight...  226 us
    psum x1, waiting for transfers between devices, body(): summed = lax.psum(stacked.astype(bf16), all_axes)  159 us
    ppermute x7, waiting for transfers between devices, butterfly_sum(): received = lax.ppermute(values, axes, partner)  72 us
    all_to_all x1, blocking collectives, body(): lax.all_to_all(send.reshape(sources, local_experts * capacity, width), 'e...  69.6 us
    all_to_all x1, waiting for transfers between devices, body(): lax.all_to_all(source_major(grad_rows_in, sources, capacity), 'expert', s...  46.4 us
    all_to_all x1, waiting for transfers between devices, body(): lax.all_to_all(grad_send.reshape(sources, local_experts * capacity, width...  37 us
    all_to_all x1, waiting for transfers between devices, body(): lax.all_to_all(source_major(results, sources, capacity), 'expert', split_...  36.6 us
    unnamed x131, local copies, waits for them, and re-layouts  28.3 us
  transfers between devices with their start and end apart: 19, of which 14 were waited for; matrix products, arithmetic and copies ran while one was open for 17% of the time, Pallas kernels for 1%

profile of v12, /device:TPU:1, one launch (start us, length us, event | category | flops | bytes accessed | tf_op | source)
XLA Modules:
  0.0 1026.0 jit_solution(5764848209373138738)
XLA Ops:
  19.5 5.5 collective-permute-done
  26.5 226.2 %all-gather.2.cloned.1.call-done = bf16[2048,4,2048]{2,0,1:T(8,128)(2,1)} async-done(((bf16[16,4,2048]{2,0,1:T(8,128)(2,1)}), bf16[2048,4,2048]{2,0,1:T(8,128)(2,1)}) %all-gather.2.cloned.1.call-update) | async-done | bytes 33554448 | tf_op jit(solution)/shard_map/all_gather | solution.py:260
  252.7 14.5 %shard_map.215 = f32[3,256,2048]{2,1,0:T(8,128)} custom-call(bf16[256,2048]{1,0:T(8,128)(2,1)} %pad_maximum_fusion.inputs_ref, bf16[4,2048,2048]{2,1,0:T(8,128)(2,1)} %bitcast.243), custom_call_target="tpu_custom_call" | custom-call | flops 6442450944 | bytes 32505856 | tf_op jit(solution)/shard_map/pallas_call | solution.py:83
  279.6 3.5 convolution_convert_fusion.2
  283.2 6.5 multiply_reduce_fusion.9
  290.9 6.7 shard_map.216
  297.6 69.6 %all_to_all.20 = bf16[32,40,2048]{2,1,0:T(8,128)(2,1)} all-to-all(bf16[32,40,2048]{2,1,0:T(8,128)(2,1)} %bitcast.250), channel_id=1, replica_groups=mesh['dp'=2,'context'=2,'expert'=32] {'expert'}, dimensions={0} | all-to-all | bytes 10485760 | tf_op jit(solution)/shard_map/all_to_all | solution.py:320
  367.2 4.9 all-to-all-start.2
  372.1 16.8 %fusion.6 = f32[1,2,1280,1024]{3,2,1,0:T(8,128)S(1)} fusion(bf16[1280,2048,1]{1,0,2:T(8,128)(2,1)} %bitcast.245, bf16[1,2,2048,1024]{3,2,1,0:T(8,128)(2,1)} %param.24), kind=kOutput, calls=%fused_computation.12 | convolution fusion | flops 10737418240 | bytes 24117248 | tf_op jit(solution)/shard_map/lrd,lkdh->lkrh/dot_general | solution.py:328
  390.6 3.3 copy-done.4
  395.5 7.3 convolution_convert_fusion.1
  402.8 37.0 %all-to-all-done.2 = bf16[32,40,2048]{2,1,0:T(8,128)(2,1)} async-done(((bf16[32,40,2048]{2,1,0:T(8,128)(2,1)}), bf16[32,40,2048]{2,1,0:T(8,128)(2,1)}, u32[]{:S(2)}, u32[]{:S(2)}) %all-to-all-start.2) | async-done | bytes 5242912 | tf_op jit(solution)/shard_map/all_to_all | solution.py:348
  439.7 6.7 all-to-all-start.1
  446.5 13.1 %fusion.28 = (bf16[1,1,1280,1024]{3,2,1,0:T(8,128)(2,1)S(1)}, bf16[1,1,1280,1024]{3,2,1,0:T(8,128)(2,1)S(1)}) fusion(f32[1,2,1280,1024]{3,2,1,0:T(8,128)} %copy-done.4, bf16[1280,2048]{1,0:T(8,128)(2,1)} %bitcast.31, bf16[1,1024,2048]{2,1,0:T(8,128)(2,1)} %param.25), kind=kOutput, calls=%fused_computation.43 | convolution fusion | flops 5385748480 | bytes 25165824 | tf_op jit(solution)/shard_map/lrd,lhd->lrh/dot_general | solution.py:356
  461.9 15.1 %bitcast_convert_fusion = bf16[1280,2048]{1,0:T(8,128)(2,1)} fusion(bf16[1,2,2048,1024]{3,2,1,0:T(8,128)(2,1)} %param.24, bf16[1,1,1280,1024]{3,2,1,0:T(8,128)(2,1)S(1)} %get-tuple-element.71, bf16[1,1,1280,1024]{3,2,1,0:T(8,128)(2,1)S(1)} %get-tuple-element.70), kind=kOutput, calls=%fused_computation.2 | convolution fusion | flops 10742661120 | bytes 18874368 | tf_op jit(solution)/shard_map/lkrh,lkdh->lrd/dot_general | solution.py:368
  477.0 36.6 %all-to-all-done.1 = bf16[32,40,2048]{2,1,0:T(8,128)(2,1)} async-done(((bf16[32,40,2048]{2,1,0:T(8,128)(2,1)}), bf16[32,40,2048]{2,1,0:T(8,128)(2,1)}, u32[]{:S(2)}, u32[]{:S(2)}) %all-to-all-start.1) | async-done | bytes 5242912 | tf_op jit(solution)/shard_map/all_to_all | solution.py:336
  513.6 7.4 all-to-all-start.3
  527.3 10.2 shard_map.217
  539.8 46.4 %all-to-all-done.3 = bf16[32,40,2048]{2,1,0:T(8,128)(2,1)} async-done(((bf16[32,40,2048]{2,1,0:T(8,128)(2,1)}), bf16[32,40,2048]{2,1,0:T(8,128)(2,1)}, u32[]{:S(2)}, u32[]{:S(2)}) %all-to-all-start.3) | async-done | bytes 5242912 | tf_op jit(solution)/shard_map/all_to_all | solution.py:371
  586.8 10.1 shard_map.218
  601.8 4.7 fusion.30
  607.0 4.8 convolution_bitcast_fusion.1
  621.8 5.9 collective-permute-start.1
  627.7 3.6 fusion.52
  631.5 4.9 collective-permute-done.1
  640.1 3.3 multiply_subtract_fusion.1
  650.4 2.9 multiply_reduce_fusion.2
  657.3 14.4 %convolution_convert_fusion = bf16[4,2048,2048]{2,1,0:T(8,128)(2,1)} fusion(bf16[1,128,2048]{2,1,0:T(8,128)(2,1)S(1)} %copy-done.27, bf16[1,128,2048]{2,1,0:T(8,128)(2,1)S(1)} %copy-done.28, bf16[1,128,2048]{2,1,0:T(8,128)(2,1)S(1)} %copy-done.29, bf16[3,128,2048]{2,1,0:T(8,128)(2,1)S(1)} %maximum_bitcast_fusion.3), kind=kOutput, calls=%fused_computation.1 | convolution fusion | flops 4315938816 | bytes 36700160 | tf_op jit(solution)/shard_map/sta,stb->sab/dot_general | solution.py:452
  671.8 15.0 %fusion.23 = f32[2,1024,2048]{2,1,0:T(8,128)S(1)} fusion(bf16[1280,2048,1]{1,0,2:T(8,128)(2,1)} %bitcast.246, bf16[1,1,1280,1024]{3,2,1,0:T(8,128)(2,1)} %copy-done.58, bf16[1,1,1280,1024]{3,2,1,0:T(8,128)(2,1)} %copy-done.57), kind=kOutput, calls=%fused_computation.38 | convolution fusion | flops 10740039680 | bytes 27262976 | tf_op jit(solution)/shard_map/lrd,lkrh->lkdh/dot_general | solution.py:365
  689.6 8.3 collective-permute-start.10
  697.8 7.9 fusion.24
  706.1 3.0 copy-done.14
  709.0 3.1 collective-permute-start.12
  712.2 4.0 collective-permute-done.12
  716.2 3.7 convert_add_fusion
  725.3 10.8 %bitcast_add_fusion = f32[2,1024,1024]{1,2,0:T(8,128)} fusion(bf16[2,1024,1024]{1,2,0:T(8,128)(2,1)} %collective-permute-done.10, f32[2,1024,2048]{2,1,0:T(8,128)} %copy-done.9, s32[]{:T(128)S(6)} %select_n.102), kind=kLoop, calls=%fused_computation.4 | loop fusion | flops 4194304 | bytes 20971524 | tf_op jit(solution)/shard_map/add | solution.py:190
  737.3 17.2 %fusion.68 = (f32[2048]{0:T(1024)S(1)}, f32[128]{0:T(128)S(1)}, f32[128,2048]{1,0:T(8,128)}) fusion(bf16[1,128,2048]{2,1,0:T(8,128)(2,1)S(1)} %copy-done.2, f32[128]{0:T(128)S(1)} %copy-done.51, f32[2048]{0:T(1024)S(1)} %copy-done.41, bf16[2048,4,2048]{2,0,1:T(8,128)(2,1)} %all-gather.2.cloned.1.call-done, bf16[128,1,2048]{2,0,1:T(8,128)(2,1)S(1)} %fusion.88, ...), kind=kOutput, calls=%fused_computation.102 | convolution fusion | flops 4299945984 | bytes 36717576 | tf_op jit(solution)/shard_map/dot_general | solution.py:434
  757.5 11.3 %collective-permute-done.3 = f32[73728]{0:T(1024)S(1)} collective-permute-done((f32[73728]{0:T(1024)S(1)}, f32[73728]{0:T(1024)S(1)}, u32[]{:S(2)}, u32[]{:S(2)}) %collective-permute-start.3) | collective-permute-done | bytes 294944 | tf_op jit(solution)/shard_map/ppermute | solution.py:221
  770.2 8.2 collective-permute-done.4
  778.4 6.3 collective-permute-start.5
  784.7 9.7 collective-permute-done.5
  794.5 9.2 collective-permute-done.6
  804.5 3.6 add_bitcast_fusion.1
  808.1 5.6 collective-permute-done.7
  815.2 28.1 %collective-permute-done.8 = f32[73728]{0:T(1024)S(1)} collective-permute-done((f32[73728]{0:T(1024)S(1)}, f32[73728]{0:T(1024)S(1)}, u32[]{:S(2)}, u32[]{:S(2)}) %collective-permute-start.8) | collective-permute-done | bytes 294944 | tf_op jit(solution)/shard_map/ppermute | solution.py:221
  844.6 5.7 add_bitcast_fusion
  850.3 5.4 copy.103
  857.6 158.9 %all-reduce.2.cloned.1.call-done = bf16[4,2048,2048]{2,1,0:T(8,128)(2,1)} async-done(((bf16[4,2048,2048]{2,1,0:T(8,128)(2,1)}), bf16[4,2048,2048]{2,1,0:T(8,128)(2,1)}) %all-reduce.2.cloned.1.call-update) | async-done | bytes 33554448 | tf_op jit(solution)/shard_map/psum | solution.py:453
  (240 shorter events, 94.1 us)
Async XLA Ops:
  7.2 282.8 %copy-start = (bf16[2048,32]{0,1:T(8,128)(2,1)S(1)}, bf16[2048,32]{0,1:T(8,128)(2,1)}, u32[]{:S(2)}) copy-start(bf16[2048,32]{0,1:T(8,128)(2,1)} %param.23) | copy-start | bytes 393220
  7.2 17.8 %copy-start.2 = (bf16[1,128,2048]{2,1,0:T(8,128)(2,1)S(1)}, bf16[1,128,2048]{2,1,0:T(8,128)(2,1)}, u32[]{:S(2)}) copy-start(bf16[1,128,2048]{2,1,0:T(8,128)(2,1)} %param.13) | copy-start | bytes 1572868
  7.2 17.8 %copy-start.41 = (f32[2048]{0:T(1024)S(1)}, f32[2048]{0:T(1024)}, u32[]{:S(2)}) copy-start(f32[2048]{0:T(1024)} %param.17) | copy-start | bytes 24580
  7.2 9.4 copy-start.52
  7.2 245.4 %all-gather.2.cloned.1.call-start = ((), (), s32[]{:S(2)}) async-start(), calls=%async_computation.4 | async-start | bytes 33816576 | tf_op jit(solution)/shard_map/all_gather | solution.py:260
  10.3 15.1 %copy-start.49 = (f32[128]{0:T(128)}, f32[128]{0:T(128)S(1)}, u32[]{:S(2)}) copy-start(f32[128]{0:T(128)S(1)} %add_rsqrt_fusion.4) | copy-start | bytes 1540
  11.5 13.4 %collective-permute-start = (bf16[128,2048]{1,0:T(8,128)(2,1)S(1)}, bf16[128,2048]{1,0:T(8,128)(2,1)S(1)}, u32[]{:S(2)}, u32[]{:S(2)}) collective-permute-start(bf16[128,2048]{1,0:T(8,128)(2,1)S(1)} %fusion.62), channel_id=1, source_target_pairs={{0,32},{32,0},{1,33},{33,1},{2,34},{34,2},{3,35},{35,3},{4,36},{36... | collective-permute-start | bytes 1572872 | tf_op jit(solution)/shard_map/ppermute | solution.py:194
  16.0 251.2 %copy-start.40 = (s32[128,8]{1,0:T(8,128)}, s32[128,8]{1,0:T(8,128)S(1)}, u32[]{:S(2)}) copy-start(s32[128,8]{1,0:T(8,128)S(1)} %fusion.101.slot_ref) | copy-start | bytes 12292
  271.1 8.6 copy-start.22
  283.2 6.6 copy-start.31
  283.2 6.6 copy-start.42
  283.2 7.1 copy-start.46
  289.8 7.8 copy-start.7
  367.2 72.5 %all-to-all-start.2 = ((bf16[32,40,2048]{2,1,0:T(8,128)(2,1)}), bf16[32,40,2048]{2,1,0:T(8,128)(2,1)}, u32[]{:S(2)}, u32[]{:S(2)}) async-start(bf16[32,40,2048]{2,1,0:T(8,128)(2,1)} %bitcast.249), calls=%async_computation.2 | async-start | bytes 10485760 | tf_op jit(solution)/shard_map/all_to_all | solution.py:348
  388.9 5.0 copy-start.4
  388.9 6.5 copy-start.56
  439.7 73.9 %all-to-all-start.1 = ((bf16[32,40,2048]{2,1,0:T(8,128)(2,1)}), bf16[32,40,2048]{2,1,0:T(8,128)(2,1)}, u32[]{:S(2)}, u32[]{:S(2)}) async-start(bf16[32,40,2048]{2,1,0:T(8,128)(2,1)} %bitcast.248), calls=%async_computation.1 | async-start | bytes 10485760 | tf_op jit(solution)/shard_map/all_to_all | solution.py:336
  513.6 7.6 copy-start.50
  513.6 8.6 copy-start.48
  513.6 11.4 %copy-start.55 = (f32[128]{0:T(128)S(1)}, f32[128]{0:T(128)}, u32[]{:S(2)}) copy-start(f32[128]{0:T(128)} %get-tuple-element.60) | copy-start | bytes 1540
  513.6 11.4 %copy-start.30 = (f32[16,128,256]{2,1,0:T(8,128)S(1)}, f32[16,128,256]{2,1,0:T(8,128)}, u32[]{:S(2)}) copy-start(f32[16,128,256]{2,1,0:T(8,128)} %fusion.100) | copy-start | bytes 6291460
  513.6 72.6 %all-to-all-start.3 = ((bf16[32,40,2048]{2,1,0:T(8,128)(2,1)}), bf16[32,40,2048]{2,1,0:T(8,128)(2,1)}, u32[]{:S(2)}, u32[]{:S(2)}) async-start(bf16[32,40,2048]{2,1,0:T(8,128)(2,1)} %bitcast.247), calls=%async_computation.3 | async-start | bytes 10485760 | tf_op jit(solution)/shard_map/all_to_all | solution.py:371
  521.0 495.5 %all-reduce.2.cloned.1.call-start = ((), (), s32[]{:S(2)}) async-start(), calls=%async_computation.5 | async-start | bytes 67108864 | tf_op jit(solution)/shard_map/psum | solution.py:453
  586.8 10.1 copy-start.8
  601.8 5.0 copy-start.32
  606.8 4.9 copy-start.23
  614.0 3.1 copy-start.11
  621.8 14.6 %collective-permute-start.1 = (bf16[128,2048]{0,1:T(8,128)(2,1)}, bf16[128,2048]{0,1:T(8,128)(2,1)S(1)}, u32[]{:S(2)}, u32[]{:S(2)}) collective-permute-start(bf16[128,2048]{0,1:T(8,128)(2,1)} %bitcast.264), channel_id=1, source_target_pairs={{0,32},{32,0},{1,33},{33,1},{2,34},{34,2},{3,35},{35,3},{4,36},{36... | collective-permute-start | bytes 1572872 | tf_op jit(solution)/shard_map/ppermute | solution.py:194
  627.7 27.8 %collective-permute-start.2 = (bf16[128,2048]{1,0:T(8,128)(2,1)}, bf16[128,2048]{1,0:T(8,128)(2,1)}, u32[]{:S(2)}, u32[]{:S(2)}) collective-permute-start(bf16[128,2048]{1,0:T(8,128)(2,1)} %copy.113), channel_id=1, source_target_pairs={{0,32},{32,0},{1,33},{33,1},{2,34},{34,2},{3,35},{35,3},{4,36},{36... | collective-permute-start | bytes 1572872 | tf_op jit(solution)/shard_map/ppermute | solution.py:194
  636.5 3.6 copy-start.10
  686.8 19.0 %copy-start.9 = (f32[2,1024,2048]{2,1,0:T(8,128)}, f32[2,1024,2048]{2,1,0:T(8,128)S(1)}, u32[]{:S(2)}) copy-start(f32[2,1024,2048]{2,1,0:T(8,128)S(1)} %fusion.23) | copy-start | bytes 50331652
  686.8 11.1 %copy-start.26 = (bf16[1,1,1280,1024]{3,2,1,0:T(8,128)(2,1)S(1)}, bf16[1,1,1280,1024]{3,2,1,0:T(8,128)(2,1)}, u32[]{:S(2)}) copy-start(bf16[1,1,1280,1024]{3,2,1,0:T(8,128)(2,1)} %copy-done.25) | copy-start | bytes 7864324
  689.6 35.7 %collective-permute-start.10 = (bf16[2,1024,1024]{1,2,0:T(8,128)(2,1)}, bf16[2,1024,1024]{1,2,0:T(8,128)(2,1)}, u32[]{:S(2)}, u32[]{:S(2)}) collective-permute-start(bf16[2,1024,1024]{1,2,0:T(8,128)(2,1)} %fusion.18), channel_id=1, source_target_pairs={{0,64},{64,0},{1,65},{65,1},{2,66},{66,2},{3,67},{67,3},{4,68},{68... | collective-permute-start | bytes 12582920 | tf_op jit(solution)/shard_map/ppermute | solution.py:189
  705.7 3.3 copy-start.14
  709.0 7.2 collective-permute-start.12
  723.0 13.1 %copy-start.13 = (bf16[128,2048]{1,0:T(8,128)(2,1)S(1)}, bf16[128,2048]{1,0:T(8,128)(2,1)}, u32[]{:S(2)}) copy-start(bf16[128,2048]{1,0:T(8,128)(2,1)} %copy-done.12) | copy-start | bytes 1572868
  723.0 81.5 %collective-permute-start.13 = (bf16[1024,512]{1,0:T(8,128)(2,1)}, bf16[1024,512]{1,0:T(8,128)(2,1)}, u32[]{:S(2)}, u32[]{:S(2)}) collective-permute-start(bf16[1024,512]{1,0:T(8,128)(2,1)} %dynamic-slice_convert_fusion.3), channel_id=1, source_target_pairs={{0,32},{32,0},{1,33},{33,1},{2,34},{34,2},{3,35},{35,3},{4,36},{36... | collective-permute-start | bytes 3145736 | tf_op jit(solution)/shard_map/ppermute | solution.py:189
  754.5 14.2 %collective-permute-start.3 = (f32[73728]{0:T(1024)S(1)}, f32[73728]{0:T(1024)S(1)}, u32[]{:S(2)}, u32[]{:S(2)}) collective-permute-start(f32[73728]{0:T(1024)S(1)} %constant_dynamic-update-slice_fusion), channel_id=1, source_target_pairs={{0,1},{1,0},{2,3},{3,2},{4,5},{5,4},{6,7},{7,6},{8,9},{9,8},{10,11... | collective-permute-start | bytes 884744 | tf_op jit(solution)/shard_map/ppermute | solution.py:221
  757.2 87.4 %collective-permute-start.11 = (bf16[2,512,1024]{1,2,0:T(8,128)(2,1)S(1)}, bf16[2,512,1024]{1,2,0:T(8,128)(2,1)}, u32[]{:S(2)}, u32[]{:S(2)}) collective-permute-start(bf16[2,512,1024]{1,2,0:T(8,128)(2,1)S(1)} %dynamic-slice_convert_fusion.2), channel_id=1, source_target_pairs={{0,32},{32,0},{1,33},{33,1},{2,34},{34,2},{3,35},{35,3},{4,36},{36... | collective-permute-start | bytes 6291464 | tf_op jit(solution)/shard_map/ppermute | solution.py:189
  768.8 9.5 collective-permute-start.4
  778.4 16.0 %collective-permute-start.5 = (f32[73728]{0:T(1024)S(1)}, f32[73728]{0:T(1024)S(1)}, u32[]{:S(2)}, u32[]{:S(2)}) collective-permute-start(f32[73728]{0:T(1024)S(1)} %add.183), channel_id=1, source_target_pairs={{0,4},{1,5},{2,6},{3,7},{4,0},{5,1},{6,2},{7,3},{8,12},{9,13},{10,... | collective-permute-start | bytes 884744 | tf_op jit(solution)/shard_map/ppermute | solution.py:221
  794.4 9.3 collective-permute-start.6
  803.7 10.1 copy-start.20
  803.7 10.1 copy-start.37
  803.8 9.9 collective-permute-start.7
  813.7 29.6 %collective-permute-start.8 = (f32[73728]{0:T(1024)S(1)}, f32[73728]{0:T(1024)S(1)}, u32[]{:S(2)}, u32[]{:S(2)}) collective-permute-start(f32[73728]{0:T(1024)S(1)} %add.186), channel_id=1, source_target_pairs={{0,32},{1,33},{2,34},{3,35},{4,36},{5,37},{6,38},{7,39},{8,40},{9,... | collective-permute-start | bytes 884744 | tf_op jit(solution)/shard_map/ppermute | solution.py:221
  843.3 12.4 %collective-permute-start.9 = (f32[73728]{0:T(1024)S(1)}, f32[73728]{0:T(1024)S(1)}, u32[]{:S(2)}, u32[]{:S(2)}) collective-permute-start(f32[73728]{0:T(1024)S(1)} %add.187), channel_id=1, source_target_pairs={{0,64},{1,65},{2,66},{3,67},{4,68},{5,69},{6,70},{7,71},{8,72},{9,... | collective-permute-start | bytes 884744 | tf_op jit(solution)/shard_map/ppermute | solution.py:221
  855.7 163.3 %copy-start.1 = (bf16[2048,32]{0,1:T(8,128)(2,1)S(1)}, bf16[2048,32]{0,1:T(8,128)(2,1)}, u32[]{:S(2)}) copy-start(bf16[2048,32]{0,1:T(8,128)(2,1)} %param.23) | copy-start | bytes 393220
  (30 other events, 48.7 us)
Sparse Core Ops, SparseCore 0:
  10.4 242.2 all-gather.1
  671.9 344.5 all-reduce.1

commit v13 on v12

--- a/solution.py
+++ b/solution.py
@@ -146,20 +146,25 @@
 def _combine_kernel(with_dots, slot_ref, weight_ref, table_ref, base_ref, other_ref, out_ref, dots_ref):
     tokens, top = slot_ref.shape
     count = table_ref.shape[0]
+    column = lax.broadcasted_iota(jnp.int32, (tokens, count), 1)
+    if not with_dots:
+        hit = slot_ref[:, 0:1] == column
+        for k in range(1, top):
+            hit = hit | (slot_ref[:, k : k + 1] == column)
+        out_ref[...] = base_ref[...] + jnp.dot(
+            hit.astype(jnp.bfloat16), table_ref[...], preferred_element_type=jnp.float32
+        )
+        dots_ref[...] = jnp.zeros_like(dots_ref)
+        return
     total = base_ref[...]
     for k in range(top):
-        pick = (
-            slot_ref[:, k : k + 1] == lax.broadcasted_iota(jnp.int32, (tokens, count), 1)
-        ).astype(jnp.bfloat16)
+        pick = (slot_ref[:, k : k + 1] == column).astype(jnp.bfloat16)
         row = jnp.dot(pick, table_ref[...], preferred_element_type=jnp.float32)
         total = total + weight_ref[:, k : k + 1] * row
-        if with_dots:
-            dots_ref[:, k : k + 1] = jnp.sum(
-                other_ref[...].astype(jnp.float32) * row, axis=1, keepdims=True
-            )
+        dots_ref[:, k : k + 1] = jnp.sum(
+            other_ref[...].astype(jnp.float32) * row, axis=1, keepdims=True
+        )
     out_ref[...] = total
-    if not with_dots:
-        dots_ref[...] = jnp.zeros_like(dots_ref)
 
 
 def combine(slots, weights, table, base, other, with_dots):

time: 1040 us -> 1030 us (level)
  no operation moved by 1% of the time
where the time goes in v13:
time: 1030 us; the launch traced here: 1020 us
  waiting for transfers between devices  593 us (58%)
  matrix products  138 us (13%)
  blocking collectives  69.6 us (7%)
  other arithmetic  67 us (7%)
  local copies, waits for them, and re-layouts  52.4 us (5%)
  starting transfers between devices  49.3 us (5%)
  Pallas kernels  37 us (4%)
  between operations  15.5 us (2%)
    all_gather x1, waiting for transfers between devices, body(): lax.all_gather(jnp.concatenate([qkv_weight.transpose(1, 0, 2), out_weight...  226 us
    psum x1, waiting for transfers between devices, body(): summed = lax.psum(stacked.astype(bf16), all_axes)  160 us
    ppermute x7, waiting for transfers between devices, butterfly_sum(): received = lax.ppermute(values, axes, partner)  73.4 us
    all_to_all x1, blocking collectives, body(): lax.all_to_all(send.reshape(sources, local_experts * capacity, width), 'e...  69.6 us
    all_to_all x1, waiting for transfers between devices, body(): lax.all_to_all(source_major(grad_rows_in, sources, capacity), 'expert', s...  46.2 us
    all_to_all x1, waiting for transfers between devices, body(): lax.all_to_all(grad_send.reshape(sources, local_experts * capacity, width...  36.9 us
    all_to_all x1, waiting for transfers between devices, body(): lax.all_to_all(source_major(results, sources, capacity), 'expert', split_...  36.6 us
    unnamed x131, local copies, waits for them, and re-layouts  28.3 us
  transfers between devices with their start and end apart: 19, of which 14 were waited for; matrix products, arithmetic and copies ran while one was open for 17% of the time, Pallas kernels for 1%

profile of v13, /device:TPU:1, one launch (start us, length us, event | category | flops | bytes accessed | tf_op | source)
XLA Modules:
  0.0 1022.0 jit_solution(10535065334744721123)
XLA Ops:
  19.5 5.5 collective-permute-done
  26.5 226.2 %all-gather.2.cloned.1.call-done = bf16[2048,4,2048]{2,0,1:T(8,128)(2,1)} async-done(((bf16[16,4,2048]{2,0,1:T(8,128)(2,1)}), bf16[2048,4,2048]{2,0,1:T(8,128)(2,1)}) %all-gather.2.cloned.1.call-update) | async-done | bytes 33554448 | tf_op jit(solution)/shard_map/all_gather | solution.py:265
  252.7 14.5 %shard_map.215 = f32[3,256,2048]{2,1,0:T(8,128)} custom-call(bf16[256,2048]{1,0:T(8,128)(2,1)} %pad_maximum_fusion.inputs_ref, bf16[4,2048,2048]{2,1,0:T(8,128)(2,1)} %bitcast.243), custom_call_target="tpu_custom_call" | custom-call | flops 6442450944 | bytes 32505856 | tf_op jit(solution)/shard_map/pallas_call | solution.py:83
  279.6 3.5 convolution_convert_fusion.2
  283.2 6.5 multiply_reduce_fusion.9
  290.9 6.7 shard_map.216
  297.6 69.6 %all_to_all.20 = bf16[32,40,2048]{2,1,0:T(8,128)(2,1)} all-to-all(bf16[32,40,2048]{2,1,0:T(8,128)(2,1)} %bitcast.250), channel_id=1, replica_groups=mesh['dp'=2,'context'=2,'expert'=32] {'expert'}, dimensions={0} | all-to-all | bytes 10485760 | tf_op jit(solution)/shard_map/all_to_all | solution.py:325
  367.2 4.9 all-to-all-start.2
  372.0 16.9 %fusion.6 = f32[1,2,1280,1024]{3,2,1,0:T(8,128)S(1)} fusion(bf16[1280,2048,1]{1,0,2:T(8,128)(2,1)} %bitcast.245, bf16[1,2,2048,1024]{3,2,1,0:T(8,128)(2,1)} %param.24), kind=kOutput, calls=%fused_computation.12 | convolution fusion | flops 10737418240 | bytes 24117248 | tf_op jit(solution)/shard_map/lrd,lkdh->lkrh/dot_general | solution.py:333
  390.6 3.3 copy-done.4
  395.4 7.3 convolution_convert_fusion.1
  402.7 36.9 %all-to-all-done.2 = bf16[32,40,2048]{2,1,0:T(8,128)(2,1)} async-done(((bf16[32,40,2048]{2,1,0:T(8,128)(2,1)}), bf16[32,40,2048]{2,1,0:T(8,128)(2,1)}, u32[]{:S(2)}, u32[]{:S(2)}) %all-to-all-start.2) | async-done | bytes 5242912 | tf_op jit(solution)/shard_map/all_to_all | solution.py:353
  439.7 6.5 all-to-all-start.1
  446.2 13.1 %fusion.28 = (bf16[1,1,1280,1024]{3,2,1,0:T(8,128)(2,1)S(1)}, bf16[1,1,1280,1024]{3,2,1,0:T(8,128)(2,1)S(1)}) fusion(f32[1,2,1280,1024]{3,2,1,0:T(8,128)} %copy-done.4, bf16[1280,2048]{1,0:T(8,128)(2,1)} %bitcast.31, bf16[1,1024,2048]{2,1,0:T(8,128)(2,1)} %param.25), kind=kOutput, calls=%fused_computation.43 | convolution fusion | flops 5385748480 | bytes 25165824 | tf_op jit(solution)/shard_map/lrd,lhd->lrh/dot_general | solution.py:361
  461.7 15.1 %bitcast_convert_fusion = bf16[1280,2048]{1,0:T(8,128)(2,1)} fusion(bf16[1,2,2048,1024]{3,2,1,0:T(8,128)(2,1)} %param.24, bf16[1,1,1280,1024]{3,2,1,0:T(8,128)(2,1)S(1)} %get-tuple-element.71, bf16[1,1,1280,1024]{3,2,1,0:T(8,128)(2,1)S(1)} %get-tuple-element.70), kind=kOutput, calls=%fused_computation.2 | convolution fusion | flops 10742661120 | bytes 18874368 | tf_op jit(solution)/shard_map/lkrh,lkdh->lrd/dot_general | solution.py:373
  476.8 36.6 %all-to-all-done.1 = bf16[32,40,2048]{2,1,0:T(8,128)(2,1)} async-done(((bf16[32,40,2048]{2,1,0:T(8,128)(2,1)}), bf16[32,40,2048]{2,1,0:T(8,128)(2,1)}, u32[]{:S(2)}, u32[]{:S(2)}) %all-to-all-start.1) | async-done | bytes 5242912 | tf_op jit(solution)/shard_map/all_to_all | solution.py:341
  513.4 7.4 all-to-all-start.3
  527.3 10.2 shard_map.217
  539.8 46.2 %all-to-all-done.3 = bf16[32,40,2048]{2,1,0:T(8,128)(2,1)} async-done(((bf16[32,40,2048]{2,1,0:T(8,128)(2,1)}), bf16[32,40,2048]{2,1,0:T(8,128)(2,1)}, u32[]{:S(2)}, u32[]{:S(2)}) %all-to-all-start.3) | async-done | bytes 5242912 | tf_op jit(solution)/shard_map/all_to_all | solution.py:376
  586.6 5.6 shard_map.218
  597.1 4.7 fusion.30
  602.3 4.9 convolution_bitcast_fusion.1
  617.2 5.9 collective-permute-start.1
  623.1 3.6 fusion.52
  626.9 4.9 collective-permute-done.1
  635.5 3.3 multiply_subtract_fusion.1
  645.8 2.9 multiply_reduce_fusion.2
  652.7 14.5 %convolution_convert_fusion = bf16[4,2048,2048]{2,1,0:T(8,128)(2,1)} fusion(bf16[1,128,2048]{2,1,0:T(8,128)(2,1)S(1)} %copy-done.27, bf16[1,128,2048]{2,1,0:T(8,128)(2,1)S(1)} %copy-done.28, bf16[1,128,2048]{2,1,0:T(8,128)(2,1)S(1)} %copy-done.29, bf16[3,128,2048]{2,1,0:T(8,128)(2,1)S(1)} %maximum_bitcast_fusion.3), kind=kOutput, calls=%fused_computation.1 | convolution fusion | flops 4315938816 | bytes 36700160 | tf_op jit(solution)/shard_map/sta,stb->sab/dot_general | solution.py:457
  667.2 15.0 %fusion.23 = f32[2,1024,2048]{2,1,0:T(8,128)S(1)} fusion(bf16[1280,2048,1]{1,0,2:T(8,128)(2,1)} %bitcast.246, bf16[1,1,1280,1024]{3,2,1,0:T(8,128)(2,1)} %copy-done.58, bf16[1,1,1280,1024]{3,2,1,0:T(8,128)(2,1)} %copy-done.57), kind=kOutput, calls=%fused_computation.38 | convolution fusion | flops 10740039680 | bytes 27262976 | tf_op jit(solution)/shard_map/lrd,lkrh->lkdh/dot_general | solution.py:370
  685.0 8.2 collective-permute-start.10
  693.3 7.9 fusion.24
  701.5 3.0 copy-done.14
  704.5 3.1 collective-permute-start.12
  707.7 4.0 collective-permute-done.12
  711.7 3.7 convert_add_fusion
  720.8 10.8 %bitcast_add_fusion = f32[2,1024,1024]{1,2,0:T(8,128)} fusion(bf16[2,1024,1024]{1,2,0:T(8,128)(2,1)} %collective-permute-done.10, f32[2,1024,2048]{2,1,0:T(8,128)} %copy-done.9, s32[]{:T(128)S(6)} %select_n.102), kind=kLoop, calls=%fused_computation.4 | loop fusion | flops 4194304 | bytes 20971524 | tf_op jit(solution)/shard_map/add | solution.py:195
  732.9 17.2 %fusion.68 = (f32[2048]{0:T(1024)S(1)}, f32[128]{0:T(128)S(1)}, f32[128,2048]{1,0:T(8,128)}) fusion(bf16[1,128,2048]{2,1,0:T(8,128)(2,1)S(1)} %copy-done.2, f32[128]{0:T(128)S(1)} %copy-done.51, f32[2048]{0:T(1024)S(1)} %copy-done.41, bf16[2048,4,2048]{2,0,1:T(8,128)(2,1)} %all-gather.2.cloned.1.call-done, bf16[128,1,2048]{2,0,1:T(8,128)(2,1)S(1)} %fusion.88, ...), kind=kOutput, calls=%fused_computation.102 | convolution fusion | flops 4299945984 | bytes 36717576 | tf_op jit(solution)/shard_map/dot_general | solution.py:439
  753.1 11.5 %collective-permute-done.3 = f32[73728]{0:T(1024)S(1)} collective-permute-done((f32[73728]{0:T(1024)S(1)}, f32[73728]{0:T(1024)S(1)}, u32[]{:S(2)}, u32[]{:S(2)}) %collective-permute-start.3) | collective-permute-done | bytes 294944 | tf_op jit(solution)/shard_map/ppermute | solution.py:226
  765.6 8.9 collective-permute-done.4
  774.5 5.2 collective-permute-start.5
  779.7 9.7 collective-permute-done.5
  789.5 10.0 collective-permute-done.6
  799.7 3.7 add_bitcast_fusion.1
  803.5 5.3 collective-permute-done.7
  810.3 27.9 %collective-permute-done.8 = f32[73728]{0:T(1024)S(1)} collective-permute-done((f32[73728]{0:T(1024)S(1)}, f32[73728]{0:T(1024)S(1)}, u32[]{:S(2)}, u32[]{:S(2)}) %collective-permute-start.8) | collective-permute-done | bytes 294944 | tf_op jit(solution)/shard_map/ppermute | solution.py:226
  839.6 5.7 add_bitcast_fusion
  845.2 5.5 copy.103
  852.7 159.7 %all-reduce.2.cloned.1.call-done = bf16[4,2048,2048]{2,1,0:T(8,128)(2,1)} async-done(((bf16[4,2048,2048]{2,1,0:T(8,128)(2,1)}), bf16[4,2048,2048]{2,1,0:T(8,128)(2,1)}) %all-reduce.2.cloned.1.call-update) | async-done | bytes 33554448 | tf_op jit(solution)/shard_map/psum | solution.py:458
  (240 shorter events, 93.4 us)
Async XLA Ops:
  7.2 282.8 %copy-start = (bf16[2048,32]{0,1:T(8,128)(2,1)S(1)}, bf16[2048,32]{0,1:T(8,128)(2,1)}, u32[]{:S(2)}) copy-start(bf16[2048,32]{0,1:T(8,128)(2,1)} %param.23) | copy-start | bytes 393220
  7.2 17.8 %copy-start.2 = (bf16[1,128,2048]{2,1,0:T(8,128)(2,1)S(1)}, bf16[1,128,2048]{2,1,0:T(8,128)(2,1)}, u32[]{:S(2)}) copy-start(bf16[1,128,2048]{2,1,0:T(8,128)(2,1)} %param.13) | copy-start | bytes 1572868
  7.2 17.8 %copy-start.41 = (f32[2048]{0:T(1024)S(1)}, f32[2048]{0:T(1024)}, u32[]{:S(2)}) copy-start(f32[2048]{0:T(1024)} %param.17) | copy-start | bytes 24580
  7.2 9.4 copy-start.52
  7.2 245.4 %all-gather.2.cloned.1.call-start = ((), (), s32[]{:S(2)}) async-start(), calls=%async_computation.4 | async-start | bytes 33816576 | tf_op jit(solution)/shard_map/all_gather | solution.py:265
  10.3 15.1 %copy-start.49 = (f32[128]{0:T(128)}, f32[128]{0:T(128)S(1)}, u32[]{:S(2)}) copy-start(f32[128]{0:T(128)S(1)} %add_rsqrt_fusion.4) | copy-start | bytes 1540
  11.5 13.4 %collective-permute-start = (bf16[128,2048]{1,0:T(8,128)(2,1)S(1)}, bf16[128,2048]{1,0:T(8,128)(2,1)S(1)}, u32[]{:S(2)}, u32[]{:S(2)}) collective-permute-start(bf16[128,2048]{1,0:T(8,128)(2,1)S(1)} %fusion.62), channel_id=1, source_target_pairs={{0,32},{32,0},{1,33},{33,1},{2,34},{34,2},{3,35},{35,3},{4,36},{36... | collective-permute-start | bytes 1572872 | tf_op jit(solution)/shard_map/ppermute | solution.py:199
  16.0 251.2 %copy-start.40 = (s32[128,8]{1,0:T(8,128)}, s32[128,8]{1,0:T(8,128)S(1)}, u32[]{:S(2)}) copy-start(s32[128,8]{1,0:T(8,128)S(1)} %fusion.101.slot_ref) | copy-start | bytes 12292
  271.1 8.6 copy-start.22
  283.2 6.6 copy-start.31
  283.2 6.6 copy-start.42
  283.2 7.1 copy-start.46
  289.8 7.8 copy-start.7
  367.2 72.5 %all-to-all-start.2 = ((bf16[32,40,2048]{2,1,0:T(8,128)(2,1)}), bf16[32,40,2048]{2,1,0:T(8,128)(2,1)}, u32[]{:S(2)}, u32[]{:S(2)}) async-start(bf16[32,40,2048]{2,1,0:T(8,128)(2,1)} %bitcast.249), calls=%async_computation.2 | async-start | bytes 10485760 | tf_op jit(solution)/shard_map/all_to_all | solution.py:353
  388.9 5.0 copy-start.4
  388.9 6.5 copy-start.56
  439.7 73.7 %all-to-all-start.1 = ((bf16[32,40,2048]{2,1,0:T(8,128)(2,1)}), bf16[32,40,2048]{2,1,0:T(8,128)(2,1)}, u32[]{:S(2)}, u32[]{:S(2)}) async-start(bf16[32,40,2048]{2,1,0:T(8,128)(2,1)} %bitcast.248), calls=%async_computation.1 | async-start | bytes 10485760 | tf_op jit(solution)/shard_map/all_to_all | solution.py:341
  513.4 7.8 copy-start.50
  513.4 8.9 copy-start.48
  513.4 11.7 %copy-start.55 = (f32[128]{0:T(128)S(1)}, f32[128]{0:T(128)}, u32[]{:S(2)}) copy-start(f32[128]{0:T(128)} %get-tuple-element.60) | copy-start | bytes 1540
  513.4 11.7 %copy-start.30 = (f32[16,128,256]{2,1,0:T(8,128)S(1)}, f32[16,128,256]{2,1,0:T(8,128)}, u32[]{:S(2)}) copy-start(f32[16,128,256]{2,1,0:T(8,128)} %fusion.100) | copy-start | bytes 6291460
  513.4 72.6 %all-to-all-start.3 = ((bf16[32,40,2048]{2,1,0:T(8,128)(2,1)}), bf16[32,40,2048]{2,1,0:T(8,128)(2,1)}, u32[]{:S(2)}, u32[]{:S(2)}) async-start(bf16[32,40,2048]{2,1,0:T(8,128)(2,1)} %bitcast.247), calls=%async_computation.3 | async-start | bytes 10485760 | tf_op jit(solution)/shard_map/all_to_all | solution.py:376
  520.8 491.6 %all-reduce.2.cloned.1.call-start = ((), (), s32[]{:S(2)}) async-start(), calls=%async_computation.5 | async-start | bytes 67108864 | tf_op jit(solution)/shard_map/psum | solution.py:458
  586.6 5.6 copy-start.8
  597.0 5.0 copy-start.32
  602.1 5.1 copy-start.23
  609.4 3.1 copy-start.11
  617.2 14.6 %collective-permute-start.1 = (bf16[128,2048]{0,1:T(8,128)(2,1)}, bf16[128,2048]{0,1:T(8,128)(2,1)S(1)}, u32[]{:S(2)}, u32[]{:S(2)}) collective-permute-start(bf16[128,2048]{0,1:T(8,128)(2,1)} %bitcast.264), channel_id=1, source_target_pairs={{0,32},{32,0},{1,33},{33,1},{2,34},{34,2},{3,35},{35,3},{4,36},{36... | collective-permute-start | bytes 1572872 | tf_op jit(solution)/shard_map/ppermute | solution.py:199
  623.1 27.8 %collective-permute-start.2 = (bf16[128,2048]{1,0:T(8,128)(2,1)}, bf16[128,2048]{1,0:T(8,128)(2,1)}, u32[]{:S(2)}, u32[]{:S(2)}) collective-permute-start(bf16[128,2048]{1,0:T(8,128)(2,1)} %copy.113), channel_id=1, source_target_pairs={{0,32},{32,0},{1,33},{33,1},{2,34},{34,2},{3,35},{35,3},{4,36},{36... | collective-permute-start | bytes 1572872 | tf_op jit(solution)/shard_map/ppermute | solution.py:199
  631.9 3.6 copy-start.10
  682.2 18.9 %copy-start.9 = (f32[2,1024,2048]{2,1,0:T(8,128)}, f32[2,1024,2048]{2,1,0:T(8,128)S(1)}, u32[]{:S(2)}) copy-start(f32[2,1024,2048]{2,1,0:T(8,128)S(1)} %fusion.23) | copy-start | bytes 50331652
  682.2 11.1 %copy-start.26 = (bf16[1,1,1280,1024]{3,2,1,0:T(8,128)(2,1)S(1)}, bf16[1,1,1280,1024]{3,2,1,0:T(8,128)(2,1)}, u32[]{:S(2)}) copy-start(bf16[1,1,1280,1024]{3,2,1,0:T(8,128)(2,1)} %copy-done.25) | copy-start | bytes 7864324
  685.0 35.7 %collective-permute-start.10 = (bf16[2,1024,1024]{1,2,0:T(8,128)(2,1)}, bf16[2,1024,1024]{1,2,0:T(8,128)(2,1)}, u32[]{:S(2)}, u32[]{:S(2)}) collective-permute-start(bf16[2,1024,1024]{1,2,0:T(8,128)(2,1)} %fusion.18), channel_id=1, source_target_pairs={{0,64},{64,0},{1,65},{65,1},{2,66},{66,2},{3,67},{67,3},{4,68},{68... | collective-permute-start | bytes 12582920 | tf_op jit(solution)/shard_map/ppermute | solution.py:194
  701.2 3.3 copy-start.14
  704.5 7.2 collective-permute-start.12
  718.4 13.2 %copy-start.13 = (bf16[128,2048]{1,0:T(8,128)(2,1)S(1)}, bf16[128,2048]{1,0:T(8,128)(2,1)}, u32[]{:S(2)}) copy-start(bf16[128,2048]{1,0:T(8,128)(2,1)} %copy-done.12) | copy-start | bytes 1572868
  718.4 81.3 %collective-permute-start.13 = (bf16[1024,512]{1,0:T(8,128)(2,1)}, bf16[1024,512]{1,0:T(8,128)(2,1)}, u32[]{:S(2)}, u32[]{:S(2)}) collective-permute-start(bf16[1024,512]{1,0:T(8,128)(2,1)} %dynamic-slice_convert_fusion.3), channel_id=1, source_target_pairs={{0,32},{32,0},{1,33},{33,1},{2,34},{34,2},{3,35},{35,3},{4,36},{36... | collective-permute-start | bytes 3145736 | tf_op jit(solution)/shard_map/ppermute | solution.py:194
  750.1 14.6 %collective-permute-start.3 = (f32[73728]{0:T(1024)S(1)}, f32[73728]{0:T(1024)S(1)}, u32[]{:S(2)}, u32[]{:S(2)}) collective-permute-start(f32[73728]{0:T(1024)S(1)} %constant_dynamic-update-slice_fusion), channel_id=1, source_target_pairs={{0,1},{1,0},{2,3},{3,2},{4,5},{5,4},{6,7},{7,6},{8,9},{9,8},{10,11... | collective-permute-start | bytes 884744 | tf_op jit(solution)/shard_map/ppermute | solution.py:226
  753.0 86.6 %collective-permute-start.11 = (bf16[2,512,1024]{1,2,0:T(8,128)(2,1)S(1)}, bf16[2,512,1024]{1,2,0:T(8,128)(2,1)}, u32[]{:S(2)}, u32[]{:S(2)}) collective-permute-start(bf16[2,512,1024]{1,2,0:T(8,128)(2,1)S(1)} %dynamic-slice_convert_fusion.2), channel_id=1, source_target_pairs={{0,32},{32,0},{1,33},{33,1},{2,34},{34,2},{3,35},{35,3},{4,36},{36... | collective-permute-start | bytes 6291464 | tf_op jit(solution)/shard_map/ppermute | solution.py:194
  764.6 9.8 collective-permute-start.4
  774.5 14.9 %collective-permute-start.5 = (f32[73728]{0:T(1024)S(1)}, f32[73728]{0:T(1024)S(1)}, u32[]{:S(2)}, u32[]{:S(2)}) collective-permute-start(f32[73728]{0:T(1024)S(1)} %add.183), channel_id=1, source_target_pairs={{0,4},{1,5},{2,6},{3,7},{4,0},{5,1},{6,2},{7,3},{8,12},{9,13},{10,... | collective-permute-start | bytes 884744 | tf_op jit(solution)/shard_map/ppermute | solution.py:226
  789.4 10.2 collective-permute-start.6
  799.6 9.3 copy-start.20
  799.6 9.3 copy-start.37
  799.6 9.1 collective-permute-start.7
  808.8 29.4 %collective-permute-start.8 = (f32[73728]{0:T(1024)S(1)}, f32[73728]{0:T(1024)S(1)}, u32[]{:S(2)}, u32[]{:S(2)}) collective-permute-start(f32[73728]{0:T(1024)S(1)} %add.186), channel_id=1, source_target_pairs={{0,32},{1,33},{2,34},{3,35},{4,36},{5,37},{6,38},{7,39},{8,40},{9,... | collective-permute-start | bytes 884744 | tf_op jit(solution)/shard_map/ppermute | solution.py:226
  838.3 12.4 %collective-permute-start.9 = (f32[73728]{0:T(1024)S(1)}, f32[73728]{0:T(1024)S(1)}, u32[]{:S(2)}, u32[]{:S(2)}) collective-permute-start(f32[73728]{0:T(1024)S(1)} %add.187), channel_id=1, source_target_pairs={{0,64},{1,65},{2,66},{3,67},{4,68},{5,69},{6,70},{7,71},{8,72},{9,... | collective-permute-start | bytes 884744 | tf_op jit(solution)/shard_map/ppermute | solution.py:226
  850.7 164.1 %copy-start.1 = (bf16[2048,32]{0,1:T(8,128)(2,1)S(1)}, bf16[2048,32]{0,1:T(8,128)(2,1)}, u32[]{:S(2)}) copy-start(bf16[2048,32]{0,1:T(8,128)(2,1)} %param.23) | copy-start | bytes 393220
  (30 other events, 48.8 us)
Sparse Core Ops, SparseCore 0:
  10.4 242.2 all-gather.1
  667.4 344.9 all-reduce.1

commit v14 on v13

--- a/solution.py
+++ b/solution.py
@@ -117,7 +117,7 @@
     grad_send_ref[...] = (slot_weight * picked_grad).astype(grad_send_ref.dtype)
 
 
-def dispatch(route_slots, route_weights, rows, grad, slots, tile=256):
+def dispatch(route_slots, route_weights, rows, grad, slots, tile=640):
     top, tokens = route_slots.shape
     width = rows.shape[1]
     out = jax.ShapeDtypeStruct((slots, width), jnp.bfloat16)

time: 1030 us -> 1030 us (level)
  no operation moved by 1% of the time
where the time goes in v14:
time: 1030 us; the launch traced here: 1020 us
  waiting for transfers between devices  590 us (57%)
  matrix products  138 us (13%)
  blocking collectives  69.4 us (7%)
  other arithmetic  67.3 us (7%)
  starting transfers between devices  53.4 us (5%)
  local copies, waits for them, and re-layouts  52.3 us (5%)
  Pallas kernels  36.8 us (4%)
  between operations  15.3 us (1%)
    all_gather x1, waiting for transfers between devices, body(): lax.all_gather(jnp.concatenate([qkv_weight.transpose(1, 0, 2), out_weight...  226 us
    psum x1, waiting for transfers between devices, body(): summed = lax.psum(stacked.astype(bf16), all_axes)  160 us
    ppermute x7, waiting for transfers between devices, butterfly_sum(): received = lax.ppermute(values, axes, partner)  70.7 us
    all_to_all x1, blocking collectives, body(): lax.all_to_all(send.reshape(sources, local_experts * capacity, width), 'e...  69.4 us
    all_to_all x1, waiting for transfers between devices, body(): lax.all_to_all(source_major(grad_rows_in, sources, capacity), 'expert', s...  45.4 us
    all_to_all x1, waiting for transfers between devices, body(): lax.all_to_all(grad_send.reshape(sources, local_experts * capacity, width...  36.7 us
    all_to_all x1, waiting for transfers between devices, body(): lax.all_to_all(source_major(results, sources, capacity), 'expert', split_...  36.5 us
    unnamed x131, local copies, waits for them, and re-layouts  28.2 us
  transfers between devices with their start and end apart: 19, of which 14 were waited for; matrix products, arithmetic and copies ran while one was open for 17% of the time, Pallas kernels for 1%

profile of v14, /device:TPU:1, one launch (start us, length us, event | category | flops | bytes accessed | tf_op | source)
XLA Modules:
  0.0 1022.4 jit_solution(17296027604191895709)
XLA Ops:
  19.5 5.5 collective-permute-done
  26.5 226.2 %all-gather.2.cloned.1.call-done = bf16[2048,4,2048]{2,0,1:T(8,128)(2,1)} async-done(((bf16[16,4,2048]{2,0,1:T(8,128)(2,1)}), bf16[2048,4,2048]{2,0,1:T(8,128)(2,1)}) %all-gather.2.cloned.1.call-update) | async-done | bytes 33554448 | tf_op jit(solution)/shard_map/all_gather | solution.py:265
  252.7 14.7 %shard_map.215 = f32[3,256,2048]{2,1,0:T(8,128)} custom-call(bf16[256,2048]{1,0:T(8,128)(2,1)} %pad_maximum_fusion.inputs_ref, bf16[4,2048,2048]{2,1,0:T(8,128)(2,1)} %bitcast.243), custom_call_target="tpu_custom_call" | custom-call | flops 6442450944 | bytes 32505856 | tf_op jit(solution)/shard_map/pallas_call | solution.py:83
  279.8 3.5 convolution_convert_fusion.2
  283.4 6.5 multiply_reduce_fusion.9
  291.1 6.3 shard_map.216
  297.4 69.4 %all_to_all.20 = bf16[32,40,2048]{2,1,0:T(8,128)(2,1)} all-to-all(bf16[32,40,2048]{2,1,0:T(8,128)(2,1)} %bitcast.250), channel_id=1, replica_groups=mesh['dp'=2,'context'=2,'expert'=32] {'expert'}, dimensions={0} | all-to-all | bytes 10485760 | tf_op jit(solution)/shard_map/all_to_all | solution.py:325
  366.8 5.1 all-to-all-start.2
  371.9 16.8 %fusion.6 = f32[1,2,1280,1024]{3,2,1,0:T(8,128)S(1)} fusion(bf16[1280,2048,1]{1,0,2:T(8,128)(2,1)} %bitcast.245, bf16[1,2,2048,1024]{3,2,1,0:T(8,128)(2,1)} %param.24), kind=kOutput, calls=%fused_computation.12 | convolution fusion | flops 10737418240 | bytes 24117248 | tf_op jit(solution)/shard_map/lrd,lkdh->lkrh/dot_general | solution.py:333
  390.5 3.3 copy-done.4
  395.3 7.3 convolution_convert_fusion.1
  402.6 36.7 %all-to-all-done.2 = bf16[32,40,2048]{2,1,0:T(8,128)(2,1)} async-done(((bf16[32,40,2048]{2,1,0:T(8,128)(2,1)}), bf16[32,40,2048]{2,1,0:T(8,128)(2,1)}, u32[]{:S(2)}, u32[]{:S(2)}) %all-to-all-start.2) | async-done | bytes 5242912 | tf_op jit(solution)/shard_map/all_to_all | solution.py:353
  439.3 6.7 all-to-all-start.1
  446.1 13.1 %fusion.28 = (bf16[1,1,1280,1024]{3,2,1,0:T(8,128)(2,1)S(1)}, bf16[1,1,1280,1024]{3,2,1,0:T(8,128)(2,1)S(1)}) fusion(f32[1,2,1280,1024]{3,2,1,0:T(8,128)} %copy-done.4, bf16[1280,2048]{1,0:T(8,128)(2,1)} %bitcast.31, bf16[1,1024,2048]{2,1,0:T(8,128)(2,1)} %param.25), kind=kOutput, calls=%fused_computation.43 | convolution fusion | flops 5385748480 | bytes 25165824 | tf_op jit(solution)/shard_map/lrd,lhd->lrh/dot_general | solution.py:361
  461.5 15.1 %bitcast_convert_fusion = bf16[1280,2048]{1,0:T(8,128)(2,1)} fusion(bf16[1,2,2048,1024]{3,2,1,0:T(8,128)(2,1)} %param.24, bf16[1,1,1280,1024]{3,2,1,0:T(8,128)(2,1)S(1)} %get-tuple-element.71, bf16[1,1,1280,1024]{3,2,1,0:T(8,128)(2,1)S(1)} %get-tuple-element.70), kind=kOutput, calls=%fused_computation.2 | convolution fusion | flops 10742661120 | bytes 18874368 | tf_op jit(solution)/shard_map/lkrh,lkdh->lrd/dot_general | solution.py:373
  476.6 36.5 %all-to-all-done.1 = bf16[32,40,2048]{2,1,0:T(8,128)(2,1)} async-done(((bf16[32,40,2048]{2,1,0:T(8,128)(2,1)}), bf16[32,40,2048]{2,1,0:T(8,128)(2,1)}, u32[]{:S(2)}, u32[]{:S(2)}) %all-to-all-start.1) | async-done | bytes 5242912 | tf_op jit(solution)/shard_map/all_to_all | solution.py:341
  513.1 7.4 all-to-all-start.3
  526.8 10.2 shard_map.217
  539.4 45.4 %all-to-all-done.3 = bf16[32,40,2048]{2,1,0:T(8,128)(2,1)} async-done(((bf16[32,40,2048]{2,1,0:T(8,128)(2,1)}), bf16[32,40,2048]{2,1,0:T(8,128)(2,1)}, u32[]{:S(2)}, u32[]{:S(2)}) %all-to-all-start.3) | async-done | bytes 5242912 | tf_op jit(solution)/shard_map/all_to_all | solution.py:376
  585.5 5.6 shard_map.218
  595.9 4.7 fusion.30
  601.1 5.0 convolution_bitcast_fusion.1
  616.1 6.9 collective-permute-start.1
  623.0 3.6 fusion.52
  626.8 4.9 collective-permute-done.1
  635.4 3.3 multiply_subtract_fusion.1
  645.7 2.9 multiply_reduce_fusion.2
  652.6 14.7 %convolution_convert_fusion = bf16[4,2048,2048]{2,1,0:T(8,128)(2,1)} fusion(bf16[1,128,2048]{2,1,0:T(8,128)(2,1)S(1)} %copy-done.27, bf16[1,128,2048]{2,1,0:T(8,128)(2,1)S(1)} %copy-done.28, bf16[1,128,2048]{2,1,0:T(8,128)(2,1)S(1)} %copy-done.29, bf16[3,128,2048]{2,1,0:T(8,128)(2,1)S(1)} %maximum_bitcast_fusion.3), kind=kOutput, calls=%fused_computation.1 | convolution fusion | flops 4315938816 | bytes 36700160 | tf_op jit(solution)/shard_map/sta,stb->sab/dot_general | solution.py:457
  667.3 15.0 %fusion.23 = f32[2,1024,2048]{2,1,0:T(8,128)S(1)} fusion(bf16[1280,2048,1]{1,0,2:T(8,128)(2,1)} %bitcast.246, bf16[1,1,1280,1024]{3,2,1,0:T(8,128)(2,1)} %copy-done.58, bf16[1,1,1280,1024]{3,2,1,0:T(8,128)(2,1)} %copy-done.57), kind=kOutput, calls=%fused_computation.38 | convolution fusion | flops 10740039680 | bytes 27262976 | tf_op jit(solution)/shard_map/lrd,lkrh->lkdh/dot_general | solution.py:370
  685.1 8.3 collective-permute-start.10
  693.4 7.8 fusion.24
  701.5 3.0 copy-done.14
  704.5 3.2 collective-permute-start.12
  707.7 3.8 collective-permute-done.12
  711.6 3.7 convert_add_fusion
  720.1 11.3 %bitcast_add_fusion = f32[2,1024,1024]{1,2,0:T(8,128)} fusion(bf16[2,1024,1024]{1,2,0:T(8,128)(2,1)} %collective-permute-done.10, f32[2,1024,2048]{2,1,0:T(8,128)} %copy-done.9, s32[]{:T(128)S(6)} %select_n.102), kind=kLoop, calls=%fused_computation.4 | loop fusion | flops 4194304 | bytes 20971524 | tf_op jit(solution)/shard_map/add | solution.py:195
  732.7 17.2 %fusion.68 = (f32[2048]{0:T(1024)S(1)}, f32[128]{0:T(128)S(1)}, f32[128,2048]{1,0:T(8,128)}) fusion(bf16[1,128,2048]{2,1,0:T(8,128)(2,1)S(1)} %copy-done.2, f32[128]{0:T(128)S(1)} %copy-done.51, f32[2048]{0:T(1024)S(1)} %copy-done.41, bf16[2048,4,2048]{2,0,1:T(8,128)(2,1)} %all-gather.2.cloned.1.call-done, bf16[128,1,2048]{2,0,1:T(8,128)(2,1)S(1)} %fusion.88, ...), kind=kOutput, calls=%fused_computation.102 | convolution fusion | flops 4299945984 | bytes 36717576 | tf_op jit(solution)/shard_map/dot_general | solution.py:439
  753.3 11.3 %collective-permute-done.3 = f32[73728]{0:T(1024)S(1)} collective-permute-done((f32[73728]{0:T(1024)S(1)}, f32[73728]{0:T(1024)S(1)}, u32[]{:S(2)}, u32[]{:S(2)}) %collective-permute-start.3) | collective-permute-done | bytes 294944 | tf_op jit(solution)/shard_map/ppermute | solution.py:226
  764.9 8.9 collective-permute-done.4
  773.9 5.1 collective-permute-start.5
  779.0 9.6 collective-permute-done.5
  791.0 8.3 collective-permute-done.6
  800.9 3.6 add_bitcast_fusion.1
  804.5 5.7 collective-permute-done.7
  811.8 27.0 %collective-permute-done.8 = f32[73728]{0:T(1024)S(1)} collective-permute-done((f32[73728]{0:T(1024)S(1)}, f32[73728]{0:T(1024)S(1)}, u32[]{:S(2)}, u32[]{:S(2)}) %collective-permute-start.8) | collective-permute-done | bytes 294944 | tf_op jit(solution)/shard_map/ppermute | solution.py:226
  840.0 5.7 add_bitcast_fusion
  845.6 5.4 copy.103
  853.0 159.9 %all-reduce.2.cloned.1.call-done = bf16[4,2048,2048]{2,1,0:T(8,128)(2,1)} async-done(((bf16[4,2048,2048]{2,1,0:T(8,128)(2,1)}), bf16[4,2048,2048]{2,1,0:T(8,128)(2,1)}) %all-reduce.2.cloned.1.call-update) | async-done | bytes 33554448 | tf_op jit(solution)/shard_map/psum | solution.py:458
  (240 shorter events, 96.1 us)
Async XLA Ops:
  7.2 283.0 %copy-start = (bf16[2048,32]{0,1:T(8,128)(2,1)S(1)}, bf16[2048,32]{0,1:T(8,128)(2,1)}, u32[]{:S(2)}) copy-start(bf16[2048,32]{0,1:T(8,128)(2,1)} %param.23) | copy-start | bytes 393220
  7.2 17.8 %copy-start.2 = (bf16[1,128,2048]{2,1,0:T(8,128)(2,1)S(1)}, bf16[1,128,2048]{2,1,0:T(8,128)(2,1)}, u32[]{:S(2)}) copy-start(bf16[1,128,2048]{2,1,0:T(8,128)(2,1)} %param.13) | copy-start | bytes 1572868
  7.2 17.8 %copy-start.41 = (f32[2048]{0:T(1024)S(1)}, f32[2048]{0:T(1024)}, u32[]{:S(2)}) copy-start(f32[2048]{0:T(1024)} %param.17) | copy-start | bytes 24580
  7.2 9.4 copy-start.52
  7.2 245.4 %all-gather.2.cloned.1.call-start = ((), (), s32[]{:S(2)}) async-start(), calls=%async_computation.4 | async-start | bytes 33816576 | tf_op jit(solution)/shard_map/all_gather | solution.py:265
  10.3 15.1 %copy-start.49 = (f32[128]{0:T(128)}, f32[128]{0:T(128)S(1)}, u32[]{:S(2)}) copy-start(f32[128]{0:T(128)S(1)} %add_rsqrt_fusion.4) | copy-start | bytes 1540
  11.5 13.4 %collective-permute-start = (bf16[128,2048]{1,0:T(8,128)(2,1)S(1)}, bf16[128,2048]{1,0:T(8,128)(2,1)S(1)}, u32[]{:S(2)}, u32[]{:S(2)}) collective-permute-start(bf16[128,2048]{1,0:T(8,128)(2,1)S(1)} %fusion.62), channel_id=1, source_target_pairs={{0,32},{32,0},{1,33},{33,1},{2,34},{34,2},{3,35},{35,3},{4,36},{36... | collective-permute-start | bytes 1572872 | tf_op jit(solution)/shard_map/ppermute | solution.py:199
  16.0 251.4 %copy-start.40 = (s32[128,8]{1,0:T(8,128)}, s32[128,8]{1,0:T(8,128)S(1)}, u32[]{:S(2)}) copy-start(s32[128,8]{1,0:T(8,128)S(1)} %fusion.101.slot_ref) | copy-start | bytes 12292
  271.2 8.6 copy-start.22
  283.4 6.6 copy-start.31
  283.4 6.6 copy-start.42
  283.4 7.1 copy-start.46
  289.9 7.5 copy-start.7
  366.8 72.5 %all-to-all-start.2 = ((bf16[32,40,2048]{2,1,0:T(8,128)(2,1)}), bf16[32,40,2048]{2,1,0:T(8,128)(2,1)}, u32[]{:S(2)}, u32[]{:S(2)}) async-start(bf16[32,40,2048]{2,1,0:T(8,128)(2,1)} %bitcast.249), calls=%async_computation.2 | async-start | bytes 10485760 | tf_op jit(solution)/shard_map/all_to_all | solution.py:353
  388.8 5.0 copy-start.4
  388.8 6.5 copy-start.56
  439.3 73.8 %all-to-all-start.1 = ((bf16[32,40,2048]{2,1,0:T(8,128)(2,1)}), bf16[32,40,2048]{2,1,0:T(8,128)(2,1)}, u32[]{:S(2)}, u32[]{:S(2)}) async-start(bf16[32,40,2048]{2,1,0:T(8,128)(2,1)} %bitcast.248), calls=%async_computation.1 | async-start | bytes 10485760 | tf_op jit(solution)/shard_map/all_to_all | solution.py:341
  513.1 7.7 copy-start.50
  513.1 8.7 copy-start.48
  513.1 11.5 %copy-start.55 = (f32[128]{0:T(128)S(1)}, f32[128]{0:T(128)}, u32[]{:S(2)}) copy-start(f32[128]{0:T(128)} %get-tuple-element.60) | copy-start | bytes 1540
  513.1 11.5 %copy-start.30 = (f32[16,128,256]{2,1,0:T(8,128)S(1)}, f32[16,128,256]{2,1,0:T(8,128)}, u32[]{:S(2)}) copy-start(f32[16,128,256]{2,1,0:T(8,128)} %fusion.100) | copy-start | bytes 6291460
  513.1 71.7 %all-to-all-start.3 = ((bf16[32,40,2048]{2,1,0:T(8,128)(2,1)}), bf16[32,40,2048]{2,1,0:T(8,128)(2,1)}, u32[]{:S(2)}, u32[]{:S(2)}) async-start(bf16[32,40,2048]{2,1,0:T(8,128)(2,1)} %bitcast.247), calls=%async_computation.3 | async-start | bytes 10485760 | tf_op jit(solution)/shard_map/all_to_all | solution.py:376
  520.6 492.3 %all-reduce.2.cloned.1.call-start = ((), (), s32[]{:S(2)}) async-start(), calls=%async_computation.5 | async-start | bytes 67108864 | tf_op jit(solution)/shard_map/psum | solution.py:458
  585.5 5.6 copy-start.8
  595.9 5.0 copy-start.32
  600.9 5.1 copy-start.23
  608.3 3.1 copy-start.11
  616.1 15.6 %collective-permute-start.1 = (bf16[128,2048]{0,1:T(8,128)(2,1)}, bf16[128,2048]{0,1:T(8,128)(2,1)S(1)}, u32[]{:S(2)}, u32[]{:S(2)}) collective-permute-start(bf16[128,2048]{0,1:T(8,128)(2,1)} %bitcast.264), channel_id=1, source_target_pairs={{0,32},{32,0},{1,33},{33,1},{2,34},{34,2},{3,35},{35,3},{4,36},{36... | collective-permute-start | bytes 1572872 | tf_op jit(solution)/shard_map/ppermute | solution.py:199
  623.0 27.8 %collective-permute-start.2 = (bf16[128,2048]{1,0:T(8,128)(2,1)}, bf16[128,2048]{1,0:T(8,128)(2,1)}, u32[]{:S(2)}, u32[]{:S(2)}) collective-permute-start(bf16[128,2048]{1,0:T(8,128)(2,1)} %copy.113), channel_id=1, source_target_pairs={{0,32},{32,0},{1,33},{33,1},{2,34},{34,2},{3,35},{35,3},{4,36},{36... | collective-permute-start | bytes 1572872 | tf_op jit(solution)/shard_map/ppermute | solution.py:199
  631.8 3.6 copy-start.10
  682.3 18.9 %copy-start.9 = (f32[2,1024,2048]{2,1,0:T(8,128)}, f32[2,1024,2048]{2,1,0:T(8,128)S(1)}, u32[]{:S(2)}) copy-start(f32[2,1024,2048]{2,1,0:T(8,128)S(1)} %fusion.23) | copy-start | bytes 50331652
  682.3 11.1 %copy-start.26 = (bf16[1,1,1280,1024]{3,2,1,0:T(8,128)(2,1)S(1)}, bf16[1,1,1280,1024]{3,2,1,0:T(8,128)(2,1)}, u32[]{:S(2)}) copy-start(bf16[1,1,1280,1024]{3,2,1,0:T(8,128)(2,1)} %copy-done.25) | copy-start | bytes 7864324
  685.1 35.1 %collective-permute-start.10 = (bf16[2,1024,1024]{1,2,0:T(8,128)(2,1)}, bf16[2,1024,1024]{1,2,0:T(8,128)(2,1)}, u32[]{:S(2)}, u32[]{:S(2)}) collective-permute-start(bf16[2,1024,1024]{1,2,0:T(8,128)(2,1)} %fusion.18), channel_id=1, source_target_pairs={{0,64},{64,0},{1,65},{65,1},{2,66},{66,2},{3,67},{67,3},{4,68},{68... | collective-permute-start | bytes 12582920 | tf_op jit(solution)/shard_map/ppermute | solution.py:194
  701.2 3.3 copy-start.14
  704.5 7.1 collective-permute-start.12
  718.4 13.0 %copy-start.13 = (bf16[128,2048]{1,0:T(8,128)(2,1)S(1)}, bf16[128,2048]{1,0:T(8,128)(2,1)}, u32[]{:S(2)}) copy-start(bf16[128,2048]{1,0:T(8,128)(2,1)} %copy-done.12) | copy-start | bytes 1572868
  718.4 82.5 %collective-permute-start.13 = (bf16[1024,512]{1,0:T(8,128)(2,1)}, bf16[1024,512]{1,0:T(8,128)(2,1)}, u32[]{:S(2)}, u32[]{:S(2)}) collective-permute-start(bf16[1024,512]{1,0:T(8,128)(2,1)} %dynamic-slice_convert_fusion.3), channel_id=1, source_target_pairs={{0,32},{32,0},{1,33},{33,1},{2,34},{34,2},{3,35},{35,3},{4,36},{36... | collective-permute-start | bytes 3145736 | tf_op jit(solution)/shard_map/ppermute | solution.py:194
  749.8 14.7 %collective-permute-start.3 = (f32[73728]{0:T(1024)S(1)}, f32[73728]{0:T(1024)S(1)}, u32[]{:S(2)}, u32[]{:S(2)}) collective-permute-start(f32[73728]{0:T(1024)S(1)} %constant_dynamic-update-slice_fusion), channel_id=1, source_target_pairs={{0,1},{1,0},{2,3},{3,2},{4,5},{5,4},{6,7},{7,6},{8,9},{9,8},{10,11... | collective-permute-start | bytes 884744 | tf_op jit(solution)/shard_map/ppermute | solution.py:226
  753.2 86.7 %collective-permute-start.11 = (bf16[2,512,1024]{1,2,0:T(8,128)(2,1)S(1)}, bf16[2,512,1024]{1,2,0:T(8,128)(2,1)}, u32[]{:S(2)}, u32[]{:S(2)}) collective-permute-start(bf16[2,512,1024]{1,2,0:T(8,128)(2,1)S(1)} %dynamic-slice_convert_fusion.2), channel_id=1, source_target_pairs={{0,32},{32,0},{1,33},{33,1},{2,34},{34,2},{3,35},{35,3},{4,36},{36... | collective-permute-start | bytes 6291464 | tf_op jit(solution)/shard_map/ppermute | solution.py:194
  764.6 9.3 collective-permute-start.4
  773.9 14.7 %collective-permute-start.5 = (f32[73728]{0:T(1024)S(1)}, f32[73728]{0:T(1024)S(1)}, u32[]{:S(2)}, u32[]{:S(2)}) collective-permute-start(f32[73728]{0:T(1024)S(1)} %add.183), channel_id=1, source_target_pairs={{0,4},{1,5},{2,6},{3,7},{4,0},{5,1},{6,2},{7,3},{8,12},{9,13},{10,... | collective-permute-start | bytes 884744 | tf_op jit(solution)/shard_map/ppermute | solution.py:226
  788.6 10.7 %collective-permute-start.6 = (f32[73728]{0:T(1024)S(1)}, f32[73728]{0:T(1024)S(1)}, u32[]{:S(2)}, u32[]{:S(2)}) collective-permute-start(f32[73728]{0:T(1024)S(1)} %add.184), channel_id=1, source_target_pairs={{0,8},{1,9},{2,10},{3,11},{4,12},{5,13},{6,14},{7,15},{8,0},{9,1},... | collective-permute-start | bytes 884744 | tf_op jit(solution)/shard_map/ppermute | solution.py:226
  799.3 11.1 %copy-start.20 = (f32[128,2048]{1,0:T(8,128)S(1)}, f32[128,2048]{1,0:T(8,128)}, u32[]{:S(2)}) copy-start(f32[128,2048]{1,0:T(8,128)} %copy-done.19) | copy-start | bytes 3145732
  799.3 11.1 %copy-start.37 = (f32[128,2048]{1,0:T(8,128)S(1)}, f32[128,2048]{1,0:T(8,128)}, u32[]{:S(2)}) copy-start(f32[128,2048]{1,0:T(8,128)} %get-tuple-element.104) | copy-start | bytes 3145732
  799.3 10.9 %collective-permute-start.7 = (f32[73728]{0:T(1024)S(1)}, f32[73728]{0:T(1024)S(1)}, u32[]{:S(2)}, u32[]{:S(2)}) collective-permute-start(f32[73728]{0:T(1024)S(1)} %add.185), channel_id=1, source_target_pairs={{0,16},{1,17},{2,18},{3,19},{4,20},{5,21},{6,22},{7,23},{8,24},{9,... | collective-permute-start | bytes 884744 | tf_op jit(solution)/shard_map/ppermute | solution.py:226
  810.3 28.4 %collective-permute-start.8 = (f32[73728]{0:T(1024)S(1)}, f32[73728]{0:T(1024)S(1)}, u32[]{:S(2)}, u32[]{:S(2)}) collective-permute-start(f32[73728]{0:T(1024)S(1)} %add.186), channel_id=1, source_target_pairs={{0,32},{1,33},{2,34},{3,35},{4,36},{5,37},{6,38},{7,39},{8,40},{9,... | collective-permute-start | bytes 884744 | tf_op jit(solution)/shard_map/ppermute | solution.py:226
  838.8 12.3 %collective-permute-start.9 = (f32[73728]{0:T(1024)S(1)}, f32[73728]{0:T(1024)S(1)}, u32[]{:S(2)}, u32[]{:S(2)}) collective-permute-start(f32[73728]{0:T(1024)S(1)} %add.187), channel_id=1, source_target_pairs={{0,64},{1,65},{2,66},{3,67},{4,68},{5,69},{6,70},{7,71},{8,72},{9,... | collective-permute-start | bytes 884744 | tf_op jit(solution)/shard_map/ppermute | solution.py:226
  851.0 164.3 %copy-start.1 = (bf16[2048,32]{0,1:T(8,128)(2,1)S(1)}, bf16[2048,32]{0,1:T(8,128)(2,1)}, u32[]{:S(2)}) copy-start(bf16[2048,32]{0,1:T(8,128)(2,1)} %param.23) | copy-start | bytes 393220
  (30 other events, 48.6 us)
Sparse Core Ops, SparseCore 0:
  10.4 242.2 all-gather.1
  667.5 345.4 all-reduce.1

commit v15 on v14

--- a/solution.py
+++ b/solution.py
@@ -401,6 +401,9 @@
     grad_mid_norm, grad_ffn_gain = rms_backward(grad_ffn_in, normed2, factor2, ffn_gain)
     grad_mid = grad + grad_mid_norm
     grad_mid_b = grad_mid.astype(bf16)
+    out_block = jnp.einsum(
+        "td,tq->dq", grad_mid_b, attended, preferred_element_type=single_precision
+    ).astype(bf16)
     grad_att = (
         jnp.einsum("td,dq->tq", grad_mid_b, out_full, preferred_element_type=single_precision)
         .astype(bf16)
@@ -450,19 +453,21 @@
 
     grad_in_shard = scatter_over_copies(grad_gate_up_w[0])[None]
     grad_down_shard = scatter_over_copies(grad_down[0])[None]
-    left = jnp.stack([attention_input] * 3 + [grad_mid_b])
-    right = jnp.concatenate(
-        [projected_gradient[:, :3].transpose(1, 0, 2), attended[None]], axis=0
-    )
-    stacked = jnp.einsum("sta,stb->sab", left, right, preferred_element_type=single_precision)
-    summed = lax.psum(stacked.astype(bf16), all_axes)
+    qkv_stack = jnp.einsum(
+        "ta,stb->sab",
+        attention_input,
+        projected_gradient[:, :3].transpose(1, 0, 2),
+        preferred_element_type=single_precision,
+    ).astype(bf16)
+    qkv_sum, out_sum = lax.psum((qkv_stack, out_block), all_axes)
     shard_rows = width // lax.axis_size(all_axes)
     start = lax.axis_index(all_axes) * shard_rows
-    weight_shard = lax.dynamic_slice_in_dim(summed, start, shard_rows, axis=1).astype(
+    grad_qkv_shard = lax.dynamic_slice_in_dim(qkv_sum, start, shard_rows, axis=1).astype(
         single_precision
     )
-    grad_qkv_shard = weight_shard[:3]
-    grad_out_shard = weight_shard[3]
+    grad_out_shard = lax.dynamic_slice_in_dim(out_sum, start, shard_rows, axis=0).astype(
+        single_precision
+    )
     small_sum = butterfly_sum(
         jnp.concatenate(
             [grad_attn_gain, grad_q_gain, grad_k_gain, grad_ffn_gain, grad_router.reshape(-1)]

time: 1030 us -> 1040 us (level)
    unnamed x131 -> x108, local copies, waits for them, and re-layouts: 28.2 us -> 32.3 us
  transfers between devices with their start and end apart: 19 -> 19, of which waited for: 14 -> 13; matrix products, arithmetic and copies ran while one was open for 17% -> 18% of each run, Pallas kernels for 1% -> 1%
where the time goes in v15:
time: 1040 us; the launch traced here: 1030 us
  waiting for transfers between devices  586 us (56%)
  matrix products  146 us (14%)
  other arithmetic  72.1 us (7%)
  blocking collectives  69.8 us (7%)
  local copies, waits for them, and re-layouts  57.4 us (6%)
  starting transfers between devices  47.3 us (5%)
  Pallas kernels  37.1 us (4%)
  between operations  15.1 us (1%)
    all_gather x1, waiting for transfers between devices, body(): lax.all_gather(jnp.concatenate([qkv_weight.transpose(1, 0, 2), out_weight...  226 us
    psum x1, waiting for transfers between devices, body(): qkv_sum, out_sum = lax.psum((qkv_stack, out_block), all_axes)  156 us
    ppermute x7, waiting for transfers between devices, butterfly_sum(): received = lax.ppermute(values, axes, partner)  73.1 us
    all_to_all x1, blocking collectives, body(): lax.all_to_all(send.reshape(sources, local_experts * capacity, width), 'e...  69.8 us
    all_to_all x1, waiting for transfers between devices, body(): lax.all_to_all(source_major(grad_rows_in, sources, capacity), 'expert', s...  47.4 us
    all_to_all x1, waiting for transfers between devices, body(): lax.all_to_all(grad_send.reshape(sources, local_experts * capacity, width...  36.8 us
    all_to_all x1, waiting for transfers between devices, body(): lax.all_to_all(source_major(results, sources, capacity), 'expert', split_...  36.4 us
    unnamed x108, local copies, waits for them, and re-layouts  32.3 us
  transfers between devices with their start and end apart: 19, of which 13 were waited for; matrix products, arithmetic and copies ran while one was open for 18% of the time, Pallas kernels for 1%

profile of v15, /device:TPU:1, one launch (start us, length us, event | category | flops | bytes accessed | tf_op | source)
XLA Modules:
  0.0 1031.4 jit_solution(14299304704754317892)
XLA Ops:
  18.9 6.1 collective-permute-done
  26.5 226.0 %all-gather.2.cloned.1.call-done = bf16[2048,4,2048]{2,0,1:T(8,128)(2,1)} async-done(((bf16[16,4,2048]{2,0,1:T(8,128)(2,1)}), bf16[2048,4,2048]{2,0,1:T(8,128)(2,1)}) %all-gather.2.cloned.1.call-update) | async-done | bytes 33554448 | tf_op jit(solution)/shard_map/all_gather | solution.py:265
  252.4 14.8 %shard_map.215 = f32[3,256,2048]{2,1,0:T(8,128)} custom-call(bf16[256,2048]{1,0:T(8,128)(2,1)} %pad_maximum_fusion.inputs_ref, bf16[4,2048,2048]{2,1,0:T(8,128)(2,1)} %bitcast.219), custom_call_target="tpu_custom_call" | custom-call | flops 6442450944 | bytes 32505856 | tf_op jit(solution)/shard_map/pallas_call | solution.py:83
  279.7 4.3 convolution_convert_fusion.2
  284.1 6.5 multiply_reduce_fusion.9
  292.7 6.4 shard_map.216
  299.1 69.8 %all_to_all.20 = bf16[32,40,2048]{2,1,0:T(8,128)(2,1)} all-to-all(bf16[32,40,2048]{2,1,0:T(8,128)(2,1)} %bitcast.226), channel_id=1, replica_groups=mesh['dp'=2,'context'=2,'expert'=32] {'expert'}, dimensions={0} | all-to-all | bytes 10485760 | tf_op jit(solution)/shard_map/all_to_all | solution.py:325
  368.9 5.1 all-to-all-start.2
  374.0 16.9 %fusion.6 = f32[1,2,1280,1024]{3,2,1,0:T(8,128)S(1)} fusion(bf16[1280,2048,1]{1,0,2:T(8,128)(2,1)} %bitcast.221, bf16[1,2,2048,1024]{3,2,1,0:T(8,128)(2,1)} %param.24), kind=kOutput, calls=%fused_computation.13 | convolution fusion | flops 10737418240 | bytes 24117248 | tf_op jit(solution)/shard_map/lrd,lkdh->lkrh/dot_general | solution.py:333
  392.6 3.3 copy-done.3
  397.4 7.3 convolution_convert_fusion
  404.7 36.8 %all-to-all-done.2 = bf16[32,40,2048]{2,1,0:T(8,128)(2,1)} async-done(((bf16[32,40,2048]{2,1,0:T(8,128)(2,1)}), bf16[32,40,2048]{2,1,0:T(8,128)(2,1)}, u32[]{:S(2)}, u32[]{:S(2)}) %all-to-all-start.2) | async-done | bytes 5242912 | tf_op jit(solution)/shard_map/all_to_all | solution.py:353
  441.5 6.9 all-to-all-start.1
  448.4 13.1 %fusion.28 = (bf16[1,1,1280,1024]{3,2,1,0:T(8,128)(2,1)S(1)}, bf16[1,1,1280,1024]{3,2,1,0:T(8,128)(2,1)S(1)}) fusion(f32[1,2,1280,1024]{3,2,1,0:T(8,128)} %copy-done.3, bf16[1280,2048]{1,0:T(8,128)(2,1)} %bitcast.32, bf16[1,1024,2048]{2,1,0:T(8,128)(2,1)} %param.25), kind=kOutput, calls=%fused_computation.44 | convolution fusion | flops 5385748480 | bytes 25165824 | tf_op jit(solution)/shard_map/lrd,lhd->lrh/dot_general | solution.py:361
  463.9 15.0 %bitcast_convert_fusion = bf16[1280,2048]{1,0:T(8,128)(2,1)} fusion(bf16[1,2,2048,1024]{3,2,1,0:T(8,128)(2,1)} %param.24, bf16[1,1,1280,1024]{3,2,1,0:T(8,128)(2,1)S(1)} %get-tuple-element.71, bf16[1,1,1280,1024]{3,2,1,0:T(8,128)(2,1)S(1)} %get-tuple-element.70), kind=kOutput, calls=%fused_computation.2 | convolution fusion | flops 10742661120 | bytes 18874368 | tf_op jit(solution)/shard_map/lkrh,lkdh->lrd/dot_general | solution.py:373
  478.9 36.4 %all-to-all-done.1 = bf16[32,40,2048]{2,1,0:T(8,128)(2,1)} async-done(((bf16[32,40,2048]{2,1,0:T(8,128)(2,1)}), bf16[32,40,2048]{2,1,0:T(8,128)(2,1)}, u32[]{:S(2)}, u32[]{:S(2)}) %all-to-all-start.1) | async-done | bytes 5242912 | tf_op jit(solution)/shard_map/all_to_all | solution.py:341
  515.3 8.2 all-to-all-start.3
  524.5 4.5 fusion.31
  529.0 10.2 shard_map.217
  541.6 47.4 %all-to-all-done.3 = bf16[32,40,2048]{2,1,0:T(8,128)(2,1)} async-done(((bf16[32,40,2048]{2,1,0:T(8,128)(2,1)}), bf16[32,40,2048]{2,1,0:T(8,128)(2,1)}, u32[]{:S(2)}, u32[]{:S(2)}) %all-to-all-start.3) | async-done | bytes 5242912 | tf_op jit(solution)/shard_map/all_to_all | solution.py:376
  589.6 5.7 shard_map.218
  598.5 5.4 fusion.30
  607.4 5.0 convolution_bitcast_fusion.1
  627.9 6.7 convolution_convert_fusion.1
  641.7 3.6 multiply_subtract_fusion.1
  656.3 3.0 fusion.71
  660.5 13.4 %convert_bitcast_fusion = bf16[3,2048,2048]{1,2,0:T(8,128)(2,1)} fusion(bf16[128,1,2048]{2,0,1:T(8,128)(2,1)S(1)} %fusion.78, bf16[128,1,2048]{2,0,1:T(8,128)(2,1)} %get-tuple-element.73, bf16[128,1,2048]{2,0,1:T(8,128)(2,1)} %get-tuple-element.72, bf16[128,2048]{1,0:T(8,128)(2,1)} %copy-done.24), kind=kOutput, calls=%fused_computation.1 | convolution fusion | flops 3235381248 | bytes 27262976 | tf_op jit(solution)/shard_map/ta,stb->sab/dot_general | solution.py:456
  673.9 15.0 %fusion.23 = f32[2,1024,2048]{2,1,0:T(8,128)S(1)} fusion(bf16[1280,2048,1]{1,0,2:T(8,128)(2,1)} %bitcast.222, bf16[1,1,1280,1024]{3,2,1,0:T(8,128)(2,1)} %copy-done.46, bf16[1,1,1280,1024]{3,2,1,0:T(8,128)(2,1)} %copy-done.45), kind=kOutput, calls=%fused_computation.39 | convolution fusion | flops 10740039680 | bytes 27262976 | tf_op jit(solution)/shard_map/lrd,lkrh->lkdh/dot_general | solution.py:370
  688.9 3.1 fusion.18
  692.0 7.9 collective-permute-start.10
  699.9 8.9 fusion.24
  712.1 3.8 collective-permute-start.12
  715.9 4.0 collective-permute-done.12
  719.9 3.8 convert_add_fusion
  728.4 10.6 %bitcast_add_fusion = f32[2,1024,1024]{1,2,0:T(8,128)} fusion(bf16[2,1024,1024]{1,2,0:T(8,128)(2,1)} %collective-permute-done.10, f32[2,1024,2048]{2,1,0:T(8,128)} %copy-done.4, s32[]{:T(128)S(6)} %select_n.103), kind=kLoop, calls=%fused_computation.4 | loop fusion | flops 4194304 | bytes 20971524 | tf_op jit(solution)/shard_map/add | solution.py:195
  740.2 18.8 %fusion.60 = (f32[2048]{0:T(1024)S(1)}, f32[128]{0:T(128)S(1)}, f32[128,2048]{1,0:T(8,128)}) fusion(bf16[1,128,2048]{2,1,0:T(8,128)(2,1)S(1)} %copy-done.10, f32[128]{0:T(128)S(1)} %copy-done.40, f32[2048]{0:T(1024)S(1)} %copy-done.34, bf16[2048,4,2048]{2,0,1:T(8,128)(2,1)} %all-gather.2.cloned.1.call-done, bf16[128,1,2048]{2,0,1:T(8,128)(2,1)S(1)} %copy-done.26, ...), kind=kOutput, calls=%fused_computation.96 | convolution fusion | flops 4299945984 | bytes 36717576 | tf_op jit(solution)/shard_map/dot_general | solution.py:442
  759.2 3.8 dynamic-slice_convert_fusion.2
  763.2 9.3 collective-permute-done.3
  773.6 9.3 collective-permute-done.4
  783.0 4.7 collective-permute-start.5
  787.7 9.5 collective-permute-done.5
  797.3 9.1 collective-permute-done.6
  806.5 3.7 add_bitcast_fusion.1
  810.2 5.3 collective-permute-done.7
  817.9 30.5 %collective-permute-done.8 = f32[73728]{0:T(1024)S(1)} collective-permute-done((f32[73728]{0:T(1024)S(1)}, f32[73728]{0:T(1024)S(1)}, u32[]{:S(2)}, u32[]{:S(2)}) %collective-permute-start.8) | collective-permute-done | bytes 294944 | tf_op jit(solution)/shard_map/ppermute | solution.py:226
  849.7 5.7 add_bitcast_fusion
  855.3 5.4 copy.103
  862.7 156.4 %all-reduce.3.cloned.1.call-done = (bf16[3,2048,2048]{1,2,0:T(8,128)(2,1)}, bf16[2048,2048]{1,0:T(8,128)(2,1)}) async-done(((bf16[3,2048,2048]{1,2,0:T(8,128)(2,1)}, bf16[2048,2048]{1,0:T(8,128)(2,1)}), (bf16[3,2048,2048]{1,2,0:T(8,128)(2,1)}, bf16[2048,2048]{1,0:T(8,128)(2,1)})) %all-reduce.3.cloned.1.call-update) | async-done | bytes 33554448 | tf_op jit(solution)/shard_map/psum | solution.py:462
  (214 shorter events, 99.8 us)
Async XLA Ops:
  7.2 284.6 %copy-start = (bf16[2048,32]{0,1:T(8,128)(2,1)S(1)}, bf16[2048,32]{0,1:T(8,128)(2,1)}, u32[]{:S(2)}) copy-start(bf16[2048,32]{0,1:T(8,128)(2,1)} %param.23) | copy-start | bytes 393220
  7.2 17.8 %copy-start.9 = (bf16[1,128,2048]{2,1,0:T(8,128)(2,1)S(1)}, bf16[1,128,2048]{2,1,0:T(8,128)(2,1)}, u32[]{:S(2)}) copy-start(bf16[1,128,2048]{2,1,0:T(8,128)(2,1)} %param.13) | copy-start | bytes 1572868
  7.2 17.8 %copy-start.33 = (f32[2048]{0:T(1024)S(1)}, f32[2048]{0:T(1024)}, u32[]{:S(2)}) copy-start(f32[2048]{0:T(1024)} %param.17) | copy-start | bytes 24580
  7.2 9.4 copy-start.38
  7.2 245.2 %all-gather.2.cloned.1.call-start = ((), (), s32[]{:S(2)}) async-start(), calls=%async_computation.4 | async-start | bytes 33816576 | tf_op jit(solution)/shard_map/all_gather | solution.py:265
  10.3 15.1 %copy-start.39 = (f32[128]{0:T(128)}, f32[128]{0:T(128)S(1)}, u32[]{:S(2)}) copy-start(f32[128]{0:T(128)S(1)} %add_rsqrt_fusion.4) | copy-start | bytes 1540
  11.5 14.9 %copy-start.24 = (bf16[128,2048]{1,0:T(8,128)(2,1)}, bf16[128,2048]{1,0:T(8,128)(2,1)S(1)}, u32[]{:S(2)}) copy-start(bf16[128,2048]{1,0:T(8,128)(2,1)S(1)} %fusion.54) | copy-start | bytes 1572868
  11.6 13.4 %collective-permute-start = (bf16[128,2048]{1,0:T(8,128)(2,1)S(1)}, bf16[128,2048]{1,0:T(8,128)(2,1)S(1)}, u32[]{:S(2)}, u32[]{:S(2)}) collective-permute-start(bf16[128,2048]{1,0:T(8,128)(2,1)S(1)} %fusion.54), channel_id=1, source_target_pairs={{0,32},{32,0},{1,33},{33,1},{2,34},{34,2},{3,35},{35,3},{4,36},{36... | collective-permute-start | bytes 1572872 | tf_op jit(solution)/shard_map/ppermute | solution.py:199
  16.0 251.2 %copy-start.29 = (s32[128,8]{1,0:T(8,128)}, s32[128,8]{1,0:T(8,128)S(1)}, u32[]{:S(2)}) copy-start(s32[128,8]{1,0:T(8,128)S(1)} %fusion.93.slot_ref) | copy-start | bytes 12292
  271.1 8.6 copy-start.19
  277.4 2.3 copy-start.36
  284.1 6.6 copy-start.30
  284.1 8.0 copy-start.35
  290.6 8.5 copy-start.5
  368.9 72.6 %all-to-all-start.2 = ((bf16[32,40,2048]{2,1,0:T(8,128)(2,1)}), bf16[32,40,2048]{2,1,0:T(8,128)(2,1)}, u32[]{:S(2)}, u32[]{:S(2)}) async-start(bf16[32,40,2048]{2,1,0:T(8,128)(2,1)} %bitcast.225), calls=%async_computation.2 | async-start | bytes 10485760 | tf_op jit(solution)/shard_map/all_to_all | solution.py:353
  390.9 5.0 copy-start.3
  390.9 6.5 copy-start.44
  441.5 73.8 %all-to-all-start.1 = ((bf16[32,40,2048]{2,1,0:T(8,128)(2,1)}), bf16[32,40,2048]{2,1,0:T(8,128)(2,1)}, u32[]{:S(2)}, u32[]{:S(2)}) async-start(bf16[32,40,2048]{2,1,0:T(8,128)(2,1)} %bitcast.224), calls=%async_computation.1 | async-start | bytes 10485760 | tf_op jit(solution)/shard_map/all_to_all | solution.py:341
  461.5 2.3 copy-start.46
  515.3 8.5 copy-start.37
  515.3 9.2 copy-start.43
  515.3 73.6 %all-to-all-start.3 = ((bf16[32,40,2048]{2,1,0:T(8,128)(2,1)}), bf16[32,40,2048]{2,1,0:T(8,128)(2,1)}, u32[]{:S(2)}, u32[]{:S(2)}) async-start(bf16[32,40,2048]{2,1,0:T(8,128)(2,1)} %bitcast.223), calls=%async_computation.3 | async-start | bytes 10485760 | tf_op jit(solution)/shard_map/all_to_all | solution.py:376
  523.6 495.5 %all-reduce.3.cloned.1.call-start = ((), (), s32[]{:S(2)}) async-start(), calls=%async_computation.5 | async-start | bytes 67108864 | tf_op jit(solution)/shard_map/psum | solution.py:462
  589.6 5.7 copy-start.6
  620.4 14.3 %collective-permute-start.1 = (bf16[128,2048]{0,1:T(8,128)(2,1)}, bf16[128,2048]{0,1:T(8,128)(2,1)}, u32[]{:S(2)}, u32[]{:S(2)}) collective-permute-start(bf16[128,2048]{0,1:T(8,128)(2,1)} %bitcast.47), channel_id=1, source_target_pairs={{0,32},{32,0},{1,33},{33,1},{2,34},{34,2},{3,35},{35,3},{4,36},{36... | collective-permute-start | bytes 1572872 | tf_op jit(solution)/shard_map/ppermute | solution.py:199
  627.9 31.4 %collective-permute-start.2 = (bf16[128,2048]{1,0:T(8,128)(2,1)}, bf16[128,2048]{1,0:T(8,128)(2,1)}, u32[]{:S(2)}, u32[]{:S(2)}) collective-permute-start(bf16[128,2048]{1,0:T(8,128)(2,1)} %copy.113), channel_id=1, source_target_pairs={{0,32},{32,0},{1,33},{33,1},{2,34},{34,2},{3,35},{35,3},{4,36},{36... | collective-permute-start | bytes 1572872 | tf_op jit(solution)/shard_map/ppermute | solution.py:199
  635.9 5.8 copy-start.8
  651.1 2.3 copy-start.42
  653.3 2.9 copy-start.20
  653.3 2.9 copy-start.21
  660.5 13.4 %copy-start.25 = (bf16[128,1,2048]{2,0,1:T(8,128)(2,1)}, bf16[128,1,2048]{2,0,1:T(8,128)(2,1)S(1)}, u32[]{:S(2)}) copy-start(bf16[128,1,2048]{2,0,1:T(8,128)(2,1)S(1)} %fusion.78) | copy-start | bytes 1572868
  688.9 19.9 %copy-start.4 = (f32[2,1024,2048]{2,1,0:T(8,128)}, f32[2,1024,2048]{2,1,0:T(8,128)S(1)}, u32[]{:S(2)}) copy-start(f32[2,1024,2048]{2,1,0:T(8,128)S(1)} %fusion.23) | copy-start | bytes 50331652
  692.0 36.4 %collective-permute-start.10 = (bf16[2,1024,1024]{1,2,0:T(8,128)(2,1)}, bf16[2,1024,1024]{1,2,0:T(8,128)(2,1)}, u32[]{:S(2)}, u32[]{:S(2)}) collective-permute-start(bf16[2,1024,1024]{1,2,0:T(8,128)(2,1)} %fusion.18), channel_id=1, source_target_pairs={{0,64},{64,0},{1,65},{65,1},{2,66},{66,2},{3,67},{67,3},{4,68},{68... | collective-permute-start | bytes 12582920 | tf_op jit(solution)/shard_map/ppermute | solution.py:194
  708.8 3.3 copy-start.13
  712.1 7.9 collective-permute-start.12
  723.7 1.9 copy-start.2
  726.8 12.2 %copy-start.12 = (bf16[128,2048]{1,0:T(8,128)(2,1)S(1)}, bf16[128,2048]{1,0:T(8,128)(2,1)}, u32[]{:S(2)}) copy-start(bf16[128,2048]{1,0:T(8,128)(2,1)} %copy-done.11) | copy-start | bytes 1572868
  726.8 79.8 %collective-permute-start.13 = (bf16[1024,512]{1,0:T(8,128)(2,1)}, bf16[1024,512]{1,0:T(8,128)(2,1)}, u32[]{:S(2)}, u32[]{:S(2)}) collective-permute-start(bf16[1024,512]{1,0:T(8,128)(2,1)} %dynamic-slice_convert_fusion.3), channel_id=1, source_target_pairs={{0,32},{32,0},{1,33},{33,1},{2,34},{34,2},{3,35},{35,3},{4,36},{36... | collective-permute-start | bytes 3145736 | tf_op jit(solution)/shard_map/ppermute | solution.py:194
  759.1 13.4 %collective-permute-start.3 = (f32[73728]{0:T(1024)S(1)}, f32[73728]{0:T(1024)S(1)}, u32[]{:S(2)}, u32[]{:S(2)}) collective-permute-start(f32[73728]{0:T(1024)S(1)} %constant_dynamic-update-slice_fusion), channel_id=1, source_target_pairs={{0,1},{1,0},{2,3},{3,2},{4,5},{5,4},{6,7},{7,6},{8,9},{9,8},{10,11... | collective-permute-start | bytes 884744 | tf_op jit(solution)/shard_map/ppermute | solution.py:226
  763.0 86.7 %collective-permute-start.11 = (bf16[2,512,1024]{1,2,0:T(8,128)(2,1)}, bf16[2,512,1024]{1,2,0:T(8,128)(2,1)}, u32[]{:S(2)}, u32[]{:S(2)}) collective-permute-start(bf16[2,512,1024]{1,2,0:T(8,128)(2,1)} %dynamic-slice_convert_fusion.2), channel_id=1, source_target_pairs={{0,32},{32,0},{1,33},{33,1},{2,34},{34,2},{3,35},{35,3},{4,36},{36... | collective-permute-start | bytes 6291464 | tf_op jit(solution)/shard_map/ppermute | solution.py:194
  772.6 10.4 %collective-permute-start.4 = (f32[73728]{0:T(1024)S(1)}, f32[73728]{0:T(1024)S(1)}, u32[]{:S(2)}, u32[]{:S(2)}) collective-permute-start(f32[73728]{0:T(1024)S(1)} %add.185), channel_id=1, source_target_pairs={{0,2},{1,3},{2,0},{3,1},{4,6},{5,7},{6,4},{7,5},{8,10},{9,11},{10,... | collective-permute-start | bytes 884744 | tf_op jit(solution)/shard_map/ppermute | solution.py:226
  783.0 14.2 %collective-permute-start.5 = (f32[73728]{0:T(1024)S(1)}, f32[73728]{0:T(1024)S(1)}, u32[]{:S(2)}, u32[]{:S(2)}) collective-permute-start(f32[73728]{0:T(1024)S(1)} %add.186), channel_id=1, source_target_pairs={{0,4},{1,5},{2,6},{3,7},{4,0},{5,1},{6,2},{7,3},{8,12},{9,13},{10,... | collective-permute-start | bytes 884744 | tf_op jit(solution)/shard_map/ppermute | solution.py:226
  797.2 9.2 collective-permute-start.6
  806.4 10.1 copy-start.27
  806.4 9.1 collective-permute-start.7
  815.6 32.8 %collective-permute-start.8 = (f32[73728]{0:T(1024)S(1)}, f32[73728]{0:T(1024)S(1)}, u32[]{:S(2)}, u32[]{:S(2)}) collective-permute-start(f32[73728]{0:T(1024)S(1)} %add.189), channel_id=1, source_target_pairs={{0,32},{1,33},{2,34},{3,35},{4,36},{5,37},{6,38},{7,39},{8,40},{9,... | collective-permute-start | bytes 884744 | tf_op jit(solution)/shard_map/ppermute | solution.py:226
  848.4 12.3 %collective-permute-start.9 = (f32[73728]{0:T(1024)S(1)}, f32[73728]{0:T(1024)S(1)}, u32[]{:S(2)}, u32[]{:S(2)}) collective-permute-start(f32[73728]{0:T(1024)S(1)} %add.190), channel_id=1, source_target_pairs={{0,64},{1,65},{2,66},{3,67},{4,68},{5,69},{6,70},{7,71},{8,72},{9,... | collective-permute-start | bytes 884744 | tf_op jit(solution)/shard_map/ppermute | solution.py:226
  1019.1 5.2 copy-start.1
  (18 other events, 24.5 us)
Sparse Core Ops, SparseCore 0:
  10.4 242.0 all-gather.1
  674.0 345.0 all-reduce.2

commit v16 on v14

--- a/solution.py
+++ b/solution.py
@@ -184,6 +184,43 @@
             bytes_accessed=2 * count * width + 10 * tokens * width,
         ),
     )(slots, weights, table, base, other)
+
+
+def _sum_rows_kernel(slot_ref, table_ref, base_ref, out_ref):
+    tokens, top = slot_ref.shape
+    chunk = table_ref.shape[0]
+    column = pl.program_id(0) * chunk + lax.broadcasted_iota(jnp.int32, (tokens, chunk), 1)
+    hit = slot_ref[:, 0:1] == column
+    for k in range(1, top):
+        hit = hit | (slot_ref[:, k : k + 1] == column)
+    part = jnp.dot(hit.astype(jnp.bfloat16), table_ref[...], preferred_element_type=jnp.float32)
+
+    @pl.when(pl.program_id(0) == 0)
+    def _():
+        out_ref[...] = base_ref[...]
+
+    out_ref[...] += part
+
+
+def sum_rows(slots, table, base, chunk=256):
+    tokens, top = slots.shape
+    count, width = table.shape
+    return pl.pallas_call(
+        _sum_rows_kernel,
+        out_shape=jax.ShapeDtypeStruct((tokens, width), jnp.float32),
+        grid=(count // chunk,),
+        in_specs=[
+            pl.BlockSpec((tokens, top), lambda i: (0, 0)),
+            pl.BlockSpec((chunk, width), lambda i: (i, 0)),
+            pl.BlockSpec((tokens, width), lambda i: (0, 0)),
+        ],
+        out_specs=pl.BlockSpec((tokens, width), lambda i: (0, 0)),
+        cost_estimate=pl.CostEstimate(
+            flops=2 * tokens * count * width,
+            transcendentals=0,
+            bytes_accessed=2 * count * width + 8 * tokens * width,
+        ),
+    )(slots, table, base)
 
 
 def sum_halves(values, axis, dim):
@@ -390,13 +427,10 @@
     grad_router = jnp.einsum(
         "td,te->de", ffn_in, grad_logits, preferred_element_type=single_precision
     )
-    grad_ffn_in, _ = combine(
+    grad_ffn_in = sum_rows(
         route_slots,
-        jnp.ones((seq_tok, top), single_precision),
         grad_back.reshape(experts * capacity, width),
         jnp.einsum("te,de->td", grad_logits, router_weight, preferred_element_type=single_precision),
-        grad_output[0],
-        False,
     )
     grad_mid_norm, grad_ffn_gain = rms_backward(grad_ffn_in, normed2, factor2, ffn_gain)
     grad_mid = grad + grad_mid_norm

time: 1030 us -> 1030 us (level)
    unnamed x131 -> x133, local copies, waits for them, and re-layouts: 28.2 us -> 28.3 us
where the time goes in v16:
time: 1030 us; the launch traced here: 1020 us
  waiting for transfers between devices  592 us (57%)
  matrix products  138 us (13%)
  blocking collectives  69.4 us (7%)
  other arithmetic  67.1 us (7%)
  local copies, waits for them, and re-layouts  51.7 us (5%)
  starting transfers between devices  50.7 us (5%)
  Pallas kernels  38.5 us (4%)
  between operations  15.3 us (1%)
    all_gather x1, waiting for transfers between devices, body(): lax.all_gather(jnp.concatenate([qkv_weight.transpose(1, 0, 2), out_weight...  226 us
    psum x1, waiting for transfers between devices, body(): summed = lax.psum(stacked.astype(bf16), all_axes)  160 us
    ppermute x7, waiting for transfers between devices, butterfly_sum(): received = lax.ppermute(values, axes, partner)  71.8 us
    all_to_all x1, blocking collectives, body(): lax.all_to_all(send.reshape(sources, local_experts * capacity, width), 'e...  69.4 us
    all_to_all x1, waiting for transfers between devices, body(): lax.all_to_all(source_major(grad_rows_in, sources, capacity), 'expert', s...  46.4 us
    all_to_all x1, waiting for transfers between devices, body(): lax.all_to_all(grad_send.reshape(sources, local_experts * capacity, width...  36.7 us
    all_to_all x1, waiting for transfers between devices, body(): lax.all_to_all(source_major(results, sources, capacity), 'expert', split_...  36.6 us
    unnamed x133, local copies, waits for them, and re-layouts  28.3 us
  transfers between devices with their start and end apart: 19, of which 14 were waited for; matrix products, arithmetic and copies ran while one was open for 17% of the time, Pallas kernels for 1%

profile of v16, /device:TPU:1, one launch (start us, length us, event | category | flops | bytes accessed | tf_op | source)
XLA Modules:
  0.0 1022.5 jit_solution(343860012010358171)
XLA Ops:
  19.5 5.5 collective-permute-done
  26.5 226.2 %all-gather.2.cloned.1.call-done = bf16[2048,4,2048]{2,0,1:T(8,128)(2,1)} async-done(((bf16[16,4,2048]{2,0,1:T(8,128)(2,1)}), bf16[2048,4,2048]{2,0,1:T(8,128)(2,1)}) %all-gather.2.cloned.1.call-update) | async-done | bytes 33554448 | tf_op jit(solution)/shard_map/all_gather | solution.py:302
  252.7 14.7 %shard_map.215 = f32[3,256,2048]{2,1,0:T(8,128)} custom-call(bf16[256,2048]{1,0:T(8,128)(2,1)} %pad_maximum_fusion.inputs_ref, bf16[4,2048,2048]{2,1,0:T(8,128)(2,1)} %bitcast.243), custom_call_target="tpu_custom_call" | custom-call | flops 6442450944 | bytes 32505856 | tf_op jit(solution)/shard_map/pallas_call | solution.py:83
  279.8 3.5 convolution_convert_fusion.2
  283.4 6.5 multiply_reduce_fusion.9
  291.1 6.3 shard_map.216
  297.4 69.4 %all_to_all.20 = bf16[32,40,2048]{2,1,0:T(8,128)(2,1)} all-to-all(bf16[32,40,2048]{2,1,0:T(8,128)(2,1)} %bitcast.250), channel_id=1, replica_groups=mesh['dp'=2,'context'=2,'expert'=32] {'expert'}, dimensions={0} | all-to-all | bytes 10485760 | tf_op jit(solution)/shard_map/all_to_all | solution.py:362
  366.8 5.1 all-to-all-start.2
  371.9 16.9 %fusion.6 = f32[1,2,1280,1024]{3,2,1,0:T(8,128)S(1)} fusion(bf16[1280,2048,1]{1,0,2:T(8,128)(2,1)} %bitcast.245, bf16[1,2,2048,1024]{3,2,1,0:T(8,128)(2,1)} %param.24), kind=kOutput, calls=%fused_computation.12 | convolution fusion | flops 10737418240 | bytes 24117248 | tf_op jit(solution)/shard_map/lrd,lkdh->lkrh/dot_general | solution.py:370
  390.5 3.3 copy-done.4
  395.3 7.3 convolution_convert_fusion.1
  402.6 36.7 %all-to-all-done.2 = bf16[32,40,2048]{2,1,0:T(8,128)(2,1)} async-done(((bf16[32,40,2048]{2,1,0:T(8,128)(2,1)}), bf16[32,40,2048]{2,1,0:T(8,128)(2,1)}, u32[]{:S(2)}, u32[]{:S(2)}) %all-to-all-start.2) | async-done | bytes 5242912 | tf_op jit(solution)/shard_map/all_to_all | solution.py:390
  439.4 6.7 all-to-all-start.1
  446.1 13.1 %fusion.28 = (bf16[1,1,1280,1024]{3,2,1,0:T(8,128)(2,1)S(1)}, bf16[1,1,1280,1024]{3,2,1,0:T(8,128)(2,1)S(1)}) fusion(f32[1,2,1280,1024]{3,2,1,0:T(8,128)} %copy-done.4, bf16[1280,2048]{1,0:T(8,128)(2,1)} %bitcast.31, bf16[1,1024,2048]{2,1,0:T(8,128)(2,1)} %param.25), kind=kOutput, calls=%fused_computation.43 | convolution fusion | flops 5385748480 | bytes 25165824 | tf_op jit(solution)/shard_map/lrd,lhd->lrh/dot_general | solution.py:398
  461.5 15.1 %bitcast_convert_fusion = bf16[1280,2048]{1,0:T(8,128)(2,1)} fusion(bf16[1,2,2048,1024]{3,2,1,0:T(8,128)(2,1)} %param.24, bf16[1,1,1280,1024]{3,2,1,0:T(8,128)(2,1)S(1)} %get-tuple-element.69, bf16[1,1,1280,1024]{3,2,1,0:T(8,128)(2,1)S(1)} %get-tuple-element.68), kind=kOutput, calls=%fused_computation.2 | convolution fusion | flops 10742661120 | bytes 18874368 | tf_op jit(solution)/shard_map/lkrh,lkdh->lrd/dot_general | solution.py:410
  476.6 36.6 %all-to-all-done.1 = bf16[32,40,2048]{2,1,0:T(8,128)(2,1)} async-done(((bf16[32,40,2048]{2,1,0:T(8,128)(2,1)}), bf16[32,40,2048]{2,1,0:T(8,128)(2,1)}, u32[]{:S(2)}, u32[]{:S(2)}) %all-to-all-start.1) | async-done | bytes 5242912 | tf_op jit(solution)/shard_map/all_to_all | solution.py:378
  513.3 7.4 all-to-all-start.3
  526.9 10.2 shard_map.217
  539.4 46.4 %all-to-all-done.3 = bf16[32,40,2048]{2,1,0:T(8,128)(2,1)} async-done(((bf16[32,40,2048]{2,1,0:T(8,128)(2,1)}), bf16[32,40,2048]{2,1,0:T(8,128)(2,1)}, u32[]{:S(2)}, u32[]{:S(2)}) %all-to-all-start.3) | async-done | bytes 5242912 | tf_op jit(solution)/shard_map/all_to_all | solution.py:413
  585.8 7.3 shard_map.218
  598.0 4.7 fusion.30
  603.2 4.8 convolution_bitcast_fusion.1
  618.0 5.9 collective-permute-start.1
  623.9 3.6 fusion.52
  627.7 4.9 collective-permute-done.1
  636.3 3.3 multiply_subtract_fusion.1
  646.6 2.9 multiply_reduce_fusion.2
  653.5 14.7 %convolution_convert_fusion = bf16[4,2048,2048]{2,1,0:T(8,128)(2,1)} fusion(bf16[1,128,2048]{2,1,0:T(8,128)(2,1)S(1)} %copy-done.27, bf16[1,128,2048]{2,1,0:T(8,128)(2,1)S(1)} %copy-done.28, bf16[1,128,2048]{2,1,0:T(8,128)(2,1)S(1)} %copy-done.29, bf16[3,128,2048]{2,1,0:T(8,128)(2,1)S(1)} %maximum_bitcast_fusion.3), kind=kOutput, calls=%fused_computation.1 | convolution fusion | flops 4315938816 | bytes 36700160 | tf_op jit(solution)/shard_map/sta,stb->sab/dot_general | solution.py:491
  668.2 15.0 %fusion.23 = f32[2,1024,2048]{2,1,0:T(8,128)S(1)} fusion(bf16[1280,2048,1]{1,0,2:T(8,128)(2,1)} %bitcast.246, bf16[1,1,1280,1024]{3,2,1,0:T(8,128)(2,1)} %copy-done.59, bf16[1,1,1280,1024]{3,2,1,0:T(8,128)(2,1)} %copy-done.58), kind=kOutput, calls=%fused_computation.38 | convolution fusion | flops 10740039680 | bytes 27262976 | tf_op jit(solution)/shard_map/lrd,lkrh->lkdh/dot_general | solution.py:407
  686.0 8.2 collective-permute-start.10
  694.3 7.9 fusion.24
  702.5 3.0 copy-done.15
  705.5 3.1 collective-permute-start.12
  708.6 4.0 collective-permute-done.12
  712.6 3.7 convert_add_fusion
  721.1 11.1 %bitcast_add_fusion = f32[2,1024,1024]{1,2,0:T(8,128)} fusion(bf16[2,1024,1024]{1,2,0:T(8,128)(2,1)} %collective-permute-done.10, f32[2,1024,2048]{2,1,0:T(8,128)} %copy-done.10, s32[]{:T(128)S(6)} %select_n.102), kind=kLoop, calls=%fused_computation.4 | loop fusion | flops 4194304 | bytes 20971524 | tf_op jit(solution)/shard_map/add | solution.py:232
  733.4 17.2 %fusion.68 = (f32[2048]{0:T(1024)S(1)}, f32[128]{0:T(128)S(1)}, f32[128,2048]{1,0:T(8,128)}) fusion(bf16[1,128,2048]{2,1,0:T(8,128)(2,1)S(1)} %copy-done.2, f32[128]{0:T(128)S(1)} %copy-done.52, f32[2048]{0:T(1024)S(1)} %copy-done.42, bf16[2048,4,2048]{2,0,1:T(8,128)(2,1)} %all-gather.2.cloned.1.call-done, bf16[128,1,2048]{2,0,1:T(8,128)(2,1)S(1)} %fusion.88, ...), kind=kOutput, calls=%fused_computation.102 | convolution fusion | flops 4299945984 | bytes 36717576 | tf_op jit(solution)/shard_map/dot_general | solution.py:473
  753.8 11.2 %collective-permute-done.3 = f32[73728]{0:T(1024)S(1)} collective-permute-done((f32[73728]{0:T(1024)S(1)}, f32[73728]{0:T(1024)S(1)}, u32[]{:S(2)}, u32[]{:S(2)}) %collective-permute-start.3) | collective-permute-done | bytes 294944 | tf_op jit(solution)/shard_map/ppermute | solution.py:263
  765.9 8.4 collective-permute-done.4
  774.3 6.2 collective-permute-start.5
  780.6 9.8 collective-permute-done.5
  790.5 9.3 collective-permute-done.6
  801.2 3.6 add_bitcast_fusion.1
  804.8 5.2 collective-permute-done.7
  811.6 27.8 %collective-permute-done.8 = f32[73728]{0:T(1024)S(1)} collective-permute-done((f32[73728]{0:T(1024)S(1)}, f32[73728]{0:T(1024)S(1)}, u32[]{:S(2)}, u32[]{:S(2)}) %collective-permute-start.8) | collective-permute-done | bytes 294944 | tf_op jit(solution)/shard_map/ppermute | solution.py:263
  840.4 5.7 add_bitcast_fusion
  846.1 5.4 copy.103
  853.5 159.5 %all-reduce.2.cloned.1.call-done = bf16[4,2048,2048]{2,1,0:T(8,128)(2,1)} async-done(((bf16[4,2048,2048]{2,1,0:T(8,128)(2,1)}), bf16[4,2048,2048]{2,1,0:T(8,128)(2,1)}) %all-reduce.2.cloned.1.call-update) | async-done | bytes 33554448 | tf_op jit(solution)/shard_map/psum | solution.py:492
  (241 shorter events, 92.9 us)
Async XLA Ops:
  7.2 283.0 %copy-start = (bf16[2048,32]{0,1:T(8,128)(2,1)S(1)}, bf16[2048,32]{0,1:T(8,128)(2,1)}, u32[]{:S(2)}) copy-start(bf16[2048,32]{0,1:T(8,128)(2,1)} %param.23) | copy-start | bytes 393220
  7.2 17.8 %copy-start.2 = (bf16[1,128,2048]{2,1,0:T(8,128)(2,1)S(1)}, bf16[1,128,2048]{2,1,0:T(8,128)(2,1)}, u32[]{:S(2)}) copy-start(bf16[1,128,2048]{2,1,0:T(8,128)(2,1)} %param.13) | copy-start | bytes 1572868
  7.2 17.8 %copy-start.42 = (f32[2048]{0:T(1024)S(1)}, f32[2048]{0:T(1024)}, u32[]{:S(2)}) copy-start(f32[2048]{0:T(1024)} %param.17) | copy-start | bytes 24580
  7.2 9.4 copy-start.53
  7.2 245.4 %all-gather.2.cloned.1.call-start = ((), (), s32[]{:S(2)}) async-start(), calls=%async_computation.4 | async-start | bytes 33816576 | tf_op jit(solution)/shard_map/all_gather | solution.py:302
  10.3 15.1 %copy-start.50 = (f32[128]{0:T(128)}, f32[128]{0:T(128)S(1)}, u32[]{:S(2)}) copy-start(f32[128]{0:T(128)S(1)} %add_rsqrt_fusion.4) | copy-start | bytes 1540
  11.5 13.4 %collective-permute-start = (bf16[128,2048]{1,0:T(8,128)(2,1)S(1)}, bf16[128,2048]{1,0:T(8,128)(2,1)S(1)}, u32[]{:S(2)}, u32[]{:S(2)}) collective-permute-start(bf16[128,2048]{1,0:T(8,128)(2,1)S(1)} %fusion.62), channel_id=1, source_target_pairs={{0,32},{32,0},{1,33},{33,1},{2,34},{34,2},{3,35},{35,3},{4,36},{36... | collective-permute-start | bytes 1572872 | tf_op jit(solution)/shard_map/ppermute | solution.py:236
  16.0 251.4 %copy-start.38 = (s32[128,8]{1,0:T(8,128)}, s32[128,8]{1,0:T(8,128)S(1)}, u32[]{:S(2)}) copy-start(s32[128,8]{1,0:T(8,128)S(1)} %fusion.101.slot_ref) | copy-start | bytes 12292
  271.2 8.6 copy-start.22
  283.4 6.6 copy-start.31
  283.4 6.6 copy-start.43
  283.4 7.1 copy-start.47
  289.9 7.5 copy-start.7
  366.8 72.5 %all-to-all-start.2 = ((bf16[32,40,2048]{2,1,0:T(8,128)(2,1)}), bf16[32,40,2048]{2,1,0:T(8,128)(2,1)}, u32[]{:S(2)}, u32[]{:S(2)}) async-start(bf16[32,40,2048]{2,1,0:T(8,128)(2,1)} %bitcast.249), calls=%async_computation.2 | async-start | bytes 10485760 | tf_op jit(solution)/shard_map/all_to_all | solution.py:390
  388.8 5.0 copy-start.4
  388.8 6.5 copy-start.57
  439.4 73.9 %all-to-all-start.1 = ((bf16[32,40,2048]{2,1,0:T(8,128)(2,1)}), bf16[32,40,2048]{2,1,0:T(8,128)(2,1)}, u32[]{:S(2)}, u32[]{:S(2)}) async-start(bf16[32,40,2048]{2,1,0:T(8,128)(2,1)} %bitcast.248), calls=%async_computation.1 | async-start | bytes 10485760 | tf_op jit(solution)/shard_map/all_to_all | solution.py:378
  513.3 7.6 copy-start.51
  513.3 8.6 copy-start.49
  513.3 11.4 %copy-start.56 = (f32[128]{0:T(128)S(1)}, f32[128]{0:T(128)}, u32[]{:S(2)}) copy-start(f32[128]{0:T(128)} %get-tuple-element.58) | copy-start | bytes 1540
  513.3 11.4 %copy-start.30 = (f32[16,128,256]{2,1,0:T(8,128)S(1)}, f32[16,128,256]{2,1,0:T(8,128)}, u32[]{:S(2)}) copy-start(f32[16,128,256]{2,1,0:T(8,128)} %fusion.100) | copy-start | bytes 6291460
  513.3 72.6 %all-to-all-start.3 = ((bf16[32,40,2048]{2,1,0:T(8,128)(2,1)}), bf16[32,40,2048]{2,1,0:T(8,128)(2,1)}, u32[]{:S(2)}, u32[]{:S(2)}) async-start(bf16[32,40,2048]{2,1,0:T(8,128)(2,1)} %bitcast.247), calls=%async_computation.3 | async-start | bytes 10485760 | tf_op jit(solution)/shard_map/all_to_all | solution.py:413
  520.6 492.4 %all-reduce.2.cloned.1.call-start = ((), (), s32[]{:S(2)}) async-start(), calls=%async_computation.5 | async-start | bytes 67108864 | tf_op jit(solution)/shard_map/psum | solution.py:492
  585.8 7.3 copy-start.8
  598.0 5.0 copy-start.32
  603.0 4.9 copy-start.23
  618.0 14.6 %collective-permute-start.1 = (bf16[128,2048]{0,1:T(8,128)(2,1)}, bf16[128,2048]{0,1:T(8,128)(2,1)S(1)}, u32[]{:S(2)}, u32[]{:S(2)}) collective-permute-start(bf16[128,2048]{0,1:T(8,128)(2,1)} %bitcast.264), channel_id=1, source_target_pairs={{0,32},{32,0},{1,33},{33,1},{2,34},{34,2},{3,35},{35,3},{4,36},{36... | collective-permute-start | bytes 1572872 | tf_op jit(solution)/shard_map/ppermute | solution.py:236
  623.9 27.8 %collective-permute-start.2 = (bf16[128,2048]{1,0:T(8,128)(2,1)}, bf16[128,2048]{1,0:T(8,128)(2,1)}, u32[]{:S(2)}, u32[]{:S(2)}) collective-permute-start(bf16[128,2048]{1,0:T(8,128)(2,1)} %copy.113), channel_id=1, source_target_pairs={{0,32},{32,0},{1,33},{33,1},{2,34},{34,2},{3,35},{35,3},{4,36},{36... | collective-permute-start | bytes 1572872 | tf_op jit(solution)/shard_map/ppermute | solution.py:236
  632.7 3.6 copy-start.11
  632.7 3.6 copy-start.40
  683.2 18.9 %copy-start.10 = (f32[2,1024,2048]{2,1,0:T(8,128)}, f32[2,1024,2048]{2,1,0:T(8,128)S(1)}, u32[]{:S(2)}) copy-start(f32[2,1024,2048]{2,1,0:T(8,128)S(1)} %fusion.23) | copy-start | bytes 50331652
  683.2 11.1 %copy-start.26 = (bf16[1,1,1280,1024]{3,2,1,0:T(8,128)(2,1)S(1)}, bf16[1,1,1280,1024]{3,2,1,0:T(8,128)(2,1)}, u32[]{:S(2)}) copy-start(bf16[1,1,1280,1024]{3,2,1,0:T(8,128)(2,1)} %copy-done.25) | copy-start | bytes 7864324
  686.0 35.1 %collective-permute-start.10 = (bf16[2,1024,1024]{1,2,0:T(8,128)(2,1)}, bf16[2,1024,1024]{1,2,0:T(8,128)(2,1)}, u32[]{:S(2)}, u32[]{:S(2)}) collective-permute-start(bf16[2,1024,1024]{1,2,0:T(8,128)(2,1)} %fusion.18), channel_id=1, source_target_pairs={{0,64},{64,0},{1,65},{65,1},{2,66},{66,2},{3,67},{67,3},{4,68},{68... | collective-permute-start | bytes 12582920 | tf_op jit(solution)/shard_map/ppermute | solution.py:231
  702.2 3.3 copy-start.15
  705.5 7.1 collective-permute-start.12
  719.4 12.8 %copy-start.14 = (bf16[128,2048]{1,0:T(8,128)(2,1)S(1)}, bf16[128,2048]{1,0:T(8,128)(2,1)}, u32[]{:S(2)}) copy-start(bf16[128,2048]{1,0:T(8,128)(2,1)} %copy-done.13) | copy-start | bytes 1572868
  719.4 81.8 %collective-permute-start.13 = (bf16[1024,512]{1,0:T(8,128)(2,1)}, bf16[1024,512]{1,0:T(8,128)(2,1)}, u32[]{:S(2)}, u32[]{:S(2)}) collective-permute-start(bf16[1024,512]{1,0:T(8,128)(2,1)} %dynamic-slice_convert_fusion.3), channel_id=1, source_target_pairs={{0,32},{32,0},{1,33},{33,1},{2,34},{34,2},{3,35},{35,3},{4,36},{36... | collective-permute-start | bytes 3145736 | tf_op jit(solution)/shard_map/ppermute | solution.py:231
  750.6 14.4 %collective-permute-start.3 = (f32[73728]{0:T(1024)S(1)}, f32[73728]{0:T(1024)S(1)}, u32[]{:S(2)}, u32[]{:S(2)}) collective-permute-start(f32[73728]{0:T(1024)S(1)} %constant_dynamic-update-slice_fusion), channel_id=1, source_target_pairs={{0,1},{1,0},{2,3},{3,2},{4,5},{5,4},{6,7},{7,6},{8,9},{9,8},{10,11... | collective-permute-start | bytes 884744 | tf_op jit(solution)/shard_map/ppermute | solution.py:263
  753.7 86.7 %collective-permute-start.11 = (bf16[2,512,1024]{1,2,0:T(8,128)(2,1)S(1)}, bf16[2,512,1024]{1,2,0:T(8,128)(2,1)}, u32[]{:S(2)}, u32[]{:S(2)}) collective-permute-start(bf16[2,512,1024]{1,2,0:T(8,128)(2,1)S(1)} %dynamic-slice_convert_fusion.2), channel_id=1, source_target_pairs={{0,32},{32,0},{1,33},{33,1},{2,34},{34,2},{3,35},{35,3},{4,36},{36... | collective-permute-start | bytes 6291464 | tf_op jit(solution)/shard_map/ppermute | solution.py:231
  765.0 9.2 collective-permute-start.4
  774.3 16.1 %collective-permute-start.5 = (f32[73728]{0:T(1024)S(1)}, f32[73728]{0:T(1024)S(1)}, u32[]{:S(2)}, u32[]{:S(2)}) collective-permute-start(f32[73728]{0:T(1024)S(1)} %add.183), channel_id=1, source_target_pairs={{0,4},{1,5},{2,6},{3,7},{4,0},{5,1},{6,2},{7,3},{8,12},{9,13},{10,... | collective-permute-start | bytes 884744 | tf_op jit(solution)/shard_map/ppermute | solution.py:263
  790.4 9.4 collective-permute-start.6
  799.8 10.3 %copy-start.20 = (f32[128,2048]{1,0:T(8,128)S(1)}, f32[128,2048]{1,0:T(8,128)}, u32[]{:S(2)}) copy-start(f32[128,2048]{1,0:T(8,128)} %copy-done.19) | copy-start | bytes 3145732
  799.9 10.3 %copy-start.37 = (f32[128,2048]{1,0:T(8,128)S(1)}, f32[128,2048]{1,0:T(8,128)}, u32[]{:S(2)}) copy-start(f32[128,2048]{1,0:T(8,128)} %get-tuple-element.102) | copy-start | bytes 3145732
  799.9 10.2 collective-permute-start.7
  810.1 29.3 %collective-permute-start.8 = (f32[73728]{0:T(1024)S(1)}, f32[73728]{0:T(1024)S(1)}, u32[]{:S(2)}, u32[]{:S(2)}) collective-permute-start(f32[73728]{0:T(1024)S(1)} %add.186), channel_id=1, source_target_pairs={{0,32},{1,33},{2,34},{3,35},{4,36},{5,37},{6,38},{7,39},{8,40},{9,... | collective-permute-start | bytes 884744 | tf_op jit(solution)/shard_map/ppermute | solution.py:263
  839.4 12.1 %collective-permute-start.9 = (f32[73728]{0:T(1024)S(1)}, f32[73728]{0:T(1024)S(1)}, u32[]{:S(2)}, u32[]{:S(2)}) collective-permute-start(f32[73728]{0:T(1024)S(1)} %add.187), channel_id=1, source_target_pairs={{0,64},{1,65},{2,66},{3,67},{4,68},{5,69},{6,70},{7,71},{8,72},{9,... | collective-permute-start | bytes 884744 | tf_op jit(solution)/shard_map/ppermute | solution.py:263
  851.5 163.9 %copy-start.1 = (bf16[2048,32]{0,1:T(8,128)(2,1)S(1)}, bf16[2048,32]{0,1:T(8,128)(2,1)}, u32[]{:S(2)}) copy-start(bf16[2048,32]{0,1:T(8,128)(2,1)} %param.23) | copy-start | bytes 393220
  (31 other events, 51.7 us)
Sparse Core Ops, SparseCore 0:
  10.4 242.2 all-gather.1
  668.4 344.6 all-reduce.1
